TPU v7x, 512 devices: a whole 4x8x8 slice. The times are simulated.
512 devices in a mesh: ctx: 64 (over z, y_hi, core), dp: 8 (over y_lo, x).
Axes of the slice: x: 4, y: 8 (y_hi: 4, y_lo: 2; y = y_hi * 2 + y_lo), z: 8, core: 2. Of those that a mesh axis runs over, the one named last changes fastest.
Arguments:
- queries: bfloat16 [8, 8192, 512], P('dp', 'ctx'), may hold values from -8 to 8
- keys: bfloat16 [8, 8192, 128], P('dp', 'ctx'), may hold values from -8 to 8
- values: bfloat16 [8, 8192, 128], P('dp', 'ctx'), may hold values from -6 to 6
- grad_out: bfloat16 [8, 8192, 512], P('dp', 'ctx'), may hold values from -60 to 60
- doc_starts: int32 [8, 8], P('dp'), may hold values from 0 to 8064, as said below
Outputs:
- attended: bfloat16 [8, 8192, 512], P('dp', 'ctx')
- grad_queries: bfloat16 [8, 8192, 512], P('dp', 'ctx')
- grad_keys: bfloat16 [8, 8192, 128], P('dp', 'ctx')
- grad_values: bfloat16 [8, 8192, 128], P('dp', 'ctx')
Inputs may be any that keep to these rules, and one draw needn't show every extreme that they name: `doc_starts`: row b lists the first positions of the 8 documents packed in sequence b: the first is 0, they rise strictly, all are multiples of 128, and in some sequence the last document has exactly 128 tokens.
All inputs are finite; a program needn't handle non-finite values.
Results may differ from a plain program's by a relative error of at most 0.034.
Values may be sent and summed in bfloat16 or wider, within the bound.
No kernel may reach another device: no remote copies, remote signals or barrier semaphores. Data moves between devices by JAX's collectives and lax.ppermute only.
A program may use at most 64 MiB of HBM per device.

v0:
```python
import math

import jax
import jax.numpy as jnp
from jax import lax
from jax.sharding import PartitionSpec as P

masked_floor = -1e30


def from_behind(block, axis, distance):
    devices = range(lax.axis_size(axis))
    route = [((i - distance) % len(devices), i) for i in devices]
    return lax.ppermute(block, axis, route)


def zig_positions(index, tok, nctx):
    block = index // tok
    rest = index % tok
    half = tok // 2
    return jnp.where(rest < half, block * half + rest, (2 * nctx - 1 - block) * half + rest - half)


def doc_number(positions, starts):
    return jnp.sum((starts[None, :] <= positions[:, None]).astype(jnp.int32), axis=1) - 1


def per_device(queries, keys, values, grad_out, doc_starts):
    tok = queries.shape[1]
    width = keys.shape[2]
    heads = queries.shape[2] // width
    nctx = lax.axis_size("ctx")
    ndata = lax.axis_size("dp")
    me = lax.axis_index("ctx")
    scale = 1.0 / math.sqrt(width)
    query3 = queries[0].reshape(tok, heads, width)
    grad3 = grad_out[0].reshape(tok, heads, width)
    starts = doc_starts[0]
    local_rows = jnp.arange(tok, dtype=jnp.int32)
    query_pos = zig_positions(me * tok + local_rows, tok, nctx)
    query_doc = doc_number(query_pos, starts)

    def visible(owners):
        group = owners.shape[0]
        key_pos = zig_positions(
            (owners[:, None] * tok + local_rows[None, :]).reshape(group * tok), tok, nctx
        )
        key_doc = doc_number(key_pos, starts).reshape(group, tok)
        key_pos = key_pos.reshape(group, tok)
        allowed = (key_pos[None, :, :] <= query_pos[:, None, None]) & (
            key_doc[None, :, :] == query_doc[:, None, None]
        )
        return allowed[:, None, :, :]

    def logits_of(key_group):
        return (
            jnp.einsum("qhd,gkd->qhgk", query3, key_group, preferred_element_type=jnp.float32)
            * scale
        )

    def forward_terms(carry, key_group, value_group, owners):
        allowed = visible(owners)
        acc, run_max, run_sum = carry
        logits = logits_of(key_group)
        block_max = jnp.max(jnp.where(allowed, logits, masked_floor), axis=3)
        expd = jnp.where(allowed, jnp.exp(logits - block_max[:, :, :, None]), 0.0)
        part = jnp.einsum(
            "qhgk,gkd->qhgd",
            expd.astype(jnp.bfloat16),
            value_group,
            preferred_element_type=jnp.float32,
        )
        new_max = jnp.maximum(run_max, jnp.max(block_max, axis=2))
        old_w = jnp.exp(run_max - new_max)
        new_w = jnp.exp(block_max - new_max[:, :, None])
        acc = acc * old_w[:, :, None] + jnp.sum(part * new_w[:, :, :, None], axis=2)
        run_sum = run_sum * old_w + jnp.sum(jnp.sum(expd, axis=3) * new_w, axis=2)
        return (acc, new_max, run_sum)

    init = (
        jnp.zeros((tok, heads, width), jnp.float32),
        jnp.full((tok, heads), masked_floor, jnp.float32),
        jnp.zeros((tok, heads), jnp.float32),
    )
    key_piece = lax.all_gather(keys, "ctx", axis=1, tiled=True)
    value_piece = lax.all_gather(values, "ctx", axis=1, tiled=True)
    count = key_piece.shape[1] // tok
    group = math.gcd(count, 4)
    steps = count // group
    key_rows = key_piece[0].reshape(steps, group, tok, width)
    value_rows = value_piece[0].reshape(steps, group, tok, width)
    owner_rows = jnp.arange(count, dtype=jnp.int32).reshape(steps, group)

    def step(state, item):
        key_group, value_group, owners = item
        return (forward_terms(state, key_group, value_group, owners), None)

    state, _ = lax.scan(step, init, (key_rows, value_rows, owner_rows))
    acc, run_max, run_sum = state
    attended = (acc / run_sum[:, :, None]).astype(jnp.bfloat16)
    log_total = run_max + jnp.log(run_sum)
    delta = jnp.sum(grad3.astype(jnp.float32) * attended.astype(jnp.float32), axis=2)
    zero_query = jnp.zeros((tok, heads, width), jnp.float32)
    zero_group = jnp.zeros((2, 2, tok, width), jnp.float32)

    def backward_terms(blocks, owners):
        allowed = visible(owners)
        key_group = blocks[:, 0]
        value_group = blocks[:, 1]
        logits = logits_of(key_group)
        prob = jnp.where(allowed, jnp.exp(logits - log_total[:, :, None, None]), 0.0)
        grad_value = jnp.einsum(
            "qhgk,qhd->gkd", prob.astype(jnp.bfloat16), grad3, preferred_element_type=jnp.float32
        )
        grad_prob = jnp.einsum(
            "qhd,gkd->qhgk", grad3, value_group, preferred_element_type=jnp.float32
        )
        grad_logit = (prob * (grad_prob - delta[:, :, None, None]) * scale).astype(jnp.bfloat16)
        grad_query = jnp.einsum(
            "qhgk,gkd->qhd", grad_logit, key_group, preferred_element_type=jnp.float32
        )
        grad_key = jnp.einsum(
            "qhgk,qhd->gkd", grad_logit, query3, preferred_element_type=jnp.float32
        )
        return (grad_query, jnp.stack([grad_key, grad_value], axis=1))

    own_pair = jnp.stack([keys[0], values[0]])
    half_loop = nctx // 2
    behind = from_behind(own_pair, "ctx", 1)

    def visit_two(turn, state):
        grad_q, pairs, grads = state
        owners = jnp.stack([(me - 2 * turn) % nctx, (me - 2 * turn - 1) % nctx])
        query_part, group_grad = backward_terms(pairs, owners)
        return (grad_q + query_part, pairs, grads + group_grad)

    def advance_two(turn, state):
        grad_q, pairs, grads = visit_two(turn, state)
        moved_pairs = from_behind(pairs, "ctx", 2)
        moved_grads = from_behind(grads, "ctx", 2)
        return (grad_q, moved_pairs, moved_grads)

    state = (zero_query, jnp.stack([own_pair, behind]), zero_group)
    state = lax.fori_loop(0, half_loop - 1, advance_two, state)
    grad_q, _, grads = visit_two(half_loop - 1, state)
    far_part = from_behind(grads[0], "ctx", 2)
    near_part = from_behind(grads[1], "ctx", 1)
    key_value_grad = far_part + near_part
    grad_key = key_value_grad[0]
    grad_value = key_value_grad[1]
    local_squares = (
        jnp.sum(grad_q * grad_q) + jnp.sum(grad_key * grad_key) + jnp.sum(grad_value * grad_value)
    )
    total = lax.psum(local_squares, ("ctx", "dp"))
    count = float(ndata * nctx * tok * (heads * width + 2 * width))
    factor = lax.rsqrt(total / count + 1e-06)
    out_attended = attended.reshape(1, tok, heads * width)
    out_query = (grad_q * factor).astype(jnp.bfloat16).reshape(1, tok, heads * width)
    out_key = (grad_key * factor).astype(jnp.bfloat16)[None]
    out_value = (grad_value * factor).astype(jnp.bfloat16)[None]
    return (out_attended, out_query, out_key, out_value)


def solution(mesh):
    in_specs = (
        P("dp", "ctx", None),
        P("dp", "ctx", None),
        P("dp", "ctx", None),
        P("dp", "ctx", None),
        P("dp", None),
    )
    out_specs = (
        P("dp", "ctx", None),
        P("dp", "ctx", None),
        P("dp", "ctx", None),
        P("dp", "ctx", None),
    )
    return jax.shard_map(
        per_device, mesh=mesh, in_specs=in_specs, out_specs=out_specs, check_vma=False
    )
```

profile of v0, /device:TPU:1, one launch (start us, length us, event | category | flops | bytes accessed | tf_op | source)
XLA Modules:
  0.0 1133.5 jit_solution(8044992128844805472)
XLA Ops:
  10.2 5.6 collective-permute-start.2
  20.2 81.3 %all-gather.3.cloned.1.call-done = bf16[1,8192,128]{2,1,0:T(8,128)(2,1)} async-done(((bf16[1,128,128]{2,1,0:T(8,128)(2,1)}), bf16[1,8192,128]{2,1,0:T(8,128)(2,1)}) %all-gather.3.cloned.1.call-update) | async-done | bytes 2097168 | tf_op jit(solution)/shard_map/all_gather | solution.py:85
  101.4 83.6 %all-gather.5.cloned.1.call-done = bf16[1,8192,128]{2,1,0:T(8,128)(2,1)} async-done(((bf16[1,128,128]{2,1,0:T(8,128)(2,1)}), bf16[1,8192,128]{2,1,0:T(8,128)(2,1)}) %all-gather.5.cloned.1.call-update) | async-done | bytes 2097168 | tf_op jit(solution)/shard_map/all_gather | solution.py:86
  185.1 66.4 %while.39 = (s32[]{:T(128)}, f32[128,4,128]{0,2,1:T(8,128)S(1)}, f32[128,4]{0,1:T(4,128)S(1)}, f32[128,4]{0,1:T(4,128)S(1)}, s32[16,4]{1,0:T(8,128)S(1)}, /*inde...) while((s32[]{:T(128)}, f32[128,4,128]{0,2,1:T(8,128)S(1)}, ...), condition=%wide.region_8.9_spmd.clone, body=%wide.region_1.8_spmd.clone.sunk | while | flops 138002432 | bytes 4965105 | solution.py:98
  251.6 713.5 %while.40 = (s32[]{:T(128)}, f32[128,4,128]{2,0,1:T(8,128)S(1)}, bf16[2,2,128,128]{3,2,0,1:T(8,128)(2,1)S(1)}, f32[2,2,128,128]{3,2,0,1:T(8,128)S(1)}, s32[]{:T(...) while((s32[]{:T(128)}, f32[128,4,128]{2,0,1:T(8,128)S(1)}, ...), condition=%wide.region_12.13_spmd.clone, body=%wide.region_10.12_spmd.clone.sunk | while | flops 169205280 | bytes 6568001 | solution.py:144
  253.9 3.8 collective-permute-start.1
  257.7 3.4 collective-permute-start
  261.4 11.7 %collective-permute-done = bf16[2,2,128,128]{3,2,0,1:T(8,128)(2,1)S(1)} collective-permute-done((bf16[2,2,128,128]{3,2,0,1:T(8,128)(2,1)S(1)}, bf16[2,2,128,128]{3,2,0,1:T(8,128)(2,1)S(1)}, u32[]{:S(2)}, u32[]{:S(2)}) %collective-permute-start) | collective-permute-done | bytes 131104 | tf_op jit(solution)/shard_map/while/body/eval_jaxpr/ppermute | solution.py:14
  275.4 2.8 collective-permute-start.1
  278.2 5.0 collective-permute-start
  283.5 13.4 %collective-permute-done = bf16[2,2,128,128]{3,2,0,1:T(8,128)(2,1)S(1)} collective-permute-done((bf16[2,2,128,128]{3,2,0,1:T(8,128)(2,1)S(1)}, bf16[2,2,128,128]{3,2,0,1:T(8,128)(2,1)S(1)}, u32[]{:S(2)}, u32[]{:S(2)}) %collective-permute-start) | collective-permute-done | bytes 131104 | tf_op jit(solution)/shard_map/while/body/eval_jaxpr/ppermute | solution.py:14
  303.2 20.0 %collective-permute-done = bf16[2,2,128,128]{3,2,0,1:T(8,128)(2,1)S(1)} collective-permute-done((bf16[2,2,128,128]{3,2,0,1:T(8,128)(2,1)S(1)}, bf16[2,2,128,128]{3,2,0,1:T(8,128)(2,1)S(1)}, u32[]{:S(2)}, u32[]{:S(2)}) %collective-permute-start) | collective-permute-done | bytes 131104 | tf_op jit(solution)/shard_map/while/body/eval_jaxpr/ppermute | solution.py:14
  329.6 15.5 %collective-permute-done = bf16[2,2,128,128]{3,2,0,1:T(8,128)(2,1)S(1)} collective-permute-done((bf16[2,2,128,128]{3,2,0,1:T(8,128)(2,1)S(1)}, bf16[2,2,128,128]{3,2,0,1:T(8,128)(2,1)S(1)}, u32[]{:S(2)}, u32[]{:S(2)}) %collective-permute-start) | collective-permute-done | bytes 131104 | tf_op jit(solution)/shard_map/while/body/eval_jaxpr/ppermute | solution.py:14
  347.3 2.1 collective-permute-start.1
  349.5 1.9 collective-permute-start
  351.7 8.7 collective-permute-done
  364.6 4.6 collective-permute-start
  369.4 8.5 collective-permute-done
  380.2 3.2 collective-permute-start.1
  383.4 6.2 collective-permute-start
  389.9 14.0 %collective-permute-done = bf16[2,2,128,128]{3,2,0,1:T(8,128)(2,1)S(1)} collective-permute-done((bf16[2,2,128,128]{3,2,0,1:T(8,128)(2,1)S(1)}, bf16[2,2,128,128]{3,2,0,1:T(8,128)(2,1)S(1)}, u32[]{:S(2)}, u32[]{:S(2)}) %collective-permute-start) | collective-permute-done | bytes 131104 | tf_op jit(solution)/shard_map/while/body/eval_jaxpr/ppermute | solution.py:14
  410.3 21.1 %collective-permute-done = bf16[2,2,128,128]{3,2,0,1:T(8,128)(2,1)S(1)} collective-permute-done((bf16[2,2,128,128]{3,2,0,1:T(8,128)(2,1)S(1)}, bf16[2,2,128,128]{3,2,0,1:T(8,128)(2,1)S(1)}, u32[]{:S(2)}, u32[]{:S(2)}) %collective-permute-start) | collective-permute-done | bytes 131104 | tf_op jit(solution)/shard_map/while/body/eval_jaxpr/ppermute | solution.py:14
  437.8 20.8 %collective-permute-done = bf16[2,2,128,128]{3,2,0,1:T(8,128)(2,1)S(1)} collective-permute-done((bf16[2,2,128,128]{3,2,0,1:T(8,128)(2,1)S(1)}, bf16[2,2,128,128]{3,2,0,1:T(8,128)(2,1)S(1)}, u32[]{:S(2)}, u32[]{:S(2)}) %collective-permute-start) | collective-permute-done | bytes 131104 | tf_op jit(solution)/shard_map/while/body/eval_jaxpr/ppermute | solution.py:14
  460.8 1.9 collective-permute-start.1
  462.7 1.9 collective-permute-start
  464.9 20.1 %collective-permute-done = bf16[2,2,128,128]{3,2,0,1:T(8,128)(2,1)S(1)} collective-permute-done((bf16[2,2,128,128]{3,2,0,1:T(8,128)(2,1)S(1)}, bf16[2,2,128,128]{3,2,0,1:T(8,128)(2,1)S(1)}, u32[]{:S(2)}, u32[]{:S(2)}) %collective-permute-start) | collective-permute-done | bytes 131104 | tf_op jit(solution)/shard_map/while/body/eval_jaxpr/ppermute | solution.py:14
  491.4 18.6 %collective-permute-done = bf16[2,2,128,128]{3,2,0,1:T(8,128)(2,1)S(1)} collective-permute-done((bf16[2,2,128,128]{3,2,0,1:T(8,128)(2,1)S(1)}, bf16[2,2,128,128]{3,2,0,1:T(8,128)(2,1)S(1)}, u32[]{:S(2)}, u32[]{:S(2)}) %collective-permute-start) | collective-permute-done | bytes 131104 | tf_op jit(solution)/shard_map/while/body/eval_jaxpr/ppermute | solution.py:14
  516.4 13.1 %collective-permute-done = bf16[2,2,128,128]{3,2,0,1:T(8,128)(2,1)S(1)} collective-permute-done((bf16[2,2,128,128]{3,2,0,1:T(8,128)(2,1)S(1)}, bf16[2,2,128,128]{3,2,0,1:T(8,128)(2,1)S(1)}, u32[]{:S(2)}, u32[]{:S(2)}) %collective-permute-start) | collective-permute-done | bytes 131104 | tf_op jit(solution)/shard_map/while/body/eval_jaxpr/ppermute | solution.py:14
  531.8 1.9 collective-permute-start.1
  533.7 1.9 collective-permute-start
  535.9 8.9 collective-permute-done
  549.0 3.5 collective-permute-start
  552.7 9.8 collective-permute-done
  564.8 4.3 collective-permute-start.1
  569.1 4.8 collective-permute-start
  574.1 15.2 %collective-permute-done = bf16[2,2,128,128]{3,2,0,1:T(8,128)(2,1)S(1)} collective-permute-done((bf16[2,2,128,128]{3,2,0,1:T(8,128)(2,1)S(1)}, bf16[2,2,128,128]{3,2,0,1:T(8,128)(2,1)S(1)}, u32[]{:S(2)}, u32[]{:S(2)}) %collective-permute-start) | collective-permute-done | bytes 131104 | tf_op jit(solution)/shard_map/while/body/eval_jaxpr/ppermute | solution.py:14
  591.6 1.9 collective-permute-start.1
  593.5 2.9 collective-permute-start
  596.6 17.8 %collective-permute-done = bf16[2,2,128,128]{3,2,0,1:T(8,128)(2,1)S(1)} collective-permute-done((bf16[2,2,128,128]{3,2,0,1:T(8,128)(2,1)S(1)}, bf16[2,2,128,128]{3,2,0,1:T(8,128)(2,1)S(1)}, u32[]{:S(2)}, u32[]{:S(2)}) %collective-permute-start) | collective-permute-done | bytes 131104 | tf_op jit(solution)/shard_map/while/body/eval_jaxpr/ppermute | solution.py:14
  620.8 21.1 %collective-permute-done = bf16[2,2,128,128]{3,2,0,1:T(8,128)(2,1)S(1)} collective-permute-done((bf16[2,2,128,128]{3,2,0,1:T(8,128)(2,1)S(1)}, bf16[2,2,128,128]{3,2,0,1:T(8,128)(2,1)S(1)}, u32[]{:S(2)}, u32[]{:S(2)}) %collective-permute-start) | collective-permute-done | bytes 131104 | tf_op jit(solution)/shard_map/while/body/eval_jaxpr/ppermute | solution.py:14
  648.3 21.4 %collective-permute-done = bf16[2,2,128,128]{3,2,0,1:T(8,128)(2,1)S(1)} collective-permute-done((bf16[2,2,128,128]{3,2,0,1:T(8,128)(2,1)S(1)}, bf16[2,2,128,128]{3,2,0,1:T(8,128)(2,1)S(1)}, u32[]{:S(2)}, u32[]{:S(2)}) %collective-permute-start) | collective-permute-done | bytes 131104 | tf_op jit(solution)/shard_map/while/body/eval_jaxpr/ppermute | solution.py:14
  676.0 16.3 %collective-permute-done = bf16[2,2,128,128]{3,2,0,1:T(8,128)(2,1)S(1)} collective-permute-done((bf16[2,2,128,128]{3,2,0,1:T(8,128)(2,1)S(1)}, bf16[2,2,128,128]{3,2,0,1:T(8,128)(2,1)S(1)}, u32[]{:S(2)}, u32[]{:S(2)}) %collective-permute-start) | collective-permute-done | bytes 131104 | tf_op jit(solution)/shard_map/while/body/eval_jaxpr/ppermute | solution.py:14
  694.6 3.1 collective-permute-start.1
  699.8 13.4 %collective-permute-done = bf16[2,2,128,128]{3,2,0,1:T(8,128)(2,1)S(1)} collective-permute-done((bf16[2,2,128,128]{3,2,0,1:T(8,128)(2,1)S(1)}, bf16[2,2,128,128]{3,2,0,1:T(8,128)(2,1)S(1)}, u32[]{:S(2)}, u32[]{:S(2)}) %collective-permute-start) | collective-permute-done | bytes 131104 | tf_op jit(solution)/shard_map/while/body/eval_jaxpr/ppermute | solution.py:14
  715.5 5.0 collective-permute-start.1
  722.7 7.7 collective-permute-done
  732.7 2.1 collective-permute-start.1
  734.9 2.5 collective-permute-start
  737.6 10.5 collective-permute-done
  752.3 6.0 collective-permute-start
  758.6 13.7 %collective-permute-done = bf16[2,2,128,128]{3,2,0,1:T(8,128)(2,1)S(1)} collective-permute-done((bf16[2,2,128,128]{3,2,0,1:T(8,128)(2,1)S(1)}, bf16[2,2,128,128]{3,2,0,1:T(8,128)(2,1)S(1)}, u32[]{:S(2)}, u32[]{:S(2)}) %collective-permute-start) | collective-permute-done | bytes 131104 | tf_op jit(solution)/shard_map/while/body/eval_jaxpr/ppermute | solution.py:14
  778.6 20.9 %collective-permute-done = bf16[2,2,128,128]{3,2,0,1:T(8,128)(2,1)S(1)} collective-permute-done((bf16[2,2,128,128]{3,2,0,1:T(8,128)(2,1)S(1)}, bf16[2,2,128,128]{3,2,0,1:T(8,128)(2,1)S(1)}, u32[]{:S(2)}, u32[]{:S(2)}) %collective-permute-start) | collective-permute-done | bytes 131104 | tf_op jit(solution)/shard_map/while/body/eval_jaxpr/ppermute | solution.py:14
  805.9 15.2 %collective-permute-done = bf16[2,2,128,128]{3,2,0,1:T(8,128)(2,1)S(1)} collective-permute-done((bf16[2,2,128,128]{3,2,0,1:T(8,128)(2,1)S(1)}, bf16[2,2,128,128]{3,2,0,1:T(8,128)(2,1)S(1)}, u32[]{:S(2)}, u32[]{:S(2)}) %collective-permute-start) | collective-permute-done | bytes 131104 | tf_op jit(solution)/shard_map/while/body/eval_jaxpr/ppermute | solution.py:14
  827.4 8.6 collective-permute-done
  842.4 13.7 %collective-permute-done = bf16[2,2,128,128]{3,2,0,1:T(8,128)(2,1)S(1)} collective-permute-done((bf16[2,2,128,128]{3,2,0,1:T(8,128)(2,1)S(1)}, bf16[2,2,128,128]{3,2,0,1:T(8,128)(2,1)S(1)}, u32[]{:S(2)}, u32[]{:S(2)}) %collective-permute-start) | collective-permute-done | bytes 131104 | tf_op jit(solution)/shard_map/while/body/eval_jaxpr/ppermute | solution.py:14
  862.5 12.6 %collective-permute-done = bf16[2,2,128,128]{3,2,0,1:T(8,128)(2,1)S(1)} collective-permute-done((bf16[2,2,128,128]{3,2,0,1:T(8,128)(2,1)S(1)}, bf16[2,2,128,128]{3,2,0,1:T(8,128)(2,1)S(1)}, u32[]{:S(2)}, u32[]{:S(2)}) %collective-permute-start) | collective-permute-done | bytes 131104 | tf_op jit(solution)/shard_map/while/body/eval_jaxpr/ppermute | solution.py:14
  879.4 3.3 collective-permute-start
  882.9 20.7 %collective-permute-done = bf16[2,2,128,128]{3,2,0,1:T(8,128)(2,1)S(1)} collective-permute-done((bf16[2,2,128,128]{3,2,0,1:T(8,128)(2,1)S(1)}, bf16[2,2,128,128]{3,2,0,1:T(8,128)(2,1)S(1)}, u32[]{:S(2)}, u32[]{:S(2)}) %collective-permute-start) | collective-permute-done | bytes 131104 | tf_op jit(solution)/shard_map/while/body/eval_jaxpr/ppermute | solution.py:14
  907.8 6.1 collective-permute-start
  914.2 23.4 %collective-permute-done = bf16[2,2,128,128]{3,2,0,1:T(8,128)(2,1)S(1)} collective-permute-done((bf16[2,2,128,128]{3,2,0,1:T(8,128)(2,1)S(1)}, bf16[2,2,128,128]{3,2,0,1:T(8,128)(2,1)S(1)}, u32[]{:S(2)}, u32[]{:S(2)}) %collective-permute-start) | collective-permute-done | bytes 131104 | tf_op jit(solution)/shard_map/while/body/eval_jaxpr/ppermute | solution.py:14
  944.0 21.1 %collective-permute-done = bf16[2,2,128,128]{3,2,0,1:T(8,128)(2,1)S(1)} collective-permute-done((bf16[2,2,128,128]{3,2,0,1:T(8,128)(2,1)S(1)}, bf16[2,2,128,128]{3,2,0,1:T(8,128)(2,1)S(1)}, u32[]{:S(2)}, u32[]{:S(2)}) %collective-permute-start) | collective-permute-done | bytes 131104 | tf_op jit(solution)/shard_map/while/body/eval_jaxpr/ppermute | solution.py:14
  968.0 39.6 %collective-permute-start.4 = (f32[2,128,128]{2,1,0:T(8,128)S(1)}, f32[2,128,128]{2,1,0:T(8,128)S(1)}, u32[]{:S(2)}, u32[]{:S(2)}) collective-permute-start(f32[2,128,128]{2,1,0:T(8,128)S(1)} %get-tuple-element.792), channel_id=1, source_target_pairs={{504,0},{0,8},{8,16},{16,24},{24,32},{32,40},{40,48},{48,56},{56,6... | collective-permute-start | bytes 393224 | tf_op jit(solution)/shard_map/ppermute | solution.py:14
  1008.7 4.9 collective-permute-done.4
  1016.9 107.6 %psum.7 = f32[]{:T(128)} all-reduce(f32[]{:T(128)S(6)} %add.648), channel_id=1, replica_groups=mesh['ctx'=64,'dp'=8] {'ctx','dp'}, use_global_device_ids=true, to_apply=%region_17.18 | all-reduce | flops 1 | bytes 8 | tf_op jit(solution)/shard_map/psum | solution.py:154
  (787 shorter events, 226.6 us)
Async XLA Ops:
  7.2 94.3 %all-gather.3.cloned.1.call-start = ((), (), s32[]{:S(2)}) async-start(), calls=%async_computation | async-start | bytes 2129920 | tf_op jit(solution)/shard_map/all_gather | solution.py:85
  7.9 177.2 %all-gather.5.cloned.1.call-start = ((), (), s32[]{:S(2)}) async-start(), calls=%async_computation.1 | async-start | bytes 2129920 | tf_op jit(solution)/shard_map/all_gather | solution.py:86
  253.9 19.2 %collective-permute-start.1 = (f32[2,2,128,128]{3,2,0,1:T(8,128)S(1)}, f32[2,2,128,128]{3,2,0,1:T(8,128)S(1)}, u32[]{:S(2)}, u32[]{:S(2)}) collective-permute-start(f32[2,2,128,128]{3,2,0,1:T(8,128)S(1)} %maximum_add_fusion.3), channel_id=1, source_target_pairs={{496,0},{504,8},{0,16},{8,24},{16,32},{24,40},{32,48},{40,56},{48,... | collective-permute-start | bytes 786440 | tf_op jit(solution)/shard_map/while/body/eval_jaxpr/ppermute | solution.py:14
  257.7 15.3 %collective-permute-start = (bf16[2,2,128,128]{3,2,0,1:T(8,128)(2,1)S(1)}, bf16[2,2,128,128]{3,2,0,1:T(8,128)(2,1)S(1)}, u32[]{:S(2)}, u32[]{:S(2)}) collective-permute-start(bf16[2,2,128,128]{3,2,0,1:T(8,128)(2,1)S(1)} %copy.128), channel_id=1, source_target_pairs={{496,0},{504,8},{0,16},{8,24},{16,32},{24,40},{32,48},{40,56},{48,... | collective-permute-start | bytes 393224 | tf_op jit(solution)/shard_map/while/body/eval_jaxpr/ppermute | solution.py:14
  275.4 21.5 %collective-permute-start.1 = (f32[2,2,128,128]{3,2,0,1:T(8,128)S(1)}, f32[2,2,128,128]{3,2,0,1:T(8,128)S(1)}, u32[]{:S(2)}, u32[]{:S(2)}) collective-permute-start(f32[2,2,128,128]{3,2,0,1:T(8,128)S(1)} %maximum_add_fusion.3), channel_id=1, source_target_pairs={{496,0},{504,8},{0,16},{8,24},{16,32},{24,40},{32,48},{40,56},{48,... | collective-permute-start | bytes 786440 | tf_op jit(solution)/shard_map/while/body/eval_jaxpr/ppermute | solution.py:14
  278.2 18.7 %collective-permute-start = (bf16[2,2,128,128]{3,2,0,1:T(8,128)(2,1)S(1)}, bf16[2,2,128,128]{3,2,0,1:T(8,128)(2,1)S(1)}, u32[]{:S(2)}, u32[]{:S(2)}) collective-permute-start(bf16[2,2,128,128]{3,2,0,1:T(8,128)(2,1)S(1)} %copy.128), channel_id=1, source_target_pairs={{496,0},{504,8},{0,16},{8,24},{16,32},{24,40},{32,48},{40,56},{48,... | collective-permute-start | bytes 393224 | tf_op jit(solution)/shard_map/while/body/eval_jaxpr/ppermute | solution.py:14
  299.1 24.1 %collective-permute-start.1 = (f32[2,2,128,128]{3,2,0,1:T(8,128)S(1)}, f32[2,2,128,128]{3,2,0,1:T(8,128)S(1)}, u32[]{:S(2)}, u32[]{:S(2)}) collective-permute-start(f32[2,2,128,128]{3,2,0,1:T(8,128)S(1)} %maximum_add_fusion.3), channel_id=1, source_target_pairs={{496,0},{504,8},{0,16},{8,24},{16,32},{24,40},{32,48},{40,56},{48,... | collective-permute-start | bytes 786440 | tf_op jit(solution)/shard_map/while/body/eval_jaxpr/ppermute | solution.py:14
  301.1 22.2 %collective-permute-start = (bf16[2,2,128,128]{3,2,0,1:T(8,128)(2,1)S(1)}, bf16[2,2,128,128]{3,2,0,1:T(8,128)(2,1)S(1)}, u32[]{:S(2)}, u32[]{:S(2)}) collective-permute-start(bf16[2,2,128,128]{3,2,0,1:T(8,128)(2,1)S(1)} %copy.128), channel_id=1, source_target_pairs={{496,0},{504,8},{0,16},{8,24},{16,32},{24,40},{32,48},{40,56},{48,... | collective-permute-start | bytes 393224 | tf_op jit(solution)/shard_map/while/body/eval_jaxpr/ppermute | solution.py:14
  325.5 19.6 %collective-permute-start.1 = (f32[2,2,128,128]{3,2,0,1:T(8,128)S(1)}, f32[2,2,128,128]{3,2,0,1:T(8,128)S(1)}, u32[]{:S(2)}, u32[]{:S(2)}) collective-permute-start(f32[2,2,128,128]{3,2,0,1:T(8,128)S(1)} %maximum_add_fusion.3), channel_id=1, source_target_pairs={{496,0},{504,8},{0,16},{8,24},{16,32},{24,40},{32,48},{40,56},{48,... | collective-permute-start | bytes 786440 | tf_op jit(solution)/shard_map/while/body/eval_jaxpr/ppermute | solution.py:14
  327.4 17.6 %collective-permute-start = (bf16[2,2,128,128]{3,2,0,1:T(8,128)(2,1)S(1)}, bf16[2,2,128,128]{3,2,0,1:T(8,128)(2,1)S(1)}, u32[]{:S(2)}, u32[]{:S(2)}) collective-permute-start(bf16[2,2,128,128]{3,2,0,1:T(8,128)(2,1)S(1)} %copy.128), channel_id=1, source_target_pairs={{496,0},{504,8},{0,16},{8,24},{16,32},{24,40},{32,48},{40,56},{48,... | collective-permute-start | bytes 393224 | tf_op jit(solution)/shard_map/while/body/eval_jaxpr/ppermute | solution.py:14
  347.3 13.0 %collective-permute-start.1 = (f32[2,2,128,128]{3,2,0,1:T(8,128)S(1)}, f32[2,2,128,128]{3,2,0,1:T(8,128)S(1)}, u32[]{:S(2)}, u32[]{:S(2)}) collective-permute-start(f32[2,2,128,128]{3,2,0,1:T(8,128)S(1)} %maximum_add_fusion.3), channel_id=1, source_target_pairs={{496,0},{504,8},{0,16},{8,24},{16,32},{24,40},{32,48},{40,56},{48,... | collective-permute-start | bytes 786440 | tf_op jit(solution)/shard_map/while/body/eval_jaxpr/ppermute | solution.py:14
  349.5 10.9 collective-permute-start
  362.6 15.3 %collective-permute-start.1 = (f32[2,2,128,128]{3,2,0,1:T(8,128)S(1)}, f32[2,2,128,128]{3,2,0,1:T(8,128)S(1)}, u32[]{:S(2)}, u32[]{:S(2)}) collective-permute-start(f32[2,2,128,128]{3,2,0,1:T(8,128)S(1)} %maximum_add_fusion.3), channel_id=1, source_target_pairs={{496,0},{504,8},{0,16},{8,24},{16,32},{24,40},{32,48},{40,56},{48,... | collective-permute-start | bytes 786440 | tf_op jit(solution)/shard_map/while/body/eval_jaxpr/ppermute | solution.py:14
  364.6 13.4 %collective-permute-start = (bf16[2,2,128,128]{3,2,0,1:T(8,128)(2,1)S(1)}, bf16[2,2,128,128]{3,2,0,1:T(8,128)(2,1)S(1)}, u32[]{:S(2)}, u32[]{:S(2)}) collective-permute-start(bf16[2,2,128,128]{3,2,0,1:T(8,128)(2,1)S(1)} %copy.128), channel_id=1, source_target_pairs={{496,0},{504,8},{0,16},{8,24},{16,32},{24,40},{32,48},{40,56},{48,... | collective-permute-start | bytes 393224 | tf_op jit(solution)/shard_map/while/body/eval_jaxpr/ppermute | solution.py:14
  380.2 23.7 %collective-permute-start.1 = (f32[2,2,128,128]{3,2,0,1:T(8,128)S(1)}, f32[2,2,128,128]{3,2,0,1:T(8,128)S(1)}, u32[]{:S(2)}, u32[]{:S(2)}) collective-permute-start(f32[2,2,128,128]{3,2,0,1:T(8,128)S(1)} %maximum_add_fusion.3), channel_id=1, source_target_pairs={{496,0},{504,8},{0,16},{8,24},{16,32},{24,40},{32,48},{40,56},{48,... | collective-permute-start | bytes 786440 | tf_op jit(solution)/shard_map/while/body/eval_jaxpr/ppermute | solution.py:14
  383.4 20.5 %collective-permute-start = (bf16[2,2,128,128]{3,2,0,1:T(8,128)(2,1)S(1)}, bf16[2,2,128,128]{3,2,0,1:T(8,128)(2,1)S(1)}, u32[]{:S(2)}, u32[]{:S(2)}) collective-permute-start(bf16[2,2,128,128]{3,2,0,1:T(8,128)(2,1)S(1)} %copy.128), channel_id=1, source_target_pairs={{496,0},{504,8},{0,16},{8,24},{16,32},{24,40},{32,48},{40,56},{48,... | collective-permute-start | bytes 393224 | tf_op jit(solution)/shard_map/while/body/eval_jaxpr/ppermute | solution.py:14
  406.1 25.2 %collective-permute-start.1 = (f32[2,2,128,128]{3,2,0,1:T(8,128)S(1)}, f32[2,2,128,128]{3,2,0,1:T(8,128)S(1)}, u32[]{:S(2)}, u32[]{:S(2)}) collective-permute-start(f32[2,2,128,128]{3,2,0,1:T(8,128)S(1)} %maximum_add_fusion.3), channel_id=1, source_target_pairs={{496,0},{504,8},{0,16},{8,24},{16,32},{24,40},{32,48},{40,56},{48,... | collective-permute-start | bytes 786440 | tf_op jit(solution)/shard_map/while/body/eval_jaxpr/ppermute | solution.py:14
  408.1 23.3 %collective-permute-start = (bf16[2,2,128,128]{3,2,0,1:T(8,128)(2,1)S(1)}, bf16[2,2,128,128]{3,2,0,1:T(8,128)(2,1)S(1)}, u32[]{:S(2)}, u32[]{:S(2)}) collective-permute-start(bf16[2,2,128,128]{3,2,0,1:T(8,128)(2,1)S(1)} %copy.128), channel_id=1, source_target_pairs={{496,0},{504,8},{0,16},{8,24},{16,32},{24,40},{32,48},{40,56},{48,... | collective-permute-start | bytes 393224 | tf_op jit(solution)/shard_map/while/body/eval_jaxpr/ppermute | solution.py:14
  433.7 24.9 %collective-permute-start.1 = (f32[2,2,128,128]{3,2,0,1:T(8,128)S(1)}, f32[2,2,128,128]{3,2,0,1:T(8,128)S(1)}, u32[]{:S(2)}, u32[]{:S(2)}) collective-permute-start(f32[2,2,128,128]{3,2,0,1:T(8,128)S(1)} %maximum_add_fusion.3), channel_id=1, source_target_pairs={{496,0},{504,8},{0,16},{8,24},{16,32},{24,40},{32,48},{40,56},{48,... | collective-permute-start | bytes 786440 | tf_op jit(solution)/shard_map/while/body/eval_jaxpr/ppermute | solution.py:14
  435.6 22.9 %collective-permute-start = (bf16[2,2,128,128]{3,2,0,1:T(8,128)(2,1)S(1)}, bf16[2,2,128,128]{3,2,0,1:T(8,128)(2,1)S(1)}, u32[]{:S(2)}, u32[]{:S(2)}) collective-permute-start(bf16[2,2,128,128]{3,2,0,1:T(8,128)(2,1)S(1)} %copy.128), channel_id=1, source_target_pairs={{496,0},{504,8},{0,16},{8,24},{16,32},{24,40},{32,48},{40,56},{48,... | collective-permute-start | bytes 393224 | tf_op jit(solution)/shard_map/while/body/eval_jaxpr/ppermute | solution.py:14
  460.8 24.2 %collective-permute-start.1 = (f32[2,2,128,128]{3,2,0,1:T(8,128)S(1)}, f32[2,2,128,128]{3,2,0,1:T(8,128)S(1)}, u32[]{:S(2)}, u32[]{:S(2)}) collective-permute-start(f32[2,2,128,128]{3,2,0,1:T(8,128)S(1)} %maximum_add_fusion.3), channel_id=1, source_target_pairs={{496,0},{504,8},{0,16},{8,24},{16,32},{24,40},{32,48},{40,56},{48,... | collective-permute-start | bytes 786440 | tf_op jit(solution)/shard_map/while/body/eval_jaxpr/ppermute | solution.py:14
  462.7 22.3 %collective-permute-start = (bf16[2,2,128,128]{3,2,0,1:T(8,128)(2,1)S(1)}, bf16[2,2,128,128]{3,2,0,1:T(8,128)(2,1)S(1)}, u32[]{:S(2)}, u32[]{:S(2)}) collective-permute-start(bf16[2,2,128,128]{3,2,0,1:T(8,128)(2,1)S(1)} %copy.128), channel_id=1, source_target_pairs={{496,0},{504,8},{0,16},{8,24},{16,32},{24,40},{32,48},{40,56},{48,... | collective-permute-start | bytes 393224 | tf_op jit(solution)/shard_map/while/body/eval_jaxpr/ppermute | solution.py:14
  487.3 22.8 %collective-permute-start.1 = (f32[2,2,128,128]{3,2,0,1:T(8,128)S(1)}, f32[2,2,128,128]{3,2,0,1:T(8,128)S(1)}, u32[]{:S(2)}, u32[]{:S(2)}) collective-permute-start(f32[2,2,128,128]{3,2,0,1:T(8,128)S(1)} %maximum_add_fusion.3), channel_id=1, source_target_pairs={{496,0},{504,8},{0,16},{8,24},{16,32},{24,40},{32,48},{40,56},{48,... | collective-permute-start | bytes 786440 | tf_op jit(solution)/shard_map/while/body/eval_jaxpr/ppermute | solution.py:14
  489.2 20.8 %collective-permute-start = (bf16[2,2,128,128]{3,2,0,1:T(8,128)(2,1)S(1)}, bf16[2,2,128,128]{3,2,0,1:T(8,128)(2,1)S(1)}, u32[]{:S(2)}, u32[]{:S(2)}) collective-permute-start(bf16[2,2,128,128]{3,2,0,1:T(8,128)(2,1)S(1)} %copy.128), channel_id=1, source_target_pairs={{496,0},{504,8},{0,16},{8,24},{16,32},{24,40},{32,48},{40,56},{48,... | collective-permute-start | bytes 393224 | tf_op jit(solution)/shard_map/while/body/eval_jaxpr/ppermute | solution.py:14
  512.3 17.2 %collective-permute-start.1 = (f32[2,2,128,128]{3,2,0,1:T(8,128)S(1)}, f32[2,2,128,128]{3,2,0,1:T(8,128)S(1)}, u32[]{:S(2)}, u32[]{:S(2)}) collective-permute-start(f32[2,2,128,128]{3,2,0,1:T(8,128)S(1)} %maximum_add_fusion.3), channel_id=1, source_target_pairs={{496,0},{504,8},{0,16},{8,24},{16,32},{24,40},{32,48},{40,56},{48,... | collective-permute-start | bytes 786440 | tf_op jit(solution)/shard_map/while/body/eval_jaxpr/ppermute | solution.py:14
  514.2 15.3 %collective-permute-start = (bf16[2,2,128,128]{3,2,0,1:T(8,128)(2,1)S(1)}, bf16[2,2,128,128]{3,2,0,1:T(8,128)(2,1)S(1)}, u32[]{:S(2)}, u32[]{:S(2)}) collective-permute-start(bf16[2,2,128,128]{3,2,0,1:T(8,128)(2,1)S(1)} %copy.128), channel_id=1, source_target_pairs={{496,0},{504,8},{0,16},{8,24},{16,32},{24,40},{32,48},{40,56},{48,... | collective-permute-start | bytes 393224 | tf_op jit(solution)/shard_map/while/body/eval_jaxpr/ppermute | solution.py:14
  531.8 13.0 %collective-permute-start.1 = (f32[2,2,128,128]{3,2,0,1:T(8,128)S(1)}, f32[2,2,128,128]{3,2,0,1:T(8,128)S(1)}, u32[]{:S(2)}, u32[]{:S(2)}) collective-permute-start(f32[2,2,128,128]{3,2,0,1:T(8,128)S(1)} %maximum_add_fusion.3), channel_id=1, source_target_pairs={{496,0},{504,8},{0,16},{8,24},{16,32},{24,40},{32,48},{40,56},{48,... | collective-permute-start | bytes 786440 | tf_op jit(solution)/shard_map/while/body/eval_jaxpr/ppermute | solution.py:14
  533.7 11.1 collective-permute-start
  547.1 15.5 %collective-permute-start.1 = (f32[2,2,128,128]{3,2,0,1:T(8,128)S(1)}, f32[2,2,128,128]{3,2,0,1:T(8,128)S(1)}, u32[]{:S(2)}, u32[]{:S(2)}) collective-permute-start(f32[2,2,128,128]{3,2,0,1:T(8,128)S(1)} %maximum_add_fusion.3), channel_id=1, source_target_pairs={{496,0},{504,8},{0,16},{8,24},{16,32},{24,40},{32,48},{40,56},{48,... | collective-permute-start | bytes 786440 | tf_op jit(solution)/shard_map/while/body/eval_jaxpr/ppermute | solution.py:14
  549.0 13.6 %collective-permute-start = (bf16[2,2,128,128]{3,2,0,1:T(8,128)(2,1)S(1)}, bf16[2,2,128,128]{3,2,0,1:T(8,128)(2,1)S(1)}, u32[]{:S(2)}, u32[]{:S(2)}) collective-permute-start(bf16[2,2,128,128]{3,2,0,1:T(8,128)(2,1)S(1)} %copy.128), channel_id=1, source_target_pairs={{496,0},{504,8},{0,16},{8,24},{16,32},{24,40},{32,48},{40,56},{48,... | collective-permute-start | bytes 393224 | tf_op jit(solution)/shard_map/while/body/eval_jaxpr/ppermute | solution.py:14
  564.8 24.5 %collective-permute-start.1 = (f32[2,2,128,128]{3,2,0,1:T(8,128)S(1)}, f32[2,2,128,128]{3,2,0,1:T(8,128)S(1)}, u32[]{:S(2)}, u32[]{:S(2)}) collective-permute-start(f32[2,2,128,128]{3,2,0,1:T(8,128)S(1)} %maximum_add_fusion.3), channel_id=1, source_target_pairs={{496,0},{504,8},{0,16},{8,24},{16,32},{24,40},{32,48},{40,56},{48,... | collective-permute-start | bytes 786440 | tf_op jit(solution)/shard_map/while/body/eval_jaxpr/ppermute | solution.py:14
  569.1 20.2 %collective-permute-start = (bf16[2,2,128,128]{3,2,0,1:T(8,128)(2,1)S(1)}, bf16[2,2,128,128]{3,2,0,1:T(8,128)(2,1)S(1)}, u32[]{:S(2)}, u32[]{:S(2)}) collective-permute-start(bf16[2,2,128,128]{3,2,0,1:T(8,128)(2,1)S(1)} %copy.128), channel_id=1, source_target_pairs={{496,0},{504,8},{0,16},{8,24},{16,32},{24,40},{32,48},{40,56},{48,... | collective-permute-start | bytes 393224 | tf_op jit(solution)/shard_map/while/body/eval_jaxpr/ppermute | solution.py:14
  591.6 22.9 %collective-permute-start.1 = (f32[2,2,128,128]{3,2,0,1:T(8,128)S(1)}, f32[2,2,128,128]{3,2,0,1:T(8,128)S(1)}, u32[]{:S(2)}, u32[]{:S(2)}) collective-permute-start(f32[2,2,128,128]{3,2,0,1:T(8,128)S(1)} %maximum_add_fusion.3), channel_id=1, source_target_pairs={{496,0},{504,8},{0,16},{8,24},{16,32},{24,40},{32,48},{40,56},{48,... | collective-permute-start | bytes 786440 | tf_op jit(solution)/shard_map/while/body/eval_jaxpr/ppermute | solution.py:14
  593.5 20.9 %collective-permute-start = (bf16[2,2,128,128]{3,2,0,1:T(8,128)(2,1)S(1)}, bf16[2,2,128,128]{3,2,0,1:T(8,128)(2,1)S(1)}, u32[]{:S(2)}, u32[]{:S(2)}) collective-permute-start(bf16[2,2,128,128]{3,2,0,1:T(8,128)(2,1)S(1)} %copy.128), channel_id=1, source_target_pairs={{496,0},{504,8},{0,16},{8,24},{16,32},{24,40},{32,48},{40,56},{48,... | collective-permute-start | bytes 393224 | tf_op jit(solution)/shard_map/while/body/eval_jaxpr/ppermute | solution.py:14
  616.7 25.2 %collective-permute-start.1 = (f32[2,2,128,128]{3,2,0,1:T(8,128)S(1)}, f32[2,2,128,128]{3,2,0,1:T(8,128)S(1)}, u32[]{:S(2)}, u32[]{:S(2)}) collective-permute-start(f32[2,2,128,128]{3,2,0,1:T(8,128)S(1)} %maximum_add_fusion.3), channel_id=1, source_target_pairs={{496,0},{504,8},{0,16},{8,24},{16,32},{24,40},{32,48},{40,56},{48,... | collective-permute-start | bytes 786440 | tf_op jit(solution)/shard_map/while/body/eval_jaxpr/ppermute | solution.py:14
  618.6 23.3 %collective-permute-start = (bf16[2,2,128,128]{3,2,0,1:T(8,128)(2,1)S(1)}, bf16[2,2,128,128]{3,2,0,1:T(8,128)(2,1)S(1)}, u32[]{:S(2)}, u32[]{:S(2)}) collective-permute-start(bf16[2,2,128,128]{3,2,0,1:T(8,128)(2,1)S(1)} %copy.128), channel_id=1, source_target_pairs={{496,0},{504,8},{0,16},{8,24},{16,32},{24,40},{32,48},{40,56},{48,... | collective-permute-start | bytes 393224 | tf_op jit(solution)/shard_map/while/body/eval_jaxpr/ppermute | solution.py:14
  644.1 25.5 %collective-permute-start.1 = (f32[2,2,128,128]{3,2,0,1:T(8,128)S(1)}, f32[2,2,128,128]{3,2,0,1:T(8,128)S(1)}, u32[]{:S(2)}, u32[]{:S(2)}) collective-permute-start(f32[2,2,128,128]{3,2,0,1:T(8,128)S(1)} %maximum_add_fusion.3), channel_id=1, source_target_pairs={{496,0},{504,8},{0,16},{8,24},{16,32},{24,40},{32,48},{40,56},{48,... | collective-permute-start | bytes 786440 | tf_op jit(solution)/shard_map/while/body/eval_jaxpr/ppermute | solution.py:14
  646.1 23.5 %collective-permute-start = (bf16[2,2,128,128]{3,2,0,1:T(8,128)(2,1)S(1)}, bf16[2,2,128,128]{3,2,0,1:T(8,128)(2,1)S(1)}, u32[]{:S(2)}, u32[]{:S(2)}) collective-permute-start(bf16[2,2,128,128]{3,2,0,1:T(8,128)(2,1)S(1)} %copy.128), channel_id=1, source_target_pairs={{496,0},{504,8},{0,16},{8,24},{16,32},{24,40},{32,48},{40,56},{48,... | collective-permute-start | bytes 393224 | tf_op jit(solution)/shard_map/while/body/eval_jaxpr/ppermute | solution.py:14
  671.9 20.4 %collective-permute-start.1 = (f32[2,2,128,128]{3,2,0,1:T(8,128)S(1)}, f32[2,2,128,128]{3,2,0,1:T(8,128)S(1)}, u32[]{:S(2)}, u32[]{:S(2)}) collective-permute-start(f32[2,2,128,128]{3,2,0,1:T(8,128)S(1)} %maximum_add_fusion.3), channel_id=1, source_target_pairs={{496,0},{504,8},{0,16},{8,24},{16,32},{24,40},{32,48},{40,56},{48,... | collective-permute-start | bytes 786440 | tf_op jit(solution)/shard_map/while/body/eval_jaxpr/ppermute | solution.py:14
  673.8 18.5 %collective-permute-start = (bf16[2,2,128,128]{3,2,0,1:T(8,128)(2,1)S(1)}, bf16[2,2,128,128]{3,2,0,1:T(8,128)(2,1)S(1)}, u32[]{:S(2)}, u32[]{:S(2)}) collective-permute-start(bf16[2,2,128,128]{3,2,0,1:T(8,128)(2,1)S(1)} %copy.128), channel_id=1, source_target_pairs={{496,0},{504,8},{0,16},{8,24},{16,32},{24,40},{32,48},{40,56},{48,... | collective-permute-start | bytes 393224 | tf_op jit(solution)/shard_map/while/body/eval_jaxpr/ppermute | solution.py:14
  694.6 18.7 %collective-permute-start.1 = (f32[2,2,128,128]{3,2,0,1:T(8,128)S(1)}, f32[2,2,128,128]{3,2,0,1:T(8,128)S(1)}, u32[]{:S(2)}, u32[]{:S(2)}) collective-permute-start(f32[2,2,128,128]{3,2,0,1:T(8,128)S(1)} %maximum_add_fusion.3), channel_id=1, source_target_pairs={{496,0},{504,8},{0,16},{8,24},{16,32},{24,40},{32,48},{40,56},{48,... | collective-permute-start | bytes 786440 | tf_op jit(solution)/shard_map/while/body/eval_jaxpr/ppermute | solution.py:14
  697.7 15.6 %collective-permute-start = (bf16[2,2,128,128]{3,2,0,1:T(8,128)(2,1)S(1)}, bf16[2,2,128,128]{3,2,0,1:T(8,128)(2,1)S(1)}, u32[]{:S(2)}, u32[]{:S(2)}) collective-permute-start(bf16[2,2,128,128]{3,2,0,1:T(8,128)(2,1)S(1)} %copy.128), channel_id=1, source_target_pairs={{496,0},{504,8},{0,16},{8,24},{16,32},{24,40},{32,48},{40,56},{48,... | collective-permute-start | bytes 393224 | tf_op jit(solution)/shard_map/while/body/eval_jaxpr/ppermute | solution.py:14
  715.5 15.0 %collective-permute-start.1 = (f32[2,2,128,128]{3,2,0,1:T(8,128)S(1)}, f32[2,2,128,128]{3,2,0,1:T(8,128)S(1)}, u32[]{:S(2)}, u32[]{:S(2)}) collective-permute-start(f32[2,2,128,128]{3,2,0,1:T(8,128)S(1)} %maximum_add_fusion.3), channel_id=1, source_target_pairs={{496,0},{504,8},{0,16},{8,24},{16,32},{24,40},{32,48},{40,56},{48,... | collective-permute-start | bytes 786440 | tf_op jit(solution)/shard_map/while/body/eval_jaxpr/ppermute | solution.py:14
  732.7 15.4 %collective-permute-start.1 = (f32[2,2,128,128]{3,2,0,1:T(8,128)S(1)}, f32[2,2,128,128]{3,2,0,1:T(8,128)S(1)}, u32[]{:S(2)}, u32[]{:S(2)}) collective-permute-start(f32[2,2,128,128]{3,2,0,1:T(8,128)S(1)} %maximum_add_fusion.3), channel_id=1, source_target_pairs={{496,0},{504,8},{0,16},{8,24},{16,32},{24,40},{32,48},{40,56},{48,... | collective-permute-start | bytes 786440 | tf_op jit(solution)/shard_map/while/body/eval_jaxpr/ppermute | solution.py:14
  734.9 13.3 %collective-permute-start = (bf16[2,2,128,128]{3,2,0,1:T(8,128)(2,1)S(1)}, bf16[2,2,128,128]{3,2,0,1:T(8,128)(2,1)S(1)}, u32[]{:S(2)}, u32[]{:S(2)}) collective-permute-start(bf16[2,2,128,128]{3,2,0,1:T(8,128)(2,1)S(1)} %copy.128), channel_id=1, source_target_pairs={{496,0},{504,8},{0,16},{8,24},{16,32},{24,40},{32,48},{40,56},{48,... | collective-permute-start | bytes 393224 | tf_op jit(solution)/shard_map/while/body/eval_jaxpr/ppermute | solution.py:14
  750.4 21.9 %collective-permute-start.1 = (f32[2,2,128,128]{3,2,0,1:T(8,128)S(1)}, f32[2,2,128,128]{3,2,0,1:T(8,128)S(1)}, u32[]{:S(2)}, u32[]{:S(2)}) collective-permute-start(f32[2,2,128,128]{3,2,0,1:T(8,128)S(1)} %maximum_add_fusion.3), channel_id=1, source_target_pairs={{496,0},{504,8},{0,16},{8,24},{16,32},{24,40},{32,48},{40,56},{48,... | collective-permute-start | bytes 786440 | tf_op jit(solution)/shard_map/while/body/eval_jaxpr/ppermute | solution.py:14
  752.3 19.9 %collective-permute-start = (bf16[2,2,128,128]{3,2,0,1:T(8,128)(2,1)S(1)}, bf16[2,2,128,128]{3,2,0,1:T(8,128)(2,1)S(1)}, u32[]{:S(2)}, u32[]{:S(2)}) collective-permute-start(bf16[2,2,128,128]{3,2,0,1:T(8,128)(2,1)S(1)} %copy.128), channel_id=1, source_target_pairs={{496,0},{504,8},{0,16},{8,24},{16,32},{24,40},{32,48},{40,56},{48,... | collective-permute-start | bytes 393224 | tf_op jit(solution)/shard_map/while/body/eval_jaxpr/ppermute | solution.py:14
  774.5 25.0 %collective-permute-start.1 = (f32[2,2,128,128]{3,2,0,1:T(8,128)S(1)}, f32[2,2,128,128]{3,2,0,1:T(8,128)S(1)}, u32[]{:S(2)}, u32[]{:S(2)}) collective-permute-start(f32[2,2,128,128]{3,2,0,1:T(8,128)S(1)} %maximum_add_fusion.3), channel_id=1, source_target_pairs={{496,0},{504,8},{0,16},{8,24},{16,32},{24,40},{32,48},{40,56},{48,... | collective-permute-start | bytes 786440 | tf_op jit(solution)/shard_map/while/body/eval_jaxpr/ppermute | solution.py:14
  776.4 23.1 %collective-permute-start = (bf16[2,2,128,128]{3,2,0,1:T(8,128)(2,1)S(1)}, bf16[2,2,128,128]{3,2,0,1:T(8,128)(2,1)S(1)}, u32[]{:S(2)}, u32[]{:S(2)}) collective-permute-start(bf16[2,2,128,128]{3,2,0,1:T(8,128)(2,1)S(1)} %copy.128), channel_id=1, source_target_pairs={{496,0},{504,8},{0,16},{8,24},{16,32},{24,40},{32,48},{40,56},{48,... | collective-permute-start | bytes 393224 | tf_op jit(solution)/shard_map/while/body/eval_jaxpr/ppermute | solution.py:14
  801.8 19.3 %collective-permute-start.1 = (f32[2,2,128,128]{3,2,0,1:T(8,128)S(1)}, f32[2,2,128,128]{3,2,0,1:T(8,128)S(1)}, u32[]{:S(2)}, u32[]{:S(2)}) collective-permute-start(f32[2,2,128,128]{3,2,0,1:T(8,128)S(1)} %maximum_add_fusion.3), channel_id=1, source_target_pairs={{496,0},{504,8},{0,16},{8,24},{16,32},{24,40},{32,48},{40,56},{48,... | collective-permute-start | bytes 786440 | tf_op jit(solution)/shard_map/while/body/eval_jaxpr/ppermute | solution.py:14
  803.7 17.3 %collective-permute-start = (bf16[2,2,128,128]{3,2,0,1:T(8,128)(2,1)S(1)}, bf16[2,2,128,128]{3,2,0,1:T(8,128)(2,1)S(1)}, u32[]{:S(2)}, u32[]{:S(2)}) collective-permute-start(bf16[2,2,128,128]{3,2,0,1:T(8,128)(2,1)S(1)} %copy.128), channel_id=1, source_target_pairs={{496,0},{504,8},{0,16},{8,24},{16,32},{24,40},{32,48},{40,56},{48,... | collective-permute-start | bytes 393224 | tf_op jit(solution)/shard_map/while/body/eval_jaxpr/ppermute | solution.py:14
  823.3 12.7 %collective-permute-start.1 = (f32[2,2,128,128]{3,2,0,1:T(8,128)S(1)}, f32[2,2,128,128]{3,2,0,1:T(8,128)S(1)}, u32[]{:S(2)}, u32[]{:S(2)}) collective-permute-start(f32[2,2,128,128]{3,2,0,1:T(8,128)S(1)} %maximum_add_fusion.3), channel_id=1, source_target_pairs={{496,0},{504,8},{0,16},{8,24},{16,32},{24,40},{32,48},{40,56},{48,... | collective-permute-start | bytes 786440 | tf_op jit(solution)/shard_map/while/body/eval_jaxpr/ppermute | solution.py:14
  838.3 17.8 %collective-permute-start.1 = (f32[2,2,128,128]{3,2,0,1:T(8,128)S(1)}, f32[2,2,128,128]{3,2,0,1:T(8,128)S(1)}, u32[]{:S(2)}, u32[]{:S(2)}) collective-permute-start(f32[2,2,128,128]{3,2,0,1:T(8,128)S(1)} %maximum_add_fusion.3), channel_id=1, source_target_pairs={{496,0},{504,8},{0,16},{8,24},{16,32},{24,40},{32,48},{40,56},{48,... | collective-permute-start | bytes 786440 | tf_op jit(solution)/shard_map/while/body/eval_jaxpr/ppermute | solution.py:14
  840.2 15.9 %collective-permute-start = (bf16[2,2,128,128]{3,2,0,1:T(8,128)(2,1)S(1)}, bf16[2,2,128,128]{3,2,0,1:T(8,128)(2,1)S(1)}, u32[]{:S(2)}, u32[]{:S(2)}) collective-permute-start(bf16[2,2,128,128]{3,2,0,1:T(8,128)(2,1)S(1)} %copy.128), channel_id=1, source_target_pairs={{496,0},{504,8},{0,16},{8,24},{16,32},{24,40},{32,48},{40,56},{48,... | collective-permute-start | bytes 393224 | tf_op jit(solution)/shard_map/while/body/eval_jaxpr/ppermute | solution.py:14
  858.4 16.7 %collective-permute-start.1 = (f32[2,2,128,128]{3,2,0,1:T(8,128)S(1)}, f32[2,2,128,128]{3,2,0,1:T(8,128)S(1)}, u32[]{:S(2)}, u32[]{:S(2)}) collective-permute-start(f32[2,2,128,128]{3,2,0,1:T(8,128)S(1)} %maximum_add_fusion.3), channel_id=1, source_target_pairs={{496,0},{504,8},{0,16},{8,24},{16,32},{24,40},{32,48},{40,56},{48,... | collective-permute-start | bytes 786440 | tf_op jit(solution)/shard_map/while/body/eval_jaxpr/ppermute | solution.py:14
  860.3 14.8 %collective-permute-start = (bf16[2,2,128,128]{3,2,0,1:T(8,128)(2,1)S(1)}, bf16[2,2,128,128]{3,2,0,1:T(8,128)(2,1)S(1)}, u32[]{:S(2)}, u32[]{:S(2)}) collective-permute-start(bf16[2,2,128,128]{3,2,0,1:T(8,128)(2,1)S(1)} %copy.128), channel_id=1, source_target_pairs={{496,0},{504,8},{0,16},{8,24},{16,32},{24,40},{32,48},{40,56},{48,... | collective-permute-start | bytes 393224 | tf_op jit(solution)/shard_map/while/body/eval_jaxpr/ppermute | solution.py:14
  877.4 26.2 %collective-permute-start.1 = (f32[2,2,128,128]{3,2,0,1:T(8,128)S(1)}, f32[2,2,128,128]{3,2,0,1:T(8,128)S(1)}, u32[]{:S(2)}, u32[]{:S(2)}) collective-permute-start(f32[2,2,128,128]{3,2,0,1:T(8,128)S(1)} %maximum_add_fusion.3), channel_id=1, source_target_pairs={{496,0},{504,8},{0,16},{8,24},{16,32},{24,40},{32,48},{40,56},{48,... | collective-permute-start | bytes 786440 | tf_op jit(solution)/shard_map/while/body/eval_jaxpr/ppermute | solution.py:14
  879.4 24.2 %collective-permute-start = (bf16[2,2,128,128]{3,2,0,1:T(8,128)(2,1)S(1)}, bf16[2,2,128,128]{3,2,0,1:T(8,128)(2,1)S(1)}, u32[]{:S(2)}, u32[]{:S(2)}) collective-permute-start(bf16[2,2,128,128]{3,2,0,1:T(8,128)(2,1)S(1)} %copy.128), channel_id=1, source_target_pairs={{496,0},{504,8},{0,16},{8,24},{16,32},{24,40},{32,48},{40,56},{48,... | collective-permute-start | bytes 393224 | tf_op jit(solution)/shard_map/while/body/eval_jaxpr/ppermute | solution.py:14
  905.8 31.8 %collective-permute-start.1 = (f32[2,2,128,128]{3,2,0,1:T(8,128)S(1)}, f32[2,2,128,128]{3,2,0,1:T(8,128)S(1)}, u32[]{:S(2)}, u32[]{:S(2)}) collective-permute-start(f32[2,2,128,128]{3,2,0,1:T(8,128)S(1)} %maximum_add_fusion.3), channel_id=1, source_target_pairs={{496,0},{504,8},{0,16},{8,24},{16,32},{24,40},{32,48},{40,56},{48,... | collective-permute-start | bytes 786440 | tf_op jit(solution)/shard_map/while/body/eval_jaxpr/ppermute | solution.py:14
  907.8 29.8 %collective-permute-start = (bf16[2,2,128,128]{3,2,0,1:T(8,128)(2,1)S(1)}, bf16[2,2,128,128]{3,2,0,1:T(8,128)(2,1)S(1)}, u32[]{:S(2)}, u32[]{:S(2)}) collective-permute-start(bf16[2,2,128,128]{3,2,0,1:T(8,128)(2,1)S(1)} %copy.128), channel_id=1, source_target_pairs={{496,0},{504,8},{0,16},{8,24},{16,32},{24,40},{32,48},{40,56},{48,... | collective-permute-start | bytes 393224 | tf_op jit(solution)/shard_map/while/body/eval_jaxpr/ppermute | solution.py:14
  939.9 25.2 %collective-permute-start.1 = (f32[2,2,128,128]{3,2,0,1:T(8,128)S(1)}, f32[2,2,128,128]{3,2,0,1:T(8,128)S(1)}, u32[]{:S(2)}, u32[]{:S(2)}) collective-permute-start(f32[2,2,128,128]{3,2,0,1:T(8,128)S(1)} %maximum_add_fusion.3), channel_id=1, source_target_pairs={{496,0},{504,8},{0,16},{8,24},{16,32},{24,40},{32,48},{40,56},{48,... | collective-permute-start | bytes 786440 | tf_op jit(solution)/shard_map/while/body/eval_jaxpr/ppermute | solution.py:14
  941.8 23.3 %collective-permute-start = (bf16[2,2,128,128]{3,2,0,1:T(8,128)(2,1)S(1)}, bf16[2,2,128,128]{3,2,0,1:T(8,128)(2,1)S(1)}, u32[]{:S(2)}, u32[]{:S(2)}) collective-permute-start(bf16[2,2,128,128]{3,2,0,1:T(8,128)(2,1)S(1)} %copy.128), channel_id=1, source_target_pairs={{496,0},{504,8},{0,16},{8,24},{16,32},{24,40},{32,48},{40,56},{48,... | collective-permute-start | bytes 393224 | tf_op jit(solution)/shard_map/while/body/eval_jaxpr/ppermute | solution.py:14
  966.1 42.6 %collective-permute-start.3 = (f32[2,128,128]{2,1,0:T(8,128)S(1)}, f32[2,128,128]{2,1,0:T(8,128)S(1)}, u32[]{:S(2)}, u32[]{:S(2)}) collective-permute-start(f32[2,128,128]{2,1,0:T(8,128)S(1)} %get-tuple-element.793), channel_id=1, source_target_pairs={{496,0},{504,8},{0,16},{8,24},{16,32},{24,40},{32,48},{40,56},{48,... | collective-permute-start | bytes 393224 | tf_op jit(solution)/shard_map/ppermute | solution.py:14
  968.0 45.6 %collective-permute-start.4 = (f32[2,128,128]{2,1,0:T(8,128)S(1)}, f32[2,128,128]{2,1,0:T(8,128)S(1)}, u32[]{:S(2)}, u32[]{:S(2)}) collective-permute-start(f32[2,128,128]{2,1,0:T(8,128)S(1)} %get-tuple-element.792), channel_id=1, source_target_pairs={{504,0},{0,8},{8,16},{16,24},{24,32},{32,40},{40,48},{48,56},{56,6... | collective-permute-start | bytes 393224 | tf_op jit(solution)/shard_map/ppermute | solution.py:14
  (3 other events, 30.7 us)
Sparse Core Ops, SparseCore 0:
  11.3 90.0 all-gather.2
  104.8 80.2 all-gather.4
where the time goes:
time: 1140 us; the launch traced here: 1130 us
  waiting for transfers between devices  649 us (57%)
  starting transfers between devices  205 us (18%)
  blocking collectives  108 us (9%)
  matrix products  81.9 us (7%)
  other arithmetic  64.3 us (6%)
  between operations  16.9 us (1%)
    ppermute x65, waiting for transfers between devices, from_behind(): return lax.ppermute(block, axis, route)  482 us
    ppermute x65, starting transfers between devices, from_behind(): return lax.ppermute(block, axis, route)  204 us
    psum x1, blocking collectives, per_device(): total = lax.psum(local_squares, ('ctx', 'dp'))  108 us
    all_gather x1, waiting for transfers between devices, per_device(): value_piece = lax.all_gather(values, 'ctx', axis=1, tiled=True)  83.6 us
    all_gather x1, waiting for transfers between devices, per_device(): key_piece = lax.all_gather(keys, 'ctx', axis=1, tiled=True)  81.3 us
    reduce_sum x49, other arithmetic, doc_number(): jnp.sum((starts[None, :] <= positions[:, None]).astype(jnp.int32), axis=1)  36.3 us
    dot_general x48, matrix products, logits_of(): jnp.einsum('qhd,gkd->qhgk', query3, key_group, preferred_element_type=jnp...  28 us
  transfers between devices with their start and end apart: 67, of which 34 were waited for; matrix products, arithmetic and copies ran while one was open for 1% of the time, Pallas kernels for 0%

commit v1 on v0

v1 whole, which is shorter than its diff:
```python
import functools
import math

import jax
import jax.numpy as jnp
from jax import lax
from jax.experimental import pallas as pl
from jax.experimental.pallas import tpu as pltpu
from jax.sharding import PartitionSpec as P

FLOOR = -1e30
GROUP = 4


def dot(a, b, ca, cb):
    return lax.dot_general(a, b, (((ca,), (cb,)), ((), ())), preferred_element_type=jnp.float32)


def attend_kernel(nctx, heads, info, q_ref, do_ref, kv_ref, att_ref, dq_ref, sq_ref, dkv_ref, s_scr):
    tok = q_ref.shape[1]
    half = tok // 2
    width = kv_ref.shape[2] // 2
    cols = heads * half
    tile = GROUP * half
    runs = 2 * nctx
    scale = 1.0 / math.sqrt(width)
    log2_scale = scale * math.log2(math.e)
    me = info[0]

    dkv_ref[...] = jnp.zeros_like(dkv_ref)

    row = lax.broadcasted_iota(jnp.int32, (tile, 1), 0)
    row_run = row // half
    row_rest = row % half
    col_rest = lax.broadcasted_iota(jnp.int32, (1, cols), 1) % half
    squares = jnp.float32(0.0)

    def stacked(ref, r0):
        return jnp.concatenate(
            [ref[0, r0 : r0 + half, h * width : (h + 1) * width] for h in range(heads)], axis=0
        )

    for side in (0, 1):
        r0 = side * half
        run = me if side == 0 else runs - 1 - me
        first = info[1 + side]
        query_pos = run * half + col_rest
        first_pos = first * half
        q2 = stacked(q_ref, r0)
        do2 = stacked(do_ref, r0)

        if side == 0:
            regions = [(0, first // GROUP, me // GROUP + 1)]
        else:
            regions = [
                (0, jnp.minimum(first // GROUP, nctx // GROUP), jnp.int32(nctx // GROUP)),
                (1, me // GROUP, (runs - 1 - jnp.maximum(first, nctx)) // GROUP + 1),
            ]

        def over(body, carry):
            for part, low, high in regions:
                carry = lax.fori_loop(low, high, functools.partial(body, part), carry)
            return carry

        def rows_of(part, t):
            return pl.ds(pl.multiple_of(part * nctx * half + t * tile, tile), tile)

        def block_of(part, t, lo, hi):
            return (
                pl.ds(t * GROUP, GROUP),
                slice(part * half, (part + 1) * half),
                slice(lo, hi),
            )

        def key_tile(part, t):
            return kv_ref[block_of(part, t, 0, width)].reshape(tile, width)

        def value_tile(part, t):
            return kv_ref[block_of(part, t, width, 2 * width)].reshape(tile, width)

        def scores(part, t, biggest):
            s = dot(key_tile(part, t), q2, 1, 1)
            block_run = t * GROUP + row_run
            key_run = block_run if part == 0 else runs - 1 - block_run
            key_pos = key_run * half + row_rest
            key_pos = jnp.where(key_pos >= first_pos, key_pos, jnp.int32(2**30))
            s = jnp.where(key_pos <= query_pos, s, FLOOR)
            s_scr[rows_of(part, t), :] = s
            return jnp.maximum(biggest, jnp.max(s.reshape(tile // 8, 8, cols), axis=0))

        biggest = over(scores, jnp.full((8, cols), FLOOR, jnp.float32))
        top = jnp.max(biggest, axis=0, keepdims=True)

        def forward(part, t, carry):
            total, acc = carry
            rows = rows_of(part, t)
            e = jnp.exp2((s_scr[rows, :] - top) * log2_scale)
            s_scr[rows, :] = e
            total = total + jnp.sum(e.reshape(tile // 8, 8, cols), axis=0)
            acc = acc + dot(value_tile(part, t), e.astype(jnp.bfloat16), 0, 0)
            return total, acc

        total, acc = over(
            forward, (jnp.zeros((8, cols), jnp.float32), jnp.zeros((width, cols), jnp.float32))
        )
        inverse = 1.0 / jnp.sum(total, axis=0, keepdims=True)
        att_t = acc * inverse
        att = att_t.T.astype(jnp.bfloat16)
        for h in range(heads):
            att_ref[0, r0 : r0 + half, h * width : (h + 1) * width] = att[h * half : (h + 1) * half]
        do_t = do2.astype(jnp.float32).T
        delta = jnp.sum(do_t * att_t.astype(jnp.bfloat16).astype(jnp.float32), axis=0, keepdims=True)

        def backward(part, t, dq_t):
            rows = rows_of(part, t)
            p = s_scr[rows, :] * inverse
            dp = dot(value_tile(part, t), do2, 1, 1)
            ds = (p * (dp - delta)).astype(jnp.bfloat16)
            dv = dot(p.astype(jnp.bfloat16), do2, 1, 0)
            dk = dot(ds, q2, 1, 0) * scale
            for lo, new in ((0, dk), (width, dv)):
                where = block_of(part, t, lo, lo + width)
                new = new.reshape(GROUP, half, width)
                if side == 1 and part == 0:
                    new = new + dkv_ref[where].astype(jnp.float32)
                dkv_ref[where] = new.astype(dkv_ref.dtype)
            return dq_t + dot(key_tile(part, t), ds, 0, 0)

        dq_t = over(backward, jnp.zeros((width, cols), jnp.float32)) * scale
        squares = squares + jnp.sum(dq_t * dq_t)
        dq = dq_t.T
        for h in range(heads):
            dq_ref[0, r0 : r0 + half, h * width : (h + 1) * width] = dq[h * half : (h + 1) * half]

    sq_ref[0, 0] = squares


def attend(info, queries, grad_out, kv, nctx):
    tok = queries.shape[1]
    width = kv.shape[2] // 2
    heads = queries.shape[2] // width
    vmem = pl.BlockSpec(memory_space=pltpu.VMEM)
    smem = pl.BlockSpec(memory_space=pltpu.SMEM)
    return pl.pallas_call(
        functools.partial(attend_kernel, nctx, heads),
        out_shape=(
            jax.ShapeDtypeStruct(queries.shape, jnp.bfloat16),
            jax.ShapeDtypeStruct(queries.shape, jnp.float32),
            jax.ShapeDtypeStruct((1, 1), jnp.float32),
            jax.ShapeDtypeStruct(kv.shape, jnp.bfloat16),
        ),
        in_specs=[smem, vmem, vmem, vmem],
        out_specs=(vmem, vmem, smem, vmem),
        scratch_shapes=[pltpu.VMEM((nctx * tok, heads * tok // 2), jnp.float32)],
        compiler_params=pltpu.CompilerParams(vmem_limit_bytes=48 * 1024 * 1024),
    )(info, queries, grad_out, kv)


def per_device(queries, keys, values, grad_out, doc_starts):
    tok = queries.shape[1]
    width = keys.shape[2]
    nctx = lax.axis_size("ctx")
    ndata = lax.axis_size("dp")
    half = tok // 2
    me = lax.axis_index("ctx")
    starts = doc_starts[0] // half
    low_first = jnp.max(jnp.where(starts <= me, starts, 0))
    high_first = jnp.max(jnp.where(starts <= 2 * nctx - 1 - me, starts, 0))
    info = jnp.stack([me, low_first, high_first]).astype(jnp.int32)

    kv = jnp.concatenate([keys, values], axis=2)
    kv = lax.all_gather(kv, "ctx", axis=0, tiled=True)
    attended, query_raw, squares, partial = attend(info, queries, grad_out, kv, nctx)
    raw = lax.psum_scatter(partial, "ctx", scatter_dimension=0, tiled=True).astype(jnp.float32)
    total = lax.psum(jnp.sum(raw * raw) + squares[0, 0], ("ctx", "dp"))
    count = float(ndata * nctx * tok * (queries.shape[2] + 2 * width))
    factor = lax.rsqrt(total / count + 1e-06)
    out_query = (query_raw * factor).astype(jnp.bfloat16)
    scaled = (raw * factor).astype(jnp.bfloat16)
    return attended, out_query, scaled[:, :, :width], scaled[:, :, width:]


def solution(mesh):
    spec = P("dp", "ctx", None)
    return jax.shard_map(
        per_device,
        mesh=mesh,
        in_specs=(spec, spec, spec, spec, P("dp", None)),
        out_specs=(spec, spec, spec, spec),
        check_vma=False,
    )
```

time: 1140 us -> 388 us (0.34)
  waiting for transfers between devices: 649 us -> 255 us
  starting transfers between devices: 205 us -> 0.08 us
  matrix products: 81.9 us -> 0 us
  other arithmetic: 64.3 us -> 7.09 us
    ppermute x65 -> x0, waiting for transfers between devices: 482 us -> none  [from_behind(): return lax.ppermute(block, axis, route)]
    ppermute x65 -> x0, starting transfers between devices: 204 us -> none  [from_behind(): return lax.ppermute(block, axis, route)]
    reduce_scatter x0 -> x1, waiting for transfers between devices: none -> 161 us  [per_device(): lax.psum_scatter(partial, 'ctx', scatter_dimension=0, tiled=True)]
    dot_general x192 -> x0, matrix products: 81.9 us -> none  [the longest x48 28 us: logits_of(): jnp.einsum('qhd,gkd->qhgk', query3, key_group, preferred_element_type=jnp...]
    all_gather x2 -> x1, waiting for transfers between devices: 165 us -> 93.7 us  [per_device(): kv = lax.all_gather(kv, 'ctx', axis=0, tiled=True)]
    reduce_sum x83 -> x1, other arithmetic: 42 us -> 1.48 us  [per_device(): total = lax.psum(jnp.sum(raw * raw) + squares[0, 0], ('ctx', 'dp'))]
  transfers between devices with their start and end apart: 67 -> 2, of which waited for: 34 -> 2; matrix products, arithmetic and copies ran while one was open for 1% -> 1% of each run, Pallas kernels for 0% -> 0%
where the time goes in v1:
time: 388 us
  waiting for transfers between devices  255 us (66%)
  blocking collectives  100 us (26%)
  between operations  16.1 us (4%)
  other arithmetic  7.09 us (2%)
  Pallas kernels  5.13 us (1%)
  local copies, waits for them, and re-layouts  4.36 us (1%)
    reduce_scatter x1, waiting for transfers between devices, per_device(): lax.psum_scatter(partial, 'ctx', scatter_dimension=0, tiled=True)  161 us
    psum x1, blocking collectives, per_device(): total = lax.psum(jnp.sum(raw * raw) + squares[0, 0], ('ctx', 'dp'))  100 us
    all_gather x1, waiting for transfers between devices, per_device(): kv = lax.all_gather(kv, 'ctx', axis=0, tiled=True)  93.7 us
  transfers between devices with their start and end apart: 2, of which 2 were waited for; matrix products, arithmetic and copies ran while one was open for 1% of the time, Pallas kernels for 0%

profile of v1, /device:TPU:1, one launch (start us, length us, event | category | flops | bytes accessed | tf_op | source)
XLA Modules:
  0.0 387.7 jit_solution(5154061269188385724)
XLA Ops:
  7.2 0.0 all-gather.2.cloned.1.call-start
  7.2 1.4 pad_maximum_fusion
  8.6 0.0 all-gather.2.cloned.1.call-update
  8.6 0.0 reduce-scatter.2.cloned.1.call-start
  8.7 1.3 fusion.2
  10.0 1.4 pad_add_fusion.info
  11.4 93.7 %all-gather.2.cloned.1.call-done.kv_ref = bf16[64,128,256]{2,1,0:T(8,128)(2,1)} async-done(((bf16[1,128,256]{2,1,0:T(8,128)(2,1)}), bf16[64,128,256]{2,1,0:T(8,128)(2,1)}) %all-gather.2.cloned.1.call-update) | async-done | bytes 4194320 | tf_op jit(solution)/shard_map/all_gather | solution.py:172
  105.1 0.0 copy-start.1
  105.1 0.9 copy-done.1
  106.0 0.0 copy-start.2
  106.0 0.9 copy-done.2
  106.9 5.1 %shard_map.84 = (bf16[1,128,512]{2,1,0:T(8,128)(2,1)}, f32[1,128,512]{2,1,0:T(8,128)S(1)}, f32[1,1]{1,0:T(1,128)}, bf16[64,128,256]{2,1,0:T(8,128)(2,1)S(1)}) custom-call(s32[3]{0:T(128)S(1)} %pad_add_fusion.info, bf16[1,128,512]{2,1,0:T(8,128)(2,1)S(1)} %copy-done.1, bf16[1,128,512]{2,1,0:T(8,128)(2,1)S(1)} %copy-done.2, ...), custom_call_target="tpu_custom_call" | custom-call | tf_op jit(solution)/shard_map/pallas_call | solution.py:144
  112.0 0.0 copy-start
  112.0 1.9 copy-done
  113.9 0.0 reduce-scatter.2.cloned.1.call-update
  114.0 161.0 %reduce-scatter.2.cloned.1.call-done = bf16[1,128,256]{2,1,0:T(8,128)(2,1)} async-done(((bf16[64,128,256]{2,1,0:T(8,128)(2,1)}), bf16[1,128,256]{2,1,0:T(8,128)(2,1)}) %reduce-scatter.2.cloned.1.call-update) | async-done | bytes 65552 | tf_op jit(solution)/shard_map/reduce_scatter | solution.py:174
  275.0 1.5 fusion
  277.7 100.2 %psum.7 = f32[]{:T(128)} all-reduce(f32[]{:T(128)S(6)} %add.11), channel_id=1, replica_groups=mesh['ctx'=64,'dp'=8] {'ctx','dp'}, use_global_device_ids=true, to_apply=%region_4.5 | all-reduce | flops 1 | bytes 8 | tf_op jit(solution)/shard_map/psum | solution.py:175
  378.7 0.7 multiply_convert_fusion
  379.3 0.9 fusion.1
  380.2 0.6 fusion.4
Async XLA Ops:
  7.2 97.9 %all-gather.2.cloned.1.call-start = ((), (), s32[]{:S(2)}) async-start(), calls=%async_computation.1 | async-start | bytes 4259840 | tf_op jit(solution)/shard_map/all_gather | solution.py:172
  8.6 266.3 %reduce-scatter.2.cloned.1.call-start = ((), (), s32[]{:S(2)}) async-start(), calls=%async_computation.2 | async-start | bytes 4259840 | tf_op jit(solution)/shard_map/reduce_scatter | solution.py:174
  105.1 0.9 copy-start.1
  106.0 0.9 copy-start.2
  112.0 1.9 copy-start
Sparse Core Ops, SparseCore 0:
  11.9 93.0 all-gather.1
  114.1 160.8 reduce-scatter.1

commit v2 on v1

v2 whole, which is shorter than its diff:
```python
import functools
import math

import jax
import jax.numpy as jnp
from jax import lax
from jax.experimental import pallas as pl
from jax.experimental.pallas import tpu as pltpu
from jax.sharding import Mesh
from jax.sharding import PartitionSpec as P

FLOOR = -1e30
NZ, NY, NC = 8, 4, 2
FIELDS = 6
VMEM = pl.BlockSpec(memory_space=pltpu.VMEM)
SMEM = pl.BlockSpec(memory_space=pltpu.SMEM)
PARAMS = pltpu.CompilerParams(vmem_limit_bytes=40 * 1024 * 1024)


def dot(a, b, ca, cb):
    return lax.dot_general(a, b, (((ca,), (cb,)), ((), ())), preferred_element_type=jnp.float32)


def visits(doc_starts, tok, z, y, c):
    nctx = NZ * NY * NC
    half = tok // 2
    source = jnp.repeat((y + jnp.arange(NY, dtype=jnp.int32)) % NY, 2)
    upper = jnp.tile(jnp.arange(2, dtype=jnp.int32), NY)
    base = (z * NY + source) * NC + c
    run = jnp.where(upper == 1, 2 * nctx - 1 - base, base)
    starts = doc_starts // half
    first = jnp.max(jnp.where(starts[None, :] <= run[:, None], starts[None, :], 0), axis=1) // 2
    last = run // 2
    low0 = (first - y + NY - 1) // NY
    high0 = jnp.minimum((last - y + NY) // NY, NZ)
    low1 = (nctx - 1 - y - last + NY - 1) // NY
    high1 = jnp.minimum((nctx - 1 - y - first + NY) // NY, NZ)
    count0 = jnp.maximum(high0 - low0, 0)
    count1 = jnp.maximum(high1 - low1, 0)
    table = jnp.stack([run, upper * NY + source, low0, count0, low1, count1], axis=1)
    own = jnp.stack([y, c]).astype(jnp.int32)
    return jnp.concatenate([table.reshape(-1).astype(jnp.int32), own])


class Tile:
    def __init__(self, info, mine_ref, other_ref, heads):
        self.info, self.mine, self.other = info, mine_ref, other_ref
        self.half = mine_ref.shape[1] // 2
        self.width = mine_ref.shape[2] // 2
        self.cols = heads * self.half
        self.keys = 2 * self.half
        self.runs = 2 * NZ * NY * NC
        self.y = info[2 * NY * FIELDS]
        self.c = info[2 * NY * FIELDS + 1]
        row = lax.broadcasted_iota(jnp.int32, (self.keys, 1), 0)
        self.row_core = jnp.where(row < self.half, self.c, 1 - self.c)
        self.row_rest = row % self.half
        self.col_rest = lax.broadcasted_iota(jnp.int32, (1, self.cols), 1) % self.half

    def field(self, j, n):
        return self.info[j * FIELDS + n]

    def count(self, j):
        return self.field(j, 3) + self.field(j, 5)

    def place(self, j, i):
        lower = self.field(j, 3)
        part = (i >= lower).astype(jnp.int32)
        z = jnp.where(part == 1, self.field(j, 4) + i - lower, self.field(j, 2) + i)
        return z, part

    def rows(self, part):
        return pl.ds(pl.multiple_of(part * self.half, self.half), self.half)

    def block(self, place, second):
        z, part = place
        lanes = slice(self.width * second, self.width * (second + 1))
        return jnp.concatenate(
            [self.mine[z, self.rows(part), lanes], self.other[z, self.rows(part), lanes]], axis=0
        )

    def allowed(self, j, place):
        z, part = place
        run = (z * NY + self.y) * NC + self.row_core
        run = jnp.where(part == 1, self.runs - 1 - run, run)
        return run * self.half + self.row_rest <= self.field(j, 0) * self.half + self.col_rest


def stack_heads(refs, out_ref, lane0, half, width, heads):
    for k, ref in enumerate(refs):
        for side in (0, 1):
            for h in range(heads):
                out_ref[2 * k + side, h * half : (h + 1) * half, :] = ref[
                    0, side * half : (side + 1) * half, lane0 + h * width : lane0 + (h + 1) * width
                ]


def forward_kernel(heads, info, a0, a1, a2, a3, mine, other, u_ref, stats_ref, q_scr, do_scr, s_scr, st_scr):
    tile = Tile(info, mine, other, heads)
    half, width, cols = tile.half, tile.width, tile.cols
    log2_scale = math.log2(math.e) / math.sqrt(width)
    stack_heads((a0, a1, a2, a3), q_scr, 0, half, width, heads)
    stack_heads((a0, a1, a2, a3), do_scr, heads * width, half, width, heads)

    def one_run(j, _):
        q2 = q_scr[j]
        count = tile.count(j)

        def scores(i, biggest):
            place = tile.place(j, i)
            s = dot(tile.block(place, 0), q2, 1, 1)
            s = jnp.where(tile.allowed(j, place), s, FLOOR)
            s_scr[i] = s
            return jnp.maximum(biggest, jnp.max(s.reshape(tile.keys // 8, 8, cols), axis=0))

        biggest = lax.fori_loop(0, count, scores, jnp.full((8, cols), FLOOR, jnp.float32))
        top = jnp.max(biggest, axis=0, keepdims=True)

        def sums(i, carry):
            total, acc = carry
            e = jnp.exp2((s_scr[i] - top) * log2_scale)
            total = total + jnp.sum(e.reshape(tile.keys // 8, 8, cols), axis=0)
            values = tile.block(tile.place(j, i), 1)
            return total, acc + dot(values, e.astype(jnp.bfloat16), 0, 0)

        total, acc = lax.fori_loop(
            0, count, sums, (jnp.zeros((8, cols), jnp.float32), jnp.zeros((width, cols), jnp.float32))
        )
        u_ref[j] = acc
        row = pl.ds(tile.field(j, 1), 1)
        st_scr[0, row, :] = top
        st_scr[1, row, :] = jnp.sum(total, axis=0, keepdims=True)
        st_scr[2, row, :] = jnp.sum(acc * do_scr[j].astype(jnp.float32).T, axis=0, keepdims=True)
        return 0

    lax.fori_loop(0, 2 * NY, one_run, 0)
    for k in range(NY):
        stats_ref[k] = st_scr[...]


def backward_kernel(
    heads, info, a0, a1, a2, a3, mine, other, u_ref, stats,
    o0, o1, o2, o3, dmine, dother, q_scr, do_scr, dacc, att_scr, dq_scr, st_scr,
):
    tile = Tile(info, mine, other, heads)
    half, width, cols = tile.half, tile.width, tile.cols
    scale = 1.0 / math.sqrt(width)
    log2_scale = scale * math.log2(math.e)
    stack_heads((a0, a1, a2, a3), q_scr, 0, half, width, heads)
    stack_heads((a0, a1, a2, a3), do_scr, heads * width, half, width, heads)
    dmine[...] = jnp.zeros_like(dmine)
    dacc[...] = jnp.zeros_like(dacc)

    tops = [stats[k, 0] for k in range(NY)]
    top = functools.reduce(jnp.maximum, tops)
    weights = [jnp.exp2((t - top) * log2_scale) for t in tops]
    den = sum(w * stats[k, 1] for k, w in enumerate(weights))
    inverse = 1.0 / den
    st_scr[0] = top * log2_scale + jnp.log2(den)
    st_scr[1] = sum(w * stats[k, 2] for k, w in enumerate(weights)) * inverse
    st_scr[2] = jnp.exp2((stats[tile.y, 0] - top) * log2_scale) * inverse

    def one_run(j, _):
        q2 = q_scr[j]
        do2 = do_scr[j]
        row = pl.ds(tile.field(j, 1), 1)
        lse2 = st_scr[0, row, :]
        delta = st_scr[1, row, :]
        att_scr[j] = (u_ref[j] * st_scr[2, row, :]).T.astype(jnp.bfloat16)

        def visit(i, dq_t):
            place = tile.place(j, i)
            keys = tile.block(place, 0)
            s = dot(keys, q2, 1, 1)
            s = jnp.where(tile.allowed(j, place), s, FLOOR)
            p = jnp.exp2(s * log2_scale - lse2)
            dp = dot(tile.block(place, 1), do2, 1, 1)
            ds = (p * (dp - delta)).astype(jnp.bfloat16)
            dk = dot(ds, q2, 1, 0)
            dv = dot(p.astype(jnp.bfloat16), do2, 1, 0)
            z, part = place
            rows = tile.rows(part)
            dmine[z, rows, :width] += dk[:half]
            dmine[z, rows, width:] += dv[:half]
            dacc[z, rows, :width] += dk[half:]
            dacc[z, rows, width:] += dv[half:]
            return dq_t + dot(keys, ds, 0, 0)

        dq_t = lax.fori_loop(0, tile.count(j), visit, jnp.zeros((width, cols), jnp.float32))
        dq_scr[j] = (dq_t * scale).T.astype(jnp.bfloat16)
        return 0

    lax.fori_loop(0, 2 * NY, one_run, 0)
    dmine[:, :, :width] = dmine[:, :, :width] * scale
    dother[:, :, :width] = (dacc[:, :, :width] * scale).astype(dother.dtype)
    dother[:, :, width:] = dacc[:, :, width:].astype(dother.dtype)
    for k, out in enumerate((o0, o1, o2, o3)):
        for side in (0, 1):
            for h in range(heads):
                where = slice(side * half, (side + 1) * half)
                part = slice(h * half, (h + 1) * half)
                lanes = slice(h * width, (h + 1) * width)
                out[0, where, lanes] = att_scr[2 * k + side, part, :]
                lanes = slice((heads + h) * width, (heads + h + 1) * width)
                out[0, where, lanes] = dq_scr[2 * k + side, part, :]


def combine_kernel(o0, o1, o2, o3, dkv, att_ref, dq_ref, dkv_ref, sq_ref):
    wide = att_ref.shape[2]
    parts = [o[0].astype(jnp.float32) for o in (o0, o1, o2, o3)]
    both = (parts[0] + parts[1]) + (parts[2] + parts[3])
    att_ref[0] = both[:, :wide].astype(att_ref.dtype)
    dq = both[:, wide:]
    dq_ref[0] = dq
    total = functools.reduce(jnp.add, [dkv[k].astype(jnp.float32) for k in range(NZ)])
    dkv_ref[0] = total
    squares = jnp.sum(dq * dq) + jnp.sum(total * total)
    sq_ref[...] = jnp.full(sq_ref.shape, squares, jnp.float32)


def scale_kernel(count, sums, dq, dkv, oq, ok, ov):
    lanes = sums.shape[2]
    total = sums[0]
    for k in range(1, sums.shape[0]):
        total = total + sums[k]
    factor = lax.rsqrt(total / count + 1e-06)
    for h in range(dq.shape[2] // lanes):
        at = slice(h * lanes, (h + 1) * lanes)
        oq[0, :, at] = (dq[0, :, at] * factor).astype(oq.dtype)
    width = ok.shape[2]
    ok[0] = (dkv[0, :, :width] * factor).astype(ok.dtype)
    ov[0] = (dkv[0, :, width:] * factor).astype(ov.dtype)


def turn(x, axis, size, by):
    return lax.ppermute(x, axis, [(i, (i + by) % size) for i in range(size)])


def per_device(queries, keys, values, grad_out, doc_starts):
    tok = queries.shape[1]
    wide = queries.shape[2]
    width = keys.shape[2]
    heads = wide // width
    half = tok // 2
    cols = heads * half
    z, y, c = (lax.axis_index(a) for a in ("z", "y", "core"))
    info = visits(doc_starts[0], tok, z, y, c)

    asked = jnp.concatenate([queries, grad_out], axis=2)
    around = [asked] + [turn(asked, "y", NY, -k) for k in range(1, NY)]
    kv = jnp.concatenate([keys, values], axis=2)
    mine = lax.all_to_all(jnp.broadcast_to(kv, (NZ, tok, 2 * width)), "z", 0, 0, tiled=True)
    other = turn(mine, "core", NC, 1)

    f32, bf16 = jnp.float32, jnp.bfloat16
    shape = jax.ShapeDtypeStruct
    u, stats = pl.pallas_call(
        functools.partial(forward_kernel, heads),
        out_shape=(shape((2 * NY, width, cols), f32), shape((NY, 3, 2 * NY, cols), f32)),
        in_specs=[SMEM] + [VMEM] * 6,
        out_specs=(VMEM, VMEM),
        scratch_shapes=[
            pltpu.VMEM((2 * NY, cols, width), bf16),
            pltpu.VMEM((2 * NY, cols, width), bf16),
            pltpu.VMEM((2 * NZ, tok, cols), f32),
            pltpu.VMEM((3, 2 * NY, cols), f32),
        ],
        compiler_params=PARAMS,
    )(info, *around, mine, other)
    stats = lax.all_to_all(stats, "y", 0, 0, tiled=True)
    *sent, dmine, dother = pl.pallas_call(
        functools.partial(backward_kernel, heads),
        out_shape=[shape(asked.shape, bf16)] * NY
        + [shape(mine.shape, f32), shape(mine.shape, bf16)],
        in_specs=[SMEM] + [VMEM] * 8,
        out_specs=[VMEM] * (NY + 2),
        scratch_shapes=[
            pltpu.VMEM((2 * NY, cols, width), bf16),
            pltpu.VMEM((2 * NY, cols, width), bf16),
            pltpu.VMEM(mine.shape, f32),
            pltpu.VMEM((2 * NY, cols, width), bf16),
            pltpu.VMEM((2 * NY, cols, width), bf16),
            pltpu.VMEM((3, 2 * NY, cols), f32),
        ],
        compiler_params=PARAMS,
    )(info, *around, mine, other, u, stats)
    back = [sent[0]] + [turn(sent[k], "y", NY, k) for k in range(1, NY)]
    from_core = turn(dother, "core", NC, 1)
    pair = (dmine + from_core.astype(f32)).astype(bf16)
    pieces = lax.all_to_all(pair, "z", 0, 0, tiled=True)
    attended, dq, dkv, squares = pl.pallas_call(
        combine_kernel,
        out_shape=(
            shape(queries.shape, bf16),
            shape(queries.shape, f32),
            shape(kv.shape, f32),
            shape((NZ * NY, 1, 128), f32),
        ),
        in_specs=[VMEM] * 5,
        out_specs=(VMEM,) * 4,
        compiler_params=PARAMS,
    )(*back, pieces)
    squares = lax.all_to_all(squares, ("z", "y"), 0, 0, tiled=True)
    ndata = lax.axis_size("dp")
    squares = jnp.broadcast_to(jnp.sum(squares, axis=0, keepdims=True), (NC * ndata, 1, 128))
    squares = lax.all_to_all(squares, ("core", "dp"), 0, 0, tiled=True)
    count = float(ndata * NZ * NY * NC * tok * (wide + 2 * width))
    out_query, out_key, out_value = pl.pallas_call(
        functools.partial(scale_kernel, count),
        out_shape=(shape(queries.shape, bf16), shape(keys.shape, bf16), shape(values.shape, bf16)),
        in_specs=[VMEM] * 3,
        out_specs=(VMEM,) * 3,
        compiler_params=PARAMS,
    )(squares, dq, dkv)
    return attended, out_query, out_key, out_value


def solution(mesh):
    ndata = mesh.shape["dp"]
    fine = Mesh(mesh.devices.reshape(NZ, NY, NC, ndata), ("z", "y", "core", "dp"))
    spec = P("dp", ("z", "y", "core"), None)
    return jax.shard_map(
        per_device,
        mesh=fine,
        in_specs=(spec, spec, spec, spec, P("dp", None)),
        out_specs=(spec, spec, spec, spec),
        check_vma=False,
    )
```

time: 388 us -> 153 us (0.39)
  waiting for transfers between devices: 255 us -> 41.3 us
  blocking collectives: 100 us -> 39.4 us
  starting transfers between devices: 0.08 us -> 56.1 us
  between operations: 16.1 us -> 0.81 us
  other arithmetic: 7.09 us -> 1.42 us
  Pallas kernels: 5.13 us -> 10.1 us
    reduce_scatter x1 -> x0, waiting for transfers between devices: 161 us -> none  [per_device(): lax.psum_scatter(partial, 'ctx', scatter_dimension=0, tiled=True)]
    psum x1 -> x0, blocking collectives: 100 us -> none  [per_device(): total = lax.psum(jnp.sum(raw * raw) + squares[0, 0], ('ctx', 'dp'))]
    all_gather x1 -> x0, waiting for transfers between devices: 93.7 us -> none  [per_device(): kv = lax.all_gather(kv, 'ctx', axis=0, tiled=True)]
    all_to_all x0 -> x3, blocking collectives: none -> 39.4 us  [the longest x1 18.2 us: per_device(): squares = lax.all_to_all(squares, ('z', 'y'), 0, 0, tiled=True)]
    ppermute x0 -> x8, starting transfers between devices: none -> 33.8 us  [turn(): return lax.ppermute(x, axis, [(i, (i + by) % size) for i in range(size)])]
    ppermute x0 -> x8, waiting for transfers between devices: none -> 26.8 us  [turn(): return lax.ppermute(x, axis, [(i, (i + by) % size) for i in range(size)])]
    all_to_all x0 -> x2, starting transfers between devices: none -> 22.2 us  [the longest x1 12.2 us: per_device(): pieces = lax.all_to_all(pair, 'z', 0, 0, tiled=True)]
    all_to_all x0 -> x2, waiting for transfers between devices: none -> 14.6 us  [the longest x1 14.6 us: per_device(): lax.all_to_all(jnp.broadcast_to(kv, (NZ, tok, 2 * width)), 'z', 0, 0, til...]
  transfers between devices with their start and end apart: 2 -> 10, of which waited for: 2 -> 6; matrix products, arithmetic and copies ran while one was open for 1% -> 1% of each run, Pallas kernels for 0% -> 0%
where the time goes in v2:
time: 153 us; the launch traced here: 152 us
  starting transfers between devices  56.1 us (37%)
  waiting for transfers between devices  41.3 us (27%)
  blocking collectives  39.4 us (26%)
  Pallas kernels  10.1 us (7%)
  local copies, waits for them, and re-layouts  3.08 us (2%)
    ppermute x8, starting transfers between devices, turn(): return lax.ppermute(x, axis, [(i, (i + by) % size) for i in range(size)])  33.8 us
    ppermute x8, waiting for transfers between devices, turn(): return lax.ppermute(x, axis, [(i, (i + by) % size) for i in range(size)])  26.8 us
    all_to_all x1, blocking collectives, per_device(): squares = lax.all_to_all(squares, ('z', 'y'), 0, 0, tiled=True)  18.2 us
    all_to_all x1, waiting for transfers between devices, per_device(): lax.all_to_all(jnp.broadcast_to(kv, (NZ, tok, 2 * width)), 'z', 0, 0, til...  14.6 us
    all_to_all x1, starting transfers between devices, per_device(): pieces = lax.all_to_all(pair, 'z', 0, 0, tiled=True)  12.2 us
    all_to_all x1, blocking collectives, per_device(): squares = lax.all_to_all(squares, ('core', 'dp'), 0, 0, tiled=True)  11.8 us
    all_to_all x1, starting transfers between devices, per_device(): lax.all_to_all(jnp.broadcast_to(kv, (NZ, tok, 2 * width)), 'z', 0, 0, til...  10 us
    all_to_all x1, blocking collectives, per_device(): stats = lax.all_to_all(stats, 'y', 0, 0, tiled=True)  9.43 us
  transfers between devices with their start and end apart: 10, of which 6 were waited for; matrix products, arithmetic and copies ran while one was open for 1% of the time, Pallas kernels for 0%

profile of v2, /device:TPU:1, one launch (start us, length us, event | category | flops | bytes accessed | tf_op | source)
XLA Modules:
  0.0 152.2 jit_solution(12971544808598942579)
XLA Ops:
  0.6 0.0 copy-start
  0.6 0.9 constant_dynamic-update-slice_fusion.1
  1.6 0.0 copy-done
  1.6 0.0 copy-start.1
  1.6 0.0 copy-start.2
  1.6 5.0 %collective-permute-start.2 = (bf16[1,128,1024]{2,1,0:T(8,128)(2,1)S(1)}, bf16[1,128,1024]{2,1,0:T(8,128)(2,1)S(1)}, u32[]{:S(2)}, u32[]{:S(2)}) collective-permute-start(bf16[1,128,1024]{2,1,0:T(8,128)(2,1)S(1)} %constant_dynamic-update-slice_fusion.a0), channel_id=1, source_target_pairs={{0,16},{16,32},{32,48},{48,0},{1,17},{17,33},{33,49},{49,1},{2,18}... | collective-permute-start | bytes 786440 | tf_op jit(solution)/shard_map/ppermute | solution.py:236
  6.7 5.7 %collective-permute-start.1 = (bf16[1,128,1024]{2,1,0:T(8,128)(2,1)S(1)}, bf16[1,128,1024]{2,1,0:T(8,128)(2,1)S(1)}, u32[]{:S(2)}, u32[]{:S(2)}) collective-permute-start(bf16[1,128,1024]{2,1,0:T(8,128)(2,1)S(1)} %constant_dynamic-update-slice_fusion.a0), channel_id=1, source_target_pairs={{0,32},{16,48},{32,0},{48,16},{1,33},{17,49},{33,1},{49,17},{2,34}... | collective-permute-start | bytes 786440 | tf_op jit(solution)/shard_map/ppermute | solution.py:236
  12.4 5.0 %collective-permute-start = (bf16[1,128,1024]{2,1,0:T(8,128)(2,1)S(1)}, bf16[1,128,1024]{2,1,0:T(8,128)(2,1)S(1)}, u32[]{:S(2)}, u32[]{:S(2)}) collective-permute-start(bf16[1,128,1024]{2,1,0:T(8,128)(2,1)S(1)} %constant_dynamic-update-slice_fusion.a0), channel_id=1, source_target_pairs={{0,48},{16,0},{32,16},{48,32},{1,49},{17,1},{33,17},{49,33},{2,50}... | collective-permute-start | bytes 786440 | tf_op jit(solution)/shard_map/ppermute | solution.py:236
  17.3 0.0 copy-done.1
  17.4 0.0 copy-done.2
  17.4 0.8 broadcast_in_dim.35
  18.2 10.0 %all-to-all-start = ((bf16[8,128,256]{2,1,0:T(8,128)(2,1)}), bf16[8,128,256]{2,1,0:T(8,128)(2,1)S(1)}, u32[]{:S(2)}, u32[]{:S(2)}) async-start(bf16[8,128,256]{2,1,0:T(8,128)(2,1)} %broadcast_in_dim.35), calls=%async_computation | async-start | bytes 1048576 | tf_op jit(solution)/shard_map/all_to_all | solution.py:252
  28.3 0.1 eq.35
  28.3 0.1 eq.34
  28.4 0.1 broadcast_in_dim.31
  28.5 0.1 add.230
  28.6 0.1 add.227
  28.7 0.1 multiply_add_fusion
  28.8 0.0 copy-start.3
  28.8 0.1 add.229
  28.8 0.6 copy-done.3
  29.4 0.2 select_reduce_fusion
  29.6 14.6 %all-to-all-done.mine = bf16[8,128,256]{2,1,0:T(8,128)(2,1)S(1)} async-done(((bf16[8,128,256]{2,1,0:T(8,128)(2,1)}), bf16[8,128,256]{2,1,0:T(8,128)(2,1)S(1)}, u32[]{:S(2)}, u32[]{:S(2)}) %all-to-all-start) | async-done | bytes 524320 | tf_op jit(solution)/shard_map/all_to_all | solution.py:252
  44.2 4.4 %collective-permute-start.3 = (bf16[8,128,256]{2,1,0:T(8,128)(2,1)S(1)}, bf16[8,128,256]{2,1,0:T(8,128)(2,1)S(1)}, u32[]{:S(2)}, u32[]{:S(2)}) collective-permute-start(bf16[8,128,256]{2,1,0:T(8,128)(2,1)S(1)} %all-to-all-done.mine), channel_id=1, source_target_pairs={{0,8},{8,0},{1,9},{9,1},{2,10},{10,2},{3,11},{11,3},{4,12},{12,4},... | collective-permute-start | bytes 1572872 | tf_op jit(solution)/shard_map/ppermute | solution.py:236
  48.7 0.1 copy.11
  48.8 0.1 reshape.438
  48.9 0.1 pad_add_fusion.info
  48.9 0.0 collective-permute-done.2.a3
  48.9 0.0 collective-permute-done.1.a2
  48.9 0.0 collective-permute-done.a1
  48.9 1.2 collective-permute-done.3.other
  50.1 3.7 %shard_map.84 = (f32[8,128,256]{2,1,0:T(8,128)S(1)}, f32[4,3,8,256]{3,2,1,0:T(8,128)S(1)}) custom-call(s32[50]{0:T(128)S(1)} %pad_add_fusion.info, bf16[1,128,1024]{2,1,0:T(8,128)(2,1)S(1)} %constant_dynamic-update-slice_fusion.a0, bf16[1,128,1024]{2,1,0:T(8,128)(2,1)S(1)} %collective-permute-done.a1, bf16[1,128,1024]{2,1,0:T(8,128)(2,1)S(1)} %collective-permute-done.1.a2, ...), custom_call_target="tpu_custom_call" | custom-call | tf_op jit(solution)/shard_map/pallas_call | solution.py:257
  53.8 9.4 %all_to_all.25.stats = f32[4,3,8,256]{3,2,1,0:T(8,128)S(1)} all-to-all(f32[4,3,8,256]{3,2,1,0:T(8,128)S(1)} %get-tuple-element.20), channel_id=1, replica_groups=mesh['z'=8,'y'=4,'core'=2,'dp'=8] {'y'}, dimensions={0} | all-to-all | bytes 196608 | tf_op jit(solution)/shard_map/all_to_all | solution.py:270
  63.2 4.7 %shard_map.85 = (bf16[1,128,1024]{2,1,0:T(8,128)(2,1)S(1)}, bf16[1,128,1024]{2,1,0:T(8,128)(2,1)S(1)}, bf16[1,128,1024]{2,1,0:T(8,128)(2,1)S(1)}, bf16[1,128,102...) custom-call(s32[50]{0:T(128)S(1)} %pad_add_fusion.info, ...), custom_call_target="tpu_custom_call" | custom-call | tf_op jit(solution)/shard_map/pallas_call | solution.py:271
  67.9 4.4 %collective-permute-start.7 = (bf16[8,128,256]{2,1,0:T(8,128)(2,1)S(1)}, bf16[8,128,256]{2,1,0:T(8,128)(2,1)S(1)}, u32[]{:S(2)}, u32[]{:S(2)}) collective-permute-start(bf16[8,128,256]{2,1,0:T(8,128)(2,1)S(1)} %get-tuple-element.26), channel_id=1, source_target_pairs={{0,8},{8,0},{1,9},{9,1},{2,10},{10,2},{3,11},{11,3},{4,12},{12,4},... | collective-permute-start | bytes 1572872 | tf_op jit(solution)/shard_map/ppermute | solution.py:236
  72.4 1.5 collective-permute-done.7
  73.9 0.9 add_convert_fusion
  74.8 12.2 %all-to-all-start.2 = ((bf16[8,128,256]{2,1,0:T(8,128)(2,1)}), bf16[8,128,256]{2,1,0:T(8,128)(2,1)S(1)}, u32[]{:S(2)}, u32[]{:S(2)}) async-start(bf16[8,128,256]{2,1,0:T(8,128)(2,1)} %add_convert_fusion), calls=%async_computation.2 | async-start | bytes 1048576 | tf_op jit(solution)/shard_map/all_to_all | solution.py:290
  87.0 1.9 %collective-permute-start.4 = (bf16[1,128,1024]{2,1,0:T(8,128)(2,1)S(1)}, bf16[1,128,1024]{2,1,0:T(8,128)(2,1)S(1)}, u32[]{:S(2)}, u32[]{:S(2)}) collective-permute-start(bf16[1,128,1024]{2,1,0:T(8,128)(2,1)S(1)} %get-tuple-element.22), channel_id=1, source_target_pairs={{0,16},{16,32},{32,48},{48,0},{1,17},{17,33},{33,49},{49,1},{2,18}... | collective-permute-start | bytes 786440 | tf_op jit(solution)/shard_map/ppermute | solution.py:236
  89.0 4.5 %collective-permute-start.5 = (bf16[1,128,1024]{2,1,0:T(8,128)(2,1)S(1)}, bf16[1,128,1024]{2,1,0:T(8,128)(2,1)S(1)}, u32[]{:S(2)}, u32[]{:S(2)}) collective-permute-start(bf16[1,128,1024]{2,1,0:T(8,128)(2,1)S(1)} %get-tuple-element.23), channel_id=1, source_target_pairs={{0,32},{16,48},{32,0},{48,16},{1,33},{17,49},{33,1},{49,17},{2,34}... | collective-permute-start | bytes 786440 | tf_op jit(solution)/shard_map/ppermute | solution.py:236
  93.5 2.9 %collective-permute-start.6 = (bf16[1,128,1024]{2,1,0:T(8,128)(2,1)S(1)}, bf16[1,128,1024]{2,1,0:T(8,128)(2,1)S(1)}, u32[]{:S(2)}, u32[]{:S(2)}) collective-permute-start(bf16[1,128,1024]{2,1,0:T(8,128)(2,1)S(1)} %get-tuple-element.24), channel_id=1, source_target_pairs={{0,48},{16,0},{32,16},{48,32},{1,49},{17,1},{33,17},{49,33},{2,50}... | collective-permute-start | bytes 786440 | tf_op jit(solution)/shard_map/ppermute | solution.py:236
  96.4 5.2 %collective-permute-done.4.o1 = bf16[1,128,1024]{2,1,0:T(8,128)(2,1)S(1)} collective-permute-done((bf16[1,128,1024]{2,1,0:T(8,128)(2,1)S(1)}, bf16[1,128,1024]{2,1,0:T(8,128)(2,1)S(1)}, u32[]{:S(2)}, u32[]{:S(2)}) %collective-permute-start.4) | collective-permute-done | bytes 262176 | tf_op jit(solution)/shard_map/ppermute | solution.py:236
  101.6 10.0 %collective-permute-done.5.o2 = bf16[1,128,1024]{2,1,0:T(8,128)(2,1)S(1)} collective-permute-done((bf16[1,128,1024]{2,1,0:T(8,128)(2,1)S(1)}, bf16[1,128,1024]{2,1,0:T(8,128)(2,1)S(1)}, u32[]{:S(2)}, u32[]{:S(2)}) %collective-permute-start.5) | collective-permute-done | bytes 262176 | tf_op jit(solution)/shard_map/ppermute | solution.py:236
  111.6 8.9 %collective-permute-done.6.o3 = bf16[1,128,1024]{2,1,0:T(8,128)(2,1)S(1)} collective-permute-done((bf16[1,128,1024]{2,1,0:T(8,128)(2,1)S(1)}, bf16[1,128,1024]{2,1,0:T(8,128)(2,1)S(1)}, u32[]{:S(2)}, u32[]{:S(2)}) %collective-permute-start.6) | collective-permute-done | bytes 262176 | tf_op jit(solution)/shard_map/ppermute | solution.py:236
  120.5 0.0 all-to-all-done.2.dkv
  120.5 1.0 shard_map.86
  121.5 18.2 %all_to_all.26 = f32[32,1,128]{2,1,0:T(1,128)S(1)} all-to-all(f32[32,1,128]{2,1,0:T(1,128)S(1)} %get-tuple-element.28), channel_id=1, replica_groups=mesh['z'=8,'y'=4,'core'=2,'dp'=8] {'z','y'}, dimensions={0} | all-to-all | bytes 32768 | tf_op jit(solution)/shard_map/all_to_all | solution.py:303
  139.6 0.1 reduce_sum.9
  139.7 11.8 %all_to_all.27.sums = f32[16,1,128]{2,1,0:T(1,128)S(1)} all-to-all(f32[16,1,128]{2,1,0:T(1,128)S(1)} %broadcast_in_dim.36), channel_id=1, replica_groups=mesh['z'=8,'y'=4,'core'=2,'dp'=8] {'core','dp'}, dimensions={0} | all-to-all | bytes 16384 | tf_op jit(solution)/shard_map/all_to_all | solution.py:306
  151.5 0.7 shard_map.87
  (10 shorter events, 0.1 us)
Async XLA Ops:
  0.6 1.0 copy-start
  1.6 15.7 %copy-start.1 = (bf16[1,128,128]{2,1,0:T(8,128)(2,1)S(1)}, bf16[1,128,128]{2,1,0:T(8,128)(2,1)}, u32[]{:S(2)}) copy-start(bf16[1,128,128]{2,1,0:T(8,128)(2,1)} %param.7) | copy-start | bytes 98308
  1.6 15.7 %copy-start.2 = (bf16[1,128,128]{2,1,0:T(8,128)(2,1)S(1)}, bf16[1,128,128]{2,1,0:T(8,128)(2,1)}, u32[]{:S(2)}) copy-start(bf16[1,128,128]{2,1,0:T(8,128)(2,1)} %param.6) | copy-start | bytes 98308
  1.6 47.3 %collective-permute-start.2 = (bf16[1,128,1024]{2,1,0:T(8,128)(2,1)S(1)}, bf16[1,128,1024]{2,1,0:T(8,128)(2,1)S(1)}, u32[]{:S(2)}, u32[]{:S(2)}) collective-permute-start(bf16[1,128,1024]{2,1,0:T(8,128)(2,1)S(1)} %constant_dynamic-update-slice_fusion.a0), channel_id=1, source_target_pairs={{0,16},{16,32},{32,48},{48,0},{1,17},{17,33},{33,49},{49,1},{2,18}... | collective-permute-start | bytes 786440 | tf_op jit(solution)/shard_map/ppermute | solution.py:236
  6.7 42.2 %collective-permute-start.1 = (bf16[1,128,1024]{2,1,0:T(8,128)(2,1)S(1)}, bf16[1,128,1024]{2,1,0:T(8,128)(2,1)S(1)}, u32[]{:S(2)}, u32[]{:S(2)}) collective-permute-start(bf16[1,128,1024]{2,1,0:T(8,128)(2,1)S(1)} %constant_dynamic-update-slice_fusion.a0), channel_id=1, source_target_pairs={{0,32},{16,48},{32,0},{48,16},{1,33},{17,49},{33,1},{49,17},{2,34}... | collective-permute-start | bytes 786440 | tf_op jit(solution)/shard_map/ppermute | solution.py:236
  12.4 36.6 %collective-permute-start = (bf16[1,128,1024]{2,1,0:T(8,128)(2,1)S(1)}, bf16[1,128,1024]{2,1,0:T(8,128)(2,1)S(1)}, u32[]{:S(2)}, u32[]{:S(2)}) collective-permute-start(bf16[1,128,1024]{2,1,0:T(8,128)(2,1)S(1)} %constant_dynamic-update-slice_fusion.a0), channel_id=1, source_target_pairs={{0,48},{16,0},{32,16},{48,32},{1,49},{17,1},{33,17},{49,33},{2,50}... | collective-permute-start | bytes 786440 | tf_op jit(solution)/shard_map/ppermute | solution.py:236
  18.2 26.0 %all-to-all-start = ((bf16[8,128,256]{2,1,0:T(8,128)(2,1)}), bf16[8,128,256]{2,1,0:T(8,128)(2,1)S(1)}, u32[]{:S(2)}, u32[]{:S(2)}) async-start(bf16[8,128,256]{2,1,0:T(8,128)(2,1)} %broadcast_in_dim.35), calls=%async_computation | async-start | bytes 1048576 | tf_op jit(solution)/shard_map/all_to_all | solution.py:252
  28.8 0.7 copy-start.3
  44.2 5.9 %collective-permute-start.3 = (bf16[8,128,256]{2,1,0:T(8,128)(2,1)S(1)}, bf16[8,128,256]{2,1,0:T(8,128)(2,1)S(1)}, u32[]{:S(2)}, u32[]{:S(2)}) collective-permute-start(bf16[8,128,256]{2,1,0:T(8,128)(2,1)S(1)} %all-to-all-done.mine), channel_id=1, source_target_pairs={{0,8},{8,0},{1,9},{9,1},{2,10},{10,2},{3,11},{11,3},{4,12},{12,4},... | collective-permute-start | bytes 1572872 | tf_op jit(solution)/shard_map/ppermute | solution.py:236
  67.9 6.0 %collective-permute-start.7 = (bf16[8,128,256]{2,1,0:T(8,128)(2,1)S(1)}, bf16[8,128,256]{2,1,0:T(8,128)(2,1)S(1)}, u32[]{:S(2)}, u32[]{:S(2)}) collective-permute-start(bf16[8,128,256]{2,1,0:T(8,128)(2,1)S(1)} %get-tuple-element.26), channel_id=1, source_target_pairs={{0,8},{8,0},{1,9},{9,1},{2,10},{10,2},{3,11},{11,3},{4,12},{12,4},... | collective-permute-start | bytes 1572872 | tf_op jit(solution)/shard_map/ppermute | solution.py:236
  74.8 45.6 %all-to-all-start.2 = ((bf16[8,128,256]{2,1,0:T(8,128)(2,1)}), bf16[8,128,256]{2,1,0:T(8,128)(2,1)S(1)}, u32[]{:S(2)}, u32[]{:S(2)}) async-start(bf16[8,128,256]{2,1,0:T(8,128)(2,1)} %add_convert_fusion), calls=%async_computation.2 | async-start | bytes 1048576 | tf_op jit(solution)/shard_map/all_to_all | solution.py:290
  87.0 14.6 %collective-permute-start.4 = (bf16[1,128,1024]{2,1,0:T(8,128)(2,1)S(1)}, bf16[1,128,1024]{2,1,0:T(8,128)(2,1)S(1)}, u32[]{:S(2)}, u32[]{:S(2)}) collective-permute-start(bf16[1,128,1024]{2,1,0:T(8,128)(2,1)S(1)} %get-tuple-element.22), channel_id=1, source_target_pairs={{0,16},{16,32},{32,48},{48,0},{1,17},{17,33},{33,49},{49,1},{2,18}... | collective-permute-start | bytes 786440 | tf_op jit(solution)/shard_map/ppermute | solution.py:236
  89.0 22.6 %collective-permute-start.5 = (bf16[1,128,1024]{2,1,0:T(8,128)(2,1)S(1)}, bf16[1,128,1024]{2,1,0:T(8,128)(2,1)S(1)}, u32[]{:S(2)}, u32[]{:S(2)}) collective-permute-start(bf16[1,128,1024]{2,1,0:T(8,128)(2,1)S(1)} %get-tuple-element.23), channel_id=1, source_target_pairs={{0,32},{16,48},{32,0},{48,16},{1,33},{17,49},{33,1},{49,17},{2,34}... | collective-permute-start | bytes 786440 | tf_op jit(solution)/shard_map/ppermute | solution.py:236
  93.5 27.0 %collective-permute-start.6 = (bf16[1,128,1024]{2,1,0:T(8,128)(2,1)S(1)}, bf16[1,128,1024]{2,1,0:T(8,128)(2,1)S(1)}, u32[]{:S(2)}, u32[]{:S(2)}) collective-permute-start(bf16[1,128,1024]{2,1,0:T(8,128)(2,1)S(1)} %get-tuple-element.24), channel_id=1, source_target_pairs={{0,48},{16,0},{32,16},{48,32},{1,49},{17,1},{33,17},{49,33},{2,50}... | collective-permute-start | bytes 786440 | tf_op jit(solution)/shard_map/ppermute | solution.py:236

commit v3 on v2

--- a/solution.py
+++ b/solution.py
@@ -43,18 +43,20 @@
 
 
 class Tile:
-    def __init__(self, info, mine_ref, other_ref, heads):
-        self.info, self.mine, self.other = info, mine_ref, other_ref
-        self.half = mine_ref.shape[1] // 2
-        self.width = mine_ref.shape[2] // 2
+    def __init__(self, info, pairs_ref, heads):
+        self.info, self.pairs = info, pairs_ref
+        self.keys = pairs_ref.shape[1]
+        self.half = self.keys // 2
+        self.width = pairs_ref.shape[2] // 2
         self.cols = heads * self.half
-        self.keys = 2 * self.half
         self.runs = 2 * NZ * NY * NC
         self.y = info[2 * NY * FIELDS]
         self.c = info[2 * NY * FIELDS + 1]
         row = lax.broadcasted_iota(jnp.int32, (self.keys, 1), 0)
-        self.row_core = jnp.where(row < self.half, self.c, 1 - self.c)
-        self.row_rest = row % self.half
+        core = jnp.where(row < self.half, self.c, 1 - self.c)
+        rest = row % self.half
+        self.row_low = core * self.half + rest
+        self.row_high = (self.runs - 1 - core) * self.half + rest
         self.col_rest = lax.broadcasted_iota(jnp.int32, (1, self.cols), 1) % self.half
 
     def field(self, j, n):
@@ -63,27 +65,42 @@
     def count(self, j):
         return self.field(j, 3) + self.field(j, 5)
 
-    def place(self, j, i):
-        lower = self.field(j, 3)
-        part = (i >= lower).astype(jnp.int32)
-        z = jnp.where(part == 1, self.field(j, 4) + i - lower, self.field(j, 2) + i)
-        return z, part
-
-    def rows(self, part):
-        return pl.ds(pl.multiple_of(part * self.half, self.half), self.half)
-
-    def block(self, place, second):
-        z, part = place
-        lanes = slice(self.width * second, self.width * (second + 1))
-        return jnp.concatenate(
-            [self.mine[z, self.rows(part), lanes], self.other[z, self.rows(part), lanes]], axis=0
-        )
-
-    def allowed(self, j, place):
-        z, part = place
-        run = (z * NY + self.y) * NC + self.row_core
-        run = jnp.where(part == 1, self.runs - 1 - run, run)
-        return run * self.half + self.row_rest <= self.field(j, 0) * self.half + self.col_rest
+    def steps(self, j):
+        return (self.count(j) + 1) // 2
+
+    def blocks(self, j, i):
+        def place(n):
+            lower = self.field(j, 3)
+            return jnp.where(n >= lower, self.field(j, 4) + NZ + n - lower, self.field(j, 2) + n)
+
+        second = jnp.minimum(2 * i + 1, self.count(j) - 1)
+        return place(2 * i), place(second)
+
+    def allowed(self, j, i, blocks):
+        parts = []
+        for n, b in enumerate(blocks):
+            step = NY * NC * self.half
+            low = b * step + self.y * NC * self.half + self.row_low
+            high = self.row_high - (b - NZ) * step - self.y * NC * self.half
+            at = jnp.where(b >= NZ, high, low)
+            if n:
+                at = jnp.where(2 * i + 1 < self.count(j), at, jnp.int32(2**30))
+            parts.append(at)
+        return jnp.concatenate(parts, axis=0) <= self.field(j, 0) * self.half + self.col_rest
+
+
+def two(ref, blocks, lanes, axis):
+    return jnp.concatenate([ref[b, :, lanes] for b in blocks], axis=axis)
+
+
+def gather_kernel(mine, other, pairs, turned):
+    half = mine.shape[1] // 2
+    width = mine.shape[2] // 2
+    for b in range(2 * NZ):
+        rows = slice((b // NZ) * half, (b // NZ + 1) * half)
+        block = jnp.concatenate([mine[b % NZ, rows], other[b % NZ, rows]], axis=0)
+        pairs[b] = block
+        turned[b] = block.astype(jnp.float32).T.astype(turned.dtype)
 
 
 def stack_heads(refs, out_ref, lane0, half, width, heads):
@@ -95,36 +112,37 @@
                 ]
 
 
-def forward_kernel(heads, info, a0, a1, a2, a3, mine, other, u_ref, stats_ref, q_scr, do_scr, s_scr, st_scr):
-    tile = Tile(info, mine, other, heads)
+def forward_kernel(heads, info, a0, a1, a2, a3, pairs, turned, u_ref, stats_ref, q_scr, do_scr, s_scr, st_scr):
+    tile = Tile(info, pairs, heads)
     half, width, cols = tile.half, tile.width, tile.cols
     log2_scale = math.log2(math.e) / math.sqrt(width)
     stack_heads((a0, a1, a2, a3), q_scr, 0, half, width, heads)
     stack_heads((a0, a1, a2, a3), do_scr, heads * width, half, width, heads)
+    groups = 2 * tile.keys // 8
 
     def one_run(j, _):
         q2 = q_scr[j]
-        count = tile.count(j)
+        steps = tile.steps(j)
 
         def scores(i, biggest):
-            place = tile.place(j, i)
-            s = dot(tile.block(place, 0), q2, 1, 1)
-            s = jnp.where(tile.allowed(j, place), s, FLOOR)
+            blocks = tile.blocks(j, i)
+            s = dot(two(pairs, blocks, slice(0, width), 0), q2, 1, 1)
+            s = jnp.where(tile.allowed(j, i, blocks), s, FLOOR)
             s_scr[i] = s
-            return jnp.maximum(biggest, jnp.max(s.reshape(tile.keys // 8, 8, cols), axis=0))
-
-        biggest = lax.fori_loop(0, count, scores, jnp.full((8, cols), FLOOR, jnp.float32))
+            return jnp.maximum(biggest, jnp.max(s.reshape(groups, 8, cols), axis=0))
+
+        biggest = lax.fori_loop(0, steps, scores, jnp.full((8, cols), FLOOR, jnp.float32))
         top = jnp.max(biggest, axis=0, keepdims=True)
 
         def sums(i, carry):
             total, acc = carry
             e = jnp.exp2((s_scr[i] - top) * log2_scale)
-            total = total + jnp.sum(e.reshape(tile.keys // 8, 8, cols), axis=0)
-            values = tile.block(tile.place(j, i), 1)
-            return total, acc + dot(values, e.astype(jnp.bfloat16), 0, 0)
+            total = total + jnp.sum(e.reshape(groups, 8, cols), axis=0)
+            values_t = jnp.concatenate([turned[b, width:, :] for b in tile.blocks(j, i)], axis=1)
+            return total, acc + dot(values_t, e.astype(jnp.bfloat16), 1, 0)
 
         total, acc = lax.fori_loop(
-            0, count, sums, (jnp.zeros((8, cols), jnp.float32), jnp.zeros((width, cols), jnp.float32))
+            0, steps, sums, (jnp.zeros((8, cols), jnp.float32), jnp.zeros((width, cols), jnp.float32))
         )
         u_ref[j] = acc
         row = pl.ds(tile.field(j, 1), 1)
@@ -139,16 +157,15 @@
 
 
 def backward_kernel(
-    heads, info, a0, a1, a2, a3, mine, other, u_ref, stats,
+    heads, info, a0, a1, a2, a3, pairs, turned, u_ref, stats,
     o0, o1, o2, o3, dmine, dother, q_scr, do_scr, dacc, att_scr, dq_scr, st_scr,
 ):
-    tile = Tile(info, mine, other, heads)
-    half, width, cols = tile.half, tile.width, tile.cols
+    tile = Tile(info, pairs, heads)
+    half, width, cols, keys = tile.half, tile.width, tile.cols, tile.keys
     scale = 1.0 / math.sqrt(width)
     log2_scale = scale * math.log2(math.e)
     stack_heads((a0, a1, a2, a3), q_scr, 0, half, width, heads)
     stack_heads((a0, a1, a2, a3), do_scr, heads * width, half, width, heads)
-    dmine[...] = jnp.zeros_like(dmine)
     dacc[...] = jnp.zeros_like(dacc)
 
     tops = [stats[k, 0] for k in range(NY)]
@@ -169,31 +186,30 @@
         att_scr[j] = (u_ref[j] * st_scr[2, row, :]).T.astype(jnp.bfloat16)
 
         def visit(i, dq_t):
-            place = tile.place(j, i)
-            keys = tile.block(place, 0)
-            s = dot(keys, q2, 1, 1)
-            s = jnp.where(tile.allowed(j, place), s, FLOOR)
+            blocks = tile.blocks(j, i)
+            s = dot(two(pairs, blocks, slice(0, width), 0), q2, 1, 1)
+            s = jnp.where(tile.allowed(j, i, blocks), s, FLOOR)
             p = jnp.exp2(s * log2_scale - lse2)
-            dp = dot(tile.block(place, 1), do2, 1, 1)
+            dp = dot(two(pairs, blocks, slice(width, 2 * width), 0), do2, 1, 1)
             ds = (p * (dp - delta)).astype(jnp.bfloat16)
             dk = dot(ds, q2, 1, 0)
             dv = dot(p.astype(jnp.bfloat16), do2, 1, 0)
-            z, part = place
-            rows = tile.rows(part)
-            dmine[z, rows, :width] += dk[:half]
-            dmine[z, rows, width:] += dv[:half]
-            dacc[z, rows, :width] += dk[half:]
-            dacc[z, rows, width:] += dv[half:]
-            return dq_t + dot(keys, ds, 0, 0)
-
-        dq_t = lax.fori_loop(0, tile.count(j), visit, jnp.zeros((width, cols), jnp.float32))
+            for n, b in enumerate(blocks):
+                dacc[b, :, :width] += dk[n * keys : (n + 1) * keys]
+                dacc[b, :, width:] += dv[n * keys : (n + 1) * keys]
+            keys_t = jnp.concatenate([turned[b, :width, :] for b in blocks], axis=1)
+            return dq_t + dot(keys_t, ds, 1, 0)
+
+        dq_t = lax.fori_loop(0, tile.steps(j), visit, jnp.zeros((width, cols), jnp.float32))
         dq_scr[j] = (dq_t * scale).T.astype(jnp.bfloat16)
         return 0
 
     lax.fori_loop(0, 2 * NY, one_run, 0)
-    dmine[:, :, :width] = dmine[:, :, :width] * scale
-    dother[:, :, :width] = (dacc[:, :, :width] * scale).astype(dother.dtype)
-    dother[:, :, width:] = dacc[:, :, width:].astype(dother.dtype)
+    for b in range(2 * NZ):
+        rows = slice((b // NZ) * half, (b // NZ + 1) * half)
+        for out, part in ((dmine, slice(0, half)), (dother, slice(half, keys))):
+            out[b % NZ, rows, :width] = (dacc[b, part, :width] * scale).astype(out.dtype)
+            out[b % NZ, rows, width:] = dacc[b, part, width:].astype(out.dtype)
     for k, out in enumerate((o0, o1, o2, o3)):
         for side in (0, 1):
             for h in range(heads):
@@ -232,6 +248,20 @@
     ov[0] = (dkv[0, :, width:] * factor).astype(ov.dtype)
 
 
+def spread_kernel(keys, values, copies):
+    width = keys.shape[2]
+    for k in range(copies.shape[0]):
+        copies[k, :, :width] = keys[0]
+        copies[k, :, width:] = values[0]
+
+
+def join_kernel(left, right, *outs):
+    wide = left.shape[2]
+    for out in outs:
+        out[:, :, :wide] = left[...]
+        out[:, :, wide:] = right[...]
+
+
 def turn(x, axis, size, by):
     return lax.ppermute(x, axis, [(i, (i + by) % size) for i in range(size)])
 
@@ -246,14 +276,22 @@
     z, y, c = (lax.axis_index(a) for a in ("z", "y", "core"))
     info = visits(doc_starts[0], tok, z, y, c)
 
-    asked = jnp.concatenate([queries, grad_out], axis=2)
-    around = [asked] + [turn(asked, "y", NY, -k) for k in range(1, NY)]
-    kv = jnp.concatenate([keys, values], axis=2)
-    mine = lax.all_to_all(jnp.broadcast_to(kv, (NZ, tok, 2 * width)), "z", 0, 0, tiled=True)
+    copies = pl.pallas_call(spread_kernel, out_shape=jax.ShapeDtypeStruct((NZ, tok, 2 * width), keys.dtype), in_specs=[VMEM] * 2, out_specs=VMEM, compiler_params=PARAMS)(keys, values)
+    mine = lax.all_to_all(copies, "z", 0, 0, tiled=True)
+    asked, *ask = pl.pallas_call(join_kernel, out_shape=[jax.ShapeDtypeStruct((1, tok, 2 * wide), keys.dtype)] * NY, in_specs=[VMEM] * 2, out_specs=[VMEM] * NY, compiler_params=PARAMS)(queries, grad_out)
+    mine = lax.all_to_all(copies, "z", 0, 0, tiled=True)
+    around = [asked] + [turn(ask[k - 1], "y", NY, -k) for k in range(1, NY)]
     other = turn(mine, "core", NC, 1)
 
     f32, bf16 = jnp.float32, jnp.bfloat16
     shape = jax.ShapeDtypeStruct
+    pairs, turned = pl.pallas_call(
+        gather_kernel,
+        out_shape=(shape((2 * NZ, tok, 2 * width), bf16), shape((2 * NZ, 2 * width, tok), bf16)),
+        in_specs=[VMEM] * 2,
+        out_specs=(VMEM,) * 2,
+        compiler_params=PARAMS,
+    )(mine, other)
     u, stats = pl.pallas_call(
         functools.partial(forward_kernel, heads),
         out_shape=(shape((2 * NY, width, cols), f32), shape((NY, 3, 2 * NY, cols), f32)),
@@ -262,11 +300,11 @@
         scratch_shapes=[
             pltpu.VMEM((2 * NY, cols, width), bf16),
             pltpu.VMEM((2 * NY, cols, width), bf16),
-            pltpu.VMEM((2 * NZ, tok, cols), f32),
+            pltpu.VMEM((NZ, 2 * tok, cols), f32),
             pltpu.VMEM((3, 2 * NY, cols), f32),
         ],
         compiler_params=PARAMS,
-    )(info, *around, mine, other)
+    )(info, *around, pairs, turned)
     stats = lax.all_to_all(stats, "y", 0, 0, tiled=True)
     *sent, dmine, dother = pl.pallas_call(
         functools.partial(backward_kernel, heads),
@@ -277,13 +315,13 @@
         scratch_shapes=[
             pltpu.VMEM((2 * NY, cols, width), bf16),
             pltpu.VMEM((2 * NY, cols, width), bf16),
-            pltpu.VMEM(mine.shape, f32),
+            pltpu.VMEM((2 * NZ, tok, 2 * width), f32),
             pltpu.VMEM((2 * NY, cols, width), bf16),
             pltpu.VMEM((2 * NY, cols, width), bf16),
             pltpu.VMEM((3, 2 * NY, cols), f32),
         ],
         compiler_params=PARAMS,
-    )(info, *around, mine, other, u, stats)
+    )(info, *around, pairs, turned, u, stats)
     back = [sent[0]] + [turn(sent[k], "y", NY, k) for k in range(1, NY)]
     from_core = turn(dother, "core", NC, 1)
     pair = (dmine + from_core.astype(f32)).astype(bf16)
@@ -293,7 +331,7 @@
         out_shape=(
             shape(queries.shape, bf16),
             shape(queries.shape, f32),
-            shape(kv.shape, f32),
+            shape((1, tok, 2 * width), f32),
             shape((NZ * NY, 1, 128), f32),
         ),
         in_specs=[VMEM] * 5,

time: 153 us -> 162 us (1.059)
  waiting for transfers between devices: 41.3 us -> 25.1 us
  blocking collectives: 39.4 us -> 51.5 us
  starting transfers between devices: 56.1 us -> 65.4 us
  Pallas kernels: 10.1 us -> 14.3 us
    all_to_all x1, waiting for transfers between devices: 14.6 us -> 2.82 us  [per_device(): mine = lax.all_to_all(copies, 'z', 0, 0, tiled=True)]
    all_to_all x1, blocking collectives: 11.8 us -> 21.2 us  [per_device(): squares = lax.all_to_all(squares, ('core', 'dp'), 0, 0, tiled=True)]
    all_to_all x1, starting transfers between devices: 12.2 us -> 19 us  [per_device(): pieces = lax.all_to_all(pair, 'z', 0, 0, tiled=True)]
    ppermute x8, waiting for transfers between devices: 26.8 us -> 22.3 us  [turn(): return lax.ppermute(x, axis, [(i, (i + by) % size) for i in range(size)])]
    pallas_call x1, Pallas kernels: 4.69 us -> 6.46 us  [per_device(): pl.pallas_call(functools.partial(backward_kernel, heads), out_shape=[shap...]
    all_to_all x1, blocking collectives: 9.43 us -> 11.1 us  [per_device(): stats = lax.all_to_all(stats, 'y', 0, 0, tiled=True)]
  transfers between devices with their start and end apart: 10 -> 10, of which waited for: 6 -> 7; matrix products, arithmetic and copies ran while one was open for 1% -> 1% of each run, Pallas kernels for 0% -> 0%
where the time goes in v3:
time: 162 us; the launch traced here: 161 us
  starting transfers between devices  65.4 us (40%)
  blocking collectives  51.5 us (32%)
  waiting for transfers between devices  25.1 us (15%)
  Pallas kernels  14.3 us (9%)
  local copies, waits for them, and re-layouts  2.79 us (2%)
    ppermute x8, starting transfers between devices, turn(): return lax.ppermute(x, axis, [(i, (i + by) % size) for i in range(size)])  35.4 us
    ppermute x8, waiting for transfers between devices, turn(): return lax.ppermute(x, axis, [(i, (i + by) % size) for i in range(size)])  22.3 us
    all_to_all x1, blocking collectives, per_device(): squares = lax.all_to_all(squares, ('core', 'dp'), 0, 0, tiled=True)  21.2 us
    all_to_all x1, blocking collectives, per_device(): squares = lax.all_to_all(squares, ('z', 'y'), 0, 0, tiled=True)  19.3 us
    all_to_all x1, starting transfers between devices, per_device(): pieces = lax.all_to_all(pair, 'z', 0, 0, tiled=True)  19 us
    all_to_all x1, blocking collectives, per_device(): stats = lax.all_to_all(stats, 'y', 0, 0, tiled=True)  11.1 us
    all_to_all x1, starting transfers between devices, per_device(): mine = lax.all_to_all(copies, 'z', 0, 0, tiled=True)  11 us
    pallas_call x1, Pallas kernels, per_device(): pl.pallas_call(functools.partial(backward_kernel, heads), out_shape=[shap...  6.46 us
  transfers between devices with their start and end apart: 10, of which 7 were waited for; matrix products, arithmetic and copies ran while one was open for 1% of the time, Pallas kernels for 0%

profile of v3, /device:TPU:1, one launch (start us, length us, event | category | flops | bytes accessed | tf_op | source)
XLA Modules:
  0.0 161.3 jit_solution(6753523690519442669)
XLA Ops:
  0.6 0.0 copy-start.2
  0.6 0.7 copy-done.2
  1.4 0.0 copy-start.3
  1.4 0.8 copy-done.3
  2.1 0.9 shard_map.85
  3.0 0.0 copy-start
  3.0 0.0 copy-start.1
  3.0 11.0 %all-to-all-start = ((bf16[8,128,256]{2,1,0:T(8,128)(2,1)}), bf16[8,128,256]{2,1,0:T(8,128)(2,1)S(1)}, u32[]{:S(2)}, u32[]{:S(2)}) async-start(bf16[8,128,256]{2,1,0:T(8,128)(2,1)} %shard_map.85), calls=%async_computation | async-start | bytes 1048576 | tf_op jit(solution)/shard_map/all_to_all | solution.py:282
  14.0 0.0 copy-done
  14.0 0.0 copy-done.1
  14.0 0.1 shard_map.84
  14.1 5.9 %collective-permute-start = (bf16[1,128,1024]{2,1,0:T(8,128)(2,1)S(1)}, bf16[1,128,1024]{2,1,0:T(8,128)(2,1)S(1)}, u32[]{:S(2)}, u32[]{:S(2)}) collective-permute-start(bf16[1,128,1024]{2,1,0:T(8,128)(2,1)S(1)} %get-tuple-element.26), channel_id=1, source_target_pairs={{0,48},{16,0},{32,16},{48,32},{1,49},{17,1},{33,17},{49,33},{2,50}... | collective-permute-start | bytes 786440 | tf_op jit(solution)/shard_map/ppermute | solution.py:266
  20.0 3.5 %collective-permute-start.1 = (bf16[1,128,1024]{2,1,0:T(8,128)(2,1)S(1)}, bf16[1,128,1024]{2,1,0:T(8,128)(2,1)S(1)}, u32[]{:S(2)}, u32[]{:S(2)}) collective-permute-start(bf16[1,128,1024]{2,1,0:T(8,128)(2,1)S(1)} %get-tuple-element.27), channel_id=1, source_target_pairs={{0,32},{16,48},{32,0},{48,16},{1,33},{17,49},{33,1},{49,17},{2,34}... | collective-permute-start | bytes 786440 | tf_op jit(solution)/shard_map/ppermute | solution.py:266
  23.5 4.2 %collective-permute-start.2 = (bf16[1,128,1024]{2,1,0:T(8,128)(2,1)S(1)}, bf16[1,128,1024]{2,1,0:T(8,128)(2,1)S(1)}, u32[]{:S(2)}, u32[]{:S(2)}) collective-permute-start(bf16[1,128,1024]{2,1,0:T(8,128)(2,1)S(1)} %get-tuple-element.28), channel_id=1, source_target_pairs={{0,16},{16,32},{32,48},{48,0},{1,17},{17,33},{33,49},{49,1},{2,18}... | collective-permute-start | bytes 786440 | tf_op jit(solution)/shard_map/ppermute | solution.py:266
  27.8 0.1 eq.35
  27.9 0.1 eq.34
  28.0 0.1 broadcast_in_dim.24
  28.0 0.1 add.230
  28.1 0.1 add.227
  28.2 0.1 multiply_add_fusion
  28.3 0.0 copy-start.4
  28.3 0.1 add.229
  28.4 0.6 copy-done.4
  29.0 0.2 select_reduce_fusion
  29.1 2.8 %all-to-all-done.mine = bf16[8,128,256]{2,1,0:T(8,128)(2,1)S(1)} async-done(((bf16[8,128,256]{2,1,0:T(8,128)(2,1)}), bf16[8,128,256]{2,1,0:T(8,128)(2,1)S(1)}, u32[]{:S(2)}, u32[]{:S(2)}) %all-to-all-start) | async-done | bytes 524320 | tf_op jit(solution)/shard_map/all_to_all | solution.py:282
  32.0 2.4 %collective-permute-start.3 = (bf16[8,128,256]{2,1,0:T(8,128)(2,1)S(1)}, bf16[8,128,256]{2,1,0:T(8,128)(2,1)S(1)}, u32[]{:S(2)}, u32[]{:S(2)}) collective-permute-start(bf16[8,128,256]{2,1,0:T(8,128)(2,1)S(1)} %all-to-all-done.mine), channel_id=1, source_target_pairs={{0,8},{8,0},{1,9},{9,1},{2,10},{10,2},{3,11},{11,3},{4,12},{12,4},... | collective-permute-start | bytes 1572872 | tf_op jit(solution)/shard_map/ppermute | solution.py:266
  34.5 0.1 copy.11
  34.5 0.1 reshape.438
  34.6 0.1 pad_add_fusion.info
  34.7 1.2 collective-permute-done.3.other
  35.9 0.3 shard_map.86
  36.2 6.4 %collective-permute-done.a1 = bf16[1,128,1024]{2,1,0:T(8,128)(2,1)S(1)} collective-permute-done((bf16[1,128,1024]{2,1,0:T(8,128)(2,1)S(1)}, bf16[1,128,1024]{2,1,0:T(8,128)(2,1)S(1)}, u32[]{:S(2)}, u32[]{:S(2)}) %collective-permute-start) | collective-permute-done | bytes 262176 | tf_op jit(solution)/shard_map/ppermute | solution.py:266
  42.6 0.0 collective-permute-done.1.a2
  42.6 0.0 collective-permute-done.2.a3
  42.6 4.9 %shard_map.87 = (f32[8,128,256]{2,1,0:T(8,128)S(1)}, f32[4,3,8,256]{3,2,1,0:T(8,128)S(1)}) custom-call(s32[50]{0:T(128)S(1)} %pad_add_fusion.info, bf16[1,128,1024]{2,1,0:T(8,128)(2,1)S(1)} %get-tuple-element.25.a0, bf16[1,128,1024]{2,1,0:T(8,128)(2,1)S(1)} %collective-permute-done.a1, bf16[1,128,1024]{2,1,0:T(8,128)(2,1)S(1)} %collective-permute-done.1.a2, ...), custom_call_target="tpu_custom_call" | custom-call | tf_op jit(solution)/shard_map/pallas_call | solution.py:295
  47.5 11.1 %all_to_all.25.stats = f32[4,3,8,256]{3,2,1,0:T(8,128)S(1)} all-to-all(f32[4,3,8,256]{3,2,1,0:T(8,128)S(1)} %get-tuple-element.32), channel_id=1, replica_groups=mesh['z'=8,'y'=4,'core'=2,'dp'=8] {'y'}, dimensions={0} | all-to-all | bytes 196608 | tf_op jit(solution)/shard_map/all_to_all | solution.py:308
  58.5 6.5 %shard_map.88 = (bf16[1,128,1024]{2,1,0:T(8,128)(2,1)S(1)}, bf16[1,128,1024]{2,1,0:T(8,128)(2,1)S(1)}, bf16[1,128,1024]{2,1,0:T(8,128)(2,1)S(1)}, bf16[1,128,102...) custom-call(s32[50]{0:T(128)S(1)} %pad_add_fusion.info, ...), custom_call_target="tpu_custom_call" | custom-call | tf_op jit(solution)/shard_map/pallas_call | solution.py:309
  65.0 9.9 %collective-permute-start.7 = (bf16[8,128,256]{2,1,0:T(8,128)(2,1)S(1)}, bf16[8,128,256]{2,1,0:T(8,128)(2,1)S(1)}, u32[]{:S(2)}, u32[]{:S(2)}) collective-permute-start(bf16[8,128,256]{2,1,0:T(8,128)(2,1)S(1)} %get-tuple-element.38), channel_id=1, source_target_pairs={{0,8},{8,0},{1,9},{9,1},{2,10},{10,2},{3,11},{11,3},{4,12},{12,4},... | collective-permute-start | bytes 1572872 | tf_op jit(solution)/shard_map/ppermute | solution.py:266
  74.9 1.5 collective-permute-done.7
  76.4 0.9 add_convert_fusion
  77.4 19.0 %all-to-all-start.2 = ((bf16[8,128,256]{2,1,0:T(8,128)(2,1)}), bf16[8,128,256]{2,1,0:T(8,128)(2,1)S(1)}, u32[]{:S(2)}, u32[]{:S(2)}) async-start(bf16[8,128,256]{2,1,0:T(8,128)(2,1)} %add_convert_fusion), calls=%async_computation.2 | async-start | bytes 1048576 | tf_op jit(solution)/shard_map/all_to_all | solution.py:328
  96.3 1.9 %collective-permute-start.4 = (bf16[1,128,1024]{2,1,0:T(8,128)(2,1)S(1)}, bf16[1,128,1024]{2,1,0:T(8,128)(2,1)S(1)}, u32[]{:S(2)}, u32[]{:S(2)}) collective-permute-start(bf16[1,128,1024]{2,1,0:T(8,128)(2,1)S(1)} %get-tuple-element.34), channel_id=1, source_target_pairs={{0,16},{16,32},{32,48},{48,0},{1,17},{17,33},{33,49},{49,1},{2,18}... | collective-permute-start | bytes 786440 | tf_op jit(solution)/shard_map/ppermute | solution.py:266
  98.3 4.9 %collective-permute-start.5 = (bf16[1,128,1024]{2,1,0:T(8,128)(2,1)S(1)}, bf16[1,128,1024]{2,1,0:T(8,128)(2,1)S(1)}, u32[]{:S(2)}, u32[]{:S(2)}) collective-permute-start(bf16[1,128,1024]{2,1,0:T(8,128)(2,1)S(1)} %get-tuple-element.35), channel_id=1, source_target_pairs={{0,32},{16,48},{32,0},{48,16},{1,33},{17,49},{33,1},{49,17},{2,34}... | collective-permute-start | bytes 786440 | tf_op jit(solution)/shard_map/ppermute | solution.py:266
  103.2 2.7 %collective-permute-start.6 = (bf16[1,128,1024]{2,1,0:T(8,128)(2,1)S(1)}, bf16[1,128,1024]{2,1,0:T(8,128)(2,1)S(1)}, u32[]{:S(2)}, u32[]{:S(2)}) collective-permute-start(bf16[1,128,1024]{2,1,0:T(8,128)(2,1)S(1)} %get-tuple-element.36), channel_id=1, source_target_pairs={{0,48},{16,0},{32,16},{48,32},{1,49},{17,1},{33,17},{49,33},{2,50}... | collective-permute-start | bytes 786440 | tf_op jit(solution)/shard_map/ppermute | solution.py:266
  105.8 2.2 %collective-permute-done.4.o1 = bf16[1,128,1024]{2,1,0:T(8,128)(2,1)S(1)} collective-permute-done((bf16[1,128,1024]{2,1,0:T(8,128)(2,1)S(1)}, bf16[1,128,1024]{2,1,0:T(8,128)(2,1)S(1)}, u32[]{:S(2)}, u32[]{:S(2)}) %collective-permute-start.4) | collective-permute-done | bytes 262176 | tf_op jit(solution)/shard_map/ppermute | solution.py:266
  108.1 5.0 %collective-permute-done.5.o2 = bf16[1,128,1024]{2,1,0:T(8,128)(2,1)S(1)} collective-permute-done((bf16[1,128,1024]{2,1,0:T(8,128)(2,1)S(1)}, bf16[1,128,1024]{2,1,0:T(8,128)(2,1)S(1)}, u32[]{:S(2)}, u32[]{:S(2)}) %collective-permute-start.5) | collective-permute-done | bytes 262176 | tf_op jit(solution)/shard_map/ppermute | solution.py:266
  113.1 6.0 %collective-permute-done.6.o3 = bf16[1,128,1024]{2,1,0:T(8,128)(2,1)S(1)} collective-permute-done((bf16[1,128,1024]{2,1,0:T(8,128)(2,1)S(1)}, bf16[1,128,1024]{2,1,0:T(8,128)(2,1)S(1)}, u32[]{:S(2)}, u32[]{:S(2)}) %collective-permute-start.6) | collective-permute-done | bytes 262176 | tf_op jit(solution)/shard_map/ppermute | solution.py:266
  119.0 0.0 all-to-all-done.2.dkv
  119.0 1.0 shard_map.89
  120.1 19.3 %all_to_all.26 = f32[32,1,128]{2,1,0:T(1,128)S(1)} all-to-all(f32[32,1,128]{2,1,0:T(1,128)S(1)} %get-tuple-element.40), channel_id=1, replica_groups=mesh['z'=8,'y'=4,'core'=2,'dp'=8] {'z','y'}, dimensions={0} | all-to-all | bytes 32768 | tf_op jit(solution)/shard_map/all_to_all | solution.py:341
  139.3 0.1 reduce_sum.9
  139.4 21.2 %all_to_all.27.sums = f32[16,1,128]{2,1,0:T(1,128)S(1)} all-to-all(f32[16,1,128]{2,1,0:T(1,128)S(1)} %broadcast_in_dim.27), channel_id=1, replica_groups=mesh['z'=8,'y'=4,'core'=2,'dp'=8] {'core','dp'}, dimensions={0} | all-to-all | bytes 16384 | tf_op jit(solution)/shard_map/all_to_all | solution.py:344
  160.6 0.7 shard_map.90
  (8 shorter events, 0.1 us)
Async XLA Ops:
  0.6 0.8 copy-start.2
  1.4 0.8 copy-start.3
  3.0 11.0 %copy-start = (bf16[1,128,512]{2,1,0:T(8,128)(2,1)S(1)}, bf16[1,128,512]{2,1,0:T(8,128)(2,1)}, u32[]{:S(2)}) copy-start(bf16[1,128,512]{2,1,0:T(8,128)(2,1)} %left.1) | copy-start | bytes 393220
  3.0 11.0 %copy-start.1 = (bf16[1,128,512]{2,1,0:T(8,128)(2,1)S(1)}, bf16[1,128,512]{2,1,0:T(8,128)(2,1)}, u32[]{:S(2)}) copy-start(bf16[1,128,512]{2,1,0:T(8,128)(2,1)} %right.1) | copy-start | bytes 393220
  3.0 29.0 %all-to-all-start = ((bf16[8,128,256]{2,1,0:T(8,128)(2,1)}), bf16[8,128,256]{2,1,0:T(8,128)(2,1)S(1)}, u32[]{:S(2)}, u32[]{:S(2)}) async-start(bf16[8,128,256]{2,1,0:T(8,128)(2,1)} %shard_map.85), calls=%async_computation | async-start | bytes 1048576 | tf_op jit(solution)/shard_map/all_to_all | solution.py:282
  14.1 28.5 %collective-permute-start = (bf16[1,128,1024]{2,1,0:T(8,128)(2,1)S(1)}, bf16[1,128,1024]{2,1,0:T(8,128)(2,1)S(1)}, u32[]{:S(2)}, u32[]{:S(2)}) collective-permute-start(bf16[1,128,1024]{2,1,0:T(8,128)(2,1)S(1)} %get-tuple-element.26), channel_id=1, source_target_pairs={{0,48},{16,0},{32,16},{48,32},{1,49},{17,1},{33,17},{49,33},{2,50}... | collective-permute-start | bytes 786440 | tf_op jit(solution)/shard_map/ppermute | solution.py:266
  20.0 22.6 %collective-permute-start.1 = (bf16[1,128,1024]{2,1,0:T(8,128)(2,1)S(1)}, bf16[1,128,1024]{2,1,0:T(8,128)(2,1)S(1)}, u32[]{:S(2)}, u32[]{:S(2)}) collective-permute-start(bf16[1,128,1024]{2,1,0:T(8,128)(2,1)S(1)} %get-tuple-element.27), channel_id=1, source_target_pairs={{0,32},{16,48},{32,0},{48,16},{1,33},{17,49},{33,1},{49,17},{2,34}... | collective-permute-start | bytes 786440 | tf_op jit(solution)/shard_map/ppermute | solution.py:266
  23.5 19.1 %collective-permute-start.2 = (bf16[1,128,1024]{2,1,0:T(8,128)(2,1)S(1)}, bf16[1,128,1024]{2,1,0:T(8,128)(2,1)S(1)}, u32[]{:S(2)}, u32[]{:S(2)}) collective-permute-start(bf16[1,128,1024]{2,1,0:T(8,128)(2,1)S(1)} %get-tuple-element.28), channel_id=1, source_target_pairs={{0,16},{16,32},{32,48},{48,0},{1,17},{17,33},{33,49},{49,1},{2,18}... | collective-permute-start | bytes 786440 | tf_op jit(solution)/shard_map/ppermute | solution.py:266
  28.3 0.7 copy-start.4
  32.0 3.9 %collective-permute-start.3 = (bf16[8,128,256]{2,1,0:T(8,128)(2,1)S(1)}, bf16[8,128,256]{2,1,0:T(8,128)(2,1)S(1)}, u32[]{:S(2)}, u32[]{:S(2)}) collective-permute-start(bf16[8,128,256]{2,1,0:T(8,128)(2,1)S(1)} %all-to-all-done.mine), channel_id=1, source_target_pairs={{0,8},{8,0},{1,9},{9,1},{2,10},{10,2},{3,11},{11,3},{4,12},{12,4},... | collective-permute-start | bytes 1572872 | tf_op jit(solution)/shard_map/ppermute | solution.py:266
  65.0 11.4 %collective-permute-start.7 = (bf16[8,128,256]{2,1,0:T(8,128)(2,1)S(1)}, bf16[8,128,256]{2,1,0:T(8,128)(2,1)S(1)}, u32[]{:S(2)}, u32[]{:S(2)}) collective-permute-start(bf16[8,128,256]{2,1,0:T(8,128)(2,1)S(1)} %get-tuple-element.38), channel_id=1, source_target_pairs={{0,8},{8,0},{1,9},{9,1},{2,10},{10,2},{3,11},{11,3},{4,12},{12,4},... | collective-permute-start | bytes 1572872 | tf_op jit(solution)/shard_map/ppermute | solution.py:266
  77.4 41.7 %all-to-all-start.2 = ((bf16[8,128,256]{2,1,0:T(8,128)(2,1)}), bf16[8,128,256]{2,1,0:T(8,128)(2,1)S(1)}, u32[]{:S(2)}, u32[]{:S(2)}) async-start(bf16[8,128,256]{2,1,0:T(8,128)(2,1)} %add_convert_fusion), calls=%async_computation.2 | async-start | bytes 1048576 | tf_op jit(solution)/shard_map/all_to_all | solution.py:328
  96.3 11.8 %collective-permute-start.4 = (bf16[1,128,1024]{2,1,0:T(8,128)(2,1)S(1)}, bf16[1,128,1024]{2,1,0:T(8,128)(2,1)S(1)}, u32[]{:S(2)}, u32[]{:S(2)}) collective-permute-start(bf16[1,128,1024]{2,1,0:T(8,128)(2,1)S(1)} %get-tuple-element.34), channel_id=1, source_target_pairs={{0,16},{16,32},{32,48},{48,0},{1,17},{17,33},{33,49},{49,1},{2,18}... | collective-permute-start | bytes 786440 | tf_op jit(solution)/shard_map/ppermute | solution.py:266
  98.3 14.8 %collective-permute-start.5 = (bf16[1,128,1024]{2,1,0:T(8,128)(2,1)S(1)}, bf16[1,128,1024]{2,1,0:T(8,128)(2,1)S(1)}, u32[]{:S(2)}, u32[]{:S(2)}) collective-permute-start(bf16[1,128,1024]{2,1,0:T(8,128)(2,1)S(1)} %get-tuple-element.35), channel_id=1, source_target_pairs={{0,32},{16,48},{32,0},{48,16},{1,33},{17,49},{33,1},{49,17},{2,34}... | collective-permute-start | bytes 786440 | tf_op jit(solution)/shard_map/ppermute | solution.py:266
  103.2 15.9 %collective-permute-start.6 = (bf16[1,128,1024]{2,1,0:T(8,128)(2,1)S(1)}, bf16[1,128,1024]{2,1,0:T(8,128)(2,1)S(1)}, u32[]{:S(2)}, u32[]{:S(2)}) collective-permute-start(bf16[1,128,1024]{2,1,0:T(8,128)(2,1)S(1)} %get-tuple-element.36), channel_id=1, source_target_pairs={{0,48},{16,0},{32,16},{48,32},{1,49},{17,1},{33,17},{49,33},{2,50}... | collective-permute-start | bytes 786440 | tf_op jit(solution)/shard_map/ppermute | solution.py:266

commit v4 on v3

--- a/solution.py
+++ b/solution.py
@@ -103,25 +103,26 @@
         turned[b] = block.astype(jnp.float32).T.astype(turned.dtype)
 
 
-def stack_heads(refs, out_ref, lane0, half, width, heads):
-    for k, ref in enumerate(refs):
-        for side in (0, 1):
-            for h in range(heads):
-                out_ref[2 * k + side, h * half : (h + 1) * half, :] = ref[
-                    0, side * half : (side + 1) * half, lane0 + h * width : lane0 + (h + 1) * width
-                ]
-
-
-def forward_kernel(heads, info, a0, a1, a2, a3, pairs, turned, u_ref, stats_ref, q_scr, do_scr, s_scr, st_scr):
+def heads_of(ref, side, second, half, width, heads):
+    rows = pl.ds(pl.multiple_of(side * half, half), half)
+    lanes = [(heads * second + h) * width for h in range(heads)]
+    return jnp.concatenate([ref[0, rows, at : at + width] for at in lanes], axis=0)
+
+
+def forward_kernel(heads, ks, before, info, *refs):
+    asked, refs = refs[: len(ks)], refs[len(ks) :]
+    pairs, turned = refs[:2]
+    earlier = refs[2 : 2 + before]
+    u_ref, stats_ref, s_scr, st_scr = refs[2 + before :]
     tile = Tile(info, pairs, heads)
     half, width, cols = tile.half, tile.width, tile.cols
     log2_scale = math.log2(math.e) / math.sqrt(width)
-    stack_heads((a0, a1, a2, a3), q_scr, 0, half, width, heads)
-    stack_heads((a0, a1, a2, a3), do_scr, heads * width, half, width, heads)
     groups = 2 * tile.keys // 8
-
-    def one_run(j, _):
-        q2 = q_scr[j]
+    st_scr[...] = sum([e[...] for e in earlier], jnp.zeros(st_scr.shape, jnp.float32))
+
+    def one_run(n, k, side):
+        j = 2 * k + side
+        q2 = heads_of(asked[n], side, 0, half, width, heads)
         steps = tile.steps(j)
 
         def scores(i, biggest):
@@ -144,28 +145,32 @@
         total, acc = lax.fori_loop(
             0, steps, sums, (jnp.zeros((8, cols), jnp.float32), jnp.zeros((width, cols), jnp.float32))
         )
-        u_ref[j] = acc
+        u_ref[2 * n + side] = acc
         row = pl.ds(tile.field(j, 1), 1)
+        do_t = heads_of(asked[n], side, 1, half, width, heads).astype(jnp.float32).T
         st_scr[0, row, :] = top
         st_scr[1, row, :] = jnp.sum(total, axis=0, keepdims=True)
-        st_scr[2, row, :] = jnp.sum(acc * do_scr[j].astype(jnp.float32).T, axis=0, keepdims=True)
-        return 0
-
-    lax.fori_loop(0, 2 * NY, one_run, 0)
-    for k in range(NY):
-        stats_ref[k] = st_scr[...]
-
-
-def backward_kernel(
-    heads, info, a0, a1, a2, a3, pairs, turned, u_ref, stats,
-    o0, o1, o2, o3, dmine, dother, q_scr, do_scr, dacc, att_scr, dq_scr, st_scr,
-):
+        st_scr[2, row, :] = jnp.sum(acc * do_t, axis=0, keepdims=True)
+
+    for n, k in enumerate(ks):
+        lax.fori_loop(0, 2, lambda side, _, n=n, k=k: (one_run(n, k, side), 0)[1], 0)
+    if before:
+        for k in range(NY):
+            stats_ref[k] = st_scr[...]
+    else:
+        stats_ref[...] = st_scr[...]
+
+
+def backward_kernel(heads, ks, info, *refs):
+    asked, refs = refs[: len(ks)], refs[len(ks) :]
+    us, refs = refs[: len(ks)], refs[len(ks) :]
+    pairs, turned, stats = refs[:3]
+    refs = refs[3:]
+    *outs, dmine, dother, dacc, st_scr = refs
     tile = Tile(info, pairs, heads)
     half, width, cols, keys = tile.half, tile.width, tile.cols, tile.keys
     scale = 1.0 / math.sqrt(width)
     log2_scale = scale * math.log2(math.e)
-    stack_heads((a0, a1, a2, a3), q_scr, 0, half, width, heads)
-    stack_heads((a0, a1, a2, a3), do_scr, heads * width, half, width, heads)
     dacc[...] = jnp.zeros_like(dacc)
 
     tops = [stats[k, 0] for k in range(NY)]
@@ -177,13 +182,13 @@
     st_scr[1] = sum(w * stats[k, 2] for k, w in enumerate(weights)) * inverse
     st_scr[2] = jnp.exp2((stats[tile.y, 0] - top) * log2_scale) * inverse
 
-    def one_run(j, _):
-        q2 = q_scr[j]
-        do2 = do_scr[j]
+    def one_run(n, k, side):
+        j = 2 * k + side
+        q2 = heads_of(asked[n], side, 0, half, width, heads)
+        do2 = heads_of(asked[n], side, 1, half, width, heads)
         row = pl.ds(tile.field(j, 1), 1)
         lse2 = st_scr[0, row, :]
         delta = st_scr[1, row, :]
-        att_scr[j] = (u_ref[j] * st_scr[2, row, :]).T.astype(jnp.bfloat16)
 
         def visit(i, dq_t):
             blocks = tile.blocks(j, i)
@@ -194,31 +199,28 @@
             ds = (p * (dp - delta)).astype(jnp.bfloat16)
             dk = dot(ds, q2, 1, 0)
             dv = dot(p.astype(jnp.bfloat16), do2, 1, 0)
-            for n, b in enumerate(blocks):
-                dacc[b, :, :width] += dk[n * keys : (n + 1) * keys]
-                dacc[b, :, width:] += dv[n * keys : (n + 1) * keys]
+            for m, b in enumerate(blocks):
+                dacc[b, :, :width] += dk[m * keys : (m + 1) * keys]
+                dacc[b, :, width:] += dv[m * keys : (m + 1) * keys]
             keys_t = jnp.concatenate([turned[b, :width, :] for b in blocks], axis=1)
             return dq_t + dot(keys_t, ds, 1, 0)
 
         dq_t = lax.fori_loop(0, tile.steps(j), visit, jnp.zeros((width, cols), jnp.float32))
-        dq_scr[j] = (dq_t * scale).T.astype(jnp.bfloat16)
-        return 0
-
-    lax.fori_loop(0, 2 * NY, one_run, 0)
+        att = (us[n][side] * st_scr[2, row, :]).T.astype(jnp.bfloat16)
+        dq = (dq_t * scale).T.astype(jnp.bfloat16)
+        rows = pl.ds(pl.multiple_of(side * half, half), half)
+        for second, whole in ((0, att), (1, dq)):
+            for h in range(heads):
+                at = (heads * second + h) * width
+                outs[n][0, rows, at : at + width] = whole[h * half : (h + 1) * half]
+
+    for n, k in enumerate(ks):
+        lax.fori_loop(0, 2, lambda side, _, n=n, k=k: (one_run(n, k, side), 0)[1], 0)
     for b in range(2 * NZ):
         rows = slice((b // NZ) * half, (b // NZ + 1) * half)
         for out, part in ((dmine, slice(0, half)), (dother, slice(half, keys))):
             out[b % NZ, rows, :width] = (dacc[b, part, :width] * scale).astype(out.dtype)
             out[b % NZ, rows, width:] = dacc[b, part, width:].astype(out.dtype)
-    for k, out in enumerate((o0, o1, o2, o3)):
-        for side in (0, 1):
-            for h in range(heads):
-                where = slice(side * half, (side + 1) * half)
-                part = slice(h * half, (h + 1) * half)
-                lanes = slice(h * width, (h + 1) * width)
-                out[0, where, lanes] = att_scr[2 * k + side, part, :]
-                lanes = slice((heads + h) * width, (heads + h + 1) * width)
-                out[0, where, lanes] = dq_scr[2 * k + side, part, :]
 
 
 def combine_kernel(o0, o1, o2, o3, dkv, att_ref, dq_ref, dkv_ref, sq_ref):
@@ -280,7 +282,8 @@
     mine = lax.all_to_all(copies, "z", 0, 0, tiled=True)
     asked, *ask = pl.pallas_call(join_kernel, out_shape=[jax.ShapeDtypeStruct((1, tok, 2 * wide), keys.dtype)] * NY, in_specs=[VMEM] * 2, out_specs=[VMEM] * NY, compiler_params=PARAMS)(queries, grad_out)
     mine = lax.all_to_all(copies, "z", 0, 0, tiled=True)
-    around = [asked] + [turn(ask[k - 1], "y", NY, -k) for k in range(1, NY)]
+    around = {k: turn(ask[k - 1], "y", NY, -k) for k in (2, 1, 3)}
+    around[0] = asked
     other = turn(mine, "core", NC, 1)
 
     f32, bf16 = jnp.float32, jnp.bfloat16
@@ -292,36 +295,35 @@
         out_specs=(VMEM,) * 2,
         compiler_params=PARAMS,
     )(mine, other)
-    u, stats = pl.pallas_call(
-        functools.partial(forward_kernel, heads),
-        out_shape=(shape((2 * NY, width, cols), f32), shape((NY, 3, 2 * NY, cols), f32)),
-        in_specs=[SMEM] + [VMEM] * 6,
-        out_specs=(VMEM, VMEM),
-        scratch_shapes=[
-            pltpu.VMEM((2 * NY, cols, width), bf16),
-            pltpu.VMEM((2 * NY, cols, width), bf16),
-            pltpu.VMEM((NZ, 2 * tok, cols), f32),
-            pltpu.VMEM((3, 2 * NY, cols), f32),
-        ],
-        compiler_params=PARAMS,
-    )(info, *around, pairs, turned)
+    stat = (3, 2 * NY, cols)
+
+    def forward(ks, earlier):
+        return pl.pallas_call(
+            functools.partial(forward_kernel, heads, ks, len(earlier)),
+            out_shape=(
+                shape((2 * len(ks), width, cols), f32),
+                shape((NY,) + stat if earlier else stat, f32),
+            ),
+            in_specs=[SMEM] + [VMEM] * (len(ks) + 2 + len(earlier)),
+            out_specs=(VMEM, VMEM),
+            scratch_shapes=[pltpu.VMEM((NZ, 2 * tok, cols), f32), pltpu.VMEM(stat, f32)],
+            compiler_params=PARAMS,
+        )(info, *[around[k] for k in ks], pairs, turned, *earlier)
+
+    u0, stats0 = forward((0,), [])
+    u1, stats1 = forward((1,), [])
+    u3, stats3 = forward((3,), [])
+    u2, stats = forward((2,), [stats0, stats1, stats3])
     stats = lax.all_to_all(stats, "y", 0, 0, tiled=True)
     *sent, dmine, dother = pl.pallas_call(
-        functools.partial(backward_kernel, heads),
+        functools.partial(backward_kernel, heads, tuple(range(NY))),
         out_shape=[shape(asked.shape, bf16)] * NY
         + [shape(mine.shape, f32), shape(mine.shape, bf16)],
-        in_specs=[SMEM] + [VMEM] * 8,
+        in_specs=[SMEM] + [VMEM] * (2 * NY + 3),
         out_specs=[VMEM] * (NY + 2),
-        scratch_shapes=[
-            pltpu.VMEM((2 * NY, cols, width), bf16),
-            pltpu.VMEM((2 * NY, cols, width), bf16),
-            pltpu.VMEM((2 * NZ, tok, 2 * width), f32),
-            pltpu.VMEM((2 * NY, cols, width), bf16),
-            pltpu.VMEM((2 * NY, cols, width), bf16),
-            pltpu.VMEM((3, 2 * NY, cols), f32),
-        ],
+        scratch_shapes=[pltpu.VMEM((2 * NZ, tok, 2 * width), f32), pltpu.VMEM(stat, f32)],
         compiler_params=PARAMS,
-    )(info, *around, pairs, turned, u, stats)
+    )(info, *[around[k] for k in range(NY)], u0, u1, u2, u3, pairs, turned, stats)
     back = [sent[0]] + [turn(sent[k], "y", NY, k) for k in range(1, NY)]
     from_core = turn(dother, "core", NC, 1)
     pair = (dmine + from_core.astype(f32)).astype(bf16)
@@ -332,16 +334,16 @@
             shape(queries.shape, bf16),
             shape(queries.shape, f32),
             shape((1, tok, 2 * width), f32),
-            shape((NZ * NY, 1, 128), f32),
+            shape((NZ * NC, 1, 128), f32),
         ),
         in_specs=[VMEM] * 5,
         out_specs=(VMEM,) * 4,
         compiler_params=PARAMS,
     )(*back, pieces)
-    squares = lax.all_to_all(squares, ("z", "y"), 0, 0, tiled=True)
+    squares = lax.all_to_all(squares, ("z", "core"), 0, 0, tiled=True)
     ndata = lax.axis_size("dp")
-    squares = jnp.broadcast_to(jnp.sum(squares, axis=0, keepdims=True), (NC * ndata, 1, 128))
-    squares = lax.all_to_all(squares, ("core", "dp"), 0, 0, tiled=True)
+    squares = jnp.broadcast_to(jnp.sum(squares, axis=0, keepdims=True), (NY * ndata, 1, 128))
+    squares = lax.all_to_all(squares, ("y", "dp"), 0, 0, tiled=True)
     count = float(ndata * NZ * NY * NC * tok * (wide + 2 * width))
     out_query, out_key, out_value = pl.pallas_call(
         functools.partial(scale_kernel, count),

time: 162 us -> 156 us (0.963)
  starting transfers between devices: 65.4 us -> 56.1 us
  waiting for transfers between devices: 25.1 us -> 33.3 us
  blocking collectives: 51.5 us -> 45.4 us
    all_to_all x1, starting transfers between devices: 19 us -> 8.22 us  [per_device(): pieces = lax.all_to_all(pair, 'z', 0, 0, tiled=True)]
    ppermute x8, waiting for transfers between devices: 22.3 us -> 30.5 us  [turn(): return lax.ppermute(x, axis, [(i, (i + by) % size) for i in range(size)])]
    all_to_all x2, blocking collectives: 40.4 us -> 34.5 us  [the longest x1 19.7 us: per_device(): squares = lax.all_to_all(squares, ('y', 'dp'), 0, 0, tiled=True)]
    pallas_call x2 -> x5, Pallas kernels: 11.3 us -> 12.7 us  [the longest x4 6.81 us: forward(): pl.pallas_call(functools.partial(forward_kernel, heads, ks, len(earlier))...]
  transfers between devices with their start and end apart: 10 -> 10, of which waited for: 7 -> 6; matrix products, arithmetic and copies ran while one was open for 1% -> 1% of each run, Pallas kernels for 0% -> 3%
where the time goes in v4:
time: 156 us
  starting transfers between devices  56.1 us (36%)
  blocking collectives  45.4 us (29%)
  waiting for transfers between devices  33.3 us (21%)
  Pallas kernels  15.7 us (10%)
  local copies, waits for them, and re-layouts  2.79 us (2%)
    ppermute x8, starting transfers between devices, turn(): return lax.ppermute(x, axis, [(i, (i + by) % size) for i in range(size)])  36.9 us
    ppermute x8, waiting for transfers between devices, turn(): return lax.ppermute(x, axis, [(i, (i + by) % size) for i in range(size)])  30.5 us
    all_to_all x1, blocking collectives, per_device(): squares = lax.all_to_all(squares, ('y', 'dp'), 0, 0, tiled=True)  19.7 us
    all_to_all x1, blocking collectives, per_device(): squares = lax.all_to_all(squares, ('z', 'core'), 0, 0, tiled=True)  14.8 us
    all_to_all x1, starting transfers between devices, per_device(): mine = lax.all_to_all(copies, 'z', 0, 0, tiled=True)  11 us
    all_to_all x1, blocking collectives, per_device(): stats = lax.all_to_all(stats, 'y', 0, 0, tiled=True)  11 us
    all_to_all x1, starting transfers between devices, per_device(): pieces = lax.all_to_all(pair, 'z', 0, 0, tiled=True)  8.22 us
    pallas_call x4, Pallas kernels, forward(): pl.pallas_call(functools.partial(forward_kernel, heads, ks, len(earlier))...  6.81 us
  transfers between devices with their start and end apart: 10, of which 6 were waited for; matrix products, arithmetic and copies ran while one was open for 1% of the time, Pallas kernels for 3%

profile of v4, /device:TPU:1, one launch (start us, length us, event | category | flops | bytes accessed | tf_op | source)
XLA Modules:
  0.0 155.5 jit_solution(3329279203554057792)
XLA Ops:
  0.6 0.0 copy-start.2
  0.6 0.7 copy-done.2
  1.4 0.0 copy-start.3
  1.4 0.8 copy-done.3
  2.1 0.9 shard_map.85
  3.0 0.0 copy-start
  3.0 0.0 copy-start.1
  3.0 11.0 %all-to-all-start = ((bf16[8,128,256]{2,1,0:T(8,128)(2,1)}), bf16[8,128,256]{2,1,0:T(8,128)(2,1)S(1)}, u32[]{:S(2)}, u32[]{:S(2)}) async-start(bf16[8,128,256]{2,1,0:T(8,128)(2,1)} %shard_map.85), calls=%async_computation | async-start | bytes 1048576 | tf_op jit(solution)/shard_map/all_to_all | solution.py:284
  14.0 0.0 copy-done
  14.0 0.0 copy-done.1
  14.0 0.1 shard_map.84
  14.1 5.9 %collective-permute-start = (bf16[1,128,1024]{2,1,0:T(8,128)(2,1)S(1)}, bf16[1,128,1024]{2,1,0:T(8,128)(2,1)S(1)}, u32[]{:S(2)}, u32[]{:S(2)}) collective-permute-start(bf16[1,128,1024]{2,1,0:T(8,128)(2,1)S(1)} %get-tuple-element.32), channel_id=1, source_target_pairs={{0,48},{16,0},{32,16},{48,32},{1,49},{17,1},{33,17},{49,33},{2,50}... | collective-permute-start | bytes 786440 | tf_op jit(solution)/shard_map/ppermute | solution.py:268
  20.0 3.5 %collective-permute-start.1 = (bf16[1,128,1024]{2,1,0:T(8,128)(2,1)S(1)}, bf16[1,128,1024]{2,1,0:T(8,128)(2,1)S(1)}, u32[]{:S(2)}, u32[]{:S(2)}) collective-permute-start(bf16[1,128,1024]{2,1,0:T(8,128)(2,1)S(1)} %get-tuple-element.33), channel_id=1, source_target_pairs={{0,32},{16,48},{32,0},{48,16},{1,33},{17,49},{33,1},{49,17},{2,34}... | collective-permute-start | bytes 786440 | tf_op jit(solution)/shard_map/ppermute | solution.py:268
  23.6 4.2 %collective-permute-start.2 = (bf16[1,128,1024]{2,1,0:T(8,128)(2,1)S(1)}, bf16[1,128,1024]{2,1,0:T(8,128)(2,1)S(1)}, u32[]{:S(2)}, u32[]{:S(2)}) collective-permute-start(bf16[1,128,1024]{2,1,0:T(8,128)(2,1)S(1)} %get-tuple-element.34), channel_id=1, source_target_pairs={{0,16},{16,32},{32,48},{48,0},{1,17},{17,33},{33,49},{49,1},{2,18}... | collective-permute-start | bytes 786440 | tf_op jit(solution)/shard_map/ppermute | solution.py:268
  27.8 0.1 eq.35
  27.9 0.1 eq.34
  28.0 0.1 broadcast_in_dim.24
  28.1 0.1 add.230
  28.1 0.1 add.227
  28.2 0.1 multiply_add_fusion
  28.3 0.0 copy-start.4
  28.3 0.1 add.229
  28.4 0.6 copy-done.4
  29.0 0.2 select_reduce_fusion
  29.2 2.8 %all-to-all-done.mine = bf16[8,128,256]{2,1,0:T(8,128)(2,1)S(1)} async-done(((bf16[8,128,256]{2,1,0:T(8,128)(2,1)}), bf16[8,128,256]{2,1,0:T(8,128)(2,1)S(1)}, u32[]{:S(2)}, u32[]{:S(2)}) %all-to-all-start) | async-done | bytes 524320 | tf_op jit(solution)/shard_map/all_to_all | solution.py:284
  32.0 2.4 %collective-permute-start.3 = (bf16[8,128,256]{2,1,0:T(8,128)(2,1)S(1)}, bf16[8,128,256]{2,1,0:T(8,128)(2,1)S(1)}, u32[]{:S(2)}, u32[]{:S(2)}) collective-permute-start(bf16[8,128,256]{2,1,0:T(8,128)(2,1)S(1)} %all-to-all-done.mine), channel_id=1, source_target_pairs={{0,8},{8,0},{1,9},{9,1},{2,10},{10,2},{3,11},{11,3},{4,12},{12,4},... | collective-permute-start | bytes 1572872 | tf_op jit(solution)/shard_map/ppermute | solution.py:268
  34.5 0.1 copy.11
  34.5 0.1 reshape.438
  34.6 0.1 pad_add_fusion.info
  34.7 1.2 collective-permute-done.3.other
  35.9 0.3 shard_map.86
  36.2 1.6 %shard_map.87 = (f32[2,128,256]{2,1,0:T(8,128)S(1)}, f32[3,8,256]{2,1,0:T(8,128)S(1)}) custom-call(s32[50]{0:T(128)S(1)} %pad_add_fusion.info, bf16[1,128,1024]{2,1,0:T(8,128)(2,1)S(1)} %get-tuple-element.31.refs_0_, bf16[16,128,256]{2,1,0:T(8,128)(2,1)S(1)} %get-tuple-element.35.refs_1_.refs_8_, bf16[16,256,128]{2,1,0:T(8,128)(2,1)S(1)} %get-tuple-element.36.refs_2_.refs_9_), custom_call_target="tpu_custom_call" | custom-call | tf_op jit(solution)/shard_map/pallas_call | solution.py:301
  37.9 3.0 %collective-permute-done.2.refs_0_.refs_3_ = bf16[1,128,1024]{2,1,0:T(8,128)(2,1)S(1)} collective-permute-done((bf16[1,128,1024]{2,1,0:T(8,128)(2,1)S(1)}, bf16[1,128,1024]{2,1,0:T(8,128)(2,1)S(1)}, u32[]{:S(2)}, u32[]{:S(2)}) %collective-permute-start.2) | collective-permute-done | bytes 262176 | tf_op jit(solution)/shard_map/ppermute | solution.py:268
  40.9 2.0 %shard_map.89 = (f32[2,128,256]{2,1,0:T(8,128)S(1)}, f32[3,8,256]{2,1,0:T(8,128)S(1)}) custom-call(s32[50]{0:T(128)S(1)} %pad_add_fusion.info, bf16[1,128,1024]{2,1,0:T(8,128)(2,1)S(1)} %collective-permute-done.2.refs_0_.refs_3_, bf16[16,128,256]{2,1,0:T(8,128)(2,1)S(1)} %get-tuple-element.35.refs_1_.refs_8_, ...), custom_call_target="tpu_custom_call" | custom-call | tf_op jit(solution)/shard_map/pallas_call | solution.py:301
  42.9 0.0 collective-permute-done.refs_0_.refs_1_
  42.9 1.2 shard_map.88
  44.1 0.0 collective-permute-done.1.refs_0_.refs_2_
  44.1 2.0 %shard_map.90 = (f32[2,128,256]{2,1,0:T(8,128)S(1)}, f32[4,3,8,256]{3,2,1,0:T(8,128)S(1)}) custom-call(s32[50]{0:T(128)S(1)} %pad_add_fusion.info, bf16[1,128,1024]{2,1,0:T(8,128)(2,1)S(1)} %collective-permute-done.1.refs_0_.refs_2_, bf16[16,128,256]{2,1,0:T(8,128)(2,1)S(1)} %get-tuple-element.35.refs_1_.refs_8_, ...), custom_call_target="tpu_custom_call" | custom-call | tf_op jit(solution)/shard_map/pallas_call | solution.py:301
  46.1 11.0 %all_to_all.25.refs_10_ = f32[4,3,8,256]{3,2,1,0:T(8,128)S(1)} all-to-all(f32[4,3,8,256]{3,2,1,0:T(8,128)S(1)} %get-tuple-element.44), channel_id=1, replica_groups=mesh['z'=8,'y'=4,'core'=2,'dp'=8] {'y'}, dimensions={0} | all-to-all | bytes 196608 | tf_op jit(solution)/shard_map/all_to_all | solution.py:317
  57.1 5.9 %shard_map.91 = (bf16[1,128,1024]{2,1,0:T(8,128)(2,1)S(1)}, bf16[1,128,1024]{2,1,0:T(8,128)(2,1)S(1)}, bf16[1,128,1024]{2,1,0:T(8,128)(2,1)S(1)}, bf16[1,128,102...) custom-call(s32[50]{0:T(128)S(1)} %pad_add_fusion.info, ...), custom_call_target="tpu_custom_call" | custom-call | tf_op jit(solution)/shard_map/pallas_call | solution.py:318
  63.0 11.4 %collective-permute-start.7 = (bf16[8,128,256]{2,1,0:T(8,128)(2,1)S(1)}, bf16[8,128,256]{2,1,0:T(8,128)(2,1)S(1)}, u32[]{:S(2)}, u32[]{:S(2)}) collective-permute-start(bf16[8,128,256]{2,1,0:T(8,128)(2,1)S(1)} %get-tuple-element.50), channel_id=1, source_target_pairs={{0,8},{8,0},{1,9},{9,1},{2,10},{10,2},{3,11},{11,3},{4,12},{12,4},... | collective-permute-start | bytes 1572872 | tf_op jit(solution)/shard_map/ppermute | solution.py:268
  74.4 1.5 collective-permute-done.7
  75.9 0.9 add_convert_fusion
  76.8 8.2 %all-to-all-start.2 = ((bf16[8,128,256]{2,1,0:T(8,128)(2,1)}), bf16[8,128,256]{2,1,0:T(8,128)(2,1)S(1)}, u32[]{:S(2)}, u32[]{:S(2)}) async-start(bf16[8,128,256]{2,1,0:T(8,128)(2,1)} %add_convert_fusion), calls=%async_computation.2 | async-start | bytes 1048576 | tf_op jit(solution)/shard_map/all_to_all | solution.py:330
  85.1 2.3 %collective-permute-start.4 = (bf16[1,128,1024]{2,1,0:T(8,128)(2,1)S(1)}, bf16[1,128,1024]{2,1,0:T(8,128)(2,1)S(1)}, u32[]{:S(2)}, u32[]{:S(2)}) collective-permute-start(bf16[1,128,1024]{2,1,0:T(8,128)(2,1)S(1)} %get-tuple-element.46), channel_id=1, source_target_pairs={{0,16},{16,32},{32,48},{48,0},{1,17},{17,33},{33,49},{49,1},{2,18}... | collective-permute-start | bytes 786440 | tf_op jit(solution)/shard_map/ppermute | solution.py:268
  87.4 3.0 %collective-permute-start.5 = (bf16[1,128,1024]{2,1,0:T(8,128)(2,1)S(1)}, bf16[1,128,1024]{2,1,0:T(8,128)(2,1)S(1)}, u32[]{:S(2)}, u32[]{:S(2)}) collective-permute-start(bf16[1,128,1024]{2,1,0:T(8,128)(2,1)S(1)} %get-tuple-element.47), channel_id=1, source_target_pairs={{0,32},{16,48},{32,0},{48,16},{1,33},{17,49},{33,1},{49,17},{2,34}... | collective-permute-start | bytes 786440 | tf_op jit(solution)/shard_map/ppermute | solution.py:268
  90.4 4.1 %collective-permute-start.6 = (bf16[1,128,1024]{2,1,0:T(8,128)(2,1)S(1)}, bf16[1,128,1024]{2,1,0:T(8,128)(2,1)S(1)}, u32[]{:S(2)}, u32[]{:S(2)}) collective-permute-start(bf16[1,128,1024]{2,1,0:T(8,128)(2,1)S(1)} %get-tuple-element.48), channel_id=1, source_target_pairs={{0,48},{16,0},{32,16},{48,32},{1,49},{17,1},{33,17},{49,33},{2,50}... | collective-permute-start | bytes 786440 | tf_op jit(solution)/shard_map/ppermute | solution.py:268
  94.5 13.0 %collective-permute-done.4.o1 = bf16[1,128,1024]{2,1,0:T(8,128)(2,1)S(1)} collective-permute-done((bf16[1,128,1024]{2,1,0:T(8,128)(2,1)S(1)}, bf16[1,128,1024]{2,1,0:T(8,128)(2,1)S(1)}, u32[]{:S(2)}, u32[]{:S(2)}) %collective-permute-start.4) | collective-permute-done | bytes 262176 | tf_op jit(solution)/shard_map/ppermute | solution.py:268
  107.5 0.0 collective-permute-done.5.o2
  107.5 11.7 %collective-permute-done.6.o3 = bf16[1,128,1024]{2,1,0:T(8,128)(2,1)S(1)} collective-permute-done((bf16[1,128,1024]{2,1,0:T(8,128)(2,1)S(1)}, bf16[1,128,1024]{2,1,0:T(8,128)(2,1)S(1)}, u32[]{:S(2)}, u32[]{:S(2)}) %collective-permute-start.6) | collective-permute-done | bytes 262176 | tf_op jit(solution)/shard_map/ppermute | solution.py:268
  119.2 0.0 all-to-all-done.2.dkv
  119.3 1.0 shard_map.92
  120.3 14.8 %all_to_all.26 = f32[16,1,128]{2,1,0:T(1,128)S(1)} all-to-all(f32[16,1,128]{2,1,0:T(1,128)S(1)} %get-tuple-element.52), channel_id=1, replica_groups=mesh['z'=8,'y'=4,'core'=2,'dp'=8] {'z','core'}, dimensions={0} | all-to-all | bytes 16384 | tf_op jit(solution)/shard_map/all_to_all | solution.py:343
  135.1 19.7 %all_to_all.27.sums = f32[32,1,128]{2,1,0:T(1,128)S(1)} all-to-all(f32[32,1,128]{2,1,0:T(1,128)S(1)} %broadcast_in_dim.27), channel_id=1, replica_groups=mesh['z'=8,'y'=4,'core'=2,'dp'=8] {'y','dp'}, dimensions={0} | all-to-all | bytes 32768 | tf_op jit(solution)/shard_map/all_to_all | solution.py:346
  154.8 0.7 shard_map.93
  (9 shorter events, 0.2 us)
Async XLA Ops:
  0.6 0.8 copy-start.2
  1.4 0.8 copy-start.3
  3.0 11.0 %copy-start = (bf16[1,128,512]{2,1,0:T(8,128)(2,1)S(1)}, bf16[1,128,512]{2,1,0:T(8,128)(2,1)}, u32[]{:S(2)}) copy-start(bf16[1,128,512]{2,1,0:T(8,128)(2,1)} %left.1) | copy-start | bytes 393220
  3.0 11.0 %copy-start.1 = (bf16[1,128,512]{2,1,0:T(8,128)(2,1)S(1)}, bf16[1,128,512]{2,1,0:T(8,128)(2,1)}, u32[]{:S(2)}) copy-start(bf16[1,128,512]{2,1,0:T(8,128)(2,1)} %right.1) | copy-start | bytes 393220
  3.0 29.0 %all-to-all-start = ((bf16[8,128,256]{2,1,0:T(8,128)(2,1)}), bf16[8,128,256]{2,1,0:T(8,128)(2,1)S(1)}, u32[]{:S(2)}, u32[]{:S(2)}) async-start(bf16[8,128,256]{2,1,0:T(8,128)(2,1)} %shard_map.85), calls=%async_computation | async-start | bytes 1048576 | tf_op jit(solution)/shard_map/all_to_all | solution.py:284
  14.1 28.8 %collective-permute-start = (bf16[1,128,1024]{2,1,0:T(8,128)(2,1)S(1)}, bf16[1,128,1024]{2,1,0:T(8,128)(2,1)S(1)}, u32[]{:S(2)}, u32[]{:S(2)}) collective-permute-start(bf16[1,128,1024]{2,1,0:T(8,128)(2,1)S(1)} %get-tuple-element.32), channel_id=1, source_target_pairs={{0,48},{16,0},{32,16},{48,32},{1,49},{17,1},{33,17},{49,33},{2,50}... | collective-permute-start | bytes 786440 | tf_op jit(solution)/shard_map/ppermute | solution.py:268
  20.0 24.1 %collective-permute-start.1 = (bf16[1,128,1024]{2,1,0:T(8,128)(2,1)S(1)}, bf16[1,128,1024]{2,1,0:T(8,128)(2,1)S(1)}, u32[]{:S(2)}, u32[]{:S(2)}) collective-permute-start(bf16[1,128,1024]{2,1,0:T(8,128)(2,1)S(1)} %get-tuple-element.33), channel_id=1, source_target_pairs={{0,32},{16,48},{32,0},{48,16},{1,33},{17,49},{33,1},{49,17},{2,34}... | collective-permute-start | bytes 786440 | tf_op jit(solution)/shard_map/ppermute | solution.py:268
  23.6 17.3 %collective-permute-start.2 = (bf16[1,128,1024]{2,1,0:T(8,128)(2,1)S(1)}, bf16[1,128,1024]{2,1,0:T(8,128)(2,1)S(1)}, u32[]{:S(2)}, u32[]{:S(2)}) collective-permute-start(bf16[1,128,1024]{2,1,0:T(8,128)(2,1)S(1)} %get-tuple-element.34), channel_id=1, source_target_pairs={{0,16},{16,32},{32,48},{48,0},{1,17},{17,33},{33,49},{49,1},{2,18}... | collective-permute-start | bytes 786440 | tf_op jit(solution)/shard_map/ppermute | solution.py:268
  28.3 0.7 copy-start.4
  32.0 3.9 %collective-permute-start.3 = (bf16[8,128,256]{2,1,0:T(8,128)(2,1)S(1)}, bf16[8,128,256]{2,1,0:T(8,128)(2,1)S(1)}, u32[]{:S(2)}, u32[]{:S(2)}) collective-permute-start(bf16[8,128,256]{2,1,0:T(8,128)(2,1)S(1)} %all-to-all-done.mine), channel_id=1, source_target_pairs={{0,8},{8,0},{1,9},{9,1},{2,10},{10,2},{3,11},{11,3},{4,12},{12,4},... | collective-permute-start | bytes 1572872 | tf_op jit(solution)/shard_map/ppermute | solution.py:268
  63.0 13.0 %collective-permute-start.7 = (bf16[8,128,256]{2,1,0:T(8,128)(2,1)S(1)}, bf16[8,128,256]{2,1,0:T(8,128)(2,1)S(1)}, u32[]{:S(2)}, u32[]{:S(2)}) collective-permute-start(bf16[8,128,256]{2,1,0:T(8,128)(2,1)S(1)} %get-tuple-element.50), channel_id=1, source_target_pairs={{0,8},{8,0},{1,9},{9,1},{2,10},{10,2},{3,11},{11,3},{4,12},{12,4},... | collective-permute-start | bytes 1572872 | tf_op jit(solution)/shard_map/ppermute | solution.py:268
  76.8 42.4 %all-to-all-start.2 = ((bf16[8,128,256]{2,1,0:T(8,128)(2,1)}), bf16[8,128,256]{2,1,0:T(8,128)(2,1)S(1)}, u32[]{:S(2)}, u32[]{:S(2)}) async-start(bf16[8,128,256]{2,1,0:T(8,128)(2,1)} %add_convert_fusion), calls=%async_computation.2 | async-start | bytes 1048576 | tf_op jit(solution)/shard_map/all_to_all | solution.py:330
  85.1 22.4 %collective-permute-start.4 = (bf16[1,128,1024]{2,1,0:T(8,128)(2,1)S(1)}, bf16[1,128,1024]{2,1,0:T(8,128)(2,1)S(1)}, u32[]{:S(2)}, u32[]{:S(2)}) collective-permute-start(bf16[1,128,1024]{2,1,0:T(8,128)(2,1)S(1)} %get-tuple-element.46), channel_id=1, source_target_pairs={{0,16},{16,32},{32,48},{48,0},{1,17},{17,33},{33,49},{49,1},{2,18}... | collective-permute-start | bytes 786440 | tf_op jit(solution)/shard_map/ppermute | solution.py:268
  87.4 20.1 %collective-permute-start.5 = (bf16[1,128,1024]{2,1,0:T(8,128)(2,1)S(1)}, bf16[1,128,1024]{2,1,0:T(8,128)(2,1)S(1)}, u32[]{:S(2)}, u32[]{:S(2)}) collective-permute-start(bf16[1,128,1024]{2,1,0:T(8,128)(2,1)S(1)} %get-tuple-element.47), channel_id=1, source_target_pairs={{0,32},{16,48},{32,0},{48,16},{1,33},{17,49},{33,1},{49,17},{2,34}... | collective-permute-start | bytes 786440 | tf_op jit(solution)/shard_map/ppermute | solution.py:268
  90.4 28.9 %collective-permute-start.6 = (bf16[1,128,1024]{2,1,0:T(8,128)(2,1)S(1)}, bf16[1,128,1024]{2,1,0:T(8,128)(2,1)S(1)}, u32[]{:S(2)}, u32[]{:S(2)}) collective-permute-start(bf16[1,128,1024]{2,1,0:T(8,128)(2,1)S(1)} %get-tuple-element.48), channel_id=1, source_target_pairs={{0,48},{16,0},{32,16},{48,32},{1,49},{17,1},{33,17},{49,33},{2,50}... | collective-permute-start | bytes 786440 | tf_op jit(solution)/shard_map/ppermute | solution.py:268

commit v5 on v4

v5 whole, which is shorter than its diff:
```python
import functools
import math

import jax
import jax.numpy as jnp
from jax import lax
from jax.experimental import pallas as pl
from jax.experimental.pallas import tpu as pltpu
from jax.sharding import Mesh
from jax.sharding import PartitionSpec as P

FLOOR = -1e30
NZ, NY, NC = 8, 4, 2
FIELDS = 4
VMEM = pl.BlockSpec(memory_space=pltpu.VMEM)
SMEM = pl.BlockSpec(memory_space=pltpu.SMEM)
PARAMS = pltpu.CompilerParams(vmem_limit_bytes=40 * 1024 * 1024)


def dot(a, b, ca, cb):
    return lax.dot_general(a, b, (((ca,), (cb,)), ((), ())), preferred_element_type=jnp.float32)


FIELDS = 4
VMEM = pl.BlockSpec(memory_space=pltpu.VMEM)
SMEM = pl.BlockSpec(memory_space=pltpu.SMEM)
PARAMS = pltpu.CompilerParams(vmem_limit_bytes=40 * 1024 * 1024)


def dot(a, b, ca, cb):
    return lax.dot_general(a, b, (((ca,), (cb,)), ((), ())), preferred_element_type=jnp.float32)


def visits(doc_starts, tok, z, y, c):
    nctx = NZ * NY * NC
    half = tok // 2
    source = jnp.tile((y + jnp.arange(NY, dtype=jnp.int32)) % NY, 2)
    upper = jnp.repeat(jnp.arange(2, dtype=jnp.int32), NY)
    base = (z * NY + source) * NC + c
    run = jnp.where(upper == 1, 2 * nctx - 1 - base, base)
    starts = doc_starts // half
    begin = jnp.max(jnp.where(starts[None, :] <= run[:, None], starts[None, :], 0), axis=1)
    first = jnp.min(begin.reshape(2, NY), axis=1) // 2
    last = jnp.max(run.reshape(2, NY), axis=1) // 2
    low0 = (first - y + NY - 1) // NY
    high0 = jnp.minimum((last - y + NY) // NY, NZ)
    low1 = (nctx - 1 - y - last + NY - 1) // NY
    high1 = jnp.minimum((nctx - 1 - y - first + NY) // NY, NZ)
    count0 = jnp.maximum(high0 - low0, 0)
    count1 = jnp.maximum(high1 - low1, 0)
    sides = jnp.stack([low0, count0, low1, count1], axis=1).reshape(-1)
    runs = jnp.stack([run, begin, upper * NY + source], axis=1).reshape(-1)
    own = jnp.stack([y, c])
    return jnp.concatenate([sides, runs, own]).astype(jnp.int32)


class Tile:
    def __init__(self, info, pairs_ref, heads):
        self.info, self.pairs = info, pairs_ref
        self.keys = pairs_ref.shape[1]
        self.half = self.keys // 2
        self.width = pairs_ref.shape[2] // 2
        self.cols = heads * self.half
        self.runs = 2 * NZ * NY * NC
        own = 2 * FIELDS + 2 * NY * 3
        self.y = info[own]
        self.c = info[own + 1]
        row = lax.broadcasted_iota(jnp.int32, (self.keys, 1), 0)
        core = jnp.where(row < self.half, self.c, 1 - self.c)
        rest = row % self.half
        self.row_low = core * self.half + rest
        self.row_high = (self.runs - 1 - core) * self.half + rest
        self.col_rest = lax.broadcasted_iota(jnp.int32, (1, self.cols), 1) % self.half

    def field(self, side, n):
        return self.info[side * FIELDS + n]

    def run(self, side, k, n):
        return self.info[2 * FIELDS + (side * NY + k) * 3 + n]

    def row(self, side, k):
        return pl.ds(self.run(side, k, 2), 1)

    def count(self, side):
        return self.field(side, 1) + self.field(side, 3)

    def steps(self, side):
        return (self.count(side) + 1) // 2

    def columns(self, side):
        own = [self.run(side, k, 0) * self.half + self.col_rest for k in range(NY)]
        first = [jnp.full((1, self.cols), self.run(side, k, 1) * self.half) for k in range(NY)]
        return jnp.concatenate(own, axis=1), jnp.concatenate(first, axis=1)

    def blocks(self, side, i):
        def place(n):
            lower = self.field(side, 1)
            return jnp.where(
                n >= lower, self.field(side, 2) + NZ + n - lower, self.field(side, 0) + n
            )

        second = jnp.minimum(2 * i + 1, self.count(side) - 1)
        return place(2 * i), place(second)

    def positions(self, side, i, blocks):
        parts = []
        for n, b in enumerate(blocks):
            step = NY * NC * self.half
            low = b * step + self.y * NC * self.half + self.row_low
            high = self.row_high - (b - NZ) * step - self.y * NC * self.half
            at = jnp.where(b >= NZ, high, low)
            if n:
                at = jnp.where(2 * i + 1 < self.count(side), at, jnp.int32(2**30))
            parts.append(at)
        return jnp.concatenate(parts, axis=0)


def two(ref, blocks, lanes, axis):
    return jnp.concatenate([ref[b, :, lanes] for b in blocks], axis=axis)


def gather_kernel(mine, other, pairs, turned):
    half = mine.shape[1] // 2
    width = mine.shape[2] // 2
    for b in range(2 * NZ):
        rows = slice((b // NZ) * half, (b // NZ + 1) * half)
        block = jnp.concatenate([mine[b % NZ, rows], other[b % NZ, rows]], axis=0)
        pairs[b] = block
        turned[b] = block.astype(jnp.float32).T.astype(turned.dtype)


def queries_of(refs, side, second, half, width, heads):
    rows = pl.ds(pl.multiple_of(side * half, half), half)
    lanes = [(heads * second + h) * width for h in range(heads)]
    return jnp.concatenate([r[0, rows, at : at + width] for r in refs for at in lanes], axis=0)


def forward_kernel(heads, info, a0, a1, a2, a3, pairs, turned, u_ref, stats_ref, s_scr, st_scr):
    tile = Tile(info, pairs, heads)
    half, width, cols = tile.half, tile.width, tile.cols
    log2_scale = math.log2(math.e) / math.sqrt(width)
    groups = 2 * tile.keys // 8
    asked = (a0, a1, a2, a3)

    def one_side(side, _):
        queries = queries_of(asked, side, 0, half, width, heads)
        own, first = tile.columns(side)
        steps = tile.steps(side)

        def scores(i, biggest):
            blocks = tile.blocks(side, i)
            at = tile.positions(side, i, blocks)
            s = dot(two(pairs, blocks, slice(0, width), 0), queries, 1, 1)
            s = jnp.where((at <= own) & (at >= first), s, FLOOR)
            s_scr[i] = s
            return jnp.maximum(biggest, jnp.max(s.reshape(groups, 8, NY * cols), axis=0))

        biggest = lax.fori_loop(0, steps, scores, jnp.full((8, NY * cols), FLOOR, jnp.float32))
        top = jnp.max(biggest, axis=0, keepdims=True)
        u_ref[side] = jnp.zeros(u_ref.shape[1:], jnp.float32)

        def sums(i, total):
            e = jnp.exp2((s_scr[i] - top) * log2_scale)
            total = total + jnp.sum(e.reshape(groups, 8, NY * cols), axis=0)
            values_t = jnp.concatenate([turned[b, width:, :] for b in tile.blocks(side, i)], axis=1)
            u_ref[side] += dot(values_t, e.astype(jnp.bfloat16), 1, 0)
            return total

        total = lax.fori_loop(0, steps, sums, jnp.zeros((8, NY * cols), jnp.float32))
        total = jnp.sum(total, axis=0, keepdims=True)
        do_t = queries_of(asked, side, 1, half, width, heads).astype(jnp.float32).T
        seen = jnp.sum(u_ref[side] * do_t, axis=0, keepdims=True)
        for k in range(NY):
            for n, whole in enumerate((top, total, seen)):
                st_scr[n, tile.row(side, k), :] = whole[:, k * cols : (k + 1) * cols]
        return 0

    lax.fori_loop(0, 2, one_side, 0)
    for k in range(NY):
        stats_ref[k] = st_scr[...]


def backward_kernel(
    heads, info, a0, a1, a2, a3, u_ref, pairs, turned, stats,
    o0, o1, o2, o3, dmine, dother, dacc, dq_scr, st_scr,
):
    tile = Tile(info, pairs, heads)
    half, width, cols, keys = tile.half, tile.width, tile.cols, tile.keys
    scale = 1.0 / math.sqrt(width)
    log2_scale = scale * math.log2(math.e)
    asked = (a0, a1, a2, a3)
    dacc[...] = jnp.zeros_like(dacc)

    tops = [stats[k, 0] for k in range(NY)]
    top = functools.reduce(jnp.maximum, tops)
    weights = [jnp.exp2((t - top) * log2_scale) for t in tops]
    den = sum(w * stats[k, 1] for k, w in enumerate(weights))
    inverse = 1.0 / den
    st_scr[0] = top * log2_scale + jnp.log2(den)
    st_scr[1] = sum(w * stats[k, 2] for k, w in enumerate(weights)) * inverse
    st_scr[2] = jnp.exp2((stats[tile.y, 0] - top) * log2_scale) * inverse

    def one_side(side, _):
        queries = queries_of(asked, side, 0, half, width, heads)
        grads = queries_of(asked, side, 1, half, width, heads)
        own, first = tile.columns(side)
        lse2, delta, share = (
            jnp.concatenate([st_scr[n, tile.row(side, k), :] for k in range(NY)], axis=1)
            for n in range(3)
        )
        dq_scr[...] = jnp.zeros_like(dq_scr)

        def visit(i, _):
            blocks = tile.blocks(side, i)
            at = tile.positions(side, i, blocks)
            s = dot(two(pairs, blocks, slice(0, width), 0), queries, 1, 1)
            s = jnp.where((at <= own) & (at >= first), s, FLOOR)
            p = jnp.exp2(s * log2_scale - lse2)
            dp = dot(two(pairs, blocks, slice(width, 2 * width), 0), grads, 1, 1)
            ds = (p * (dp - delta)).astype(jnp.bfloat16)
            dk = dot(ds, queries, 1, 0)
            dv = dot(p.astype(jnp.bfloat16), grads, 1, 0)
            for m, b in enumerate(blocks):
                dacc[b, :, :width] += dk[m * keys : (m + 1) * keys]
                dacc[b, :, width:] += dv[m * keys : (m + 1) * keys]
            keys_t = jnp.concatenate([turned[b, :width, :] for b in blocks], axis=1)
            dq_scr[...] += dot(keys_t, ds, 1, 0)
            return 0

        lax.fori_loop(0, tile.steps(side), visit, 0)
        att = (u_ref[side] * share).T.astype(jnp.bfloat16)
        dq = (dq_scr[...] * scale).T.astype(jnp.bfloat16)
        rows = pl.ds(pl.multiple_of(side * half, half), half)
        for second, whole in ((0, att), (1, dq)):
            for k, out in enumerate((o0, o1, o2, o3)):
                for h in range(heads):
                    at = (heads * second + h) * width
                    out[0, rows, at : at + width] = whole[k * cols + h * half : k * cols + (h + 1) * half]
        return 0

    lax.fori_loop(0, 2, one_side, 0)
    for b in range(2 * NZ):
        rows = slice((b // NZ) * half, (b // NZ + 1) * half)
        for out, part in ((dmine, slice(0, half)), (dother, slice(half, keys))):
            out[b % NZ, rows, :width] = (dacc[b, part, :width] * scale).astype(out.dtype)
            out[b % NZ, rows, width:] = dacc[b, part, width:].astype(out.dtype)


def combine_kernel(o0, o1, o2, o3, dkv, att_ref, dq_ref, dkv_ref, sq_ref):
    wide = att_ref.shape[2]
    parts = [o[0].astype(jnp.float32) for o in (o0, o1, o2, o3)]
    both = (parts[0] + parts[1]) + (parts[2] + parts[3])
    att_ref[0] = both[:, :wide].astype(att_ref.dtype)
    dq = both[:, wide:]
    dq_ref[0] = dq
    total = functools.reduce(jnp.add, [dkv[k].astype(jnp.float32) for k in range(NZ)])
    dkv_ref[0] = total
    squares = jnp.sum(dq * dq) + jnp.sum(total * total)
    sq_ref[...] = jnp.full(sq_ref.shape, squares, jnp.float32)


def scale_kernel(count, sums, dq, dkv, oq, ok, ov):
    lanes = sums.shape[2]
    total = sums[0]
    for k in range(1, sums.shape[0]):
        total = total + sums[k]
    factor = lax.rsqrt(total / count + 1e-06)
    for h in range(dq.shape[2] // lanes):
        at = slice(h * lanes, (h + 1) * lanes)
        oq[0, :, at] = (dq[0, :, at] * factor).astype(oq.dtype)
    width = ok.shape[2]
    ok[0] = (dkv[0, :, :width] * factor).astype(ok.dtype)
    ov[0] = (dkv[0, :, width:] * factor).astype(ov.dtype)


def spread_kernel(keys, values, copies):
    width = keys.shape[2]
    for k in range(copies.shape[0]):
        copies[k, :, :width] = keys[0]
        copies[k, :, width:] = values[0]


def join_kernel(left, right, *outs):
    wide = left.shape[2]
    for out in outs:
        out[:, :, :wide] = left[...]
        out[:, :, wide:] = right[...]


def turn(x, axis, size, by):
    return lax.ppermute(x, axis, [(i, (i + by) % size) for i in range(size)])


def per_device(queries, keys, values, grad_out, doc_starts):
    tok = queries.shape[1]
    wide = queries.shape[2]
    width = keys.shape[2]
    heads = wide // width
    half = tok // 2
    cols = heads * half
    z, y, c = (lax.axis_index(a) for a in ("z", "y", "core"))
    info = visits(doc_starts[0], tok, z, y, c)

    copies = pl.pallas_call(spread_kernel, out_shape=jax.ShapeDtypeStruct((NZ, tok, 2 * width), keys.dtype), in_specs=[VMEM] * 2, out_specs=VMEM, compiler_params=PARAMS)(keys, values)
    mine = lax.all_to_all(copies, "z", 0, 0, tiled=True)
    asked, *ask = pl.pallas_call(join_kernel, out_shape=[jax.ShapeDtypeStruct((1, tok, 2 * wide), keys.dtype)] * NY, in_specs=[VMEM] * 2, out_specs=[VMEM] * NY, compiler_params=PARAMS)(queries, grad_out)
    mine = lax.all_to_all(copies, "z", 0, 0, tiled=True)
    around = {k: turn(ask[k - 1], "y", NY, -k) for k in (2, 1, 3)}
    around[0] = asked
    other = turn(mine, "core", NC, 1)

    f32, bf16 = jnp.float32, jnp.bfloat16
    shape = jax.ShapeDtypeStruct
    pairs, turned = pl.pallas_call(
        gather_kernel,
        out_shape=(shape((2 * NZ, tok, 2 * width), bf16), shape((2 * NZ, 2 * width, tok), bf16)),
        in_specs=[VMEM] * 2,
        out_specs=(VMEM,) * 2,
        compiler_params=PARAMS,
    )(mine, other)
    stat = (3, 2 * NY, cols)

    asks = [around[k] for k in range(NY)]
    u, stats = pl.pallas_call(
        functools.partial(forward_kernel, heads),
        out_shape=(shape((2, width, NY * cols), f32), shape((NY,) + stat, f32)),
        in_specs=[SMEM] + [VMEM] * (NY + 2),
        out_specs=(VMEM, VMEM),
        scratch_shapes=[pltpu.VMEM((NZ, 2 * tok, NY * cols), f32), pltpu.VMEM(stat, f32)],
        compiler_params=PARAMS,
    )(info, *asks, pairs, turned)
    stats = lax.all_to_all(stats, "y", 0, 0, tiled=True)
    *sent, dmine, dother = pl.pallas_call(
        functools.partial(backward_kernel, heads),
        out_shape=[shape(asked.shape, bf16)] * NY
        + [shape(mine.shape, f32), shape(mine.shape, bf16)],
        in_specs=[SMEM] + [VMEM] * (NY + 4),
        out_specs=[VMEM] * (NY + 2),
        scratch_shapes=[
            pltpu.VMEM((2 * NZ, tok, 2 * width), f32),
            pltpu.VMEM((width, NY * cols), f32),
            pltpu.VMEM(stat, f32),
        ],
        compiler_params=PARAMS,
    )(info, *asks, u, pairs, turned, stats)
    back = [sent[0]] + [turn(sent[k], "y", NY, k) for k in range(1, NY)]
    from_core = turn(dother, "core", NC, 1)
    pair = (dmine + from_core.astype(f32)).astype(bf16)
    pieces = lax.all_to_all(pair, "z", 0, 0, tiled=True)
    attended, dq, dkv, squares = pl.pallas_call(
        combine_kernel,
        out_shape=(
            shape(queries.shape, bf16),
            shape(queries.shape, f32),
            shape((1, tok, 2 * width), f32),
            shape((NZ * NC, 1, 128), f32),
        ),
        in_specs=[VMEM] * 5,
        out_specs=(VMEM,) * 4,
        compiler_params=PARAMS,
    )(*back, pieces)
    squares = lax.all_to_all(squares, ("z", "core"), 0, 0, tiled=True)
    ndata = lax.axis_size("dp")
    squares = jnp.broadcast_to(jnp.sum(squares, axis=0, keepdims=True), (NY * ndata, 1, 128))
    squares = lax.all_to_all(squares, ("y", "dp"), 0, 0, tiled=True)
    count = float(ndata * NZ * NY * NC * tok * (wide + 2 * width))
    out_query, out_key, out_value = pl.pallas_call(
        functools.partial(scale_kernel, count),
        out_shape=(shape(queries.shape, bf16), shape(keys.shape, bf16), shape(values.shape, bf16)),
        in_specs=[VMEM] * 3,
        out_specs=(VMEM,) * 3,
        compiler_params=PARAMS,
    )(squares, dq, dkv)
    return attended, out_query, out_key, out_value


def solution(mesh):
    ndata = mesh.shape["dp"]
    fine = Mesh(mesh.devices.reshape(NZ, NY, NC, ndata), ("z", "y", "core", "dp"))
    spec = P("dp", ("z", "y", "core"), None)
    return jax.shard_map(
        per_device,
        mesh=fine,
        in_specs=(spec, spec, spec, spec, P("dp", None)),
        out_specs=(spec, spec, spec, spec),
        check_vma=False,
    )
```

time: 156 us -> 146 us (0.936)
  Pallas kernels: 15.7 us -> 8.73 us
  blocking collectives: 45.4 us -> 41.1 us
  waiting for transfers between devices: 33.3 us -> 34.9 us
    pallas_call x5 -> x2, Pallas kernels: 12.7 us -> 5.7 us  [the longest x1 3.32 us: per_device(): pl.pallas_call(functools.partial(backward_kernel, heads), out_shape=[shap...]
    all_to_all x1, blocking collectives: 19.7 us -> 14.3 us  [per_device(): squares = lax.all_to_all(squares, ('y', 'dp'), 0, 0, tiled=True)]
    ppermute x8, waiting for transfers between devices: 30.5 us -> 32.3 us  [turn(): return lax.ppermute(x, axis, [(i, (i + by) % size) for i in range(size)])]
    all_to_all x1, blocking collectives: 11 us -> 12.6 us  [per_device(): stats = lax.all_to_all(stats, 'y', 0, 0, tiled=True)]
  transfers between devices with their start and end apart: 10 -> 10, of which waited for: 6 -> 7; matrix products, arithmetic and copies ran while one was open for 1% -> 1% of each run, Pallas kernels for 3% -> 0%
where the time goes in v5:
time: 146 us; the launch traced here: 145 us
  starting transfers between devices  55.3 us (38%)
  blocking collectives  41.1 us (28%)
  waiting for transfers between devices  34.9 us (24%)
  Pallas kernels  8.73 us (6%)
  local copies, waits for them, and re-layouts  3.02 us (2%)
  other arithmetic  1.58 us (1%)
    ppermute x8, starting transfers between devices, turn(): return lax.ppermute(x, axis, [(i, (i + by) % size) for i in range(size)])  36.5 us
    ppermute x8, waiting for transfers between devices, turn(): return lax.ppermute(x, axis, [(i, (i + by) % size) for i in range(size)])  32.3 us
    all_to_all x1, blocking collectives, per_device(): squares = lax.all_to_all(squares, ('y', 'dp'), 0, 0, tiled=True)  14.3 us
    all_to_all x1, blocking collectives, per_device(): squares = lax.all_to_all(squares, ('z', 'core'), 0, 0, tiled=True)  14.2 us
    all_to_all x1, blocking collectives, per_device(): stats = lax.all_to_all(stats, 'y', 0, 0, tiled=True)  12.6 us
    all_to_all x1, starting transfers between devices, per_device(): mine = lax.all_to_all(copies, 'z', 0, 0, tiled=True)  11 us
    all_to_all x1, starting transfers between devices, per_device(): pieces = lax.all_to_all(pair, 'z', 0, 0, tiled=True)  7.84 us
    pallas_call x1, Pallas kernels, per_device(): pl.pallas_call(functools.partial(backward_kernel, heads), out_shape=[shap...  3.32 us
  transfers between devices with their start and end apart: 10, of which 7 were waited for; matrix products, arithmetic and copies ran while one was open for 1% of the time, Pallas kernels for 0%

profile of v5, /device:TPU:1, one launch (start us, length us, event | category | flops | bytes accessed | tf_op | source)
XLA Modules:
  0.0 145.5 jit_solution(12587541105824968761)
XLA Ops:
  0.6 0.0 copy-start.2
  0.6 0.7 copy-done.2
  1.4 0.0 copy-start.3
  1.4 0.8 copy-done.3
  2.1 0.9 shard_map.85
  3.0 0.0 copy-start
  3.0 0.0 copy-start.1
  3.0 11.0 %all-to-all-start = ((bf16[8,128,256]{2,1,0:T(8,128)(2,1)}), bf16[8,128,256]{2,1,0:T(8,128)(2,1)S(1)}, u32[]{:S(2)}, u32[]{:S(2)}) async-start(bf16[8,128,256]{2,1,0:T(8,128)(2,1)} %shard_map.85), calls=%async_computation | async-start | bytes 1048576 | tf_op jit(solution)/shard_map/all_to_all | solution.py:307
  14.0 0.0 copy-done
  14.0 0.0 copy-done.1
  14.0 0.1 shard_map.84
  14.1 5.9 %collective-permute-start = (bf16[1,128,1024]{2,1,0:T(8,128)(2,1)S(1)}, bf16[1,128,1024]{2,1,0:T(8,128)(2,1)S(1)}, u32[]{:S(2)}, u32[]{:S(2)}) collective-permute-start(bf16[1,128,1024]{2,1,0:T(8,128)(2,1)S(1)} %get-tuple-element.26), channel_id=1, source_target_pairs={{0,48},{16,0},{32,16},{48,32},{1,49},{17,1},{33,17},{49,33},{2,50}... | collective-permute-start | bytes 786440 | tf_op jit(solution)/shard_map/ppermute | solution.py:291
  20.0 3.5 %collective-permute-start.1 = (bf16[1,128,1024]{2,1,0:T(8,128)(2,1)S(1)}, bf16[1,128,1024]{2,1,0:T(8,128)(2,1)S(1)}, u32[]{:S(2)}, u32[]{:S(2)}) collective-permute-start(bf16[1,128,1024]{2,1,0:T(8,128)(2,1)S(1)} %get-tuple-element.27), channel_id=1, source_target_pairs={{0,32},{16,48},{32,0},{48,16},{1,33},{17,49},{33,1},{49,17},{2,34}... | collective-permute-start | bytes 786440 | tf_op jit(solution)/shard_map/ppermute | solution.py:291
  23.5 4.2 %collective-permute-start.2 = (bf16[1,128,1024]{2,1,0:T(8,128)(2,1)S(1)}, bf16[1,128,1024]{2,1,0:T(8,128)(2,1)S(1)}, u32[]{:S(2)}, u32[]{:S(2)}) collective-permute-start(bf16[1,128,1024]{2,1,0:T(8,128)(2,1)S(1)} %get-tuple-element.28), channel_id=1, source_target_pairs={{0,16},{16,32},{32,48},{48,0},{1,17},{17,33},{33,49},{49,1},{2,18}... | collective-permute-start | bytes 786440 | tf_op jit(solution)/shard_map/ppermute | solution.py:291
  27.8 0.0 copy-start.4
  27.8 0.6 copy-done.4
  28.5 0.1 eq.26
  28.6 0.1 eq.25
  28.6 0.1 add.218
  28.7 0.1 add.215
  28.8 0.2 select_reduce_fusion
  29.0 0.1 reshape.448
  29.1 0.1 reduce_min.11
  29.2 0.1 select_reduce_fusion.1
  29.4 2.6 %all-to-all-done.mine = bf16[8,128,256]{2,1,0:T(8,128)(2,1)S(1)} async-done(((bf16[8,128,256]{2,1,0:T(8,128)(2,1)}), bf16[8,128,256]{2,1,0:T(8,128)(2,1)S(1)}, u32[]{:S(2)}, u32[]{:S(2)}) %all-to-all-start) | async-done | bytes 524320 | tf_op jit(solution)/shard_map/all_to_all | solution.py:307
  32.0 2.4 %collective-permute-start.3 = (bf16[8,128,256]{2,1,0:T(8,128)(2,1)S(1)}, bf16[8,128,256]{2,1,0:T(8,128)(2,1)S(1)}, u32[]{:S(2)}, u32[]{:S(2)}) collective-permute-start(bf16[8,128,256]{2,1,0:T(8,128)(2,1)S(1)} %all-to-all-done.mine), channel_id=1, source_target_pairs={{0,8},{8,0},{1,9},{9,1},{2,10},{10,2},{3,11},{11,3},{4,12},{12,4},... | collective-permute-start | bytes 1572872 | tf_op jit(solution)/shard_map/ppermute | solution.py:291
  34.4 0.1 copy.13
  34.5 0.1 reshape.449
  34.6 0.1 add.220
  34.7 0.1 copy.14
  34.8 0.1 reshape.450
  34.8 0.1 pad_add_fusion.2.info
  34.9 1.0 collective-permute-done.3.other
  35.9 0.3 shard_map.86
  36.2 6.4 %collective-permute-done.a1 = bf16[1,128,1024]{2,1,0:T(8,128)(2,1)S(1)} collective-permute-done((bf16[1,128,1024]{2,1,0:T(8,128)(2,1)S(1)}, bf16[1,128,1024]{2,1,0:T(8,128)(2,1)S(1)}, u32[]{:S(2)}, u32[]{:S(2)}) %collective-permute-start) | collective-permute-done | bytes 262176 | tf_op jit(solution)/shard_map/ppermute | solution.py:291
  42.6 0.0 collective-permute-done.1.a2
  42.6 0.0 collective-permute-done.2.a3
  42.6 2.4 %shard_map.87 = (f32[2,128,1024]{2,1,0:T(8,128)S(1)}, f32[4,3,8,256]{3,2,1,0:T(8,128)S(1)}) custom-call(s32[34]{0:T(128)S(1)} %pad_add_fusion.2.info, bf16[1,128,1024]{2,1,0:T(8,128)(2,1)S(1)} %get-tuple-element.25.a0, bf16[1,128,1024]{2,1,0:T(8,128)(2,1)S(1)} %collective-permute-done.a1, bf16[1,128,1024]{2,1,0:T(8,128)(2,1)S(1)} %collective-permute-done.1.a2, ...), custom_call_target="tpu_custom_call" | custom-call | tf_op jit(solution)/shard_map/pallas_call | solution.py:324
  45.0 12.6 %all_to_all.25.stats = f32[4,3,8,256]{3,2,1,0:T(8,128)S(1)} all-to-all(f32[4,3,8,256]{3,2,1,0:T(8,128)S(1)} %get-tuple-element.32), channel_id=1, replica_groups=mesh['z'=8,'y'=4,'core'=2,'dp'=8] {'y'}, dimensions={0} | all-to-all | bytes 196608 | tf_op jit(solution)/shard_map/all_to_all | solution.py:332
  57.6 3.3 %shard_map.88 = (bf16[1,128,1024]{2,1,0:T(8,128)(2,1)S(1)}, bf16[1,128,1024]{2,1,0:T(8,128)(2,1)S(1)}, bf16[1,128,1024]{2,1,0:T(8,128)(2,1)S(1)}, bf16[1,128,102...) custom-call(s32[34]{0:T(128)S(1)} %pad_add_fusion.2.info, ...), custom_call_target="tpu_custom_call" | custom-call | tf_op jit(solution)/shard_map/pallas_call | solution.py:333
  60.9 9.5 %collective-permute-start.7 = (bf16[8,128,256]{2,1,0:T(8,128)(2,1)S(1)}, bf16[8,128,256]{2,1,0:T(8,128)(2,1)S(1)}, u32[]{:S(2)}, u32[]{:S(2)}) collective-permute-start(bf16[8,128,256]{2,1,0:T(8,128)(2,1)S(1)} %get-tuple-element.38), channel_id=1, source_target_pairs={{0,8},{8,0},{1,9},{9,1},{2,10},{10,2},{3,11},{11,3},{4,12},{12,4},... | collective-permute-start | bytes 1572872 | tf_op jit(solution)/shard_map/ppermute | solution.py:291
  70.4 1.5 %collective-permute-done.7 = bf16[8,128,256]{2,1,0:T(8,128)(2,1)S(1)} collective-permute-done((bf16[8,128,256]{2,1,0:T(8,128)(2,1)S(1)}, bf16[8,128,256]{2,1,0:T(8,128)(2,1)S(1)}, u32[]{:S(2)}, u32[]{:S(2)}) %collective-permute-start.7) | collective-permute-done | bytes 524320 | tf_op jit(solution)/shard_map/ppermute | solution.py:291
  71.9 0.9 add_convert_fusion
  72.9 7.8 %all-to-all-start.2 = ((bf16[8,128,256]{2,1,0:T(8,128)(2,1)}), bf16[8,128,256]{2,1,0:T(8,128)(2,1)S(1)}, u32[]{:S(2)}, u32[]{:S(2)}) async-start(bf16[8,128,256]{2,1,0:T(8,128)(2,1)} %add_convert_fusion), calls=%async_computation.2 | async-start | bytes 1048576 | tf_op jit(solution)/shard_map/all_to_all | solution.py:349
  80.7 2.7 %collective-permute-start.4 = (bf16[1,128,1024]{2,1,0:T(8,128)(2,1)S(1)}, bf16[1,128,1024]{2,1,0:T(8,128)(2,1)S(1)}, u32[]{:S(2)}, u32[]{:S(2)}) collective-permute-start(bf16[1,128,1024]{2,1,0:T(8,128)(2,1)S(1)} %get-tuple-element.34), channel_id=1, source_target_pairs={{0,16},{16,32},{32,48},{48,0},{1,17},{17,33},{33,49},{49,1},{2,18}... | collective-permute-start | bytes 786440 | tf_op jit(solution)/shard_map/ppermute | solution.py:291
  83.4 4.0 %collective-permute-start.5 = (bf16[1,128,1024]{2,1,0:T(8,128)(2,1)S(1)}, bf16[1,128,1024]{2,1,0:T(8,128)(2,1)S(1)}, u32[]{:S(2)}, u32[]{:S(2)}) collective-permute-start(bf16[1,128,1024]{2,1,0:T(8,128)(2,1)S(1)} %get-tuple-element.35), channel_id=1, source_target_pairs={{0,32},{16,48},{32,0},{48,16},{1,33},{17,49},{33,1},{49,17},{2,34}... | collective-permute-start | bytes 786440 | tf_op jit(solution)/shard_map/ppermute | solution.py:291
  87.4 4.3 %collective-permute-start.6 = (bf16[1,128,1024]{2,1,0:T(8,128)(2,1)S(1)}, bf16[1,128,1024]{2,1,0:T(8,128)(2,1)S(1)}, u32[]{:S(2)}, u32[]{:S(2)}) collective-permute-start(bf16[1,128,1024]{2,1,0:T(8,128)(2,1)S(1)} %get-tuple-element.36), channel_id=1, source_target_pairs={{0,48},{16,0},{32,16},{48,32},{1,49},{17,1},{33,17},{49,33},{2,50}... | collective-permute-start | bytes 786440 | tf_op jit(solution)/shard_map/ppermute | solution.py:291
  91.7 2.9 %collective-permute-done.4.o1 = bf16[1,128,1024]{2,1,0:T(8,128)(2,1)S(1)} collective-permute-done((bf16[1,128,1024]{2,1,0:T(8,128)(2,1)S(1)}, bf16[1,128,1024]{2,1,0:T(8,128)(2,1)S(1)}, u32[]{:S(2)}, u32[]{:S(2)}) %collective-permute-start.4) | collective-permute-done | bytes 262176 | tf_op jit(solution)/shard_map/ppermute | solution.py:291
  94.6 6.3 %collective-permute-done.5.o2 = bf16[1,128,1024]{2,1,0:T(8,128)(2,1)S(1)} collective-permute-done((bf16[1,128,1024]{2,1,0:T(8,128)(2,1)S(1)}, bf16[1,128,1024]{2,1,0:T(8,128)(2,1)S(1)}, u32[]{:S(2)}, u32[]{:S(2)}) %collective-permute-start.5) | collective-permute-done | bytes 262176 | tf_op jit(solution)/shard_map/ppermute | solution.py:291
  100.9 14.3 %collective-permute-done.6.o3 = bf16[1,128,1024]{2,1,0:T(8,128)(2,1)S(1)} collective-permute-done((bf16[1,128,1024]{2,1,0:T(8,128)(2,1)S(1)}, bf16[1,128,1024]{2,1,0:T(8,128)(2,1)S(1)}, u32[]{:S(2)}, u32[]{:S(2)}) %collective-permute-start.6) | collective-permute-done | bytes 262176 | tf_op jit(solution)/shard_map/ppermute | solution.py:291
  115.1 0.0 all-to-all-done.2.dkv
  115.1 1.0 shard_map.89
  116.2 14.2 %all_to_all.26 = f32[16,1,128]{2,1,0:T(1,128)S(1)} all-to-all(f32[16,1,128]{2,1,0:T(1,128)S(1)} %get-tuple-element.40), channel_id=1, replica_groups=mesh['z'=8,'y'=4,'core'=2,'dp'=8] {'z','core'}, dimensions={0} | all-to-all | bytes 16384 | tf_op jit(solution)/shard_map/all_to_all | solution.py:362
  130.4 14.3 %all_to_all.27.sums = f32[32,1,128]{2,1,0:T(1,128)S(1)} all-to-all(f32[32,1,128]{2,1,0:T(1,128)S(1)} %broadcast_in_dim.31), channel_id=1, replica_groups=mesh['z'=8,'y'=4,'core'=2,'dp'=8] {'y','dp'}, dimensions={0} | all-to-all | bytes 32768 | tf_op jit(solution)/shard_map/all_to_all | solution.py:365
  144.8 0.7 shard_map.90
  (12 shorter events, 0.2 us)
Async XLA Ops:
  0.6 0.8 copy-start.2
  1.4 0.8 copy-start.3
  3.0 11.0 %copy-start = (bf16[1,128,512]{2,1,0:T(8,128)(2,1)S(1)}, bf16[1,128,512]{2,1,0:T(8,128)(2,1)}, u32[]{:S(2)}) copy-start(bf16[1,128,512]{2,1,0:T(8,128)(2,1)} %left.1) | copy-start | bytes 393220
  3.0 11.0 %copy-start.1 = (bf16[1,128,512]{2,1,0:T(8,128)(2,1)S(1)}, bf16[1,128,512]{2,1,0:T(8,128)(2,1)}, u32[]{:S(2)}) copy-start(bf16[1,128,512]{2,1,0:T(8,128)(2,1)} %right.1) | copy-start | bytes 393220
  3.0 29.0 %all-to-all-start = ((bf16[8,128,256]{2,1,0:T(8,128)(2,1)}), bf16[8,128,256]{2,1,0:T(8,128)(2,1)S(1)}, u32[]{:S(2)}, u32[]{:S(2)}) async-start(bf16[8,128,256]{2,1,0:T(8,128)(2,1)} %shard_map.85), calls=%async_computation | async-start | bytes 1048576 | tf_op jit(solution)/shard_map/all_to_all | solution.py:307
  14.1 28.5 %collective-permute-start = (bf16[1,128,1024]{2,1,0:T(8,128)(2,1)S(1)}, bf16[1,128,1024]{2,1,0:T(8,128)(2,1)S(1)}, u32[]{:S(2)}, u32[]{:S(2)}) collective-permute-start(bf16[1,128,1024]{2,1,0:T(8,128)(2,1)S(1)} %get-tuple-element.26), channel_id=1, source_target_pairs={{0,48},{16,0},{32,16},{48,32},{1,49},{17,1},{33,17},{49,33},{2,50}... | collective-permute-start | bytes 786440 | tf_op jit(solution)/shard_map/ppermute | solution.py:291
  20.0 22.6 %collective-permute-start.1 = (bf16[1,128,1024]{2,1,0:T(8,128)(2,1)S(1)}, bf16[1,128,1024]{2,1,0:T(8,128)(2,1)S(1)}, u32[]{:S(2)}, u32[]{:S(2)}) collective-permute-start(bf16[1,128,1024]{2,1,0:T(8,128)(2,1)S(1)} %get-tuple-element.27), channel_id=1, source_target_pairs={{0,32},{16,48},{32,0},{48,16},{1,33},{17,49},{33,1},{49,17},{2,34}... | collective-permute-start | bytes 786440 | tf_op jit(solution)/shard_map/ppermute | solution.py:291
  23.5 19.1 %collective-permute-start.2 = (bf16[1,128,1024]{2,1,0:T(8,128)(2,1)S(1)}, bf16[1,128,1024]{2,1,0:T(8,128)(2,1)S(1)}, u32[]{:S(2)}, u32[]{:S(2)}) collective-permute-start(bf16[1,128,1024]{2,1,0:T(8,128)(2,1)S(1)} %get-tuple-element.28), channel_id=1, source_target_pairs={{0,16},{16,32},{32,48},{48,0},{1,17},{17,33},{33,49},{49,1},{2,18}... | collective-permute-start | bytes 786440 | tf_op jit(solution)/shard_map/ppermute | solution.py:291
  27.8 0.7 copy-start.4
  32.0 3.9 %collective-permute-start.3 = (bf16[8,128,256]{2,1,0:T(8,128)(2,1)S(1)}, bf16[8,128,256]{2,1,0:T(8,128)(2,1)S(1)}, u32[]{:S(2)}, u32[]{:S(2)}) collective-permute-start(bf16[8,128,256]{2,1,0:T(8,128)(2,1)S(1)} %all-to-all-done.mine), channel_id=1, source_target_pairs={{0,8},{8,0},{1,9},{9,1},{2,10},{10,2},{3,11},{11,3},{4,12},{12,4},... | collective-permute-start | bytes 1572872 | tf_op jit(solution)/shard_map/ppermute | solution.py:291
  60.9 11.0 %collective-permute-start.7 = (bf16[8,128,256]{2,1,0:T(8,128)(2,1)S(1)}, bf16[8,128,256]{2,1,0:T(8,128)(2,1)S(1)}, u32[]{:S(2)}, u32[]{:S(2)}) collective-permute-start(bf16[8,128,256]{2,1,0:T(8,128)(2,1)S(1)} %get-tuple-element.38), channel_id=1, source_target_pairs={{0,8},{8,0},{1,9},{9,1},{2,10},{10,2},{3,11},{11,3},{4,12},{12,4},... | collective-permute-start | bytes 1572872 | tf_op jit(solution)/shard_map/ppermute | solution.py:291
  72.9 42.3 %all-to-all-start.2 = ((bf16[8,128,256]{2,1,0:T(8,128)(2,1)}), bf16[8,128,256]{2,1,0:T(8,128)(2,1)S(1)}, u32[]{:S(2)}, u32[]{:S(2)}) async-start(bf16[8,128,256]{2,1,0:T(8,128)(2,1)} %add_convert_fusion), calls=%async_computation.2 | async-start | bytes 1048576 | tf_op jit(solution)/shard_map/all_to_all | solution.py:349
  80.7 13.9 %collective-permute-start.4 = (bf16[1,128,1024]{2,1,0:T(8,128)(2,1)S(1)}, bf16[1,128,1024]{2,1,0:T(8,128)(2,1)S(1)}, u32[]{:S(2)}, u32[]{:S(2)}) collective-permute-start(bf16[1,128,1024]{2,1,0:T(8,128)(2,1)S(1)} %get-tuple-element.34), channel_id=1, source_target_pairs={{0,16},{16,32},{32,48},{48,0},{1,17},{17,33},{33,49},{49,1},{2,18}... | collective-permute-start | bytes 786440 | tf_op jit(solution)/shard_map/ppermute | solution.py:291
  83.4 17.5 %collective-permute-start.5 = (bf16[1,128,1024]{2,1,0:T(8,128)(2,1)S(1)}, bf16[1,128,1024]{2,1,0:T(8,128)(2,1)S(1)}, u32[]{:S(2)}, u32[]{:S(2)}) collective-permute-start(bf16[1,128,1024]{2,1,0:T(8,128)(2,1)S(1)} %get-tuple-element.35), channel_id=1, source_target_pairs={{0,32},{16,48},{32,0},{48,16},{1,33},{17,49},{33,1},{49,17},{2,34}... | collective-permute-start | bytes 786440 | tf_op jit(solution)/shard_map/ppermute | solution.py:291
  87.4 27.7 %collective-permute-start.6 = (bf16[1,128,1024]{2,1,0:T(8,128)(2,1)S(1)}, bf16[1,128,1024]{2,1,0:T(8,128)(2,1)S(1)}, u32[]{:S(2)}, u32[]{:S(2)}) collective-permute-start(bf16[1,128,1024]{2,1,0:T(8,128)(2,1)S(1)} %get-tuple-element.36), channel_id=1, source_target_pairs={{0,48},{16,0},{32,16},{48,32},{1,49},{17,1},{33,17},{49,33},{2,50}... | collective-permute-start | bytes 786440 | tf_op jit(solution)/shard_map/ppermute | solution.py:291

commit v6 on v5

--- a/solution.py
+++ b/solution.py
@@ -182,7 +182,7 @@
 
 def backward_kernel(
     heads, info, a0, a1, a2, a3, u_ref, pairs, turned, stats,
-    o0, o1, o2, o3, dmine, dother, dacc, dq_scr, st_scr,
+    t0, t1, t2, t3, o0, o1, o2, o3, dmine, dother, dacc, dq_scr, st_scr,
 ):
     tile = Tile(info, pairs, heads)
     half, width, cols, keys = tile.half, tile.width, tile.cols, tile.keys
@@ -231,11 +231,11 @@
         att = (u_ref[side] * share).T.astype(jnp.bfloat16)
         dq = (dq_scr[...] * scale).T.astype(jnp.bfloat16)
         rows = pl.ds(pl.multiple_of(side * half, half), half)
-        for second, whole in ((0, att), (1, dq)):
-            for k, out in enumerate((o0, o1, o2, o3)):
+        for whole, outs in ((att, (t0, t1, t2, t3)), (dq, (o0, o1, o2, o3))):
+            for k, out in enumerate(outs):
                 for h in range(heads):
-                    at = (heads * second + h) * width
-                    out[0, rows, at : at + width] = whole[k * cols + h * half : k * cols + (h + 1) * half]
+                    at = k * cols + h * half
+                    out[0, rows, h * width : (h + 1) * width] = whole[at : at + half]
         return 0
 
     lax.fori_loop(0, 2, one_side, 0)
@@ -246,17 +246,32 @@
             out[b % NZ, rows, width:] = dacc[b, part, width:].astype(out.dtype)
 
 
-def combine_kernel(o0, o1, o2, o3, dkv, att_ref, dq_ref, dkv_ref, sq_ref):
-    wide = att_ref.shape[2]
+def combine_kernel(o0, o1, o2, o3, dkv, dq_ref, dkv_ref, sq_ref):
     parts = [o[0].astype(jnp.float32) for o in (o0, o1, o2, o3)]
-    both = (parts[0] + parts[1]) + (parts[2] + parts[3])
-    att_ref[0] = both[:, :wide].astype(att_ref.dtype)
-    dq = both[:, wide:]
+    dq = (parts[0] + parts[1]) + (parts[2] + parts[3])
     dq_ref[0] = dq
     total = functools.reduce(jnp.add, [dkv[k].astype(jnp.float32) for k in range(NZ)])
     dkv_ref[0] = total
     squares = jnp.sum(dq * dq) + jnp.sum(total * total)
     sq_ref[...] = jnp.full(sq_ref.shape, squares, jnp.float32)
+
+
+def release_kernel(order, *refs):
+    del order
+    count = len(refs) // 2
+    for a, b in zip(refs[:count], refs[count:]):
+        b[...] = a[...]
+
+
+def attended_kernel(a0, a1, a2, a3, out):
+    parts = [a[...].astype(jnp.float32) for a in (a0, a1, a2, a3)]
+    out[...] = ((parts[0] + parts[1]) + (parts[2] + parts[3])).astype(out.dtype)
+
+
+def fold_kernel(parts, out):
+    total = functools.reduce(jnp.add, [parts[k] for k in range(parts.shape[0])])
+    for k in range(out.shape[0]):
+        out[k] = total
 
 
 def scale_kernel(count, sums, dq, dkv, oq, ok, ov):
@@ -273,7 +288,8 @@
     ov[0] = (dkv[0, :, width:] * factor).astype(ov.dtype)
 
 
-def spread_kernel(keys, values, copies):
+def spread_kernel(keys, values, order, copies):
+    del order
     width = keys.shape[2]
     for k in range(copies.shape[0]):
         copies[k, :, :width] = keys[0]
@@ -301,12 +317,30 @@
     z, y, c = (lax.axis_index(a) for a in ("z", "y", "core"))
     info = visits(doc_starts[0], tok, z, y, c)
 
-    copies = pl.pallas_call(spread_kernel, out_shape=jax.ShapeDtypeStruct((NZ, tok, 2 * width), keys.dtype), in_specs=[VMEM] * 2, out_specs=VMEM, compiler_params=PARAMS)(keys, values)
+    block = jax.ShapeDtypeStruct((1, tok, 2 * wide), keys.dtype)
+    far = pl.pallas_call(
+        join_kernel,
+        out_shape=[block],
+        in_specs=[VMEM] * 2,
+        out_specs=[VMEM],
+        compiler_params=PARAMS,
+    )(queries, grad_out)
+    copies = pl.pallas_call(
+        spread_kernel,
+        out_shape=jax.ShapeDtypeStruct((NZ, tok, 2 * width), keys.dtype),
+        in_specs=[VMEM] * 3,
+        out_specs=VMEM,
+        compiler_params=PARAMS,
+    )(keys, values, far[0])
+    asked, *near = pl.pallas_call(
+        join_kernel,
+        out_shape=[block] * (NY - 1),
+        in_specs=[VMEM] * 2,
+        out_specs=[VMEM] * (NY - 1),
+        compiler_params=PARAMS,
+    )(queries, grad_out)
     mine = lax.all_to_all(copies, "z", 0, 0, tiled=True)
-    asked, *ask = pl.pallas_call(join_kernel, out_shape=[jax.ShapeDtypeStruct((1, tok, 2 * wide), keys.dtype)] * NY, in_specs=[VMEM] * 2, out_specs=[VMEM] * NY, compiler_params=PARAMS)(queries, grad_out)
-    mine = lax.all_to_all(copies, "z", 0, 0, tiled=True)
-    around = {k: turn(ask[k - 1], "y", NY, -k) for k in (2, 1, 3)}
-    around[0] = asked
+    around = {0: asked, 1: turn(near[0], "y", NY, -1), 2: turn(far[0], "y", NY, -2), 3: turn(near[1], "y", NY, -3)}
     other = turn(mine, "core", NC, 1)
 
     f32, bf16 = jnp.float32, jnp.bfloat16
@@ -332,10 +366,10 @@
     stats = lax.all_to_all(stats, "y", 0, 0, tiled=True)
     *sent, dmine, dother = pl.pallas_call(
         functools.partial(backward_kernel, heads),
-        out_shape=[shape(asked.shape, bf16)] * NY
+        out_shape=[shape(queries.shape, bf16)] * (2 * NY)
         + [shape(mine.shape, f32), shape(mine.shape, bf16)],
         in_specs=[SMEM] + [VMEM] * (NY + 4),
-        out_specs=[VMEM] * (NY + 2),
+        out_specs=[VMEM] * (2 * NY + 2),
         scratch_shapes=[
             pltpu.VMEM((2 * NZ, tok, 2 * width), f32),
             pltpu.VMEM((width, NY * cols), f32),
@@ -343,26 +377,48 @@
         ],
         compiler_params=PARAMS,
     )(info, *asks, u, pairs, turned, stats)
+    seen, sent = sent[:NY], sent[NY:]
     back = [sent[0]] + [turn(sent[k], "y", NY, k) for k in range(1, NY)]
     from_core = turn(dother, "core", NC, 1)
     pair = (dmine + from_core.astype(f32)).astype(bf16)
     pieces = lax.all_to_all(pair, "z", 0, 0, tiled=True)
-    attended, dq, dkv, squares = pl.pallas_call(
+    dq, dkv, squares = pl.pallas_call(
         combine_kernel,
-        out_shape=(
-            shape(queries.shape, bf16),
+        out_shape=[
             shape(queries.shape, f32),
             shape((1, tok, 2 * width), f32),
             shape((NZ * NC, 1, 128), f32),
-        ),
-        in_specs=[VMEM] * 5,
-        out_specs=(VMEM,) * 4,
+        ],
+        in_specs=[VMEM] * (NY + 1),
+        out_specs=[VMEM] * 3,
         compiler_params=PARAMS,
     )(*back, pieces)
+    released = pl.pallas_call(
+        release_kernel,
+        out_shape=[shape(queries.shape, bf16)] * (NY - 1),
+        in_specs=[VMEM] * NY,
+        out_specs=[VMEM] * (NY - 1),
+        compiler_params=PARAMS,
+    )(squares, *seen[1:])
     squares = lax.all_to_all(squares, ("z", "core"), 0, 0, tiled=True)
+    home = [seen[0]] + [turn(released[k - 1], "y", NY, k) for k in range(1, NY)]
     ndata = lax.axis_size("dp")
-    squares = jnp.broadcast_to(jnp.sum(squares, axis=0, keepdims=True), (NY * ndata, 1, 128))
+    squares = pl.pallas_call(
+        fold_kernel,
+        out_shape=shape((NY * ndata, 1, 128), f32),
+        in_specs=[VMEM],
+        out_specs=VMEM,
+        compiler_params=PARAMS,
+        cost_estimate=pl.CostEstimate(flops=10**9, transcendentals=0, bytes_accessed=0),
+    )(squares)
     squares = lax.all_to_all(squares, ("y", "dp"), 0, 0, tiled=True)
+    attended = pl.pallas_call(
+        attended_kernel,
+        out_shape=shape(queries.shape, bf16),
+        in_specs=[VMEM] * NY,
+        out_specs=VMEM,
+        compiler_params=PARAMS,
+    )(*home)
     count = float(ndata * NZ * NY * NC * tok * (wide + 2 * width))
     out_query, out_key, out_value = pl.pallas_call(
         functools.partial(scale_kernel, count),

time: 146 us -> 135 us (0.925)
  blocking collectives: 41.1 us -> 27 us
  waiting for transfers between devices: 34.9 us -> 23.9 us
  starting transfers between devices: 55.3 us -> 65.6 us
  Pallas kernels: 8.73 us -> 11.8 us
    ppermute x8 -> x11, waiting for transfers between devices: 32.3 us -> 14.7 us  [turn(): return lax.ppermute(x, axis, [(i, (i + by) % size) for i in range(size)])]
    all_to_all x1 -> x0, blocking collectives: 14.2 us -> none  [per_device(): squares = lax.all_to_all(squares, ('z', 'core'), 0, 0, tiled=True)]
    all_to_all x0 -> x1, starting transfers between devices: none -> 7.53 us  [per_device(): squares = lax.all_to_all(squares, ('z', 'core'), 0, 0, tiled=True)]
    all_to_all x1, waiting for transfers between devices: 2.59 us -> 9.15 us  [per_device(): mine = lax.all_to_all(copies, 'z', 0, 0, tiled=True)]
    ppermute x8 -> x11, starting transfers between devices: 36.5 us -> 42.1 us  [turn(): return lax.ppermute(x, axis, [(i, (i + by) % size) for i in range(size)])]
    all_to_all x1, blocking collectives: 14.3 us -> 17.5 us  [per_device(): squares = lax.all_to_all(squares, ('y', 'dp'), 0, 0, tiled=True)]
    all_to_all x1, blocking collectives: 12.6 us -> 9.5 us  [per_device(): stats = lax.all_to_all(stats, 'y', 0, 0, tiled=True)]
    all_to_all x1, starting transfers between devices: 7.84 us -> 5.8 us  [per_device(): pieces = lax.all_to_all(pair, 'z', 0, 0, tiled=True)]
  transfers between devices with their start and end apart: 10 -> 14, of which waited for: 7 -> 6; matrix products, arithmetic and copies ran while one was open for 1% -> 1% of each run, Pallas kernels for 0% -> 2%
where the time goes in v6:
time: 135 us; the launch traced here: 134 us
  starting transfers between devices  65.6 us (49%)
  blocking collectives  27 us (20%)
  waiting for transfers between devices  23.9 us (18%)
  Pallas kernels  11.8 us (9%)
  local copies, waits for them, and re-layouts  3.31 us (2%)
  other arithmetic  1.57 us (1%)
    ppermute x11, starting transfers between devices, turn(): return lax.ppermute(x, axis, [(i, (i + by) % size) for i in range(size)])  42.1 us
    all_to_all x1, blocking collectives, per_device(): squares = lax.all_to_all(squares, ('y', 'dp'), 0, 0, tiled=True)  17.5 us
    ppermute x11, waiting for transfers between devices, turn(): return lax.ppermute(x, axis, [(i, (i + by) % size) for i in range(size)])  14.7 us
    all_to_all x1, starting transfers between devices, per_device(): mine = lax.all_to_all(copies, 'z', 0, 0, tiled=True)  10.2 us
    all_to_all x1, blocking collectives, per_device(): stats = lax.all_to_all(stats, 'y', 0, 0, tiled=True)  9.5 us
    all_to_all x1, waiting for transfers between devices, per_device(): mine = lax.all_to_all(copies, 'z', 0, 0, tiled=True)  9.15 us
    all_to_all x1, starting transfers between devices, per_device(): squares = lax.all_to_all(squares, ('z', 'core'), 0, 0, tiled=True)  7.53 us
    all_to_all x1, starting transfers between devices, per_device(): pieces = lax.all_to_all(pair, 'z', 0, 0, tiled=True)  5.8 us
  transfers between devices with their start and end apart: 14, of which 6 were waited for; matrix products, arithmetic and copies ran while one was open for 1% of the time, Pallas kernels for 2%

profile of v6, /device:TPU:1, one launch (start us, length us, event | category | flops | bytes accessed | tf_op | source)
XLA Modules:
  0.0 134.0 jit_solution(13754919496771496241)
XLA Ops:
  0.6 0.0 copy-start
  0.6 0.9 copy-done
  1.5 0.0 copy-start.2
  1.5 0.9 copy-done.2
  2.5 8.3 %collective-permute-start.1 = (bf16[1,128,1024]{2,1,0:T(8,128)(2,1)S(1)}, bf16[1,128,1024]{2,1,0:T(8,128)(2,1)S(1)}, u32[]{:S(2)}, u32[]{:S(2)}) collective-permute-start(bf16[1,128,1024]{2,1,0:T(8,128)(2,1)S(1)} %shard_map.85.order), channel_id=1, source_target_pairs={{0,32},{16,48},{32,0},{48,16},{1,33},{17,49},{33,1},{49,17},{2,34}... | collective-permute-start | bytes 786440 | tf_op jit(solution)/shard_map/ppermute | solution.py:307
  10.8 0.0 copy-done.4
  10.8 0.0 copy-done.5
  10.8 0.9 shard_map.86
  11.7 10.2 %all-to-all-start = ((bf16[8,128,256]{2,1,0:T(8,128)(2,1)}), bf16[8,128,256]{2,1,0:T(8,128)(2,1)S(1)}, u32[]{:S(2)}, u32[]{:S(2)}) async-start(bf16[8,128,256]{2,1,0:T(8,128)(2,1)} %shard_map.86), calls=%async_computation | async-start | bytes 1048576 | tf_op jit(solution)/shard_map/all_to_all | solution.py:342
  21.8 0.0 copy-done.1
  21.8 0.0 copy-done.3
  21.8 0.1 shard_map.84
  21.9 2.0 %collective-permute-start = (bf16[1,128,1024]{2,1,0:T(8,128)(2,1)S(1)}, bf16[1,128,1024]{2,1,0:T(8,128)(2,1)S(1)}, u32[]{:S(2)}, u32[]{:S(2)}) collective-permute-start(bf16[1,128,1024]{2,1,0:T(8,128)(2,1)S(1)} %get-tuple-element.31), channel_id=1, source_target_pairs={{0,48},{16,0},{32,16},{48,32},{1,49},{17,1},{33,17},{49,33},{2,50}... | collective-permute-start | bytes 786440 | tf_op jit(solution)/shard_map/ppermute | solution.py:307
  23.9 4.2 %collective-permute-start.2 = (bf16[1,128,1024]{2,1,0:T(8,128)(2,1)S(1)}, bf16[1,128,1024]{2,1,0:T(8,128)(2,1)S(1)}, u32[]{:S(2)}, u32[]{:S(2)}) collective-permute-start(bf16[1,128,1024]{2,1,0:T(8,128)(2,1)S(1)} %get-tuple-element.32), channel_id=1, source_target_pairs={{0,16},{16,32},{32,48},{48,0},{1,17},{17,33},{33,49},{49,1},{2,18}... | collective-permute-start | bytes 786440 | tf_op jit(solution)/shard_map/ppermute | solution.py:307
  28.1 0.0 copy-start.6
  28.1 0.6 copy-done.6
  28.8 0.1 eq.26
  28.9 0.1 eq.25
  29.0 0.1 add.218
  29.1 0.1 add.215
  29.2 0.2 select_reduce_fusion
  29.3 0.1 reshape.443
  29.4 0.1 reduce_min.11
  29.6 0.1 select_reduce_fusion.1
  29.7 9.1 %all-to-all-done.mine = bf16[8,128,256]{2,1,0:T(8,128)(2,1)S(1)} async-done(((bf16[8,128,256]{2,1,0:T(8,128)(2,1)}), bf16[8,128,256]{2,1,0:T(8,128)(2,1)S(1)}, u32[]{:S(2)}, u32[]{:S(2)}) %all-to-all-start) | async-done | bytes 524320 | tf_op jit(solution)/shard_map/all_to_all | solution.py:342
  38.9 3.3 %collective-permute-start.3 = (bf16[8,128,256]{2,1,0:T(8,128)(2,1)S(1)}, bf16[8,128,256]{2,1,0:T(8,128)(2,1)S(1)}, u32[]{:S(2)}, u32[]{:S(2)}) collective-permute-start(bf16[8,128,256]{2,1,0:T(8,128)(2,1)S(1)} %all-to-all-done.mine), channel_id=1, source_target_pairs={{0,8},{8,0},{1,9},{9,1},{2,10},{10,2},{3,11},{11,3},{4,12},{12,4},... | collective-permute-start | bytes 1572872 | tf_op jit(solution)/shard_map/ppermute | solution.py:307
  42.2 0.1 copy.13
  42.3 0.1 reshape.444
  42.4 0.1 add.220
  42.5 0.1 copy.14
  42.6 0.1 reshape.445
  42.7 0.1 pad_add_fusion.2.info
  42.7 1.0 collective-permute-done.3.other
  43.7 0.3 shard_map.87
  44.1 0.0 collective-permute-done.1.a2
  44.1 0.0 collective-permute-done.a1
  44.1 0.0 collective-permute-done.2.a3
  44.1 3.0 %shard_map.88 = (f32[2,128,1024]{2,1,0:T(8,128)S(1)}, f32[4,3,8,256]{3,2,1,0:T(8,128)S(1)}) custom-call(s32[34]{0:T(128)S(1)} %pad_add_fusion.2.info, bf16[1,128,1024]{2,1,0:T(8,128)(2,1)S(1)} %get-tuple-element.30.a0, bf16[1,128,1024]{2,1,0:T(8,128)(2,1)S(1)} %collective-permute-done.a1, bf16[1,128,1024]{2,1,0:T(8,128)(2,1)S(1)} %collective-permute-done.1.a2, ...), custom_call_target="tpu_custom_call" | custom-call | tf_op jit(solution)/shard_map/pallas_call | solution.py:358
  47.1 9.5 %all_to_all.25.stats = f32[4,3,8,256]{3,2,1,0:T(8,128)S(1)} all-to-all(f32[4,3,8,256]{3,2,1,0:T(8,128)S(1)} %get-tuple-element.36), channel_id=1, replica_groups=mesh['z'=8,'y'=4,'core'=2,'dp'=8] {'y'}, dimensions={0} | all-to-all | bytes 196608 | tf_op jit(solution)/shard_map/all_to_all | solution.py:366
  56.6 4.2 %shard_map.89 = (bf16[1,128,512]{2,1,0:T(8,128)(2,1)S(1)}, bf16[1,128,512]{2,1,0:T(8,128)(2,1)S(1)}, bf16[1,128,512]{2,1,0:T(8,128)(2,1)S(1)}, bf16[1,128,512]{2...) custom-call(s32[34]{0:T(128)S(1)} %pad_add_fusion.2.info, ...), custom_call_target="tpu_custom_call" | custom-call | tf_op jit(solution)/shard_map/pallas_call | solution.py:367
  60.9 3.9 %collective-permute-start.7 = (bf16[8,128,256]{2,1,0:T(8,128)(2,1)S(1)}, bf16[8,128,256]{2,1,0:T(8,128)(2,1)S(1)}, u32[]{:S(2)}, u32[]{:S(2)}) collective-permute-start(bf16[8,128,256]{2,1,0:T(8,128)(2,1)S(1)} %get-tuple-element.43), channel_id=1, source_target_pairs={{0,8},{8,0},{1,9},{9,1},{2,10},{10,2},{3,11},{11,3},{4,12},{12,4},... | collective-permute-start | bytes 1572872 | tf_op jit(solution)/shard_map/ppermute | solution.py:307
  64.8 1.5 %collective-permute-done.7 = bf16[8,128,256]{2,1,0:T(8,128)(2,1)S(1)} collective-permute-done((bf16[8,128,256]{2,1,0:T(8,128)(2,1)S(1)}, bf16[8,128,256]{2,1,0:T(8,128)(2,1)S(1)}, u32[]{:S(2)}, u32[]{:S(2)}) %collective-permute-start.7) | collective-permute-done | bytes 524320 | tf_op jit(solution)/shard_map/ppermute | solution.py:307
  66.3 1.0 add_convert_fusion
  67.2 5.8 %all-to-all-start.2 = ((bf16[8,128,256]{2,1,0:T(8,128)(2,1)}), bf16[8,128,256]{2,1,0:T(8,128)(2,1)S(1)}, u32[]{:S(2)}, u32[]{:S(2)}) async-start(bf16[8,128,256]{2,1,0:T(8,128)(2,1)} %add_convert_fusion), calls=%async_computation.2 | async-start | bytes 1048576 | tf_op jit(solution)/shard_map/all_to_all | solution.py:384
  73.0 2.8 %collective-permute-start.4 = (bf16[1,128,512]{2,1,0:T(8,128)(2,1)S(1)}, bf16[1,128,512]{2,1,0:T(8,128)(2,1)S(1)}, u32[]{:S(2)}, u32[]{:S(2)}) collective-permute-start(bf16[1,128,512]{2,1,0:T(8,128)(2,1)S(1)} %get-tuple-element.39), channel_id=1, source_target_pairs={{0,16},{16,32},{32,48},{48,0},{1,17},{17,33},{33,49},{49,1},{2,18}... | collective-permute-start | bytes 393224 | tf_op jit(solution)/shard_map/ppermute | solution.py:307
  75.9 4.9 %collective-permute-start.5 = (bf16[1,128,512]{2,1,0:T(8,128)(2,1)S(1)}, bf16[1,128,512]{2,1,0:T(8,128)(2,1)S(1)}, u32[]{:S(2)}, u32[]{:S(2)}) collective-permute-start(bf16[1,128,512]{2,1,0:T(8,128)(2,1)S(1)} %get-tuple-element.40), channel_id=1, source_target_pairs={{0,32},{16,48},{32,0},{48,16},{1,33},{17,49},{33,1},{49,17},{2,34}... | collective-permute-start | bytes 393224 | tf_op jit(solution)/shard_map/ppermute | solution.py:307
  80.8 2.7 %collective-permute-start.6 = (bf16[1,128,512]{2,1,0:T(8,128)(2,1)S(1)}, bf16[1,128,512]{2,1,0:T(8,128)(2,1)S(1)}, u32[]{:S(2)}, u32[]{:S(2)}) collective-permute-start(bf16[1,128,512]{2,1,0:T(8,128)(2,1)S(1)} %get-tuple-element.41), channel_id=1, source_target_pairs={{0,48},{16,0},{32,16},{48,32},{1,49},{17,1},{33,17},{49,33},{2,50}... | collective-permute-start | bytes 393224 | tf_op jit(solution)/shard_map/ppermute | solution.py:307
  83.5 0.4 collective-permute-done.4.o1
  83.9 4.3 %collective-permute-done.5.o2 = bf16[1,128,512]{2,1,0:T(8,128)(2,1)S(1)} collective-permute-done((bf16[1,128,512]{2,1,0:T(8,128)(2,1)S(1)}, bf16[1,128,512]{2,1,0:T(8,128)(2,1)S(1)}, u32[]{:S(2)}, u32[]{:S(2)}) %collective-permute-start.5) | collective-permute-done | bytes 131104 | tf_op jit(solution)/shard_map/ppermute | solution.py:307
  88.1 7.6 %collective-permute-done.6.o3 = bf16[1,128,512]{2,1,0:T(8,128)(2,1)S(1)} collective-permute-done((bf16[1,128,512]{2,1,0:T(8,128)(2,1)S(1)}, bf16[1,128,512]{2,1,0:T(8,128)(2,1)S(1)}, u32[]{:S(2)}, u32[]{:S(2)}) %collective-permute-start.6) | collective-permute-done | bytes 131104 | tf_op jit(solution)/shard_map/ppermute | solution.py:307
  95.7 0.0 all-to-all-done.2.dkv
  95.7 1.0 shard_map.90
  96.7 7.5 %all-to-all-start.3 = ((f32[16,1,128]{2,1,0:T(1,128)}), f32[16,1,128]{2,1,0:T(1,128)S(1)}, u32[]{:S(2)}, u32[]{:S(2)}) async-start(f32[16,1,128]{2,1,0:T(1,128)} %get-tuple-element.44.order), calls=%async_computation.3 | async-start | bytes 16384 | tf_op jit(solution)/shard_map/all_to_all | solution.py:403
  104.2 0.8 shard_map.91
  105.0 2.2 %collective-permute-start.8 = (bf16[1,128,512]{2,1,0:T(8,128)(2,1)S(1)}, bf16[1,128,512]{2,1,0:T(8,128)(2,1)S(1)}, u32[]{:S(2)}, u32[]{:S(2)}) collective-permute-start(bf16[1,128,512]{2,1,0:T(8,128)(2,1)S(1)} %get-tuple-element.48), channel_id=1, source_target_pairs={{0,16},{16,32},{32,48},{48,0},{1,17},{17,33},{33,49},{49,1},{2,18}... | collective-permute-start | bytes 393224 | tf_op jit(solution)/shard_map/ppermute | solution.py:307
  107.2 4.4 %collective-permute-start.9 = (bf16[1,128,512]{2,1,0:T(8,128)(2,1)S(1)}, bf16[1,128,512]{2,1,0:T(8,128)(2,1)S(1)}, u32[]{:S(2)}, u32[]{:S(2)}) collective-permute-start(bf16[1,128,512]{2,1,0:T(8,128)(2,1)S(1)} %get-tuple-element.49), channel_id=1, source_target_pairs={{0,32},{16,48},{32,0},{48,16},{1,33},{17,49},{33,1},{49,17},{2,34}... | collective-permute-start | bytes 393224 | tf_op jit(solution)/shard_map/ppermute | solution.py:307
  111.6 3.4 %collective-permute-start.10 = (bf16[1,128,512]{2,1,0:T(8,128)(2,1)S(1)}, bf16[1,128,512]{2,1,0:T(8,128)(2,1)S(1)}, u32[]{:S(2)}, u32[]{:S(2)}) collective-permute-start(bf16[1,128,512]{2,1,0:T(8,128)(2,1)S(1)} %get-tuple-element.50), channel_id=1, source_target_pairs={{0,48},{16,0},{32,16},{48,32},{1,49},{17,1},{33,17},{49,33},{2,50}... | collective-permute-start | bytes 393224 | tf_op jit(solution)/shard_map/ppermute | solution.py:307
  115.0 0.0 all-to-all-done.3.parts
  115.1 17.5 %all_to_all.26.sums = f32[32,1,128]{2,1,0:T(1,128)S(1)} all-to-all(f32[32,1,128]{2,1,0:T(1,128)S(1)} %shard_map.93), channel_id=1, replica_groups=mesh['z'=8,'y'=4,'core'=2,'dp'=8] {'y','dp'}, dimensions={0} | all-to-all | bytes 32768 | tf_op jit(solution)/shard_map/all_to_all | solution.py:414
  132.6 0.7 shard_map.94
  133.3 0.0 collective-permute-done.8.a1
  133.3 0.0 collective-permute-done.9.a2
  133.3 0.0 collective-permute-done.10.a3
  133.3 0.7 shard_map.92
  (16 shorter events, 0.2 us)
Async XLA Ops:
  0.6 0.9 copy-start
  1.5 0.9 copy-start.2
  2.4 8.3 %copy-start.4 = (bf16[1,128,128]{2,1,0:T(8,128)(2,1)S(1)}, bf16[1,128,128]{2,1,0:T(8,128)(2,1)}, u32[]{:S(2)}) copy-start(bf16[1,128,128]{2,1,0:T(8,128)(2,1)} %keys.1) | copy-start | bytes 98308
  2.4 8.3 %copy-start.5 = (bf16[1,128,128]{2,1,0:T(8,128)(2,1)S(1)}, bf16[1,128,128]{2,1,0:T(8,128)(2,1)}, u32[]{:S(2)}) copy-start(bf16[1,128,128]{2,1,0:T(8,128)(2,1)} %values.1) | copy-start | bytes 98308
  2.5 41.6 %collective-permute-start.1 = (bf16[1,128,1024]{2,1,0:T(8,128)(2,1)S(1)}, bf16[1,128,1024]{2,1,0:T(8,128)(2,1)S(1)}, u32[]{:S(2)}, u32[]{:S(2)}) collective-permute-start(bf16[1,128,1024]{2,1,0:T(8,128)(2,1)S(1)} %shard_map.85.order), channel_id=1, source_target_pairs={{0,32},{16,48},{32,0},{48,16},{1,33},{17,49},{33,1},{49,17},{2,34}... | collective-permute-start | bytes 786440 | tf_op jit(solution)/shard_map/ppermute | solution.py:307
  11.7 10.2 %copy-start.1 = (bf16[1,128,512]{2,1,0:T(8,128)(2,1)S(1)}, bf16[1,128,512]{2,1,0:T(8,128)(2,1)}, u32[]{:S(2)}) copy-start(bf16[1,128,512]{2,1,0:T(8,128)(2,1)} %left.3) | copy-start | bytes 393220
  11.7 10.2 %copy-start.3 = (bf16[1,128,512]{2,1,0:T(8,128)(2,1)S(1)}, bf16[1,128,512]{2,1,0:T(8,128)(2,1)}, u32[]{:S(2)}) copy-start(bf16[1,128,512]{2,1,0:T(8,128)(2,1)} %right.3) | copy-start | bytes 393220
  11.7 27.2 %all-to-all-start = ((bf16[8,128,256]{2,1,0:T(8,128)(2,1)}), bf16[8,128,256]{2,1,0:T(8,128)(2,1)S(1)}, u32[]{:S(2)}, u32[]{:S(2)}) async-start(bf16[8,128,256]{2,1,0:T(8,128)(2,1)} %shard_map.86), calls=%async_computation | async-start | bytes 1048576 | tf_op jit(solution)/shard_map/all_to_all | solution.py:342
  21.9 22.2 %collective-permute-start = (bf16[1,128,1024]{2,1,0:T(8,128)(2,1)S(1)}, bf16[1,128,1024]{2,1,0:T(8,128)(2,1)S(1)}, u32[]{:S(2)}, u32[]{:S(2)}) collective-permute-start(bf16[1,128,1024]{2,1,0:T(8,128)(2,1)S(1)} %get-tuple-element.31), channel_id=1, source_target_pairs={{0,48},{16,0},{32,16},{48,32},{1,49},{17,1},{33,17},{49,33},{2,50}... | collective-permute-start | bytes 786440 | tf_op jit(solution)/shard_map/ppermute | solution.py:307
  23.9 20.2 %collective-permute-start.2 = (bf16[1,128,1024]{2,1,0:T(8,128)(2,1)S(1)}, bf16[1,128,1024]{2,1,0:T(8,128)(2,1)S(1)}, u32[]{:S(2)}, u32[]{:S(2)}) collective-permute-start(bf16[1,128,1024]{2,1,0:T(8,128)(2,1)S(1)} %get-tuple-element.32), channel_id=1, source_target_pairs={{0,16},{16,32},{32,48},{48,0},{1,17},{17,33},{33,49},{49,1},{2,18}... | collective-permute-start | bytes 786440 | tf_op jit(solution)/shard_map/ppermute | solution.py:307
  28.1 0.7 copy-start.6
  38.9 4.8 %collective-permute-start.3 = (bf16[8,128,256]{2,1,0:T(8,128)(2,1)S(1)}, bf16[8,128,256]{2,1,0:T(8,128)(2,1)S(1)}, u32[]{:S(2)}, u32[]{:S(2)}) collective-permute-start(bf16[8,128,256]{2,1,0:T(8,128)(2,1)S(1)} %all-to-all-done.mine), channel_id=1, source_target_pairs={{0,8},{8,0},{1,9},{9,1},{2,10},{10,2},{3,11},{11,3},{4,12},{12,4},... | collective-permute-start | bytes 1572872 | tf_op jit(solution)/shard_map/ppermute | solution.py:307
  60.9 5.4 %collective-permute-start.7 = (bf16[8,128,256]{2,1,0:T(8,128)(2,1)S(1)}, bf16[8,128,256]{2,1,0:T(8,128)(2,1)S(1)}, u32[]{:S(2)}, u32[]{:S(2)}) collective-permute-start(bf16[8,128,256]{2,1,0:T(8,128)(2,1)S(1)} %get-tuple-element.43), channel_id=1, source_target_pairs={{0,8},{8,0},{1,9},{9,1},{2,10},{10,2},{3,11},{11,3},{4,12},{12,4},... | collective-permute-start | bytes 1572872 | tf_op jit(solution)/shard_map/ppermute | solution.py:307
  67.2 28.5 %all-to-all-start.2 = ((bf16[8,128,256]{2,1,0:T(8,128)(2,1)}), bf16[8,128,256]{2,1,0:T(8,128)(2,1)S(1)}, u32[]{:S(2)}, u32[]{:S(2)}) async-start(bf16[8,128,256]{2,1,0:T(8,128)(2,1)} %add_convert_fusion), calls=%async_computation.2 | async-start | bytes 1048576 | tf_op jit(solution)/shard_map/all_to_all | solution.py:384
  73.0 10.8 %collective-permute-start.4 = (bf16[1,128,512]{2,1,0:T(8,128)(2,1)S(1)}, bf16[1,128,512]{2,1,0:T(8,128)(2,1)S(1)}, u32[]{:S(2)}, u32[]{:S(2)}) collective-permute-start(bf16[1,128,512]{2,1,0:T(8,128)(2,1)S(1)} %get-tuple-element.39), channel_id=1, source_target_pairs={{0,16},{16,32},{32,48},{48,0},{1,17},{17,33},{33,49},{49,1},{2,18}... | collective-permute-start | bytes 393224 | tf_op jit(solution)/shard_map/ppermute | solution.py:307
  75.9 12.3 %collective-permute-start.5 = (bf16[1,128,512]{2,1,0:T(8,128)(2,1)S(1)}, bf16[1,128,512]{2,1,0:T(8,128)(2,1)S(1)}, u32[]{:S(2)}, u32[]{:S(2)}) collective-permute-start(bf16[1,128,512]{2,1,0:T(8,128)(2,1)S(1)} %get-tuple-element.40), channel_id=1, source_target_pairs={{0,32},{16,48},{32,0},{48,16},{1,33},{17,49},{33,1},{49,17},{2,34}... | collective-permute-start | bytes 393224 | tf_op jit(solution)/shard_map/ppermute | solution.py:307
  80.8 14.9 %collective-permute-start.6 = (bf16[1,128,512]{2,1,0:T(8,128)(2,1)S(1)}, bf16[1,128,512]{2,1,0:T(8,128)(2,1)S(1)}, u32[]{:S(2)}, u32[]{:S(2)}) collective-permute-start(bf16[1,128,512]{2,1,0:T(8,128)(2,1)S(1)} %get-tuple-element.41), channel_id=1, source_target_pairs={{0,48},{16,0},{32,16},{48,32},{1,49},{17,1},{33,17},{49,33},{2,50}... | collective-permute-start | bytes 393224 | tf_op jit(solution)/shard_map/ppermute | solution.py:307
  96.7 18.4 %all-to-all-start.3 = ((f32[16,1,128]{2,1,0:T(1,128)}), f32[16,1,128]{2,1,0:T(1,128)S(1)}, u32[]{:S(2)}, u32[]{:S(2)}) async-start(f32[16,1,128]{2,1,0:T(1,128)} %get-tuple-element.44.order), calls=%async_computation.3 | async-start | bytes 16384 | tf_op jit(solution)/shard_map/all_to_all | solution.py:403
  105.0 28.3 %collective-permute-start.8 = (bf16[1,128,512]{2,1,0:T(8,128)(2,1)S(1)}, bf16[1,128,512]{2,1,0:T(8,128)(2,1)S(1)}, u32[]{:S(2)}, u32[]{:S(2)}) collective-permute-start(bf16[1,128,512]{2,1,0:T(8,128)(2,1)S(1)} %get-tuple-element.48), channel_id=1, source_target_pairs={{0,16},{16,32},{32,48},{48,0},{1,17},{17,33},{33,49},{49,1},{2,18}... | collective-permute-start | bytes 393224 | tf_op jit(solution)/shard_map/ppermute | solution.py:307
  107.2 26.1 %collective-permute-start.9 = (bf16[1,128,512]{2,1,0:T(8,128)(2,1)S(1)}, bf16[1,128,512]{2,1,0:T(8,128)(2,1)S(1)}, u32[]{:S(2)}, u32[]{:S(2)}) collective-permute-start(bf16[1,128,512]{2,1,0:T(8,128)(2,1)S(1)} %get-tuple-element.49), channel_id=1, source_target_pairs={{0,32},{16,48},{32,0},{48,16},{1,33},{17,49},{33,1},{49,17},{2,34}... | collective-permute-start | bytes 393224 | tf_op jit(solution)/shard_map/ppermute | solution.py:307
  111.6 21.7 %collective-permute-start.10 = (bf16[1,128,512]{2,1,0:T(8,128)(2,1)S(1)}, bf16[1,128,512]{2,1,0:T(8,128)(2,1)S(1)}, u32[]{:S(2)}, u32[]{:S(2)}) collective-permute-start(bf16[1,128,512]{2,1,0:T(8,128)(2,1)S(1)} %get-tuple-element.50), channel_id=1, source_target_pairs={{0,48},{16,0},{32,16},{48,32},{1,49},{17,1},{33,17},{49,33},{2,50}... | collective-permute-start | bytes 393224 | tf_op jit(solution)/shard_map/ppermute | solution.py:307

commit v7 on v6

--- a/solution.py
+++ b/solution.py
@@ -13,7 +13,9 @@
 NZ, NY, NC = 8, 4, 2
 FIELDS = 4
 VMEM = pl.BlockSpec(memory_space=pltpu.VMEM)
+FAR = pl.BlockSpec(memory_space=pl.ANY)
 SMEM = pl.BlockSpec(memory_space=pltpu.SMEM)
+ALONE = pltpu.CompilerParams(vmem_limit_bytes=62 * 1024 * 1024)
 PARAMS = pltpu.CompilerParams(vmem_limit_bytes=40 * 1024 * 1024)
 
 
@@ -23,7 +25,9 @@
 
 FIELDS = 4
 VMEM = pl.BlockSpec(memory_space=pltpu.VMEM)
+FAR = pl.BlockSpec(memory_space=pl.ANY)
 SMEM = pl.BlockSpec(memory_space=pltpu.SMEM)
+ALONE = pltpu.CompilerParams(vmem_limit_bytes=62 * 1024 * 1024)
 PARAMS = pltpu.CompilerParams(vmem_limit_bytes=40 * 1024 * 1024)
 
 
@@ -256,13 +260,6 @@
     sq_ref[...] = jnp.full(sq_ref.shape, squares, jnp.float32)
 
 
-def release_kernel(order, *refs):
-    del order
-    count = len(refs) // 2
-    for a, b in zip(refs[:count], refs[count:]):
-        b[...] = a[...]
-
-
 def attended_kernel(a0, a1, a2, a3, out):
     parts = [a[...].astype(jnp.float32) for a in (a0, a1, a2, a3)]
     out[...] = ((parts[0] + parts[1]) + (parts[2] + parts[3])).astype(out.dtype)
@@ -288,19 +285,28 @@
     ov[0] = (dkv[0, :, width:] * factor).astype(ov.dtype)
 
 
-def spread_kernel(keys, values, order, copies):
+def run_copies(pairs, sems):
+    copies = [pltpu.make_async_copy(a, b, sems.at[n]) for n, (a, b) in enumerate(pairs)]
+    for copy in copies:
+        copy.start()
+    for copy in copies:
+        copy.wait()
+
+
+def spread_kernel(keys, values, order, copies, sems):
     del order
     width = keys.shape[2]
-    for k in range(copies.shape[0]):
-        copies[k, :, :width] = keys[0]
-        copies[k, :, width:] = values[0]
-
-
-def join_kernel(left, right, *outs):
+    sides = ((keys, slice(0, width)), (values, slice(width, 2 * width)))
+    run_copies(
+        [(x.at[0], copies.at[k, :, at]) for k in range(copies.shape[0]) for x, at in sides], sems
+    )
+
+
+def join_kernel(left, right, *refs):
+    *outs, sems = refs
     wide = left.shape[2]
-    for out in outs:
-        out[:, :, :wide] = left[...]
-        out[:, :, wide:] = right[...]
+    sides = ((left, slice(0, wide)), (right, slice(wide, 2 * wide)))
+    run_copies([(x, out.at[:, :, at]) for out in outs for x, at in sides], sems)
 
 
 def turn(x, axis, size, by):
@@ -321,23 +327,26 @@
     far = pl.pallas_call(
         join_kernel,
         out_shape=[block],
-        in_specs=[VMEM] * 2,
+        in_specs=[FAR] * 2,
         out_specs=[VMEM],
-        compiler_params=PARAMS,
+        scratch_shapes=[pltpu.SemaphoreType.DMA((2,))],
+        compiler_params=ALONE,
     )(queries, grad_out)
     copies = pl.pallas_call(
         spread_kernel,
         out_shape=jax.ShapeDtypeStruct((NZ, tok, 2 * width), keys.dtype),
-        in_specs=[VMEM] * 3,
+        in_specs=[FAR] * 3,
         out_specs=VMEM,
-        compiler_params=PARAMS,
+        scratch_shapes=[pltpu.SemaphoreType.DMA((2 * NZ,))],
+        compiler_params=ALONE,
     )(keys, values, far[0])
     asked, *near = pl.pallas_call(
         join_kernel,
         out_shape=[block] * (NY - 1),
-        in_specs=[VMEM] * 2,
+        in_specs=[FAR] * 2,
         out_specs=[VMEM] * (NY - 1),
-        compiler_params=PARAMS,
+        scratch_shapes=[pltpu.SemaphoreType.DMA((2 * (NY - 1),))],
+        compiler_params=ALONE,
     )(queries, grad_out)
     mine = lax.all_to_all(copies, "z", 0, 0, tiled=True)
     around = {0: asked, 1: turn(near[0], "y", NY, -1), 2: turn(far[0], "y", NY, -2), 3: turn(near[1], "y", NY, -3)}
@@ -393,15 +402,8 @@
         out_specs=[VMEM] * 3,
         compiler_params=PARAMS,
     )(*back, pieces)
-    released = pl.pallas_call(
-        release_kernel,
-        out_shape=[shape(queries.shape, bf16)] * (NY - 1),
-        in_specs=[VMEM] * NY,
-        out_specs=[VMEM] * (NY - 1),
-        compiler_params=PARAMS,
-    )(squares, *seen[1:])
     squares = lax.all_to_all(squares, ("z", "core"), 0, 0, tiled=True)
-    home = [seen[0]] + [turn(released[k - 1], "y", NY, k) for k in range(1, NY)]
+    home = [seen[0]] + [turn(seen[k], "y", NY, k) for k in range(1, NY)]
     ndata = lax.axis_size("dp")
     squares = pl.pallas_call(
         fold_kernel,
@@ -409,7 +411,6 @@
         in_specs=[VMEM],
         out_specs=VMEM,
         compiler_params=PARAMS,
-        cost_estimate=pl.CostEstimate(flops=10**9, transcendentals=0, bytes_accessed=0),
     )(squares)
     squares = lax.all_to_all(squares, ("y", "dp"), 0, 0, tiled=True)
     attended = pl.pallas_call(

time: 135 us -> 137 us (1.015)
  starting transfers between devices: 65.6 us -> 72.8 us
  waiting for transfers between devices: 23.9 us -> 17.3 us
  Pallas kernels: 11.8 us -> 16.1 us
  local copies, waits for them, and re-layouts: 3.31 us -> 1.5 us
    ppermute x11, waiting for transfers between devices: 14.7 us -> 2.5 us  [turn(): return lax.ppermute(x, axis, [(i, (i + by) % size) for i in range(size)])]
    all_to_all x1, waiting for transfers between devices: 0.01 us -> 7.75 us  [per_device(): squares = lax.all_to_all(squares, ('y', 'dp'), 0, 0, tiled=True)]
    ppermute x11, starting transfers between devices: 42.1 us -> 45.9 us  [turn(): return lax.ppermute(x, axis, [(i, (i + by) % size) for i in range(size)])]
    pallas_call x3 -> x2, Pallas kernels: 0.83 us -> 3.89 us  [the longest x1 2.21 us: per_device(): pl.pallas_call(join_kernel, out_shape=[block] * (NY - 1), in_specs=[FAR]...]
    all_to_all x1, starting transfers between devices: 5.8 us -> 8.81 us  [per_device(): pieces = lax.all_to_all(pair, 'z', 0, 0, tiled=True)]
    all_to_all x1, waiting for transfers between devices: 9.15 us -> 7.01 us  [per_device(): mine = lax.all_to_all(copies, 'z', 0, 0, tiled=True)]
    unnamed x14 -> x4, local copies, waits for them, and re-layouts: 2.47 us -> 0.65 us
  transfers between devices with their start and end apart: 14 -> 14, of which waited for: 6 -> 4; matrix products, arithmetic and copies ran while one was open for 1% -> 1% of each run, Pallas kernels for 2% -> 5%
where the time goes in v7:
time: 137 us; the launch traced here: 136 us
  starting transfers between devices  72.8 us (53%)
  blocking collectives  25.8 us (19%)
  waiting for transfers between devices  17.3 us (13%)
  Pallas kernels  16.1 us (12%)
  other arithmetic  1.54 us (1%)
  local copies, waits for them, and re-layouts  1.5 us (1%)
    ppermute x11, starting transfers between devices, turn(): return lax.ppermute(x, axis, [(i, (i + by) % size) for i in range(size)])  45.9 us
    all_to_all x1, blocking collectives, per_device(): squares = lax.all_to_all(squares, ('z', 'core'), 0, 0, tiled=True)  16.4 us
    all_to_all x1, starting transfers between devices, per_device(): mine = lax.all_to_all(copies, 'z', 0, 0, tiled=True)  10 us
    all_to_all x1, blocking collectives, per_device(): stats = lax.all_to_all(stats, 'y', 0, 0, tiled=True)  9.45 us
    all_to_all x1, starting transfers between devices, per_device(): pieces = lax.all_to_all(pair, 'z', 0, 0, tiled=True)  8.81 us
    all_to_all x1, starting transfers between devices, per_device(): squares = lax.all_to_all(squares, ('y', 'dp'), 0, 0, tiled=True)  8.02 us
    all_to_all x1, waiting for transfers between devices, per_device(): squares = lax.all_to_all(squares, ('y', 'dp'), 0, 0, tiled=True)  7.75 us
    all_to_all x1, waiting for transfers between devices, per_device(): mine = lax.all_to_all(copies, 'z', 0, 0, tiled=True)  7.01 us
  transfers between devices with their start and end apart: 14, of which 4 were waited for; matrix products, arithmetic and copies ran while one was open for 1% of the time, Pallas kernels for 5%

profile of v7, /device:TPU:1, one launch (start us, length us, event | category | flops | bytes accessed | tf_op | source)
XLA Modules:
  0.0 135.9 jit_solution(16838132581383123487)
XLA Ops:
  0.6 1.7 %shard_map.85.order = bf16[1,128,1024]{2,1,0:T(8,128)(2,1)} custom-call(bf16[1,128,512]{2,1,0:T(8,128)(2,1)} %left.3, bf16[1,128,512]{2,1,0:T(8,128)(2,1)} %right.3), custom_call_target="tpu_custom_call" | custom-call | tf_op jit(solution)/shard_map/pallas_call | solution.py:327
  2.3 8.3 %collective-permute-start.1 = (bf16[1,128,1024]{2,1,0:T(8,128)(2,1)}, bf16[1,128,1024]{2,1,0:T(8,128)(2,1)S(1)}, u32[]{:S(2)}, u32[]{:S(2)}) collective-permute-start(bf16[1,128,1024]{2,1,0:T(8,128)(2,1)} %shard_map.85.order), channel_id=1, source_target_pairs={{0,32},{16,48},{32,0},{48,16},{1,33},{17,49},{33,1},{49,17},{2,34}... | collective-permute-start | bytes 786440 | tf_op jit(solution)/shard_map/ppermute | solution.py:313
  10.6 2.2 %shard_map.86 = bf16[8,128,256]{2,1,0:T(8,128)(2,1)} custom-call(bf16[1,128,128]{2,1,0:T(8,128)(2,1)} %keys.1, bf16[1,128,128]{2,1,0:T(8,128)(2,1)} %values.1, bf16[1,128,1024]{2,1,0:T(8,128)(2,1)} %shard_map.85.order), custom_call_target="tpu_custom_call" | custom-call | tf_op jit(solution)/shard_map/pallas_call | solution.py:335
  12.8 10.0 %all-to-all-start = ((bf16[8,128,256]{2,1,0:T(8,128)(2,1)}), bf16[8,128,256]{2,1,0:T(8,128)(2,1)S(1)}, u32[]{:S(2)}, u32[]{:S(2)}) async-start(bf16[8,128,256]{2,1,0:T(8,128)(2,1)} %shard_map.86), calls=%async_computation | async-start | bytes 1048576 | tf_op jit(solution)/shard_map/all_to_all | solution.py:351
  22.8 2.2 %shard_map.84 = (bf16[1,128,1024]{2,1,0:T(8,128)(2,1)}, bf16[1,128,1024]{2,1,0:T(8,128)(2,1)}, bf16[1,128,1024]{2,1,0:T(8,128)(2,1)}) custom-call(bf16[1,128,512]{2,1,0:T(8,128)(2,1)} %left.3, bf16[1,128,512]{2,1,0:T(8,128)(2,1)} %right.3), custom_call_target="tpu_custom_call" | custom-call | tf_op jit(solution)/shard_map/pallas_call | solution.py:343
  25.1 2.0 %collective-permute-start = (bf16[1,128,1024]{2,1,0:T(8,128)(2,1)}, bf16[1,128,1024]{2,1,0:T(8,128)(2,1)S(1)}, u32[]{:S(2)}, u32[]{:S(2)}) collective-permute-start(bf16[1,128,1024]{2,1,0:T(8,128)(2,1)} %get-tuple-element.28), channel_id=1, source_target_pairs={{0,48},{16,0},{32,16},{48,32},{1,49},{17,1},{33,17},{49,33},{2,50}... | collective-permute-start | bytes 786440 | tf_op jit(solution)/shard_map/ppermute | solution.py:313
  27.0 4.2 %collective-permute-start.2 = (bf16[1,128,1024]{2,1,0:T(8,128)(2,1)}, bf16[1,128,1024]{2,1,0:T(8,128)(2,1)S(1)}, u32[]{:S(2)}, u32[]{:S(2)}) collective-permute-start(bf16[1,128,1024]{2,1,0:T(8,128)(2,1)} %get-tuple-element.29), channel_id=1, source_target_pairs={{0,16},{16,32},{32,48},{48,0},{1,17},{17,33},{33,49},{49,1},{2,18}... | collective-permute-start | bytes 786440 | tf_op jit(solution)/shard_map/ppermute | solution.py:313
  31.3 0.0 copy-start.1
  31.3 0.6 copy-done.1
  32.0 0.1 eq.26
  32.0 0.1 eq.25
  32.1 0.1 add.218
  32.2 0.1 add.215
  32.3 0.2 select_reduce_fusion
  32.5 0.1 reshape.443
  32.6 0.1 reduce_min.11
  32.7 0.1 select_reduce_fusion.1
  32.9 7.0 %all-to-all-done.mine = bf16[8,128,256]{2,1,0:T(8,128)(2,1)S(1)} async-done(((bf16[8,128,256]{2,1,0:T(8,128)(2,1)}), bf16[8,128,256]{2,1,0:T(8,128)(2,1)S(1)}, u32[]{:S(2)}, u32[]{:S(2)}) %all-to-all-start) | async-done | bytes 524320 | tf_op jit(solution)/shard_map/all_to_all | solution.py:351
  39.9 3.3 %collective-permute-start.3 = (bf16[8,128,256]{2,1,0:T(8,128)(2,1)S(1)}, bf16[8,128,256]{2,1,0:T(8,128)(2,1)S(1)}, u32[]{:S(2)}, u32[]{:S(2)}) collective-permute-start(bf16[8,128,256]{2,1,0:T(8,128)(2,1)S(1)} %all-to-all-done.mine), channel_id=1, source_target_pairs={{0,8},{8,0},{1,9},{9,1},{2,10},{10,2},{3,11},{11,3},{4,12},{12,4},... | collective-permute-start | bytes 1572872 | tf_op jit(solution)/shard_map/ppermute | solution.py:313
  43.2 0.1 copy.13
  43.3 0.1 reshape.444
  43.4 0.1 add.220
  43.5 0.1 copy.14
  43.6 0.1 reshape.445
  43.7 0.1 pad_add_fusion.2.info
  43.7 0.0 copy-start
  43.7 1.0 collective-permute-done.3.other
  44.7 0.3 shard_map.87
  45.1 0.0 collective-permute-done.1.a2
  45.1 0.0 collective-permute-done.a1
  45.1 0.0 collective-permute-done.2.a3
  45.1 0.0 copy-done
  45.1 3.0 %shard_map.88 = (f32[2,128,1024]{2,1,0:T(8,128)S(1)}, f32[4,3,8,256]{3,2,1,0:T(8,128)S(1)}) custom-call(s32[34]{0:T(128)S(1)} %pad_add_fusion.2.info, bf16[1,128,1024]{2,1,0:T(8,128)(2,1)S(1)} %copy-done, bf16[1,128,1024]{2,1,0:T(8,128)(2,1)S(1)} %collective-permute-done.a1, bf16[1,128,1024]{2,1,0:T(8,128)(2,1)S(1)} %collective-permute-done.1.a2, ...), custom_call_target="tpu_custom_call" | custom-call | tf_op jit(solution)/shard_map/pallas_call | solution.py:367
  48.2 9.5 %all_to_all.25.stats = f32[4,3,8,256]{3,2,1,0:T(8,128)S(1)} all-to-all(f32[4,3,8,256]{3,2,1,0:T(8,128)S(1)} %get-tuple-element.33), channel_id=1, replica_groups=mesh['z'=8,'y'=4,'core'=2,'dp'=8] {'y'}, dimensions={0} | all-to-all | bytes 196608 | tf_op jit(solution)/shard_map/all_to_all | solution.py:375
  57.6 4.2 %shard_map.89 = (bf16[1,128,512]{2,1,0:T(8,128)(2,1)S(1)}, bf16[1,128,512]{2,1,0:T(8,128)(2,1)S(1)}, bf16[1,128,512]{2,1,0:T(8,128)(2,1)S(1)}, bf16[1,128,512]{2...) custom-call(s32[34]{0:T(128)S(1)} %pad_add_fusion.2.info, ...), custom_call_target="tpu_custom_call" | custom-call | tf_op jit(solution)/shard_map/pallas_call | solution.py:376
  61.9 4.2 %collective-permute-start.10 = (bf16[8,128,256]{2,1,0:T(8,128)(2,1)S(1)}, bf16[8,128,256]{2,1,0:T(8,128)(2,1)S(1)}, u32[]{:S(2)}, u32[]{:S(2)}) collective-permute-start(bf16[8,128,256]{2,1,0:T(8,128)(2,1)S(1)} %get-tuple-element.43), channel_id=1, source_target_pairs={{0,8},{8,0},{1,9},{9,1},{2,10},{10,2},{3,11},{11,3},{4,12},{12,4},... | collective-permute-start | bytes 1572872 | tf_op jit(solution)/shard_map/ppermute | solution.py:313
  66.0 1.5 %collective-permute-done.10 = bf16[8,128,256]{2,1,0:T(8,128)(2,1)S(1)} collective-permute-done((bf16[8,128,256]{2,1,0:T(8,128)(2,1)S(1)}, bf16[8,128,256]{2,1,0:T(8,128)(2,1)S(1)}, u32[]{:S(2)}, u32[]{:S(2)}) %collective-permute-start.10) | collective-permute-done | bytes 524320 | tf_op jit(solution)/shard_map/ppermute | solution.py:313
  67.5 0.9 add_convert_fusion
  68.5 8.8 %all-to-all-start.2 = ((bf16[8,128,256]{2,1,0:T(8,128)(2,1)}), bf16[8,128,256]{2,1,0:T(8,128)(2,1)S(1)}, u32[]{:S(2)}, u32[]{:S(2)}) async-start(bf16[8,128,256]{2,1,0:T(8,128)(2,1)} %add_convert_fusion), calls=%async_computation.2 | async-start | bytes 1048576 | tf_op jit(solution)/shard_map/all_to_all | solution.py:393
  77.3 1.9 %collective-permute-start.7 = (bf16[1,128,512]{2,1,0:T(8,128)(2,1)S(1)}, bf16[1,128,512]{2,1,0:T(8,128)(2,1)S(1)}, u32[]{:S(2)}, u32[]{:S(2)}) collective-permute-start(bf16[1,128,512]{2,1,0:T(8,128)(2,1)S(1)} %get-tuple-element.39), channel_id=1, source_target_pairs={{0,16},{16,32},{32,48},{48,0},{1,17},{17,33},{33,49},{49,1},{2,18}... | collective-permute-start | bytes 393224 | tf_op jit(solution)/shard_map/ppermute | solution.py:313
  79.2 4.8 %collective-permute-start.8 = (bf16[1,128,512]{2,1,0:T(8,128)(2,1)S(1)}, bf16[1,128,512]{2,1,0:T(8,128)(2,1)S(1)}, u32[]{:S(2)}, u32[]{:S(2)}) collective-permute-start(bf16[1,128,512]{2,1,0:T(8,128)(2,1)S(1)} %get-tuple-element.40), channel_id=1, source_target_pairs={{0,32},{16,48},{32,0},{48,16},{1,33},{17,49},{33,1},{49,17},{2,34}... | collective-permute-start | bytes 393224 | tf_op jit(solution)/shard_map/ppermute | solution.py:313
  84.0 3.1 %collective-permute-start.9 = (bf16[1,128,512]{2,1,0:T(8,128)(2,1)S(1)}, bf16[1,128,512]{2,1,0:T(8,128)(2,1)S(1)}, u32[]{:S(2)}, u32[]{:S(2)}) collective-permute-start(bf16[1,128,512]{2,1,0:T(8,128)(2,1)S(1)} %get-tuple-element.41), channel_id=1, source_target_pairs={{0,48},{16,0},{32,16},{48,32},{1,49},{17,1},{33,17},{49,33},{2,50}... | collective-permute-start | bytes 393224 | tf_op jit(solution)/shard_map/ppermute | solution.py:313
  87.2 3.4 %collective-permute-start.4 = (bf16[1,128,512]{2,1,0:T(8,128)(2,1)S(1)}, bf16[1,128,512]{2,1,0:T(8,128)(2,1)S(1)}, u32[]{:S(2)}, u32[]{:S(2)}) collective-permute-start(bf16[1,128,512]{2,1,0:T(8,128)(2,1)S(1)} %get-tuple-element.35), channel_id=1, source_target_pairs={{0,16},{16,32},{32,48},{48,0},{1,17},{17,33},{33,49},{49,1},{2,18}... | collective-permute-start | bytes 393224 | tf_op jit(solution)/shard_map/ppermute | solution.py:313
  90.6 5.2 %collective-permute-start.5 = (bf16[1,128,512]{2,1,0:T(8,128)(2,1)S(1)}, bf16[1,128,512]{2,1,0:T(8,128)(2,1)S(1)}, u32[]{:S(2)}, u32[]{:S(2)}) collective-permute-start(bf16[1,128,512]{2,1,0:T(8,128)(2,1)S(1)} %get-tuple-element.36), channel_id=1, source_target_pairs={{0,32},{16,48},{32,0},{48,16},{1,33},{17,49},{33,1},{49,17},{2,34}... | collective-permute-start | bytes 393224 | tf_op jit(solution)/shard_map/ppermute | solution.py:313
  95.8 0.0 collective-permute-done.7.o1
  95.8 5.5 %collective-permute-start.6 = (bf16[1,128,512]{2,1,0:T(8,128)(2,1)S(1)}, bf16[1,128,512]{2,1,0:T(8,128)(2,1)S(1)}, u32[]{:S(2)}, u32[]{:S(2)}) collective-permute-start(bf16[1,128,512]{2,1,0:T(8,128)(2,1)S(1)} %get-tuple-element.37), channel_id=1, source_target_pairs={{0,48},{16,0},{32,16},{48,32},{1,49},{17,1},{33,17},{49,33},{2,50}... | collective-permute-start | bytes 393224 | tf_op jit(solution)/shard_map/ppermute | solution.py:313
  101.3 0.0 collective-permute-done.8.o2
  101.3 0.0 collective-permute-done.9.o3
  101.3 0.0 all-to-all-done.2.dkv
  101.3 0.3 shard_map.91
  101.7 16.4 %all_to_all.26.parts = f32[16,1,128]{2,1,0:T(1,128)S(1)} all-to-all(f32[16,1,128]{2,1,0:T(1,128)S(1)} %get-tuple-element.44), channel_id=1, replica_groups=mesh['z'=8,'y'=4,'core'=2,'dp'=8] {'z','core'}, dimensions={0} | all-to-all | bytes 16384 | tf_op jit(solution)/shard_map/all_to_all | solution.py:405
  118.0 0.6 shard_map.92
  118.6 8.0 %all-to-all-start.4 = ((f32[32,1,128]{2,1,0:T(1,128)}), f32[32,1,128]{2,1,0:T(1,128)S(1)}, u32[]{:S(2)}, u32[]{:S(2)}) async-start(f32[32,1,128]{2,1,0:T(1,128)} %shard_map.92), calls=%async_computation.4 | async-start | bytes 32768 | tf_op jit(solution)/shard_map/all_to_all | solution.py:415
  126.7 0.0 collective-permute-done.4.a1
  126.7 0.0 collective-permute-done.5.a2
  126.7 0.0 collective-permute-done.6.a3
  126.7 0.7 shard_map.90
  127.4 7.8 %all-to-all-done.4.sums = f32[32,1,128]{2,1,0:T(1,128)S(1)} async-done(((f32[32,1,128]{2,1,0:T(1,128)}), f32[32,1,128]{2,1,0:T(1,128)S(1)}, u32[]{:S(2)}, u32[]{:S(2)}) %all-to-all-start.4) | async-done | bytes 16416 | tf_op jit(solution)/shard_map/all_to_all | solution.py:415
  135.2 0.7 shard_map.93
  (10 shorter events, 0.1 us)
Async XLA Ops:
  2.3 42.7 %collective-permute-start.1 = (bf16[1,128,1024]{2,1,0:T(8,128)(2,1)}, bf16[1,128,1024]{2,1,0:T(8,128)(2,1)S(1)}, u32[]{:S(2)}, u32[]{:S(2)}) collective-permute-start(bf16[1,128,1024]{2,1,0:T(8,128)(2,1)} %shard_map.85.order), channel_id=1, source_target_pairs={{0,32},{16,48},{32,0},{48,16},{1,33},{17,49},{33,1},{49,17},{2,34}... | collective-permute-start | bytes 786440 | tf_op jit(solution)/shard_map/ppermute | solution.py:313
  12.8 27.1 %all-to-all-start = ((bf16[8,128,256]{2,1,0:T(8,128)(2,1)}), bf16[8,128,256]{2,1,0:T(8,128)(2,1)S(1)}, u32[]{:S(2)}, u32[]{:S(2)}) async-start(bf16[8,128,256]{2,1,0:T(8,128)(2,1)} %shard_map.86), calls=%async_computation | async-start | bytes 1048576 | tf_op jit(solution)/shard_map/all_to_all | solution.py:351
  25.1 20.0 %collective-permute-start = (bf16[1,128,1024]{2,1,0:T(8,128)(2,1)}, bf16[1,128,1024]{2,1,0:T(8,128)(2,1)S(1)}, u32[]{:S(2)}, u32[]{:S(2)}) collective-permute-start(bf16[1,128,1024]{2,1,0:T(8,128)(2,1)} %get-tuple-element.28), channel_id=1, source_target_pairs={{0,48},{16,0},{32,16},{48,32},{1,49},{17,1},{33,17},{49,33},{2,50}... | collective-permute-start | bytes 786440 | tf_op jit(solution)/shard_map/ppermute | solution.py:313
  27.0 18.1 %collective-permute-start.2 = (bf16[1,128,1024]{2,1,0:T(8,128)(2,1)}, bf16[1,128,1024]{2,1,0:T(8,128)(2,1)S(1)}, u32[]{:S(2)}, u32[]{:S(2)}) collective-permute-start(bf16[1,128,1024]{2,1,0:T(8,128)(2,1)} %get-tuple-element.29), channel_id=1, source_target_pairs={{0,16},{16,32},{32,48},{48,0},{1,17},{17,33},{33,49},{49,1},{2,18}... | collective-permute-start | bytes 786440 | tf_op jit(solution)/shard_map/ppermute | solution.py:313
  31.3 0.7 copy-start.1
  39.9 4.8 %collective-permute-start.3 = (bf16[8,128,256]{2,1,0:T(8,128)(2,1)S(1)}, bf16[8,128,256]{2,1,0:T(8,128)(2,1)S(1)}, u32[]{:S(2)}, u32[]{:S(2)}) collective-permute-start(bf16[8,128,256]{2,1,0:T(8,128)(2,1)S(1)} %all-to-all-done.mine), channel_id=1, source_target_pairs={{0,8},{8,0},{1,9},{9,1},{2,10},{10,2},{3,11},{11,3},{4,12},{12,4},... | collective-permute-start | bytes 1572872 | tf_op jit(solution)/shard_map/ppermute | solution.py:313
  43.7 1.4 copy-start
  61.9 5.7 %collective-permute-start.10 = (bf16[8,128,256]{2,1,0:T(8,128)(2,1)S(1)}, bf16[8,128,256]{2,1,0:T(8,128)(2,1)S(1)}, u32[]{:S(2)}, u32[]{:S(2)}) collective-permute-start(bf16[8,128,256]{2,1,0:T(8,128)(2,1)S(1)} %get-tuple-element.43), channel_id=1, source_target_pairs={{0,8},{8,0},{1,9},{9,1},{2,10},{10,2},{3,11},{11,3},{4,12},{12,4},... | collective-permute-start | bytes 1572872 | tf_op jit(solution)/shard_map/ppermute | solution.py:313
  68.5 32.9 %all-to-all-start.2 = ((bf16[8,128,256]{2,1,0:T(8,128)(2,1)}), bf16[8,128,256]{2,1,0:T(8,128)(2,1)S(1)}, u32[]{:S(2)}, u32[]{:S(2)}) async-start(bf16[8,128,256]{2,1,0:T(8,128)(2,1)} %add_convert_fusion), calls=%async_computation.2 | async-start | bytes 1048576 | tf_op jit(solution)/shard_map/all_to_all | solution.py:393
  77.3 18.5 %collective-permute-start.7 = (bf16[1,128,512]{2,1,0:T(8,128)(2,1)S(1)}, bf16[1,128,512]{2,1,0:T(8,128)(2,1)S(1)}, u32[]{:S(2)}, u32[]{:S(2)}) collective-permute-start(bf16[1,128,512]{2,1,0:T(8,128)(2,1)S(1)} %get-tuple-element.39), channel_id=1, source_target_pairs={{0,16},{16,32},{32,48},{48,0},{1,17},{17,33},{33,49},{49,1},{2,18}... | collective-permute-start | bytes 393224 | tf_op jit(solution)/shard_map/ppermute | solution.py:313
  79.2 22.1 %collective-permute-start.8 = (bf16[1,128,512]{2,1,0:T(8,128)(2,1)S(1)}, bf16[1,128,512]{2,1,0:T(8,128)(2,1)S(1)}, u32[]{:S(2)}, u32[]{:S(2)}) collective-permute-start(bf16[1,128,512]{2,1,0:T(8,128)(2,1)S(1)} %get-tuple-element.40), channel_id=1, source_target_pairs={{0,32},{16,48},{32,0},{48,16},{1,33},{17,49},{33,1},{49,17},{2,34}... | collective-permute-start | bytes 393224 | tf_op jit(solution)/shard_map/ppermute | solution.py:313
  84.0 17.3 %collective-permute-start.9 = (bf16[1,128,512]{2,1,0:T(8,128)(2,1)S(1)}, bf16[1,128,512]{2,1,0:T(8,128)(2,1)S(1)}, u32[]{:S(2)}, u32[]{:S(2)}) collective-permute-start(bf16[1,128,512]{2,1,0:T(8,128)(2,1)S(1)} %get-tuple-element.41), channel_id=1, source_target_pairs={{0,48},{16,0},{32,16},{48,32},{1,49},{17,1},{33,17},{49,33},{2,50}... | collective-permute-start | bytes 393224 | tf_op jit(solution)/shard_map/ppermute | solution.py:313
  87.2 39.5 %collective-permute-start.4 = (bf16[1,128,512]{2,1,0:T(8,128)(2,1)S(1)}, bf16[1,128,512]{2,1,0:T(8,128)(2,1)S(1)}, u32[]{:S(2)}, u32[]{:S(2)}) collective-permute-start(bf16[1,128,512]{2,1,0:T(8,128)(2,1)S(1)} %get-tuple-element.35), channel_id=1, source_target_pairs={{0,16},{16,32},{32,48},{48,0},{1,17},{17,33},{33,49},{49,1},{2,18}... | collective-permute-start | bytes 393224 | tf_op jit(solution)/shard_map/ppermute | solution.py:313
  90.6 36.1 %collective-permute-start.5 = (bf16[1,128,512]{2,1,0:T(8,128)(2,1)S(1)}, bf16[1,128,512]{2,1,0:T(8,128)(2,1)S(1)}, u32[]{:S(2)}, u32[]{:S(2)}) collective-permute-start(bf16[1,128,512]{2,1,0:T(8,128)(2,1)S(1)} %get-tuple-element.36), channel_id=1, source_target_pairs={{0,32},{16,48},{32,0},{48,16},{1,33},{17,49},{33,1},{49,17},{2,34}... | collective-permute-start | bytes 393224 | tf_op jit(solution)/shard_map/ppermute | solution.py:313
  95.8 30.9 %collective-permute-start.6 = (bf16[1,128,512]{2,1,0:T(8,128)(2,1)S(1)}, bf16[1,128,512]{2,1,0:T(8,128)(2,1)S(1)}, u32[]{:S(2)}, u32[]{:S(2)}) collective-permute-start(bf16[1,128,512]{2,1,0:T(8,128)(2,1)S(1)} %get-tuple-element.37), channel_id=1, source_target_pairs={{0,48},{16,0},{32,16},{48,32},{1,49},{17,1},{33,17},{49,33},{2,50}... | collective-permute-start | bytes 393224 | tf_op jit(solution)/shard_map/ppermute | solution.py:313
  118.6 16.5 %all-to-all-start.4 = ((f32[32,1,128]{2,1,0:T(1,128)}), f32[32,1,128]{2,1,0:T(1,128)S(1)}, u32[]{:S(2)}, u32[]{:S(2)}) async-start(f32[32,1,128]{2,1,0:T(1,128)} %shard_map.92), calls=%async_computation.4 | async-start | bytes 32768 | tf_op jit(solution)/shard_map/all_to_all | solution.py:415

commit v8 on v6

--- a/solution.py
+++ b/solution.py
@@ -13,7 +13,9 @@
 NZ, NY, NC = 8, 4, 2
 FIELDS = 4
 VMEM = pl.BlockSpec(memory_space=pltpu.VMEM)
+FAR = pl.BlockSpec(memory_space=pl.ANY)
 SMEM = pl.BlockSpec(memory_space=pltpu.SMEM)
+ALONE = pltpu.CompilerParams(vmem_limit_bytes=62 * 1024 * 1024)
 PARAMS = pltpu.CompilerParams(vmem_limit_bytes=40 * 1024 * 1024)
 
 
@@ -23,7 +25,9 @@
 
 FIELDS = 4
 VMEM = pl.BlockSpec(memory_space=pltpu.VMEM)
+FAR = pl.BlockSpec(memory_space=pl.ANY)
 SMEM = pl.BlockSpec(memory_space=pltpu.SMEM)
+ALONE = pltpu.CompilerParams(vmem_limit_bytes=62 * 1024 * 1024)
 PARAMS = pltpu.CompilerParams(vmem_limit_bytes=40 * 1024 * 1024)
 
 
@@ -256,14 +260,8 @@
     sq_ref[...] = jnp.full(sq_ref.shape, squares, jnp.float32)
 
 
-def release_kernel(order, *refs):
+def attended_kernel(order, a0, a1, a2, a3, out):
     del order
-    count = len(refs) // 2
-    for a, b in zip(refs[:count], refs[count:]):
-        b[...] = a[...]
-
-
-def attended_kernel(a0, a1, a2, a3, out):
     parts = [a[...].astype(jnp.float32) for a in (a0, a1, a2, a3)]
     out[...] = ((parts[0] + parts[1]) + (parts[2] + parts[3])).astype(out.dtype)
 
@@ -274,12 +272,13 @@
         out[k] = total
 
 
-def scale_kernel(count, sums, dq, dkv, oq, ok, ov):
+def scale_kernel(count, sums, dq, dkv, oq, ok, ov, used):
     lanes = sums.shape[2]
     total = sums[0]
     for k in range(1, sums.shape[0]):
         total = total + sums[k]
     factor = lax.rsqrt(total / count + 1e-06)
+    used[...] = factor
     for h in range(dq.shape[2] // lanes):
         at = slice(h * lanes, (h + 1) * lanes)
         oq[0, :, at] = (dq[0, :, at] * factor).astype(oq.dtype)
@@ -301,6 +300,18 @@
     for out in outs:
         out[:, :, :wide] = left[...]
         out[:, :, wide:] = right[...]
+
+
+def far_kernel(left, right, out, sems):
+    wide = left.shape[2]
+    copies = [
+        pltpu.make_async_copy(left, out.at[:, :, :wide], sems.at[0]),
+        pltpu.make_async_copy(right, out.at[:, :, wide:], sems.at[1]),
+    ]
+    for copy in copies:
+        copy.start()
+    for copy in copies:
+        copy.wait()
 
 
 def turn(x, axis, size, by):
@@ -319,11 +330,12 @@
 
     block = jax.ShapeDtypeStruct((1, tok, 2 * wide), keys.dtype)
     far = pl.pallas_call(
-        join_kernel,
+        far_kernel,
         out_shape=[block],
-        in_specs=[VMEM] * 2,
+        in_specs=[FAR] * 2,
         out_specs=[VMEM],
-        compiler_params=PARAMS,
+        scratch_shapes=[pltpu.SemaphoreType.DMA((2,))],
+        compiler_params=ALONE,
     )(queries, grad_out)
     copies = pl.pallas_call(
         spread_kernel,
@@ -393,15 +405,8 @@
         out_specs=[VMEM] * 3,
         compiler_params=PARAMS,
     )(*back, pieces)
-    released = pl.pallas_call(
-        release_kernel,
-        out_shape=[shape(queries.shape, bf16)] * (NY - 1),
-        in_specs=[VMEM] * NY,
-        out_specs=[VMEM] * (NY - 1),
-        compiler_params=PARAMS,
-    )(squares, *seen[1:])
     squares = lax.all_to_all(squares, ("z", "core"), 0, 0, tiled=True)
-    home = [seen[0]] + [turn(released[k - 1], "y", NY, k) for k in range(1, NY)]
+    home = [seen[0]] + [turn(seen[k], "y", NY, k) for k in range(1, NY)]
     ndata = lax.axis_size("dp")
     squares = pl.pallas_call(
         fold_kernel,
@@ -409,24 +414,28 @@
         in_specs=[VMEM],
         out_specs=VMEM,
         compiler_params=PARAMS,
-        cost_estimate=pl.CostEstimate(flops=10**9, transcendentals=0, bytes_accessed=0),
     )(squares)
     squares = lax.all_to_all(squares, ("y", "dp"), 0, 0, tiled=True)
+    count = float(ndata * NZ * NY * NC * tok * (wide + 2 * width))
+    out_query, out_key, out_value, used = pl.pallas_call(
+        functools.partial(scale_kernel, count),
+        out_shape=(
+            shape(queries.shape, bf16),
+            shape(keys.shape, bf16),
+            shape(values.shape, bf16),
+            shape((1, 128), f32),
+        ),
+        in_specs=[VMEM] * 3,
+        out_specs=(VMEM,) * 4,
+        compiler_params=PARAMS,
+    )(squares, dq, dkv)
     attended = pl.pallas_call(
         attended_kernel,
         out_shape=shape(queries.shape, bf16),
-        in_specs=[VMEM] * NY,
+        in_specs=[VMEM] + [VMEM] * NY,
         out_specs=VMEM,
         compiler_params=PARAMS,
-    )(*home)
-    count = float(ndata * NZ * NY * NC * tok * (wide + 2 * width))
-    out_query, out_key, out_value = pl.pallas_call(
-        functools.partial(scale_kernel, count),
-        out_shape=(shape(queries.shape, bf16), shape(keys.shape, bf16), shape(values.shape, bf16)),
-        in_specs=[VMEM] * 3,
-        out_specs=(VMEM,) * 3,
-        compiler_params=PARAMS,
-    )(squares, dq, dkv)
+    )(used, *home)
     return attended, out_query, out_key, out_value
 
 

time: 135 us -> 134 us (level)
  blocking collectives: 27 us -> 43.3 us
  waiting for transfers between devices: 23.9 us -> 11.7 us
  starting transfers between devices: 65.6 us -> 60.8 us
    all_to_all x0 -> x1, blocking collectives: none -> 16.4 us  [per_device(): squares = lax.all_to_all(squares, ('z', 'core'), 0, 0, tiled=True)]
    ppermute x11, waiting for transfers between devices: 14.7 us -> 2.5 us  [turn(): return lax.ppermute(x, axis, [(i, (i + by) % size) for i in range(size)])]
    all_to_all x1 -> x0, starting transfers between devices: 7.53 us -> none  [per_device(): squares = lax.all_to_all(squares, ('z', 'core'), 0, 0, tiled=True)]
    ppermute x11, starting transfers between devices: 42.1 us -> 45.6 us  [turn(): return lax.ppermute(x, axis, [(i, (i + by) % size) for i in range(size)])]
  transfers between devices with their start and end apart: 14 -> 13, of which waited for: 6 -> 3; matrix products, arithmetic and copies ran while one was open for 1% -> 1% of each run, Pallas kernels for 2% -> 2%
where the time goes in v8:
time: 134 us; the launch traced here: 133 us
  starting transfers between devices  60.8 us (45%)
  blocking collectives  43.3 us (32%)
  Pallas kernels  12 us (9%)
  waiting for transfers between devices  11.7 us (9%)
  local copies, waits for them, and re-layouts  2.48 us (2%)
  other arithmetic  1.52 us (1%)
    ppermute x11, starting transfers between devices, turn(): return lax.ppermute(x, axis, [(i, (i + by) % size) for i in range(size)])  45.6 us
    all_to_all x1, blocking collectives, per_device(): squares = lax.all_to_all(squares, ('y', 'dp'), 0, 0, tiled=True)  17.4 us
    all_to_all x1, blocking collectives, per_device(): squares = lax.all_to_all(squares, ('z', 'core'), 0, 0, tiled=True)  16.4 us
    all_to_all x1, starting transfers between devices, per_device(): mine = lax.all_to_all(copies, 'z', 0, 0, tiled=True)  10.2 us
    all_to_all x1, blocking collectives, per_device(): stats = lax.all_to_all(stats, 'y', 0, 0, tiled=True)  9.53 us
    all_to_all x1, waiting for transfers between devices, per_device(): mine = lax.all_to_all(copies, 'z', 0, 0, tiled=True)  9.15 us
    all_to_all x1, starting transfers between devices, per_device(): pieces = lax.all_to_all(pair, 'z', 0, 0, tiled=True)  5.07 us
    pallas_call x1, Pallas kernels, per_device(): pl.pallas_call(functools.partial(backward_kernel, heads), out_shape=[shap...  4.23 us
  transfers between devices with their start and end apart: 13, of which 3 were waited for; matrix products, arithmetic and copies ran while one was open for 1% of the time, Pallas kernels for 2%

profile of v8, /device:TPU:1, one launch (start us, length us, event | category | flops | bytes accessed | tf_op | source)
XLA Modules:
  0.0 132.8 jit_solution(15481488044740196243)
XLA Ops:
  0.6 0.0 copy-start.4
  0.6 0.0 copy-start.3
  0.7 1.7 %shard_map.85.order = bf16[1,128,1024]{2,1,0:T(8,128)(2,1)} custom-call(bf16[1,128,512]{2,1,0:T(8,128)(2,1)} %left.3, bf16[1,128,512]{2,1,0:T(8,128)(2,1)} %right.3), custom_call_target="tpu_custom_call" | custom-call | tf_op jit(solution)/shard_map/pallas_call | solution.py:332
  2.4 8.3 %collective-permute-start.1 = (bf16[1,128,1024]{2,1,0:T(8,128)(2,1)}, bf16[1,128,1024]{2,1,0:T(8,128)(2,1)S(1)}, u32[]{:S(2)}, u32[]{:S(2)}) collective-permute-start(bf16[1,128,1024]{2,1,0:T(8,128)(2,1)} %shard_map.85.order), channel_id=1, source_target_pairs={{0,32},{16,48},{32,0},{48,16},{1,33},{17,49},{33,1},{49,17},{2,34}... | collective-permute-start | bytes 786440 | tf_op jit(solution)/shard_map/ppermute | solution.py:318
  10.6 0.0 copy-done.4
  10.7 0.0 copy-done.3
  10.7 0.0 copy-start
  10.7 1.0 copy-done
  11.6 0.9 shard_map.86
  12.5 0.0 copy-start.1
  12.5 10.2 %all-to-all-start = ((bf16[8,128,256]{2,1,0:T(8,128)(2,1)}), bf16[8,128,256]{2,1,0:T(8,128)(2,1)S(1)}, u32[]{:S(2)}, u32[]{:S(2)}) async-start(bf16[8,128,256]{2,1,0:T(8,128)(2,1)} %shard_map.86), calls=%async_computation | async-start | bytes 1048576 | tf_op jit(solution)/shard_map/all_to_all | solution.py:354
  22.7 0.0 copy-done.1
  22.7 0.0 copy-done.2
  22.7 0.1 shard_map.84
  22.8 2.0 %collective-permute-start = (bf16[1,128,1024]{2,1,0:T(8,128)(2,1)S(1)}, bf16[1,128,1024]{2,1,0:T(8,128)(2,1)S(1)}, u32[]{:S(2)}, u32[]{:S(2)}) collective-permute-start(bf16[1,128,1024]{2,1,0:T(8,128)(2,1)S(1)} %get-tuple-element.29), channel_id=1, source_target_pairs={{0,48},{16,0},{32,16},{48,32},{1,49},{17,1},{33,17},{49,33},{2,50}... | collective-permute-start | bytes 786440 | tf_op jit(solution)/shard_map/ppermute | solution.py:318
  24.7 4.2 %collective-permute-start.2 = (bf16[1,128,1024]{2,1,0:T(8,128)(2,1)S(1)}, bf16[1,128,1024]{2,1,0:T(8,128)(2,1)S(1)}, u32[]{:S(2)}, u32[]{:S(2)}) collective-permute-start(bf16[1,128,1024]{2,1,0:T(8,128)(2,1)S(1)} %get-tuple-element.30), channel_id=1, source_target_pairs={{0,16},{16,32},{32,48},{48,0},{1,17},{17,33},{33,49},{49,1},{2,18}... | collective-permute-start | bytes 786440 | tf_op jit(solution)/shard_map/ppermute | solution.py:318
  29.0 0.0 copy-start.5
  29.0 0.6 copy-done.5
  29.7 0.1 eq.26
  29.7 0.1 eq.25
  29.8 0.1 add.218
  29.9 0.1 add.215
  30.0 0.2 select_reduce_fusion
  30.2 0.1 reshape.443
  30.3 0.1 reduce_min.11
  30.4 0.1 select_reduce_fusion.1
  30.6 9.1 %all-to-all-done.mine = bf16[8,128,256]{2,1,0:T(8,128)(2,1)S(1)} async-done(((bf16[8,128,256]{2,1,0:T(8,128)(2,1)}), bf16[8,128,256]{2,1,0:T(8,128)(2,1)S(1)}, u32[]{:S(2)}, u32[]{:S(2)}) %all-to-all-start) | async-done | bytes 524320 | tf_op jit(solution)/shard_map/all_to_all | solution.py:354
  39.7 3.3 %collective-permute-start.3 = (bf16[8,128,256]{2,1,0:T(8,128)(2,1)S(1)}, bf16[8,128,256]{2,1,0:T(8,128)(2,1)S(1)}, u32[]{:S(2)}, u32[]{:S(2)}) collective-permute-start(bf16[8,128,256]{2,1,0:T(8,128)(2,1)S(1)} %all-to-all-done.mine), channel_id=1, source_target_pairs={{0,8},{8,0},{1,9},{9,1},{2,10},{10,2},{3,11},{11,3},{4,12},{12,4},... | collective-permute-start | bytes 1572872 | tf_op jit(solution)/shard_map/ppermute | solution.py:318
  43.1 0.1 copy.13
  43.2 0.1 reshape.444
  43.2 0.1 add.220
  43.3 0.1 copy.14
  43.4 0.1 reshape.445
  43.5 0.1 pad_add_fusion.2.info
  43.6 1.0 collective-permute-done.3.other
  44.6 0.3 shard_map.87
  44.9 0.0 collective-permute-done.1.a2
  44.9 0.0 collective-permute-done.a1
  44.9 0.0 collective-permute-done.2.a3
  44.9 3.0 %shard_map.88 = (f32[2,128,1024]{2,1,0:T(8,128)S(1)}, f32[4,3,8,256]{3,2,1,0:T(8,128)S(1)}) custom-call(s32[34]{0:T(128)S(1)} %pad_add_fusion.2.info, bf16[1,128,1024]{2,1,0:T(8,128)(2,1)S(1)} %get-tuple-element.28.a0, bf16[1,128,1024]{2,1,0:T(8,128)(2,1)S(1)} %collective-permute-done.a1, bf16[1,128,1024]{2,1,0:T(8,128)(2,1)S(1)} %collective-permute-done.1.a2, ...), custom_call_target="tpu_custom_call" | custom-call | tf_op jit(solution)/shard_map/pallas_call | solution.py:370
  48.0 9.5 %all_to_all.25.stats = f32[4,3,8,256]{3,2,1,0:T(8,128)S(1)} all-to-all(f32[4,3,8,256]{3,2,1,0:T(8,128)S(1)} %get-tuple-element.34), channel_id=1, replica_groups=mesh['z'=8,'y'=4,'core'=2,'dp'=8] {'y'}, dimensions={0} | all-to-all | bytes 196608 | tf_op jit(solution)/shard_map/all_to_all | solution.py:378
  57.5 4.2 %shard_map.89 = (bf16[1,128,512]{2,1,0:T(8,128)(2,1)S(1)}, bf16[1,128,512]{2,1,0:T(8,128)(2,1)S(1)}, bf16[1,128,512]{2,1,0:T(8,128)(2,1)S(1)}, bf16[1,128,512]{2...) custom-call(s32[34]{0:T(128)S(1)} %pad_add_fusion.2.info, ...), custom_call_target="tpu_custom_call" | custom-call | tf_op jit(solution)/shard_map/pallas_call | solution.py:379
  61.8 3.9 %collective-permute-start.7 = (bf16[8,128,256]{2,1,0:T(8,128)(2,1)S(1)}, bf16[8,128,256]{2,1,0:T(8,128)(2,1)S(1)}, u32[]{:S(2)}, u32[]{:S(2)}) collective-permute-start(bf16[8,128,256]{2,1,0:T(8,128)(2,1)S(1)} %get-tuple-element.40), channel_id=1, source_target_pairs={{0,8},{8,0},{1,9},{9,1},{2,10},{10,2},{3,11},{11,3},{4,12},{12,4},... | collective-permute-start | bytes 1572872 | tf_op jit(solution)/shard_map/ppermute | solution.py:318
  65.6 1.5 %collective-permute-done.7 = bf16[8,128,256]{2,1,0:T(8,128)(2,1)S(1)} collective-permute-done((bf16[8,128,256]{2,1,0:T(8,128)(2,1)S(1)}, bf16[8,128,256]{2,1,0:T(8,128)(2,1)S(1)}, u32[]{:S(2)}, u32[]{:S(2)}) %collective-permute-start.7) | collective-permute-done | bytes 524320 | tf_op jit(solution)/shard_map/ppermute | solution.py:318
  67.1 0.9 add_convert_fusion
  68.1 5.1 %all-to-all-start.2 = ((bf16[8,128,256]{2,1,0:T(8,128)(2,1)}), bf16[8,128,256]{2,1,0:T(8,128)(2,1)S(1)}, u32[]{:S(2)}, u32[]{:S(2)}) async-start(bf16[8,128,256]{2,1,0:T(8,128)(2,1)} %add_convert_fusion), calls=%async_computation.2 | async-start | bytes 1048576 | tf_op jit(solution)/shard_map/all_to_all | solution.py:396
  73.1 2.3 %collective-permute-start.4 = (bf16[1,128,512]{2,1,0:T(8,128)(2,1)S(1)}, bf16[1,128,512]{2,1,0:T(8,128)(2,1)S(1)}, u32[]{:S(2)}, u32[]{:S(2)}) collective-permute-start(bf16[1,128,512]{2,1,0:T(8,128)(2,1)S(1)} %get-tuple-element.36), channel_id=1, source_target_pairs={{0,16},{16,32},{32,48},{48,0},{1,17},{17,33},{33,49},{49,1},{2,18}... | collective-permute-start | bytes 393224 | tf_op jit(solution)/shard_map/ppermute | solution.py:318
  75.4 3.7 %collective-permute-start.5 = (bf16[1,128,512]{2,1,0:T(8,128)(2,1)S(1)}, bf16[1,128,512]{2,1,0:T(8,128)(2,1)S(1)}, u32[]{:S(2)}, u32[]{:S(2)}) collective-permute-start(bf16[1,128,512]{2,1,0:T(8,128)(2,1)S(1)} %get-tuple-element.37), channel_id=1, source_target_pairs={{0,32},{16,48},{32,0},{48,16},{1,33},{17,49},{33,1},{49,17},{2,34}... | collective-permute-start | bytes 393224 | tf_op jit(solution)/shard_map/ppermute | solution.py:318
  79.2 3.7 %collective-permute-start.6 = (bf16[1,128,512]{2,1,0:T(8,128)(2,1)S(1)}, bf16[1,128,512]{2,1,0:T(8,128)(2,1)S(1)}, u32[]{:S(2)}, u32[]{:S(2)}) collective-permute-start(bf16[1,128,512]{2,1,0:T(8,128)(2,1)S(1)} %get-tuple-element.38), channel_id=1, source_target_pairs={{0,48},{16,0},{32,16},{48,32},{1,49},{17,1},{33,17},{49,33},{2,50}... | collective-permute-start | bytes 393224 | tf_op jit(solution)/shard_map/ppermute | solution.py:318
  82.9 3.6 %collective-permute-start.8 = (bf16[1,128,512]{2,1,0:T(8,128)(2,1)S(1)}, bf16[1,128,512]{2,1,0:T(8,128)(2,1)S(1)}, u32[]{:S(2)}, u32[]{:S(2)}) collective-permute-start(bf16[1,128,512]{2,1,0:T(8,128)(2,1)S(1)} %get-tuple-element.46), channel_id=1, source_target_pairs={{0,16},{16,32},{32,48},{48,0},{1,17},{17,33},{33,49},{49,1},{2,18}... | collective-permute-start | bytes 393224 | tf_op jit(solution)/shard_map/ppermute | solution.py:318
  86.5 5.2 %collective-permute-start.9 = (bf16[1,128,512]{2,1,0:T(8,128)(2,1)S(1)}, bf16[1,128,512]{2,1,0:T(8,128)(2,1)S(1)}, u32[]{:S(2)}, u32[]{:S(2)}) collective-permute-start(bf16[1,128,512]{2,1,0:T(8,128)(2,1)S(1)} %get-tuple-element.47), channel_id=1, source_target_pairs={{0,32},{16,48},{32,0},{48,16},{1,33},{17,49},{33,1},{49,17},{2,34}... | collective-permute-start | bytes 393224 | tf_op jit(solution)/shard_map/ppermute | solution.py:318
  91.7 0.0 collective-permute-done.4.o1
  91.7 5.5 %collective-permute-start.10 = (bf16[1,128,512]{2,1,0:T(8,128)(2,1)S(1)}, bf16[1,128,512]{2,1,0:T(8,128)(2,1)S(1)}, u32[]{:S(2)}, u32[]{:S(2)}) collective-permute-start(bf16[1,128,512]{2,1,0:T(8,128)(2,1)S(1)} %get-tuple-element.48), channel_id=1, source_target_pairs={{0,48},{16,0},{32,16},{48,32},{1,49},{17,1},{33,17},{49,33},{2,50}... | collective-permute-start | bytes 393224 | tf_op jit(solution)/shard_map/ppermute | solution.py:318
  97.1 0.0 collective-permute-done.5.o2
  97.2 0.0 collective-permute-done.6.o3
  97.2 0.0 all-to-all-done.2.dkv
  97.2 0.3 shard_map.90
  97.5 16.4 %all_to_all.26.parts = f32[16,1,128]{2,1,0:T(1,128)S(1)} all-to-all(f32[16,1,128]{2,1,0:T(1,128)S(1)} %get-tuple-element.41), channel_id=1, replica_groups=mesh['z'=8,'y'=4,'core'=2,'dp'=8] {'z','core'}, dimensions={0} | all-to-all | bytes 16384 | tf_op jit(solution)/shard_map/all_to_all | solution.py:408
  113.9 17.4 %all_to_all.27.sums = f32[32,1,128]{2,1,0:T(1,128)S(1)} all-to-all(f32[32,1,128]{2,1,0:T(1,128)S(1)} %shard_map.91), channel_id=1, replica_groups=mesh['z'=8,'y'=4,'core'=2,'dp'=8] {'y','dp'}, dimensions={0} | all-to-all | bytes 32768 | tf_op jit(solution)/shard_map/all_to_all | solution.py:418
  131.3 0.7 shard_map.92
  132.1 0.0 collective-permute-done.8.a1
  132.1 0.0 collective-permute-done.9.a2
  132.1 0.0 collective-permute-done.10.a3
  132.1 0.7 shard_map.93
  (12 shorter events, 0.1 us)
Async XLA Ops:
  0.6 10.0 %copy-start.4 = (bf16[1,128,128]{2,1,0:T(8,128)(2,1)S(1)}, bf16[1,128,128]{2,1,0:T(8,128)(2,1)}, u32[]{:S(2)}) copy-start(bf16[1,128,128]{2,1,0:T(8,128)(2,1)} %values.1) | copy-start | bytes 98308
  0.6 10.0 %copy-start.3 = (bf16[1,128,128]{2,1,0:T(8,128)(2,1)S(1)}, bf16[1,128,128]{2,1,0:T(8,128)(2,1)}, u32[]{:S(2)}) copy-start(bf16[1,128,128]{2,1,0:T(8,128)(2,1)} %keys.1) | copy-start | bytes 98308
  2.4 42.5 %collective-permute-start.1 = (bf16[1,128,1024]{2,1,0:T(8,128)(2,1)}, bf16[1,128,1024]{2,1,0:T(8,128)(2,1)S(1)}, u32[]{:S(2)}, u32[]{:S(2)}) collective-permute-start(bf16[1,128,1024]{2,1,0:T(8,128)(2,1)} %shard_map.85.order), channel_id=1, source_target_pairs={{0,32},{16,48},{32,0},{48,16},{1,33},{17,49},{33,1},{49,17},{2,34}... | collective-permute-start | bytes 786440 | tf_op jit(solution)/shard_map/ppermute | solution.py:318
  10.7 1.0 copy-start
  12.5 10.2 %copy-start.1 = (bf16[1,128,512]{2,1,0:T(8,128)(2,1)S(1)}, bf16[1,128,512]{2,1,0:T(8,128)(2,1)}, u32[]{:S(2)}) copy-start(bf16[1,128,512]{2,1,0:T(8,128)(2,1)} %left.3) | copy-start | bytes 393220
  12.5 10.2 %copy-start.2 = (bf16[1,128,512]{2,1,0:T(8,128)(2,1)S(1)}, bf16[1,128,512]{2,1,0:T(8,128)(2,1)}, u32[]{:S(2)}) copy-start(bf16[1,128,512]{2,1,0:T(8,128)(2,1)} %right.3) | copy-start | bytes 393220
  12.5 27.2 %all-to-all-start = ((bf16[8,128,256]{2,1,0:T(8,128)(2,1)}), bf16[8,128,256]{2,1,0:T(8,128)(2,1)S(1)}, u32[]{:S(2)}, u32[]{:S(2)}) async-start(bf16[8,128,256]{2,1,0:T(8,128)(2,1)} %shard_map.86), calls=%async_computation | async-start | bytes 1048576 | tf_op jit(solution)/shard_map/all_to_all | solution.py:354
  22.8 22.2 %collective-permute-start = (bf16[1,128,1024]{2,1,0:T(8,128)(2,1)S(1)}, bf16[1,128,1024]{2,1,0:T(8,128)(2,1)S(1)}, u32[]{:S(2)}, u32[]{:S(2)}) collective-permute-start(bf16[1,128,1024]{2,1,0:T(8,128)(2,1)S(1)} %get-tuple-element.29), channel_id=1, source_target_pairs={{0,48},{16,0},{32,16},{48,32},{1,49},{17,1},{33,17},{49,33},{2,50}... | collective-permute-start | bytes 786440 | tf_op jit(solution)/shard_map/ppermute | solution.py:318
  24.7 20.2 %collective-permute-start.2 = (bf16[1,128,1024]{2,1,0:T(8,128)(2,1)S(1)}, bf16[1,128,1024]{2,1,0:T(8,128)(2,1)S(1)}, u32[]{:S(2)}, u32[]{:S(2)}) collective-permute-start(bf16[1,128,1024]{2,1,0:T(8,128)(2,1)S(1)} %get-tuple-element.30), channel_id=1, source_target_pairs={{0,16},{16,32},{32,48},{48,0},{1,17},{17,33},{33,49},{49,1},{2,18}... | collective-permute-start | bytes 786440 | tf_op jit(solution)/shard_map/ppermute | solution.py:318
  29.0 0.7 copy-start.5
  39.7 4.8 %collective-permute-start.3 = (bf16[8,128,256]{2,1,0:T(8,128)(2,1)S(1)}, bf16[8,128,256]{2,1,0:T(8,128)(2,1)S(1)}, u32[]{:S(2)}, u32[]{:S(2)}) collective-permute-start(bf16[8,128,256]{2,1,0:T(8,128)(2,1)S(1)} %all-to-all-done.mine), channel_id=1, source_target_pairs={{0,8},{8,0},{1,9},{9,1},{2,10},{10,2},{3,11},{11,3},{4,12},{12,4},... | collective-permute-start | bytes 1572872 | tf_op jit(solution)/shard_map/ppermute | solution.py:318
  61.8 5.4 %collective-permute-start.7 = (bf16[8,128,256]{2,1,0:T(8,128)(2,1)S(1)}, bf16[8,128,256]{2,1,0:T(8,128)(2,1)S(1)}, u32[]{:S(2)}, u32[]{:S(2)}) collective-permute-start(bf16[8,128,256]{2,1,0:T(8,128)(2,1)S(1)} %get-tuple-element.40), channel_id=1, source_target_pairs={{0,8},{8,0},{1,9},{9,1},{2,10},{10,2},{3,11},{11,3},{4,12},{12,4},... | collective-permute-start | bytes 1572872 | tf_op jit(solution)/shard_map/ppermute | solution.py:318
  68.1 29.1 %all-to-all-start.2 = ((bf16[8,128,256]{2,1,0:T(8,128)(2,1)}), bf16[8,128,256]{2,1,0:T(8,128)(2,1)S(1)}, u32[]{:S(2)}, u32[]{:S(2)}) async-start(bf16[8,128,256]{2,1,0:T(8,128)(2,1)} %add_convert_fusion), calls=%async_computation.2 | async-start | bytes 1048576 | tf_op jit(solution)/shard_map/all_to_all | solution.py:396
  73.1 18.5 %collective-permute-start.4 = (bf16[1,128,512]{2,1,0:T(8,128)(2,1)S(1)}, bf16[1,128,512]{2,1,0:T(8,128)(2,1)S(1)}, u32[]{:S(2)}, u32[]{:S(2)}) collective-permute-start(bf16[1,128,512]{2,1,0:T(8,128)(2,1)S(1)} %get-tuple-element.36), channel_id=1, source_target_pairs={{0,16},{16,32},{32,48},{48,0},{1,17},{17,33},{33,49},{49,1},{2,18}... | collective-permute-start | bytes 393224 | tf_op jit(solution)/shard_map/ppermute | solution.py:318
  75.4 21.7 %collective-permute-start.5 = (bf16[1,128,512]{2,1,0:T(8,128)(2,1)S(1)}, bf16[1,128,512]{2,1,0:T(8,128)(2,1)S(1)}, u32[]{:S(2)}, u32[]{:S(2)}) collective-permute-start(bf16[1,128,512]{2,1,0:T(8,128)(2,1)S(1)} %get-tuple-element.37), channel_id=1, source_target_pairs={{0,32},{16,48},{32,0},{48,16},{1,33},{17,49},{33,1},{49,17},{2,34}... | collective-permute-start | bytes 393224 | tf_op jit(solution)/shard_map/ppermute | solution.py:318
  79.2 18.0 %collective-permute-start.6 = (bf16[1,128,512]{2,1,0:T(8,128)(2,1)S(1)}, bf16[1,128,512]{2,1,0:T(8,128)(2,1)S(1)}, u32[]{:S(2)}, u32[]{:S(2)}) collective-permute-start(bf16[1,128,512]{2,1,0:T(8,128)(2,1)S(1)} %get-tuple-element.38), channel_id=1, source_target_pairs={{0,48},{16,0},{32,16},{48,32},{1,49},{17,1},{33,17},{49,33},{2,50}... | collective-permute-start | bytes 393224 | tf_op jit(solution)/shard_map/ppermute | solution.py:318
  82.9 49.2 %collective-permute-start.8 = (bf16[1,128,512]{2,1,0:T(8,128)(2,1)S(1)}, bf16[1,128,512]{2,1,0:T(8,128)(2,1)S(1)}, u32[]{:S(2)}, u32[]{:S(2)}) collective-permute-start(bf16[1,128,512]{2,1,0:T(8,128)(2,1)S(1)} %get-tuple-element.46), channel_id=1, source_target_pairs={{0,16},{16,32},{32,48},{48,0},{1,17},{17,33},{33,49},{49,1},{2,18}... | collective-permute-start | bytes 393224 | tf_op jit(solution)/shard_map/ppermute | solution.py:318
  86.5 45.6 %collective-permute-start.9 = (bf16[1,128,512]{2,1,0:T(8,128)(2,1)S(1)}, bf16[1,128,512]{2,1,0:T(8,128)(2,1)S(1)}, u32[]{:S(2)}, u32[]{:S(2)}) collective-permute-start(bf16[1,128,512]{2,1,0:T(8,128)(2,1)S(1)} %get-tuple-element.47), channel_id=1, source_target_pairs={{0,32},{16,48},{32,0},{48,16},{1,33},{17,49},{33,1},{49,17},{2,34}... | collective-permute-start | bytes 393224 | tf_op jit(solution)/shard_map/ppermute | solution.py:318
  91.7 40.4 %collective-permute-start.10 = (bf16[1,128,512]{2,1,0:T(8,128)(2,1)S(1)}, bf16[1,128,512]{2,1,0:T(8,128)(2,1)S(1)}, u32[]{:S(2)}, u32[]{:S(2)}) collective-permute-start(bf16[1,128,512]{2,1,0:T(8,128)(2,1)S(1)} %get-tuple-element.48), channel_id=1, source_target_pairs={{0,48},{16,0},{32,16},{48,32},{1,49},{17,1},{33,17},{49,33},{2,50}... | collective-permute-start | bytes 393224 | tf_op jit(solution)/shard_map/ppermute | solution.py:318

commit v9 on v8

--- a/solution.py
+++ b/solution.py
@@ -186,7 +186,7 @@
 
 def backward_kernel(
     heads, info, a0, a1, a2, a3, u_ref, pairs, turned, stats,
-    t0, t1, t2, t3, o0, o1, o2, o3, dmine, dother, dacc, dq_scr, st_scr,
+    t0, t1, t3, o0, o1, o2, o3, dmine, dother, dacc, dq_scr, st_scr,
 ):
     tile = Tile(info, pairs, heads)
     half, width, cols, keys = tile.half, tile.width, tile.cols, tile.keys
@@ -235,11 +235,16 @@
         att = (u_ref[side] * share).T.astype(jnp.bfloat16)
         dq = (dq_scr[...] * scale).T.astype(jnp.bfloat16)
         rows = pl.ds(pl.multiple_of(side * half, half), half)
-        for whole, outs in ((att, (t0, t1, t2, t3)), (dq, (o0, o1, o2, o3))):
-            for k, out in enumerate(outs):
+        wide = heads * width
+        for whole, outs in (
+            (dq, ((o0, 0), (o1, 0), (o2, 0), (o3, 0))),
+            (att, ((t0, 0), (t1, 0), (o2, wide), (t3, 0))),
+        ):
+            for k, (out, lane) in enumerate(outs):
                 for h in range(heads):
                     at = k * cols + h * half
-                    out[0, rows, h * width : (h + 1) * width] = whole[at : at + half]
+                    lanes = slice(lane + h * width, lane + (h + 1) * width)
+                    out[0, rows, lanes] = whole[at : at + half]
         return 0
 
     lax.fori_loop(0, 2, one_side, 0)
@@ -251,7 +256,8 @@
 
 
 def combine_kernel(o0, o1, o2, o3, dkv, dq_ref, dkv_ref, sq_ref):
-    parts = [o[0].astype(jnp.float32) for o in (o0, o1, o2, o3)]
+    wide = dq_ref.shape[2]
+    parts = [o[0, :, :wide].astype(jnp.float32) for o in (o0, o1, o2, o3)]
     dq = (parts[0] + parts[1]) + (parts[2] + parts[3])
     dq_ref[0] = dq
     total = functools.reduce(jnp.add, [dkv[k].astype(jnp.float32) for k in range(NZ)])
@@ -262,7 +268,9 @@
 
 def attended_kernel(order, a0, a1, a2, a3, out):
     del order
-    parts = [a[...].astype(jnp.float32) for a in (a0, a1, a2, a3)]
+    wide = out.shape[2]
+    parts = [a[...].astype(jnp.float32) for a in (a0, a1, a2)]
+    parts.append(a3[:, :, wide:].astype(jnp.float32))
     out[...] = ((parts[0] + parts[1]) + (parts[2] + parts[3])).astype(out.dtype)
 
 
@@ -302,7 +310,7 @@
         out[:, :, wide:] = right[...]
 
 
-def far_kernel(left, right, out, sems):
+def far_kernel(left, right, out, done, sems):
     wide = left.shape[2]
     copies = [
         pltpu.make_async_copy(left, out.at[:, :, :wide], sems.at[0]),
@@ -310,6 +318,7 @@
     ]
     for copy in copies:
         copy.start()
+    done[...] = jnp.zeros_like(done)
     for copy in copies:
         copy.wait()
 
@@ -331,9 +340,9 @@
     block = jax.ShapeDtypeStruct((1, tok, 2 * wide), keys.dtype)
     far = pl.pallas_call(
         far_kernel,
-        out_shape=[block],
+        out_shape=[block, jax.ShapeDtypeStruct((8, 128), jnp.float32)],
         in_specs=[FAR] * 2,
-        out_specs=[VMEM],
+        out_specs=[VMEM] * 2,
         scratch_shapes=[pltpu.SemaphoreType.DMA((2,))],
         compiler_params=ALONE,
     )(queries, grad_out)
@@ -343,7 +352,7 @@
         in_specs=[VMEM] * 3,
         out_specs=VMEM,
         compiler_params=PARAMS,
-    )(keys, values, far[0])
+    )(keys, values, far[1])
     asked, *near = pl.pallas_call(
         join_kernel,
         out_shape=[block] * (NY - 1),
@@ -378,10 +387,11 @@
     stats = lax.all_to_all(stats, "y", 0, 0, tiled=True)
     *sent, dmine, dother = pl.pallas_call(
         functools.partial(backward_kernel, heads),
-        out_shape=[shape(queries.shape, bf16)] * (2 * NY)
+        out_shape=[shape(queries.shape, bf16)] * (NY + 1)
+        + [shape(asked.shape, bf16), shape(queries.shape, bf16)]
         + [shape(mine.shape, f32), shape(mine.shape, bf16)],
         in_specs=[SMEM] + [VMEM] * (NY + 4),
-        out_specs=[VMEM] * (2 * NY + 2),
+        out_specs=[VMEM] * (2 * NY + 1),
         scratch_shapes=[
             pltpu.VMEM((2 * NZ, tok, 2 * width), f32),
             pltpu.VMEM((width, NY * cols), f32),
@@ -389,7 +399,7 @@
         ],
         compiler_params=PARAMS,
     )(info, *asks, u, pairs, turned, stats)
-    seen, sent = sent[:NY], sent[NY:]
+    seen, sent = {0: sent[0], 1: sent[1], 3: sent[2]}, sent[3:]
     back = [sent[0]] + [turn(sent[k], "y", NY, k) for k in range(1, NY)]
     from_core = turn(dother, "core", NC, 1)
     pair = (dmine + from_core.astype(f32)).astype(bf16)
@@ -406,7 +416,7 @@
         compiler_params=PARAMS,
     )(*back, pieces)
     squares = lax.all_to_all(squares, ("z", "core"), 0, 0, tiled=True)
-    home = [seen[0]] + [turn(seen[k], "y", NY, k) for k in range(1, NY)]
+    home = [seen[0]] + [turn(seen[k], "y", NY, k) for k in (1, 3)] + [back[2]]
     ndata = lax.axis_size("dp")
     squares = pl.pallas_call(
         fold_kernel,

time: 134 us -> 137 us (1.022)
  waiting for transfers between devices: 11.7 us -> 24.3 us
  starting transfers between devices: 60.8 us -> 55.6 us
  blocking collectives: 43.3 us -> 41 us
  Pallas kernels: 12 us -> 10.5 us
    ppermute x11 -> x10, waiting for transfers between devices: 2.5 us -> 15.2 us  [turn(): return lax.ppermute(x, axis, [(i, (i + by) % size) for i in range(size)])]
    ppermute x11 -> x10, starting transfers between devices: 45.6 us -> 38.6 us  [turn(): return lax.ppermute(x, axis, [(i, (i + by) % size) for i in range(size)])]
    all_to_all x1, blocking collectives: 16.4 us -> 14.3 us  [per_device(): squares = lax.all_to_all(squares, ('z', 'core'), 0, 0, tiled=True)]
    all_to_all x1, starting transfers between devices: 5.07 us -> 6.79 us  [per_device(): pieces = lax.all_to_all(pair, 'z', 0, 0, tiled=True)]
  transfers between devices with their start and end apart: 13 -> 12, of which waited for: 3 -> 5; matrix products, arithmetic and copies ran while one was open for 1% -> 1% of each run, Pallas kernels for 2% -> 2%
where the time goes in v9:
time: 137 us; the launch traced here: 136 us
  starting transfers between devices  55.6 us (41%)
  blocking collectives  41 us (30%)
  waiting for transfers between devices  24.3 us (18%)
  Pallas kernels  10.5 us (8%)
  local copies, waits for them, and re-layouts  2.19 us (2%)
  other arithmetic  1.54 us (1%)
    ppermute x10, starting transfers between devices, turn(): return lax.ppermute(x, axis, [(i, (i + by) % size) for i in range(size)])  38.6 us
    all_to_all x1, blocking collectives, per_device(): squares = lax.all_to_all(squares, ('y', 'dp'), 0, 0, tiled=True)  17.3 us
    ppermute x10, waiting for transfers between devices, turn(): return lax.ppermute(x, axis, [(i, (i + by) % size) for i in range(size)])  15.2 us
    all_to_all x1, blocking collectives, per_device(): squares = lax.all_to_all(squares, ('z', 'core'), 0, 0, tiled=True)  14.3 us
    all_to_all x1, starting transfers between devices, per_device(): mine = lax.all_to_all(copies, 'z', 0, 0, tiled=True)  10.2 us
    all_to_all x1, blocking collectives, per_device(): stats = lax.all_to_all(stats, 'y', 0, 0, tiled=True)  9.43 us
    all_to_all x1, waiting for transfers between devices, per_device(): mine = lax.all_to_all(copies, 'z', 0, 0, tiled=True)  9.15 us
    all_to_all x1, starting transfers between devices, per_device(): pieces = lax.all_to_all(pair, 'z', 0, 0, tiled=True)  6.79 us
  transfers between devices with their start and end apart: 12, of which 5 were waited for; matrix products, arithmetic and copies ran while one was open for 1% of the time, Pallas kernels for 2%

profile of v9, /device:TPU:1, one launch (start us, length us, event | category | flops | bytes accessed | tf_op | source)
XLA Modules:
  0.0 136.0 jit_solution(4090741646817434057)
XLA Ops:
  0.6 0.0 copy-start.3
  0.6 0.0 copy-start.2
  0.7 1.7 %shard_map.85 = (bf16[1,128,1024]{2,1,0:T(8,128)(2,1)}, f32[8,128]{1,0:T(8,128)}) custom-call(bf16[1,128,512]{2,1,0:T(8,128)(2,1)} %left.3, bf16[1,128,512]{2,1,0:T(8,128)(2,1)} %right.3), custom_call_target="tpu_custom_call" | custom-call | tf_op jit(solution)/shard_map/pallas_call | solution.py:341
  2.4 8.3 %collective-permute-start.1 = (bf16[1,128,1024]{2,1,0:T(8,128)(2,1)}, bf16[1,128,1024]{2,1,0:T(8,128)(2,1)S(1)}, u32[]{:S(2)}, u32[]{:S(2)}) collective-permute-start(bf16[1,128,1024]{2,1,0:T(8,128)(2,1)} %get-tuple-element.31), channel_id=1, source_target_pairs={{0,32},{16,48},{32,0},{48,16},{1,33},{17,49},{33,1},{49,17},{2,34}... | collective-permute-start | bytes 786440 | tf_op jit(solution)/shard_map/ppermute | solution.py:327
  10.6 0.0 copy-done.3
  10.7 0.0 copy-done.2
  10.7 0.0 copy-start.4
  10.7 0.7 copy-done.4
  11.4 0.9 shard_map.86
  12.2 0.0 copy-start
  12.2 0.0 copy-start.1
  12.2 10.2 %all-to-all-start = ((bf16[8,128,256]{2,1,0:T(8,128)(2,1)}), bf16[8,128,256]{2,1,0:T(8,128)(2,1)S(1)}, u32[]{:S(2)}, u32[]{:S(2)}) async-start(bf16[8,128,256]{2,1,0:T(8,128)(2,1)} %shard_map.86), calls=%async_computation | async-start | bytes 1048576 | tf_op jit(solution)/shard_map/all_to_all | solution.py:363
  22.4 0.0 copy-done
  22.4 0.0 copy-done.1
  22.4 0.1 shard_map.84
  22.5 2.0 %collective-permute-start = (bf16[1,128,1024]{2,1,0:T(8,128)(2,1)S(1)}, bf16[1,128,1024]{2,1,0:T(8,128)(2,1)S(1)}, u32[]{:S(2)}, u32[]{:S(2)}) collective-permute-start(bf16[1,128,1024]{2,1,0:T(8,128)(2,1)S(1)} %get-tuple-element.30), channel_id=1, source_target_pairs={{0,48},{16,0},{32,16},{48,32},{1,49},{17,1},{33,17},{49,33},{2,50}... | collective-permute-start | bytes 786440 | tf_op jit(solution)/shard_map/ppermute | solution.py:327
  24.4 4.2 %collective-permute-start.2 = (bf16[1,128,1024]{2,1,0:T(8,128)(2,1)S(1)}, bf16[1,128,1024]{2,1,0:T(8,128)(2,1)S(1)}, u32[]{:S(2)}, u32[]{:S(2)}) collective-permute-start(bf16[1,128,1024]{2,1,0:T(8,128)(2,1)S(1)} %get-tuple-element.32), channel_id=1, source_target_pairs={{0,16},{16,32},{32,48},{48,0},{1,17},{17,33},{33,49},{49,1},{2,18}... | collective-permute-start | bytes 786440 | tf_op jit(solution)/shard_map/ppermute | solution.py:327
  28.7 0.0 copy-start.5
  28.7 0.6 copy-done.5
  29.4 0.1 eq.26
  29.5 0.1 eq.25
  29.5 0.1 add.218
  29.6 0.1 add.215
  29.7 0.2 select_reduce_fusion
  29.9 0.1 reshape.443
  30.0 0.1 reduce_min.11
  30.1 0.1 select_reduce_fusion.1
  30.3 9.1 %all-to-all-done.mine = bf16[8,128,256]{2,1,0:T(8,128)(2,1)S(1)} async-done(((bf16[8,128,256]{2,1,0:T(8,128)(2,1)}), bf16[8,128,256]{2,1,0:T(8,128)(2,1)S(1)}, u32[]{:S(2)}, u32[]{:S(2)}) %all-to-all-start) | async-done | bytes 524320 | tf_op jit(solution)/shard_map/all_to_all | solution.py:363
  39.4 3.3 %collective-permute-start.3 = (bf16[8,128,256]{2,1,0:T(8,128)(2,1)S(1)}, bf16[8,128,256]{2,1,0:T(8,128)(2,1)S(1)}, u32[]{:S(2)}, u32[]{:S(2)}) collective-permute-start(bf16[8,128,256]{2,1,0:T(8,128)(2,1)S(1)} %all-to-all-done.mine), channel_id=1, source_target_pairs={{0,8},{8,0},{1,9},{9,1},{2,10},{10,2},{3,11},{11,3},{4,12},{12,4},... | collective-permute-start | bytes 1572872 | tf_op jit(solution)/shard_map/ppermute | solution.py:327
  42.8 0.1 copy.13
  42.9 0.1 reshape.444
  43.0 0.1 add.220
  43.1 0.1 copy.14
  43.1 0.1 reshape.445
  43.2 0.1 pad_add_fusion.2.info
  43.3 1.0 collective-permute-done.3.other
  44.3 0.3 shard_map.87
  44.6 0.0 collective-permute-done.1.a2
  44.6 0.0 collective-permute-done.a1
  44.6 0.0 collective-permute-done.2.a3
  44.6 2.4 %shard_map.88 = (f32[2,128,1024]{2,1,0:T(8,128)S(1)}, f32[4,3,8,256]{3,2,1,0:T(8,128)S(1)}) custom-call(s32[34]{0:T(128)S(1)} %pad_add_fusion.2.info, bf16[1,128,1024]{2,1,0:T(8,128)(2,1)S(1)} %get-tuple-element.29.a0, bf16[1,128,1024]{2,1,0:T(8,128)(2,1)S(1)} %collective-permute-done.a1, bf16[1,128,1024]{2,1,0:T(8,128)(2,1)S(1)} %collective-permute-done.1.a2, ...), custom_call_target="tpu_custom_call" | custom-call | tf_op jit(solution)/shard_map/pallas_call | solution.py:379
  47.0 9.4 %all_to_all.25.stats = f32[4,3,8,256]{3,2,1,0:T(8,128)S(1)} all-to-all(f32[4,3,8,256]{3,2,1,0:T(8,128)S(1)} %get-tuple-element.37), channel_id=1, replica_groups=mesh['z'=8,'y'=4,'core'=2,'dp'=8] {'y'}, dimensions={0} | all-to-all | bytes 196608 | tf_op jit(solution)/shard_map/all_to_all | solution.py:387
  56.5 3.3 %shard_map.89 = (bf16[1,128,512]{2,1,0:T(8,128)(2,1)S(1)}, bf16[1,128,512]{2,1,0:T(8,128)(2,1)S(1)}, bf16[1,128,512]{2,1,0:T(8,128)(2,1)S(1)}, bf16[1,128,512]{2...) custom-call(s32[34]{0:T(128)S(1)} %pad_add_fusion.2.info, ...), custom_call_target="tpu_custom_call" | custom-call | tf_op jit(solution)/shard_map/pallas_call | solution.py:388
  59.8 4.2 %collective-permute-start.7 = (bf16[8,128,256]{2,1,0:T(8,128)(2,1)S(1)}, bf16[8,128,256]{2,1,0:T(8,128)(2,1)S(1)}, u32[]{:S(2)}, u32[]{:S(2)}) collective-permute-start(bf16[8,128,256]{2,1,0:T(8,128)(2,1)S(1)} %get-tuple-element.43), channel_id=1, source_target_pairs={{0,8},{8,0},{1,9},{9,1},{2,10},{10,2},{3,11},{11,3},{4,12},{12,4},... | collective-permute-start | bytes 1572872 | tf_op jit(solution)/shard_map/ppermute | solution.py:327
  64.0 1.5 %collective-permute-done.7 = bf16[8,128,256]{2,1,0:T(8,128)(2,1)S(1)} collective-permute-done((bf16[8,128,256]{2,1,0:T(8,128)(2,1)S(1)}, bf16[8,128,256]{2,1,0:T(8,128)(2,1)S(1)}, u32[]{:S(2)}, u32[]{:S(2)}) %collective-permute-start.7) | collective-permute-done | bytes 524320 | tf_op jit(solution)/shard_map/ppermute | solution.py:327
  65.5 0.9 add_convert_fusion
  66.4 6.8 %all-to-all-start.2 = ((bf16[8,128,256]{2,1,0:T(8,128)(2,1)}), bf16[8,128,256]{2,1,0:T(8,128)(2,1)S(1)}, u32[]{:S(2)}, u32[]{:S(2)}) async-start(bf16[8,128,256]{2,1,0:T(8,128)(2,1)} %add_convert_fusion), calls=%async_computation.2 | async-start | bytes 1048576 | tf_op jit(solution)/shard_map/all_to_all | solution.py:406
  73.2 1.9 %collective-permute-start.5 = (bf16[1,128,1024]{2,1,0:T(8,128)(2,1)S(1)}, bf16[1,128,1024]{2,1,0:T(8,128)(2,1)S(1)}, u32[]{:S(2)}, u32[]{:S(2)}) collective-permute-start(bf16[1,128,1024]{2,1,0:T(8,128)(2,1)S(1)} %get-tuple-element.40), channel_id=1, source_target_pairs={{0,32},{16,48},{32,0},{48,16},{1,33},{17,49},{33,1},{49,17},{2,34}... | collective-permute-start | bytes 786440 | tf_op jit(solution)/shard_map/ppermute | solution.py:327
  75.2 3.9 %collective-permute-start.4 = (bf16[1,128,512]{2,1,0:T(8,128)(2,1)S(1)}, bf16[1,128,512]{2,1,0:T(8,128)(2,1)S(1)}, u32[]{:S(2)}, u32[]{:S(2)}) collective-permute-start(bf16[1,128,512]{2,1,0:T(8,128)(2,1)S(1)} %get-tuple-element.39), channel_id=1, source_target_pairs={{0,16},{16,32},{32,48},{48,0},{1,17},{17,33},{33,49},{49,1},{2,18}... | collective-permute-start | bytes 393224 | tf_op jit(solution)/shard_map/ppermute | solution.py:327
  79.1 3.5 %collective-permute-start.6 = (bf16[1,128,512]{2,1,0:T(8,128)(2,1)S(1)}, bf16[1,128,512]{2,1,0:T(8,128)(2,1)S(1)}, u32[]{:S(2)}, u32[]{:S(2)}) collective-permute-start(bf16[1,128,512]{2,1,0:T(8,128)(2,1)S(1)} %get-tuple-element.41), channel_id=1, source_target_pairs={{0,48},{16,0},{32,16},{48,32},{1,49},{17,1},{33,17},{49,33},{2,50}... | collective-permute-start | bytes 393224 | tf_op jit(solution)/shard_map/ppermute | solution.py:327
  82.6 4.0 %collective-permute-start.8 = (bf16[1,128,512]{2,1,0:T(8,128)(2,1)S(1)}, bf16[1,128,512]{2,1,0:T(8,128)(2,1)S(1)}, u32[]{:S(2)}, u32[]{:S(2)}) collective-permute-start(bf16[1,128,512]{2,1,0:T(8,128)(2,1)S(1)} %get-tuple-element.49), channel_id=1, source_target_pairs={{0,16},{16,32},{32,48},{48,0},{1,17},{17,33},{33,49},{49,1},{2,18}... | collective-permute-start | bytes 393224 | tf_op jit(solution)/shard_map/ppermute | solution.py:327
  86.6 3.4 %collective-permute-start.9 = (bf16[1,128,512]{2,1,0:T(8,128)(2,1)S(1)}, bf16[1,128,512]{2,1,0:T(8,128)(2,1)S(1)}, u32[]{:S(2)}, u32[]{:S(2)}) collective-permute-start(bf16[1,128,512]{2,1,0:T(8,128)(2,1)S(1)} %get-tuple-element.50), channel_id=1, source_target_pairs={{0,48},{16,0},{32,16},{48,32},{1,49},{17,1},{33,17},{49,33},{2,50}... | collective-permute-start | bytes 393224 | tf_op jit(solution)/shard_map/ppermute | solution.py:327
  90.0 1.6 %collective-permute-done.4.o1 = bf16[1,128,512]{2,1,0:T(8,128)(2,1)S(1)} collective-permute-done((bf16[1,128,512]{2,1,0:T(8,128)(2,1)S(1)}, bf16[1,128,512]{2,1,0:T(8,128)(2,1)S(1)}, u32[]{:S(2)}, u32[]{:S(2)}) %collective-permute-start.4) | collective-permute-done | bytes 131104 | tf_op jit(solution)/shard_map/ppermute | solution.py:327
  91.5 11.1 %collective-permute-done.6.o3 = bf16[1,128,512]{2,1,0:T(8,128)(2,1)S(1)} collective-permute-done((bf16[1,128,512]{2,1,0:T(8,128)(2,1)S(1)}, bf16[1,128,512]{2,1,0:T(8,128)(2,1)S(1)}, u32[]{:S(2)}, u32[]{:S(2)}) %collective-permute-start.6) | collective-permute-done | bytes 131104 | tf_op jit(solution)/shard_map/ppermute | solution.py:327
  102.6 0.0 collective-permute-done.5.o2.a3
  102.6 0.0 all-to-all-done.2.dkv
  102.6 0.3 shard_map.90
  103.0 14.3 %all_to_all.26.parts = f32[16,1,128]{2,1,0:T(1,128)S(1)} all-to-all(f32[16,1,128]{2,1,0:T(1,128)S(1)} %get-tuple-element.44), channel_id=1, replica_groups=mesh['z'=8,'y'=4,'core'=2,'dp'=8] {'z','core'}, dimensions={0} | all-to-all | bytes 16384 | tf_op jit(solution)/shard_map/all_to_all | solution.py:418
  117.3 17.3 %all_to_all.27.sums = f32[32,1,128]{2,1,0:T(1,128)S(1)} all-to-all(f32[32,1,128]{2,1,0:T(1,128)S(1)} %shard_map.91), channel_id=1, replica_groups=mesh['z'=8,'y'=4,'core'=2,'dp'=8] {'y','dp'}, dimensions={0} | all-to-all | bytes 32768 | tf_op jit(solution)/shard_map/all_to_all | solution.py:428
  134.6 0.7 shard_map.92
  135.3 0.0 collective-permute-done.8.a1
  135.3 0.0 collective-permute-done.9.a2
  135.3 0.7 shard_map.93
  (11 shorter events, 0.1 us)
Async XLA Ops:
  0.6 10.0 %copy-start.3 = (bf16[1,128,128]{2,1,0:T(8,128)(2,1)S(1)}, bf16[1,128,128]{2,1,0:T(8,128)(2,1)}, u32[]{:S(2)}) copy-start(bf16[1,128,128]{2,1,0:T(8,128)(2,1)} %values.1) | copy-start | bytes 98308
  0.6 10.0 %copy-start.2 = (bf16[1,128,128]{2,1,0:T(8,128)(2,1)S(1)}, bf16[1,128,128]{2,1,0:T(8,128)(2,1)}, u32[]{:S(2)}) copy-start(bf16[1,128,128]{2,1,0:T(8,128)(2,1)} %keys.1) | copy-start | bytes 98308
  2.4 42.3 %collective-permute-start.1 = (bf16[1,128,1024]{2,1,0:T(8,128)(2,1)}, bf16[1,128,1024]{2,1,0:T(8,128)(2,1)S(1)}, u32[]{:S(2)}, u32[]{:S(2)}) collective-permute-start(bf16[1,128,1024]{2,1,0:T(8,128)(2,1)} %get-tuple-element.31), channel_id=1, source_target_pairs={{0,32},{16,48},{32,0},{48,16},{1,33},{17,49},{33,1},{49,17},{2,34}... | collective-permute-start | bytes 786440 | tf_op jit(solution)/shard_map/ppermute | solution.py:327
  10.7 0.7 copy-start.4
  12.2 10.2 %copy-start = (bf16[1,128,512]{2,1,0:T(8,128)(2,1)S(1)}, bf16[1,128,512]{2,1,0:T(8,128)(2,1)}, u32[]{:S(2)}) copy-start(bf16[1,128,512]{2,1,0:T(8,128)(2,1)} %left.3) | copy-start | bytes 393220
  12.2 10.2 %copy-start.1 = (bf16[1,128,512]{2,1,0:T(8,128)(2,1)S(1)}, bf16[1,128,512]{2,1,0:T(8,128)(2,1)}, u32[]{:S(2)}) copy-start(bf16[1,128,512]{2,1,0:T(8,128)(2,1)} %right.3) | copy-start | bytes 393220
  12.2 27.2 %all-to-all-start = ((bf16[8,128,256]{2,1,0:T(8,128)(2,1)}), bf16[8,128,256]{2,1,0:T(8,128)(2,1)S(1)}, u32[]{:S(2)}, u32[]{:S(2)}) async-start(bf16[8,128,256]{2,1,0:T(8,128)(2,1)} %shard_map.86), calls=%async_computation | async-start | bytes 1048576 | tf_op jit(solution)/shard_map/all_to_all | solution.py:363
  22.5 22.2 %collective-permute-start = (bf16[1,128,1024]{2,1,0:T(8,128)(2,1)S(1)}, bf16[1,128,1024]{2,1,0:T(8,128)(2,1)S(1)}, u32[]{:S(2)}, u32[]{:S(2)}) collective-permute-start(bf16[1,128,1024]{2,1,0:T(8,128)(2,1)S(1)} %get-tuple-element.30), channel_id=1, source_target_pairs={{0,48},{16,0},{32,16},{48,32},{1,49},{17,1},{33,17},{49,33},{2,50}... | collective-permute-start | bytes 786440 | tf_op jit(solution)/shard_map/ppermute | solution.py:327
  24.4 20.2 %collective-permute-start.2 = (bf16[1,128,1024]{2,1,0:T(8,128)(2,1)S(1)}, bf16[1,128,1024]{2,1,0:T(8,128)(2,1)S(1)}, u32[]{:S(2)}, u32[]{:S(2)}) collective-permute-start(bf16[1,128,1024]{2,1,0:T(8,128)(2,1)S(1)} %get-tuple-element.32), channel_id=1, source_target_pairs={{0,16},{16,32},{32,48},{48,0},{1,17},{17,33},{33,49},{49,1},{2,18}... | collective-permute-start | bytes 786440 | tf_op jit(solution)/shard_map/ppermute | solution.py:327
  28.7 0.7 copy-start.5
  39.4 4.8 %collective-permute-start.3 = (bf16[8,128,256]{2,1,0:T(8,128)(2,1)S(1)}, bf16[8,128,256]{2,1,0:T(8,128)(2,1)S(1)}, u32[]{:S(2)}, u32[]{:S(2)}) collective-permute-start(bf16[8,128,256]{2,1,0:T(8,128)(2,1)S(1)} %all-to-all-done.mine), channel_id=1, source_target_pairs={{0,8},{8,0},{1,9},{9,1},{2,10},{10,2},{3,11},{11,3},{4,12},{12,4},... | collective-permute-start | bytes 1572872 | tf_op jit(solution)/shard_map/ppermute | solution.py:327
  59.8 5.7 %collective-permute-start.7 = (bf16[8,128,256]{2,1,0:T(8,128)(2,1)S(1)}, bf16[8,128,256]{2,1,0:T(8,128)(2,1)S(1)}, u32[]{:S(2)}, u32[]{:S(2)}) collective-permute-start(bf16[8,128,256]{2,1,0:T(8,128)(2,1)S(1)} %get-tuple-element.43), channel_id=1, source_target_pairs={{0,8},{8,0},{1,9},{9,1},{2,10},{10,2},{3,11},{11,3},{4,12},{12,4},... | collective-permute-start | bytes 1572872 | tf_op jit(solution)/shard_map/ppermute | solution.py:327
  66.4 36.2 %all-to-all-start.2 = ((bf16[8,128,256]{2,1,0:T(8,128)(2,1)}), bf16[8,128,256]{2,1,0:T(8,128)(2,1)S(1)}, u32[]{:S(2)}, u32[]{:S(2)}) async-start(bf16[8,128,256]{2,1,0:T(8,128)(2,1)} %add_convert_fusion), calls=%async_computation.2 | async-start | bytes 1048576 | tf_op jit(solution)/shard_map/all_to_all | solution.py:406
  73.2 29.4 %collective-permute-start.5 = (bf16[1,128,1024]{2,1,0:T(8,128)(2,1)S(1)}, bf16[1,128,1024]{2,1,0:T(8,128)(2,1)S(1)}, u32[]{:S(2)}, u32[]{:S(2)}) collective-permute-start(bf16[1,128,1024]{2,1,0:T(8,128)(2,1)S(1)} %get-tuple-element.40), channel_id=1, source_target_pairs={{0,32},{16,48},{32,0},{48,16},{1,33},{17,49},{33,1},{49,17},{2,34}... | collective-permute-start | bytes 786440 | tf_op jit(solution)/shard_map/ppermute | solution.py:327
  75.2 16.4 %collective-permute-start.4 = (bf16[1,128,512]{2,1,0:T(8,128)(2,1)S(1)}, bf16[1,128,512]{2,1,0:T(8,128)(2,1)S(1)}, u32[]{:S(2)}, u32[]{:S(2)}) collective-permute-start(bf16[1,128,512]{2,1,0:T(8,128)(2,1)S(1)} %get-tuple-element.39), channel_id=1, source_target_pairs={{0,16},{16,32},{32,48},{48,0},{1,17},{17,33},{33,49},{49,1},{2,18}... | collective-permute-start | bytes 393224 | tf_op jit(solution)/shard_map/ppermute | solution.py:327
  79.1 23.5 %collective-permute-start.6 = (bf16[1,128,512]{2,1,0:T(8,128)(2,1)S(1)}, bf16[1,128,512]{2,1,0:T(8,128)(2,1)S(1)}, u32[]{:S(2)}, u32[]{:S(2)}) collective-permute-start(bf16[1,128,512]{2,1,0:T(8,128)(2,1)S(1)} %get-tuple-element.41), channel_id=1, source_target_pairs={{0,48},{16,0},{32,16},{48,32},{1,49},{17,1},{33,17},{49,33},{2,50}... | collective-permute-start | bytes 393224 | tf_op jit(solution)/shard_map/ppermute | solution.py:327
  82.6 52.7 %collective-permute-start.8 = (bf16[1,128,512]{2,1,0:T(8,128)(2,1)S(1)}, bf16[1,128,512]{2,1,0:T(8,128)(2,1)S(1)}, u32[]{:S(2)}, u32[]{:S(2)}) collective-permute-start(bf16[1,128,512]{2,1,0:T(8,128)(2,1)S(1)} %get-tuple-element.49), channel_id=1, source_target_pairs={{0,16},{16,32},{32,48},{48,0},{1,17},{17,33},{33,49},{49,1},{2,18}... | collective-permute-start | bytes 393224 | tf_op jit(solution)/shard_map/ppermute | solution.py:327
  86.6 48.8 %collective-permute-start.9 = (bf16[1,128,512]{2,1,0:T(8,128)(2,1)S(1)}, bf16[1,128,512]{2,1,0:T(8,128)(2,1)S(1)}, u32[]{:S(2)}, u32[]{:S(2)}) collective-permute-start(bf16[1,128,512]{2,1,0:T(8,128)(2,1)S(1)} %get-tuple-element.50), channel_id=1, source_target_pairs={{0,48},{16,0},{32,16},{48,32},{1,49},{17,1},{33,17},{49,33},{2,50}... | collective-permute-start | bytes 393224 | tf_op jit(solution)/shard_map/ppermute | solution.py:327

commit v10 on v9

--- a/solution.py
+++ b/solution.py
@@ -266,6 +266,12 @@
     sq_ref[...] = jnp.full(sq_ref.shape, squares, jnp.float32)
 
 
+def release_kernel(order, a1, a3, b1, b3):
+    del order
+    b1[...] = a1[...]
+    b3[...] = a3[...]
+
+
 def attended_kernel(order, a0, a1, a2, a3, out):
     del order
     wide = out.shape[2]
@@ -415,8 +421,15 @@
         out_specs=[VMEM] * 3,
         compiler_params=PARAMS,
     )(*back, pieces)
+    near1, near3 = pl.pallas_call(
+        release_kernel,
+        out_shape=[shape(queries.shape, bf16)] * 2,
+        in_specs=[VMEM] * 3,
+        out_specs=[VMEM] * 2,
+        compiler_params=PARAMS,
+    )(squares, seen[1], seen[3])
     squares = lax.all_to_all(squares, ("z", "core"), 0, 0, tiled=True)
-    home = [seen[0]] + [turn(seen[k], "y", NY, k) for k in (1, 3)] + [back[2]]
+    home = [seen[0], turn(near1, "y", NY, 1), turn(near3, "y", NY, 3), back[2]]
     ndata = lax.axis_size("dp")
     squares = pl.pallas_call(
         fold_kernel,
@@ -424,6 +437,7 @@
         in_specs=[VMEM],
         out_specs=VMEM,
         compiler_params=PARAMS,
+        cost_estimate=pl.CostEstimate(flops=10**9, transcendentals=0, bytes_accessed=0),
     )(squares)
     squares = lax.all_to_all(squares, ("y", "dp"), 0, 0, tiled=True)
     count = float(ndata * NZ * NY * NC * tok * (wide + 2 * width))

time: 137 us -> 132 us (0.964)
  blocking collectives: 41 us -> 22.9 us
  starting transfers between devices: 55.6 us -> 60.5 us
  waiting for transfers between devices: 24.3 us -> 29.2 us
  Pallas kernels: 10.5 us -> 13.5 us
    all_to_all x1 -> x0, blocking collectives: 14.3 us -> none  [per_device(): squares = lax.all_to_all(squares, ('z', 'core'), 0, 0, tiled=True)]
    all_to_all x0 -> x1, starting transfers between devices: none -> 7.43 us  [per_device(): squares = lax.all_to_all(squares, ('z', 'core'), 0, 0, tiled=True)]
    ppermute x10, waiting for transfers between devices: 15.2 us -> 20.1 us  [turn(): return lax.ppermute(x, axis, [(i, (i + by) % size) for i in range(size)])]
    all_to_all x1, blocking collectives: 17.3 us -> 13.4 us  [per_device(): squares = lax.all_to_all(squares, ('y', 'dp'), 0, 0, tiled=True)]
    all_to_all x1, starting transfers between devices: 6.79 us -> 4.44 us  [per_device(): pieces = lax.all_to_all(pair, 'z', 0, 0, tiled=True)]
  transfers between devices with their start and end apart: 12 -> 13, of which waited for: 5 -> 5; matrix products, arithmetic and copies ran while one was open for 1% -> 1% of each run, Pallas kernels for 2% -> 2%
where the time goes in v10:
time: 132 us; the launch traced here: 131 us
  starting transfers between devices  60.5 us (46%)
  waiting for transfers between devices  29.2 us (22%)
  blocking collectives  22.9 us (17%)
  Pallas kernels  13.5 us (10%)
  local copies, waits for them, and re-layouts  2.19 us (2%)
  other arithmetic  1.55 us (1%)
    ppermute x10, starting transfers between devices, turn(): return lax.ppermute(x, axis, [(i, (i + by) % size) for i in range(size)])  38.5 us
    ppermute x10, waiting for transfers between devices, turn(): return lax.ppermute(x, axis, [(i, (i + by) % size) for i in range(size)])  20.1 us
    all_to_all x1, blocking collectives, per_device(): squares = lax.all_to_all(squares, ('y', 'dp'), 0, 0, tiled=True)  13.4 us
    all_to_all x1, starting transfers between devices, per_device(): mine = lax.all_to_all(copies, 'z', 0, 0, tiled=True)  10.2 us
    all_to_all x1, blocking collectives, per_device(): stats = lax.all_to_all(stats, 'y', 0, 0, tiled=True)  9.53 us
    all_to_all x1, waiting for transfers between devices, per_device(): mine = lax.all_to_all(copies, 'z', 0, 0, tiled=True)  9.15 us
    all_to_all x1, starting transfers between devices, per_device(): squares = lax.all_to_all(squares, ('z', 'core'), 0, 0, tiled=True)  7.43 us
    all_to_all x1, starting transfers between devices, per_device(): pieces = lax.all_to_all(pair, 'z', 0, 0, tiled=True)  4.44 us
  transfers between devices with their start and end apart: 13, of which 5 were waited for; matrix products, arithmetic and copies ran while one was open for 1% of the time, Pallas kernels for 2%

profile of v10, /device:TPU:1, one launch (start us, length us, event | category | flops | bytes accessed | tf_op | source)
XLA Modules:
  0.0 130.8 jit_solution(3473628756205908126)
XLA Ops:
  0.6 0.0 copy-start.3
  0.6 0.0 copy-start.2
  0.7 1.7 %shard_map.85 = (bf16[1,128,1024]{2,1,0:T(8,128)(2,1)}, f32[8,128]{1,0:T(8,128)}) custom-call(bf16[1,128,512]{2,1,0:T(8,128)(2,1)} %left.3, bf16[1,128,512]{2,1,0:T(8,128)(2,1)} %right.3), custom_call_target="tpu_custom_call" | custom-call | tf_op jit(solution)/shard_map/pallas_call | solution.py:347
  2.3 8.3 %collective-permute-start.1 = (bf16[1,128,1024]{2,1,0:T(8,128)(2,1)}, bf16[1,128,1024]{2,1,0:T(8,128)(2,1)S(1)}, u32[]{:S(2)}, u32[]{:S(2)}) collective-permute-start(bf16[1,128,1024]{2,1,0:T(8,128)(2,1)} %get-tuple-element.33), channel_id=1, source_target_pairs={{0,32},{16,48},{32,0},{48,16},{1,33},{17,49},{33,1},{49,17},{2,34}... | collective-permute-start | bytes 786440 | tf_op jit(solution)/shard_map/ppermute | solution.py:333
  10.6 0.0 copy-done.3
  10.6 0.0 copy-done.2
  10.7 0.0 copy-start.4
  10.7 0.7 copy-done.4
  11.3 0.9 shard_map.86
  12.2 0.0 copy-start
  12.2 10.2 %all-to-all-start = ((bf16[8,128,256]{2,1,0:T(8,128)(2,1)}), bf16[8,128,256]{2,1,0:T(8,128)(2,1)S(1)}, u32[]{:S(2)}, u32[]{:S(2)}) async-start(bf16[8,128,256]{2,1,0:T(8,128)(2,1)} %shard_map.86), calls=%async_computation | async-start | bytes 1048576 | tf_op jit(solution)/shard_map/all_to_all | solution.py:369
  22.4 0.0 copy-done
  22.4 0.0 copy-done.1
  22.4 0.1 shard_map.84
  22.5 2.0 %collective-permute-start = (bf16[1,128,1024]{2,1,0:T(8,128)(2,1)S(1)}, bf16[1,128,1024]{2,1,0:T(8,128)(2,1)S(1)}, u32[]{:S(2)}, u32[]{:S(2)}) collective-permute-start(bf16[1,128,1024]{2,1,0:T(8,128)(2,1)S(1)} %get-tuple-element.32), channel_id=1, source_target_pairs={{0,48},{16,0},{32,16},{48,32},{1,49},{17,1},{33,17},{49,33},{2,50}... | collective-permute-start | bytes 786440 | tf_op jit(solution)/shard_map/ppermute | solution.py:333
  24.4 4.2 %collective-permute-start.2 = (bf16[1,128,1024]{2,1,0:T(8,128)(2,1)S(1)}, bf16[1,128,1024]{2,1,0:T(8,128)(2,1)S(1)}, u32[]{:S(2)}, u32[]{:S(2)}) collective-permute-start(bf16[1,128,1024]{2,1,0:T(8,128)(2,1)S(1)} %get-tuple-element.34), channel_id=1, source_target_pairs={{0,16},{16,32},{32,48},{48,0},{1,17},{17,33},{33,49},{49,1},{2,18}... | collective-permute-start | bytes 786440 | tf_op jit(solution)/shard_map/ppermute | solution.py:333
  28.7 0.0 copy-start.5
  28.7 0.6 copy-done.5
  29.4 0.1 eq.26
  29.5 0.1 eq.25
  29.5 0.1 add.218
  29.6 0.1 add.215
  29.7 0.2 select_reduce_fusion
  29.9 0.1 reshape.443
  30.0 0.1 reduce_min.11
  30.1 0.1 select_reduce_fusion.1
  30.3 9.1 %all-to-all-done.mine = bf16[8,128,256]{2,1,0:T(8,128)(2,1)S(1)} async-done(((bf16[8,128,256]{2,1,0:T(8,128)(2,1)}), bf16[8,128,256]{2,1,0:T(8,128)(2,1)S(1)}, u32[]{:S(2)}, u32[]{:S(2)}) %all-to-all-start) | async-done | bytes 524320 | tf_op jit(solution)/shard_map/all_to_all | solution.py:369
  39.4 3.3 %collective-permute-start.3 = (bf16[8,128,256]{2,1,0:T(8,128)(2,1)S(1)}, bf16[8,128,256]{2,1,0:T(8,128)(2,1)S(1)}, u32[]{:S(2)}, u32[]{:S(2)}) collective-permute-start(bf16[8,128,256]{2,1,0:T(8,128)(2,1)S(1)} %all-to-all-done.mine), channel_id=1, source_target_pairs={{0,8},{8,0},{1,9},{9,1},{2,10},{10,2},{3,11},{11,3},{4,12},{12,4},... | collective-permute-start | bytes 1572872 | tf_op jit(solution)/shard_map/ppermute | solution.py:333
  42.8 0.1 copy.13
  42.9 0.1 reshape.444
  43.0 0.1 add.220
  43.1 0.1 copy.14
  43.1 0.1 reshape.445
  43.2 0.1 pad_add_fusion.2.info
  43.3 1.0 collective-permute-done.3.other
  44.3 0.3 shard_map.87
  44.6 0.0 collective-permute-done.1.a2
  44.6 0.0 collective-permute-done.a1
  44.6 0.0 collective-permute-done.2.a3
  44.6 3.1 %shard_map.88 = (f32[2,128,1024]{2,1,0:T(8,128)S(1)}, f32[4,3,8,256]{3,2,1,0:T(8,128)S(1)}) custom-call(s32[34]{0:T(128)S(1)} %pad_add_fusion.2.info, bf16[1,128,1024]{2,1,0:T(8,128)(2,1)S(1)} %get-tuple-element.31.a0, bf16[1,128,1024]{2,1,0:T(8,128)(2,1)S(1)} %collective-permute-done.a1, bf16[1,128,1024]{2,1,0:T(8,128)(2,1)S(1)} %collective-permute-done.1.a2, ...), custom_call_target="tpu_custom_call" | custom-call | tf_op jit(solution)/shard_map/pallas_call | solution.py:385
  47.7 9.5 %all_to_all.25.stats = f32[4,3,8,256]{3,2,1,0:T(8,128)S(1)} all-to-all(f32[4,3,8,256]{3,2,1,0:T(8,128)S(1)} %get-tuple-element.39), channel_id=1, replica_groups=mesh['z'=8,'y'=4,'core'=2,'dp'=8] {'y'}, dimensions={0} | all-to-all | bytes 196608 | tf_op jit(solution)/shard_map/all_to_all | solution.py:393
  57.2 4.2 %shard_map.89 = (bf16[1,128,512]{2,1,0:T(8,128)(2,1)S(1)}, bf16[1,128,512]{2,1,0:T(8,128)(2,1)S(1)}, bf16[1,128,512]{2,1,0:T(8,128)(2,1)S(1)}, bf16[1,128,512]{2...) custom-call(s32[34]{0:T(128)S(1)} %pad_add_fusion.2.info, ...), custom_call_target="tpu_custom_call" | custom-call | tf_op jit(solution)/shard_map/pallas_call | solution.py:394
  61.5 3.9 %collective-permute-start.7 = (bf16[8,128,256]{2,1,0:T(8,128)(2,1)S(1)}, bf16[8,128,256]{2,1,0:T(8,128)(2,1)S(1)}, u32[]{:S(2)}, u32[]{:S(2)}) collective-permute-start(bf16[8,128,256]{2,1,0:T(8,128)(2,1)S(1)} %get-tuple-element.45), channel_id=1, source_target_pairs={{0,8},{8,0},{1,9},{9,1},{2,10},{10,2},{3,11},{11,3},{4,12},{12,4},... | collective-permute-start | bytes 1572872 | tf_op jit(solution)/shard_map/ppermute | solution.py:333
  65.4 1.5 %collective-permute-done.7 = bf16[8,128,256]{2,1,0:T(8,128)(2,1)S(1)} collective-permute-done((bf16[8,128,256]{2,1,0:T(8,128)(2,1)S(1)}, bf16[8,128,256]{2,1,0:T(8,128)(2,1)S(1)}, u32[]{:S(2)}, u32[]{:S(2)}) %collective-permute-start.7) | collective-permute-done | bytes 524320 | tf_op jit(solution)/shard_map/ppermute | solution.py:333
  66.9 0.9 add_convert_fusion
  67.8 4.4 %all-to-all-start.2 = ((bf16[8,128,256]{2,1,0:T(8,128)(2,1)}), bf16[8,128,256]{2,1,0:T(8,128)(2,1)S(1)}, u32[]{:S(2)}, u32[]{:S(2)}) async-start(bf16[8,128,256]{2,1,0:T(8,128)(2,1)} %add_convert_fusion), calls=%async_computation.2 | async-start | bytes 1048576 | tf_op jit(solution)/shard_map/all_to_all | solution.py:412
  72.3 2.1 %collective-permute-start.5 = (bf16[1,128,1024]{2,1,0:T(8,128)(2,1)S(1)}, bf16[1,128,1024]{2,1,0:T(8,128)(2,1)S(1)}, u32[]{:S(2)}, u32[]{:S(2)}) collective-permute-start(bf16[1,128,1024]{2,1,0:T(8,128)(2,1)S(1)} %get-tuple-element.42), channel_id=1, source_target_pairs={{0,32},{16,48},{32,0},{48,16},{1,33},{17,49},{33,1},{49,17},{2,34}... | collective-permute-start | bytes 786440 | tf_op jit(solution)/shard_map/ppermute | solution.py:333
  74.3 5.2 %collective-permute-start.4 = (bf16[1,128,512]{2,1,0:T(8,128)(2,1)S(1)}, bf16[1,128,512]{2,1,0:T(8,128)(2,1)S(1)}, u32[]{:S(2)}, u32[]{:S(2)}) collective-permute-start(bf16[1,128,512]{2,1,0:T(8,128)(2,1)S(1)} %get-tuple-element.41), channel_id=1, source_target_pairs={{0,16},{16,32},{32,48},{48,0},{1,17},{17,33},{33,49},{49,1},{2,18}... | collective-permute-start | bytes 393224 | tf_op jit(solution)/shard_map/ppermute | solution.py:333
  79.5 2.2 %collective-permute-start.6 = (bf16[1,128,512]{2,1,0:T(8,128)(2,1)S(1)}, bf16[1,128,512]{2,1,0:T(8,128)(2,1)S(1)}, u32[]{:S(2)}, u32[]{:S(2)}) collective-permute-start(bf16[1,128,512]{2,1,0:T(8,128)(2,1)S(1)} %get-tuple-element.43), channel_id=1, source_target_pairs={{0,48},{16,0},{32,16},{48,32},{1,49},{17,1},{33,17},{49,33},{2,50}... | collective-permute-start | bytes 393224 | tf_op jit(solution)/shard_map/ppermute | solution.py:333
  81.7 9.7 %collective-permute-done.4.o1 = bf16[1,128,512]{2,1,0:T(8,128)(2,1)S(1)} collective-permute-done((bf16[1,128,512]{2,1,0:T(8,128)(2,1)S(1)}, bf16[1,128,512]{2,1,0:T(8,128)(2,1)S(1)}, u32[]{:S(2)}, u32[]{:S(2)}) %collective-permute-start.4) | collective-permute-done | bytes 131104 | tf_op jit(solution)/shard_map/ppermute | solution.py:333
  91.4 7.9 %collective-permute-done.6.o3 = bf16[1,128,512]{2,1,0:T(8,128)(2,1)S(1)} collective-permute-done((bf16[1,128,512]{2,1,0:T(8,128)(2,1)S(1)}, bf16[1,128,512]{2,1,0:T(8,128)(2,1)S(1)}, u32[]{:S(2)}, u32[]{:S(2)}) %collective-permute-start.6) | collective-permute-done | bytes 131104 | tf_op jit(solution)/shard_map/ppermute | solution.py:333
  99.3 0.0 collective-permute-done.5.o2.a3
  99.3 0.0 all-to-all-done.2.dkv
  99.3 1.0 shard_map.90
  100.3 7.4 %all-to-all-start.3 = ((f32[16,1,128]{2,1,0:T(1,128)}), f32[16,1,128]{2,1,0:T(1,128)S(1)}, u32[]{:S(2)}, u32[]{:S(2)}) async-start(f32[16,1,128]{2,1,0:T(1,128)} %get-tuple-element.46.order), calls=%async_computation.3 | async-start | bytes 16384 | tf_op jit(solution)/shard_map/all_to_all | solution.py:431
  107.7 0.7 shard_map.93
  108.5 4.3 %collective-permute-start.8 = (bf16[1,128,512]{2,1,0:T(8,128)(2,1)S(1)}, bf16[1,128,512]{2,1,0:T(8,128)(2,1)S(1)}, u32[]{:S(2)}, u32[]{:S(2)}) collective-permute-start(bf16[1,128,512]{2,1,0:T(8,128)(2,1)S(1)} %get-tuple-element.53), channel_id=1, source_target_pairs={{0,16},{16,32},{32,48},{48,0},{1,17},{17,33},{33,49},{49,1},{2,18}... | collective-permute-start | bytes 393224 | tf_op jit(solution)/shard_map/ppermute | solution.py:333
  112.8 3.1 %collective-permute-start.9 = (bf16[1,128,512]{2,1,0:T(8,128)(2,1)S(1)}, bf16[1,128,512]{2,1,0:T(8,128)(2,1)S(1)}, u32[]{:S(2)}, u32[]{:S(2)}) collective-permute-start(bf16[1,128,512]{2,1,0:T(8,128)(2,1)S(1)} %get-tuple-element.54), channel_id=1, source_target_pairs={{0,48},{16,0},{32,16},{48,32},{1,49},{17,1},{33,17},{49,33},{2,50}... | collective-permute-start | bytes 393224 | tf_op jit(solution)/shard_map/ppermute | solution.py:333
  115.9 0.0 all-to-all-done.3.parts
  116.0 13.4 %all_to_all.26.sums = f32[32,1,128]{2,1,0:T(1,128)S(1)} all-to-all(f32[32,1,128]{2,1,0:T(1,128)S(1)} %shard_map.91), channel_id=1, replica_groups=mesh['z'=8,'y'=4,'core'=2,'dp'=8] {'y','dp'}, dimensions={0} | all-to-all | bytes 32768 | tf_op jit(solution)/shard_map/all_to_all | solution.py:442
  129.4 0.7 shard_map.92
  130.1 0.0 collective-permute-done.8.a1
  130.1 0.0 collective-permute-done.9.a2
  130.1 0.7 shard_map.94
  (12 shorter events, 0.1 us)
Async XLA Ops:
  0.6 10.0 %copy-start.3 = (bf16[1,128,128]{2,1,0:T(8,128)(2,1)S(1)}, bf16[1,128,128]{2,1,0:T(8,128)(2,1)}, u32[]{:S(2)}) copy-start(bf16[1,128,128]{2,1,0:T(8,128)(2,1)} %values.1) | copy-start | bytes 98308
  0.6 10.0 %copy-start.2 = (bf16[1,128,128]{2,1,0:T(8,128)(2,1)S(1)}, bf16[1,128,128]{2,1,0:T(8,128)(2,1)}, u32[]{:S(2)}) copy-start(bf16[1,128,128]{2,1,0:T(8,128)(2,1)} %keys.1) | copy-start | bytes 98308
  2.3 42.3 %collective-permute-start.1 = (bf16[1,128,1024]{2,1,0:T(8,128)(2,1)}, bf16[1,128,1024]{2,1,0:T(8,128)(2,1)S(1)}, u32[]{:S(2)}, u32[]{:S(2)}) collective-permute-start(bf16[1,128,1024]{2,1,0:T(8,128)(2,1)} %get-tuple-element.33), channel_id=1, source_target_pairs={{0,32},{16,48},{32,0},{48,16},{1,33},{17,49},{33,1},{49,17},{2,34}... | collective-permute-start | bytes 786440 | tf_op jit(solution)/shard_map/ppermute | solution.py:333
  10.7 0.7 copy-start.4
  12.2 10.2 %copy-start = (bf16[1,128,512]{2,1,0:T(8,128)(2,1)S(1)}, bf16[1,128,512]{2,1,0:T(8,128)(2,1)}, u32[]{:S(2)}) copy-start(bf16[1,128,512]{2,1,0:T(8,128)(2,1)} %left.3) | copy-start | bytes 393220
  12.2 10.2 %copy-start.1 = (bf16[1,128,512]{2,1,0:T(8,128)(2,1)S(1)}, bf16[1,128,512]{2,1,0:T(8,128)(2,1)}, u32[]{:S(2)}) copy-start(bf16[1,128,512]{2,1,0:T(8,128)(2,1)} %right.3) | copy-start | bytes 393220
  12.2 27.2 %all-to-all-start = ((bf16[8,128,256]{2,1,0:T(8,128)(2,1)}), bf16[8,128,256]{2,1,0:T(8,128)(2,1)S(1)}, u32[]{:S(2)}, u32[]{:S(2)}) async-start(bf16[8,128,256]{2,1,0:T(8,128)(2,1)} %shard_map.86), calls=%async_computation | async-start | bytes 1048576 | tf_op jit(solution)/shard_map/all_to_all | solution.py:369
  22.5 22.2 %collective-permute-start = (bf16[1,128,1024]{2,1,0:T(8,128)(2,1)S(1)}, bf16[1,128,1024]{2,1,0:T(8,128)(2,1)S(1)}, u32[]{:S(2)}, u32[]{:S(2)}) collective-permute-start(bf16[1,128,1024]{2,1,0:T(8,128)(2,1)S(1)} %get-tuple-element.32), channel_id=1, source_target_pairs={{0,48},{16,0},{32,16},{48,32},{1,49},{17,1},{33,17},{49,33},{2,50}... | collective-permute-start | bytes 786440 | tf_op jit(solution)/shard_map/ppermute | solution.py:333
  24.4 20.2 %collective-permute-start.2 = (bf16[1,128,1024]{2,1,0:T(8,128)(2,1)S(1)}, bf16[1,128,1024]{2,1,0:T(8,128)(2,1)S(1)}, u32[]{:S(2)}, u32[]{:S(2)}) collective-permute-start(bf16[1,128,1024]{2,1,0:T(8,128)(2,1)S(1)} %get-tuple-element.34), channel_id=1, source_target_pairs={{0,16},{16,32},{32,48},{48,0},{1,17},{17,33},{33,49},{49,1},{2,18}... | collective-permute-start | bytes 786440 | tf_op jit(solution)/shard_map/ppermute | solution.py:333
  28.7 0.7 copy-start.5
  39.4 4.8 %collective-permute-start.3 = (bf16[8,128,256]{2,1,0:T(8,128)(2,1)S(1)}, bf16[8,128,256]{2,1,0:T(8,128)(2,1)S(1)}, u32[]{:S(2)}, u32[]{:S(2)}) collective-permute-start(bf16[8,128,256]{2,1,0:T(8,128)(2,1)S(1)} %all-to-all-done.mine), channel_id=1, source_target_pairs={{0,8},{8,0},{1,9},{9,1},{2,10},{10,2},{3,11},{11,3},{4,12},{12,4},... | collective-permute-start | bytes 1572872 | tf_op jit(solution)/shard_map/ppermute | solution.py:333
  61.5 5.4 %collective-permute-start.7 = (bf16[8,128,256]{2,1,0:T(8,128)(2,1)S(1)}, bf16[8,128,256]{2,1,0:T(8,128)(2,1)S(1)}, u32[]{:S(2)}, u32[]{:S(2)}) collective-permute-start(bf16[8,128,256]{2,1,0:T(8,128)(2,1)S(1)} %get-tuple-element.45), channel_id=1, source_target_pairs={{0,8},{8,0},{1,9},{9,1},{2,10},{10,2},{3,11},{11,3},{4,12},{12,4},... | collective-permute-start | bytes 1572872 | tf_op jit(solution)/shard_map/ppermute | solution.py:333
  67.8 31.5 %all-to-all-start.2 = ((bf16[8,128,256]{2,1,0:T(8,128)(2,1)}), bf16[8,128,256]{2,1,0:T(8,128)(2,1)S(1)}, u32[]{:S(2)}, u32[]{:S(2)}) async-start(bf16[8,128,256]{2,1,0:T(8,128)(2,1)} %add_convert_fusion), calls=%async_computation.2 | async-start | bytes 1048576 | tf_op jit(solution)/shard_map/all_to_all | solution.py:412
  72.3 27.1 %collective-permute-start.5 = (bf16[1,128,1024]{2,1,0:T(8,128)(2,1)S(1)}, bf16[1,128,1024]{2,1,0:T(8,128)(2,1)S(1)}, u32[]{:S(2)}, u32[]{:S(2)}) collective-permute-start(bf16[1,128,1024]{2,1,0:T(8,128)(2,1)S(1)} %get-tuple-element.42), channel_id=1, source_target_pairs={{0,32},{16,48},{32,0},{48,16},{1,33},{17,49},{33,1},{49,17},{2,34}... | collective-permute-start | bytes 786440 | tf_op jit(solution)/shard_map/ppermute | solution.py:333
  74.3 17.1 %collective-permute-start.4 = (bf16[1,128,512]{2,1,0:T(8,128)(2,1)S(1)}, bf16[1,128,512]{2,1,0:T(8,128)(2,1)S(1)}, u32[]{:S(2)}, u32[]{:S(2)}) collective-permute-start(bf16[1,128,512]{2,1,0:T(8,128)(2,1)S(1)} %get-tuple-element.41), channel_id=1, source_target_pairs={{0,16},{16,32},{32,48},{48,0},{1,17},{17,33},{33,49},{49,1},{2,18}... | collective-permute-start | bytes 393224 | tf_op jit(solution)/shard_map/ppermute | solution.py:333
  79.5 19.8 %collective-permute-start.6 = (bf16[1,128,512]{2,1,0:T(8,128)(2,1)S(1)}, bf16[1,128,512]{2,1,0:T(8,128)(2,1)S(1)}, u32[]{:S(2)}, u32[]{:S(2)}) collective-permute-start(bf16[1,128,512]{2,1,0:T(8,128)(2,1)S(1)} %get-tuple-element.43), channel_id=1, source_target_pairs={{0,48},{16,0},{32,16},{48,32},{1,49},{17,1},{33,17},{49,33},{2,50}... | collective-permute-start | bytes 393224 | tf_op jit(solution)/shard_map/ppermute | solution.py:333
  100.3 15.6 %all-to-all-start.3 = ((f32[16,1,128]{2,1,0:T(1,128)}), f32[16,1,128]{2,1,0:T(1,128)S(1)}, u32[]{:S(2)}, u32[]{:S(2)}) async-start(f32[16,1,128]{2,1,0:T(1,128)} %get-tuple-element.46.order), calls=%async_computation.3 | async-start | bytes 16384 | tf_op jit(solution)/shard_map/all_to_all | solution.py:431
  108.5 21.6 %collective-permute-start.8 = (bf16[1,128,512]{2,1,0:T(8,128)(2,1)S(1)}, bf16[1,128,512]{2,1,0:T(8,128)(2,1)S(1)}, u32[]{:S(2)}, u32[]{:S(2)}) collective-permute-start(bf16[1,128,512]{2,1,0:T(8,128)(2,1)S(1)} %get-tuple-element.53), channel_id=1, source_target_pairs={{0,16},{16,32},{32,48},{48,0},{1,17},{17,33},{33,49},{49,1},{2,18}... | collective-permute-start | bytes 393224 | tf_op jit(solution)/shard_map/ppermute | solution.py:333
  112.8 17.3 %collective-permute-start.9 = (bf16[1,128,512]{2,1,0:T(8,128)(2,1)S(1)}, bf16[1,128,512]{2,1,0:T(8,128)(2,1)S(1)}, u32[]{:S(2)}, u32[]{:S(2)}) collective-permute-start(bf16[1,128,512]{2,1,0:T(8,128)(2,1)S(1)} %get-tuple-element.54), channel_id=1, source_target_pairs={{0,48},{16,0},{32,16},{48,32},{1,49},{17,1},{33,17},{49,33},{2,50}... | collective-permute-start | bytes 393224 | tf_op jit(solution)/shard_map/ppermute | solution.py:333

commit v11 on v9

--- a/solution.py
+++ b/solution.py
@@ -266,8 +266,7 @@
     sq_ref[...] = jnp.full(sq_ref.shape, squares, jnp.float32)
 
 
-def attended_kernel(order, a0, a1, a2, a3, out):
-    del order
+def attended_kernel(a0, a1, a2, a3, out):
     wide = out.shape[2]
     parts = [a[...].astype(jnp.float32) for a in (a0, a1, a2)]
     parts.append(a3[:, :, wide:].astype(jnp.float32))
@@ -280,13 +279,12 @@
         out[k] = total
 
 
-def scale_kernel(count, sums, dq, dkv, oq, ok, ov, used):
+def scale_kernel(count, sums, dq, dkv, oq, ok, ov):
     lanes = sums.shape[2]
     total = sums[0]
     for k in range(1, sums.shape[0]):
         total = total + sums[k]
     factor = lax.rsqrt(total / count + 1e-06)
-    used[...] = factor
     for h in range(dq.shape[2] // lanes):
         at = slice(h * lanes, (h + 1) * lanes)
         oq[0, :, at] = (dq[0, :, at] * factor).astype(oq.dtype)
@@ -318,7 +316,7 @@
     ]
     for copy in copies:
         copy.start()
-    done[...] = jnp.zeros_like(done)
+    done[0, 0] = 0
     for copy in copies:
         copy.wait()
 
@@ -340,16 +338,16 @@
     block = jax.ShapeDtypeStruct((1, tok, 2 * wide), keys.dtype)
     far = pl.pallas_call(
         far_kernel,
-        out_shape=[block, jax.ShapeDtypeStruct((8, 128), jnp.float32)],
+        out_shape=[block, jax.ShapeDtypeStruct((1, 1), jnp.int32)],
         in_specs=[FAR] * 2,
-        out_specs=[VMEM] * 2,
+        out_specs=[VMEM, SMEM],
         scratch_shapes=[pltpu.SemaphoreType.DMA((2,))],
         compiler_params=ALONE,
     )(queries, grad_out)
     copies = pl.pallas_call(
         spread_kernel,
         out_shape=jax.ShapeDtypeStruct((NZ, tok, 2 * width), keys.dtype),
-        in_specs=[VMEM] * 3,
+        in_specs=[VMEM] * 2 + [SMEM],
         out_specs=VMEM,
         compiler_params=PARAMS,
     )(keys, values, far[1])
@@ -427,25 +425,24 @@
     )(squares)
     squares = lax.all_to_all(squares, ("y", "dp"), 0, 0, tiled=True)
     count = float(ndata * NZ * NY * NC * tok * (wide + 2 * width))
-    out_query, out_key, out_value, used = pl.pallas_call(
+    out_query, out_key, out_value = pl.pallas_call(
         functools.partial(scale_kernel, count),
         out_shape=(
             shape(queries.shape, bf16),
             shape(keys.shape, bf16),
             shape(values.shape, bf16),
-            shape((1, 128), f32),
         ),
         in_specs=[VMEM] * 3,
-        out_specs=(VMEM,) * 4,
+        out_specs=(VMEM,) * 3,
         compiler_params=PARAMS,
     )(squares, dq, dkv)
     attended = pl.pallas_call(
         attended_kernel,
         out_shape=shape(queries.shape, bf16),
-        in_specs=[VMEM] + [VMEM] * NY,
+        in_specs=[VMEM] * NY,
         out_specs=VMEM,
         compiler_params=PARAMS,
-    )(used, *home)
+    )(*home)
     return attended, out_query, out_key, out_value
 
 

time: 137 us -> 132 us (0.964)
  blocking collectives: 41 us -> 23.8 us
  waiting for transfers between devices: 24.3 us -> 30 us
  starting transfers between devices: 55.6 us -> 60.4 us
  Pallas kernels: 10.5 us -> 13.3 us
    all_to_all x1 -> x0, blocking collectives: 17.3 us -> none  [per_device(): squares = lax.all_to_all(squares, ('y', 'dp'), 0, 0, tiled=True)]
    all_to_all x0 -> x1, waiting for transfers between devices: none -> 7.76 us  [per_device(): squares = lax.all_to_all(squares, ('y', 'dp'), 0, 0, tiled=True)]
    all_to_all x0 -> x1, starting transfers between devices: none -> 5.16 us  [per_device(): squares = lax.all_to_all(squares, ('y', 'dp'), 0, 0, tiled=True)]
    ppermute x10, waiting for transfers between devices: 15.2 us -> 13.1 us  [turn(): return lax.ppermute(x, axis, [(i, (i + by) % size) for i in range(size)])]
  transfers between devices with their start and end apart: 12 -> 13, of which waited for: 5 -> 6; matrix products, arithmetic and copies ran while one was open for 1% -> 1% of each run, Pallas kernels for 2% -> 3%
where the time goes in v11:
time: 132 us; the launch traced here: 131 us
  starting transfers between devices  60.4 us (46%)
  waiting for transfers between devices  30 us (23%)
  blocking collectives  23.8 us (18%)
  Pallas kernels  13.3 us (10%)
  other arithmetic  1.55 us (1%)
  local copies, waits for them, and re-layouts  1.51 us (1%)
    ppermute x10, starting transfers between devices, turn(): return lax.ppermute(x, axis, [(i, (i + by) % size) for i in range(size)])  38.5 us
    all_to_all x1, blocking collectives, per_device(): squares = lax.all_to_all(squares, ('z', 'core'), 0, 0, tiled=True)  14.3 us
    ppermute x10, waiting for transfers between devices, turn(): return lax.ppermute(x, axis, [(i, (i + by) % size) for i in range(size)])  13.1 us
    all_to_all x1, starting transfers between devices, per_device(): mine = lax.all_to_all(copies, 'z', 0, 0, tiled=True)  10.2 us
    all_to_all x1, blocking collectives, per_device(): stats = lax.all_to_all(stats, 'y', 0, 0, tiled=True)  9.48 us
    all_to_all x1, waiting for transfers between devices, per_device(): mine = lax.all_to_all(copies, 'z', 0, 0, tiled=True)  9.15 us
    all_to_all x1, waiting for transfers between devices, per_device(): squares = lax.all_to_all(squares, ('y', 'dp'), 0, 0, tiled=True)  7.76 us
    all_to_all x1, starting transfers between devices, per_device(): pieces = lax.all_to_all(pair, 'z', 0, 0, tiled=True)  6.51 us
  transfers between devices with their start and end apart: 13, of which 6 were waited for; matrix products, arithmetic and copies ran while one was open for 1% of the time, Pallas kernels for 3%

profile of v11, /device:TPU:1, one launch (start us, length us, event | category | flops | bytes accessed | tf_op | source)
XLA Modules:
  0.0 131.5 jit_solution(5355061350814330197)
XLA Ops:
  0.6 0.0 copy-start.3
  0.6 0.0 copy-start.2
  0.7 1.7 %shard_map.85 = (bf16[1,128,1024]{2,1,0:T(8,128)(2,1)}, s32[1,1]{1,0:T(1,128)}) custom-call(bf16[1,128,512]{2,1,0:T(8,128)(2,1)} %left.3, bf16[1,128,512]{2,1,0:T(8,128)(2,1)} %right.3), custom_call_target="tpu_custom_call" | custom-call | tf_op jit(solution)/shard_map/pallas_call | solution.py:339
  2.4 8.3 %collective-permute-start.1 = (bf16[1,128,1024]{2,1,0:T(8,128)(2,1)}, bf16[1,128,1024]{2,1,0:T(8,128)(2,1)S(1)}, u32[]{:S(2)}, u32[]{:S(2)}) collective-permute-start(bf16[1,128,1024]{2,1,0:T(8,128)(2,1)} %get-tuple-element.30), channel_id=1, source_target_pairs={{0,32},{16,48},{32,0},{48,16},{1,33},{17,49},{33,1},{49,17},{2,34}... | collective-permute-start | bytes 786440 | tf_op jit(solution)/shard_map/ppermute | solution.py:325
  10.7 0.0 copy-done.3
  10.7 0.0 copy-done.2
  10.7 1.5 %shard_map.86 = bf16[8,128,256]{2,1,0:T(8,128)(2,1)} custom-call(bf16[1,128,128]{2,1,0:T(8,128)(2,1)S(1)} %copy-done.2, bf16[1,128,128]{2,1,0:T(8,128)(2,1)S(1)} %copy-done.3, s32[1,1]{1,0:T(1,128)} %get-tuple-element.32.order), custom_call_target="tpu_custom_call" | custom-call | tf_op jit(solution)/shard_map/pallas_call | solution.py:347
  12.2 0.0 copy-start
  12.2 0.0 copy-start.1
  12.2 10.2 %all-to-all-start = ((bf16[8,128,256]{2,1,0:T(8,128)(2,1)}), bf16[8,128,256]{2,1,0:T(8,128)(2,1)S(1)}, u32[]{:S(2)}, u32[]{:S(2)}) async-start(bf16[8,128,256]{2,1,0:T(8,128)(2,1)} %shard_map.86), calls=%async_computation | async-start | bytes 1048576 | tf_op jit(solution)/shard_map/all_to_all | solution.py:361
  22.4 0.0 copy-done
  22.4 0.0 copy-done.1
  22.4 0.1 shard_map.84
  22.4 2.0 %collective-permute-start = (bf16[1,128,1024]{2,1,0:T(8,128)(2,1)S(1)}, bf16[1,128,1024]{2,1,0:T(8,128)(2,1)S(1)}, u32[]{:S(2)}, u32[]{:S(2)}) collective-permute-start(bf16[1,128,1024]{2,1,0:T(8,128)(2,1)S(1)} %get-tuple-element.29), channel_id=1, source_target_pairs={{0,48},{16,0},{32,16},{48,32},{1,49},{17,1},{33,17},{49,33},{2,50}... | collective-permute-start | bytes 786440 | tf_op jit(solution)/shard_map/ppermute | solution.py:325
  24.4 4.2 %collective-permute-start.2 = (bf16[1,128,1024]{2,1,0:T(8,128)(2,1)S(1)}, bf16[1,128,1024]{2,1,0:T(8,128)(2,1)S(1)}, u32[]{:S(2)}, u32[]{:S(2)}) collective-permute-start(bf16[1,128,1024]{2,1,0:T(8,128)(2,1)S(1)} %get-tuple-element.31), channel_id=1, source_target_pairs={{0,16},{16,32},{32,48},{48,0},{1,17},{17,33},{33,49},{49,1},{2,18}... | collective-permute-start | bytes 786440 | tf_op jit(solution)/shard_map/ppermute | solution.py:325
  28.7 0.0 copy-start.4
  28.7 0.6 copy-done.4
  29.3 0.1 eq.26
  29.4 0.1 eq.25
  29.5 0.1 add.218
  29.6 0.1 add.215
  29.7 0.2 select_reduce_fusion
  29.9 0.1 reshape.443
  30.0 0.1 reduce_min.11
  30.1 0.1 select_reduce_fusion.1
  30.3 9.1 %all-to-all-done.mine = bf16[8,128,256]{2,1,0:T(8,128)(2,1)S(1)} async-done(((bf16[8,128,256]{2,1,0:T(8,128)(2,1)}), bf16[8,128,256]{2,1,0:T(8,128)(2,1)S(1)}, u32[]{:S(2)}, u32[]{:S(2)}) %all-to-all-start) | async-done | bytes 524320 | tf_op jit(solution)/shard_map/all_to_all | solution.py:361
  39.4 3.3 %collective-permute-start.3 = (bf16[8,128,256]{2,1,0:T(8,128)(2,1)S(1)}, bf16[8,128,256]{2,1,0:T(8,128)(2,1)S(1)}, u32[]{:S(2)}, u32[]{:S(2)}) collective-permute-start(bf16[8,128,256]{2,1,0:T(8,128)(2,1)S(1)} %all-to-all-done.mine), channel_id=1, source_target_pairs={{0,8},{8,0},{1,9},{9,1},{2,10},{10,2},{3,11},{11,3},{4,12},{12,4},... | collective-permute-start | bytes 1572872 | tf_op jit(solution)/shard_map/ppermute | solution.py:325
  42.8 0.1 copy.13
  42.8 0.1 reshape.444
  42.9 0.1 add.220
  43.0 0.1 copy.14
  43.1 0.1 reshape.445
  43.2 0.1 pad_add_fusion.2.info
  43.3 1.0 collective-permute-done.3.other
  44.2 0.3 shard_map.87
  44.6 0.0 collective-permute-done.1.a2
  44.6 0.0 collective-permute-done.a1
  44.6 0.0 collective-permute-done.2.a3
  44.6 3.0 %shard_map.88 = (f32[2,128,1024]{2,1,0:T(8,128)S(1)}, f32[4,3,8,256]{3,2,1,0:T(8,128)S(1)}) custom-call(s32[34]{0:T(128)S(1)} %pad_add_fusion.2.info, bf16[1,128,1024]{2,1,0:T(8,128)(2,1)S(1)} %get-tuple-element.28.a0, bf16[1,128,1024]{2,1,0:T(8,128)(2,1)S(1)} %collective-permute-done.a1, bf16[1,128,1024]{2,1,0:T(8,128)(2,1)S(1)} %collective-permute-done.1.a2, ...), custom_call_target="tpu_custom_call" | custom-call | tf_op jit(solution)/shard_map/pallas_call | solution.py:377
  47.7 9.5 %all_to_all.25.stats = f32[4,3,8,256]{3,2,1,0:T(8,128)S(1)} all-to-all(f32[4,3,8,256]{3,2,1,0:T(8,128)S(1)} %get-tuple-element.36), channel_id=1, replica_groups=mesh['z'=8,'y'=4,'core'=2,'dp'=8] {'y'}, dimensions={0} | all-to-all | bytes 196608 | tf_op jit(solution)/shard_map/all_to_all | solution.py:385
  57.2 4.2 %shard_map.89 = (bf16[1,128,512]{2,1,0:T(8,128)(2,1)S(1)}, bf16[1,128,512]{2,1,0:T(8,128)(2,1)S(1)}, bf16[1,128,512]{2,1,0:T(8,128)(2,1)S(1)}, bf16[1,128,512]{2...) custom-call(s32[34]{0:T(128)S(1)} %pad_add_fusion.2.info, ...), custom_call_target="tpu_custom_call" | custom-call | tf_op jit(solution)/shard_map/pallas_call | solution.py:386
  61.4 4.1 %collective-permute-start.9 = (bf16[8,128,256]{2,1,0:T(8,128)(2,1)S(1)}, bf16[8,128,256]{2,1,0:T(8,128)(2,1)S(1)}, u32[]{:S(2)}, u32[]{:S(2)}) collective-permute-start(bf16[8,128,256]{2,1,0:T(8,128)(2,1)S(1)} %get-tuple-element.45), channel_id=1, source_target_pairs={{0,8},{8,0},{1,9},{9,1},{2,10},{10,2},{3,11},{11,3},{4,12},{12,4},... | collective-permute-start | bytes 1572872 | tf_op jit(solution)/shard_map/ppermute | solution.py:325
  65.5 1.5 %collective-permute-done.9 = bf16[8,128,256]{2,1,0:T(8,128)(2,1)S(1)} collective-permute-done((bf16[8,128,256]{2,1,0:T(8,128)(2,1)S(1)}, bf16[8,128,256]{2,1,0:T(8,128)(2,1)S(1)}, u32[]{:S(2)}, u32[]{:S(2)}) %collective-permute-start.9) | collective-permute-done | bytes 524320 | tf_op jit(solution)/shard_map/ppermute | solution.py:325
  67.0 0.9 add_convert_fusion
  67.9 6.5 %all-to-all-start.2 = ((bf16[8,128,256]{2,1,0:T(8,128)(2,1)}), bf16[8,128,256]{2,1,0:T(8,128)(2,1)S(1)}, u32[]{:S(2)}, u32[]{:S(2)}) async-start(bf16[8,128,256]{2,1,0:T(8,128)(2,1)} %add_convert_fusion), calls=%async_computation.2 | async-start | bytes 1048576 | tf_op jit(solution)/shard_map/all_to_all | solution.py:404
  74.5 1.9 %collective-permute-start.6 = (bf16[1,128,1024]{2,1,0:T(8,128)(2,1)S(1)}, bf16[1,128,1024]{2,1,0:T(8,128)(2,1)S(1)}, u32[]{:S(2)}, u32[]{:S(2)}) collective-permute-start(bf16[1,128,1024]{2,1,0:T(8,128)(2,1)S(1)} %get-tuple-element.40), channel_id=1, source_target_pairs={{0,32},{16,48},{32,0},{48,16},{1,33},{17,49},{33,1},{49,17},{2,34}... | collective-permute-start | bytes 786440 | tf_op jit(solution)/shard_map/ppermute | solution.py:325
  76.4 4.1 %collective-permute-start.7 = (bf16[1,128,512]{2,1,0:T(8,128)(2,1)S(1)}, bf16[1,128,512]{2,1,0:T(8,128)(2,1)S(1)}, u32[]{:S(2)}, u32[]{:S(2)}) collective-permute-start(bf16[1,128,512]{2,1,0:T(8,128)(2,1)S(1)} %get-tuple-element.42), channel_id=1, source_target_pairs={{0,16},{16,32},{32,48},{48,0},{1,17},{17,33},{33,49},{49,1},{2,18}... | collective-permute-start | bytes 393224 | tf_op jit(solution)/shard_map/ppermute | solution.py:325
  80.5 3.3 %collective-permute-start.8 = (bf16[1,128,512]{2,1,0:T(8,128)(2,1)S(1)}, bf16[1,128,512]{2,1,0:T(8,128)(2,1)S(1)}, u32[]{:S(2)}, u32[]{:S(2)}) collective-permute-start(bf16[1,128,512]{2,1,0:T(8,128)(2,1)S(1)} %get-tuple-element.43), channel_id=1, source_target_pairs={{0,48},{16,0},{32,16},{48,32},{1,49},{17,1},{33,17},{49,33},{2,50}... | collective-permute-start | bytes 393224 | tf_op jit(solution)/shard_map/ppermute | solution.py:325
  83.8 4.0 %collective-permute-start.4 = (bf16[1,128,512]{2,1,0:T(8,128)(2,1)S(1)}, bf16[1,128,512]{2,1,0:T(8,128)(2,1)S(1)}, u32[]{:S(2)}, u32[]{:S(2)}) collective-permute-start(bf16[1,128,512]{2,1,0:T(8,128)(2,1)S(1)} %get-tuple-element.38), channel_id=1, source_target_pairs={{0,16},{16,32},{32,48},{48,0},{1,17},{17,33},{33,49},{49,1},{2,18}... | collective-permute-start | bytes 393224 | tf_op jit(solution)/shard_map/ppermute | solution.py:325
  87.8 3.4 %collective-permute-start.5 = (bf16[1,128,512]{2,1,0:T(8,128)(2,1)S(1)}, bf16[1,128,512]{2,1,0:T(8,128)(2,1)S(1)}, u32[]{:S(2)}, u32[]{:S(2)}) collective-permute-start(bf16[1,128,512]{2,1,0:T(8,128)(2,1)S(1)} %get-tuple-element.39), channel_id=1, source_target_pairs={{0,48},{16,0},{32,16},{48,32},{1,49},{17,1},{33,17},{49,33},{2,50}... | collective-permute-start | bytes 393224 | tf_op jit(solution)/shard_map/ppermute | solution.py:325
  91.2 2.0 %collective-permute-done.7.o1 = bf16[1,128,512]{2,1,0:T(8,128)(2,1)S(1)} collective-permute-done((bf16[1,128,512]{2,1,0:T(8,128)(2,1)S(1)}, bf16[1,128,512]{2,1,0:T(8,128)(2,1)S(1)}, u32[]{:S(2)}, u32[]{:S(2)}) %collective-permute-start.7) | collective-permute-done | bytes 131104 | tf_op jit(solution)/shard_map/ppermute | solution.py:325
  93.2 8.6 %collective-permute-done.8.o3 = bf16[1,128,512]{2,1,0:T(8,128)(2,1)S(1)} collective-permute-done((bf16[1,128,512]{2,1,0:T(8,128)(2,1)S(1)}, bf16[1,128,512]{2,1,0:T(8,128)(2,1)S(1)}, u32[]{:S(2)}, u32[]{:S(2)}) %collective-permute-start.8) | collective-permute-done | bytes 131104 | tf_op jit(solution)/shard_map/ppermute | solution.py:325
  101.8 0.0 collective-permute-done.6.a3.o2
  101.8 0.0 all-to-all-done.2.dkv
  101.8 0.3 shard_map.91
  102.1 14.3 %all_to_all.26.parts = f32[16,1,128]{2,1,0:T(1,128)S(1)} all-to-all(f32[16,1,128]{2,1,0:T(1,128)S(1)} %get-tuple-element.46), channel_id=1, replica_groups=mesh['z'=8,'y'=4,'core'=2,'dp'=8] {'z','core'}, dimensions={0} | all-to-all | bytes 16384 | tf_op jit(solution)/shard_map/all_to_all | solution.py:416
  116.4 0.6 shard_map.92
  117.1 5.2 %all-to-all-start.4 = ((f32[32,1,128]{2,1,0:T(1,128)}), f32[32,1,128]{2,1,0:T(1,128)S(1)}, u32[]{:S(2)}, u32[]{:S(2)}) async-start(f32[32,1,128]{2,1,0:T(1,128)} %shard_map.92), calls=%async_computation.4 | async-start | bytes 32768 | tf_op jit(solution)/shard_map/all_to_all | solution.py:426
  122.2 0.0 collective-permute-done.4.a1
  122.2 0.0 collective-permute-done.5.a2
  122.2 0.7 shard_map.90
  123.0 7.8 %all-to-all-done.4.sums = f32[32,1,128]{2,1,0:T(1,128)S(1)} async-done(((f32[32,1,128]{2,1,0:T(1,128)}), f32[32,1,128]{2,1,0:T(1,128)S(1)}, u32[]{:S(2)}, u32[]{:S(2)}) %all-to-all-start.4) | async-done | bytes 16416 | tf_op jit(solution)/shard_map/all_to_all | solution.py:426
  130.7 0.7 shard_map.93
  (10 shorter events, 0.1 us)
Async XLA Ops:
  0.6 10.0 %copy-start.3 = (bf16[1,128,128]{2,1,0:T(8,128)(2,1)S(1)}, bf16[1,128,128]{2,1,0:T(8,128)(2,1)}, u32[]{:S(2)}) copy-start(bf16[1,128,128]{2,1,0:T(8,128)(2,1)} %values.1) | copy-start | bytes 98308
  0.6 10.0 %copy-start.2 = (bf16[1,128,128]{2,1,0:T(8,128)(2,1)S(1)}, bf16[1,128,128]{2,1,0:T(8,128)(2,1)}, u32[]{:S(2)}) copy-start(bf16[1,128,128]{2,1,0:T(8,128)(2,1)} %keys.1) | copy-start | bytes 98308
  2.4 42.2 %collective-permute-start.1 = (bf16[1,128,1024]{2,1,0:T(8,128)(2,1)}, bf16[1,128,1024]{2,1,0:T(8,128)(2,1)S(1)}, u32[]{:S(2)}, u32[]{:S(2)}) collective-permute-start(bf16[1,128,1024]{2,1,0:T(8,128)(2,1)} %get-tuple-element.30), channel_id=1, source_target_pairs={{0,32},{16,48},{32,0},{48,16},{1,33},{17,49},{33,1},{49,17},{2,34}... | collective-permute-start | bytes 786440 | tf_op jit(solution)/shard_map/ppermute | solution.py:325
  12.2 10.2 %copy-start = (bf16[1,128,512]{2,1,0:T(8,128)(2,1)S(1)}, bf16[1,128,512]{2,1,0:T(8,128)(2,1)}, u32[]{:S(2)}) copy-start(bf16[1,128,512]{2,1,0:T(8,128)(2,1)} %left.3) | copy-start | bytes 393220
  12.2 10.2 %copy-start.1 = (bf16[1,128,512]{2,1,0:T(8,128)(2,1)S(1)}, bf16[1,128,512]{2,1,0:T(8,128)(2,1)}, u32[]{:S(2)}) copy-start(bf16[1,128,512]{2,1,0:T(8,128)(2,1)} %right.3) | copy-start | bytes 393220
  12.2 27.2 %all-to-all-start = ((bf16[8,128,256]{2,1,0:T(8,128)(2,1)}), bf16[8,128,256]{2,1,0:T(8,128)(2,1)S(1)}, u32[]{:S(2)}, u32[]{:S(2)}) async-start(bf16[8,128,256]{2,1,0:T(8,128)(2,1)} %shard_map.86), calls=%async_computation | async-start | bytes 1048576 | tf_op jit(solution)/shard_map/all_to_all | solution.py:361
  22.4 22.2 %collective-permute-start = (bf16[1,128,1024]{2,1,0:T(8,128)(2,1)S(1)}, bf16[1,128,1024]{2,1,0:T(8,128)(2,1)S(1)}, u32[]{:S(2)}, u32[]{:S(2)}) collective-permute-start(bf16[1,128,1024]{2,1,0:T(8,128)(2,1)S(1)} %get-tuple-element.29), channel_id=1, source_target_pairs={{0,48},{16,0},{32,16},{48,32},{1,49},{17,1},{33,17},{49,33},{2,50}... | collective-permute-start | bytes 786440 | tf_op jit(solution)/shard_map/ppermute | solution.py:325
  24.4 20.2 %collective-permute-start.2 = (bf16[1,128,1024]{2,1,0:T(8,128)(2,1)S(1)}, bf16[1,128,1024]{2,1,0:T(8,128)(2,1)S(1)}, u32[]{:S(2)}, u32[]{:S(2)}) collective-permute-start(bf16[1,128,1024]{2,1,0:T(8,128)(2,1)S(1)} %get-tuple-element.31), channel_id=1, source_target_pairs={{0,16},{16,32},{32,48},{48,0},{1,17},{17,33},{33,49},{49,1},{2,18}... | collective-permute-start | bytes 786440 | tf_op jit(solution)/shard_map/ppermute | solution.py:325
  28.7 0.7 copy-start.4
  39.4 4.8 %collective-permute-start.3 = (bf16[8,128,256]{2,1,0:T(8,128)(2,1)S(1)}, bf16[8,128,256]{2,1,0:T(8,128)(2,1)S(1)}, u32[]{:S(2)}, u32[]{:S(2)}) collective-permute-start(bf16[8,128,256]{2,1,0:T(8,128)(2,1)S(1)} %all-to-all-done.mine), channel_id=1, source_target_pairs={{0,8},{8,0},{1,9},{9,1},{2,10},{10,2},{3,11},{11,3},{4,12},{12,4},... | collective-permute-start | bytes 1572872 | tf_op jit(solution)/shard_map/ppermute | solution.py:325
  61.4 5.6 %collective-permute-start.9 = (bf16[8,128,256]{2,1,0:T(8,128)(2,1)S(1)}, bf16[8,128,256]{2,1,0:T(8,128)(2,1)S(1)}, u32[]{:S(2)}, u32[]{:S(2)}) collective-permute-start(bf16[8,128,256]{2,1,0:T(8,128)(2,1)S(1)} %get-tuple-element.45), channel_id=1, source_target_pairs={{0,8},{8,0},{1,9},{9,1},{2,10},{10,2},{3,11},{11,3},{4,12},{12,4},... | collective-permute-start | bytes 1572872 | tf_op jit(solution)/shard_map/ppermute | solution.py:325
  67.9 33.9 %all-to-all-start.2 = ((bf16[8,128,256]{2,1,0:T(8,128)(2,1)}), bf16[8,128,256]{2,1,0:T(8,128)(2,1)S(1)}, u32[]{:S(2)}, u32[]{:S(2)}) async-start(bf16[8,128,256]{2,1,0:T(8,128)(2,1)} %add_convert_fusion), calls=%async_computation.2 | async-start | bytes 1048576 | tf_op jit(solution)/shard_map/all_to_all | solution.py:404
  74.5 27.4 %collective-permute-start.6 = (bf16[1,128,1024]{2,1,0:T(8,128)(2,1)S(1)}, bf16[1,128,1024]{2,1,0:T(8,128)(2,1)S(1)}, u32[]{:S(2)}, u32[]{:S(2)}) collective-permute-start(bf16[1,128,1024]{2,1,0:T(8,128)(2,1)S(1)} %get-tuple-element.40), channel_id=1, source_target_pairs={{0,32},{16,48},{32,0},{48,16},{1,33},{17,49},{33,1},{49,17},{2,34}... | collective-permute-start | bytes 786440 | tf_op jit(solution)/shard_map/ppermute | solution.py:325
  76.4 16.8 %collective-permute-start.7 = (bf16[1,128,512]{2,1,0:T(8,128)(2,1)S(1)}, bf16[1,128,512]{2,1,0:T(8,128)(2,1)S(1)}, u32[]{:S(2)}, u32[]{:S(2)}) collective-permute-start(bf16[1,128,512]{2,1,0:T(8,128)(2,1)S(1)} %get-tuple-element.42), channel_id=1, source_target_pairs={{0,16},{16,32},{32,48},{48,0},{1,17},{17,33},{33,49},{49,1},{2,18}... | collective-permute-start | bytes 393224 | tf_op jit(solution)/shard_map/ppermute | solution.py:325
  80.5 21.3 %collective-permute-start.8 = (bf16[1,128,512]{2,1,0:T(8,128)(2,1)S(1)}, bf16[1,128,512]{2,1,0:T(8,128)(2,1)S(1)}, u32[]{:S(2)}, u32[]{:S(2)}) collective-permute-start(bf16[1,128,512]{2,1,0:T(8,128)(2,1)S(1)} %get-tuple-element.43), channel_id=1, source_target_pairs={{0,48},{16,0},{32,16},{48,32},{1,49},{17,1},{33,17},{49,33},{2,50}... | collective-permute-start | bytes 393224 | tf_op jit(solution)/shard_map/ppermute | solution.py:325
  83.8 38.5 %collective-permute-start.4 = (bf16[1,128,512]{2,1,0:T(8,128)(2,1)S(1)}, bf16[1,128,512]{2,1,0:T(8,128)(2,1)S(1)}, u32[]{:S(2)}, u32[]{:S(2)}) collective-permute-start(bf16[1,128,512]{2,1,0:T(8,128)(2,1)S(1)} %get-tuple-element.38), channel_id=1, source_target_pairs={{0,16},{16,32},{32,48},{48,0},{1,17},{17,33},{33,49},{49,1},{2,18}... | collective-permute-start | bytes 393224 | tf_op jit(solution)/shard_map/ppermute | solution.py:325
  87.8 34.5 %collective-permute-start.5 = (bf16[1,128,512]{2,1,0:T(8,128)(2,1)S(1)}, bf16[1,128,512]{2,1,0:T(8,128)(2,1)S(1)}, u32[]{:S(2)}, u32[]{:S(2)}) collective-permute-start(bf16[1,128,512]{2,1,0:T(8,128)(2,1)S(1)} %get-tuple-element.39), channel_id=1, source_target_pairs={{0,48},{16,0},{32,16},{48,32},{1,49},{17,1},{33,17},{49,33},{2,50}... | collective-permute-start | bytes 393224 | tf_op jit(solution)/shard_map/ppermute | solution.py:325
  117.1 13.7 %all-to-all-start.4 = ((f32[32,1,128]{2,1,0:T(1,128)}), f32[32,1,128]{2,1,0:T(1,128)S(1)}, u32[]{:S(2)}, u32[]{:S(2)}) async-start(f32[32,1,128]{2,1,0:T(1,128)} %shard_map.92), calls=%async_computation.4 | async-start | bytes 32768 | tf_op jit(solution)/shard_map/all_to_all | solution.py:426

commit v12 on v11

--- a/solution.py
+++ b/solution.py
@@ -293,8 +293,7 @@
     ov[0] = (dkv[0, :, width:] * factor).astype(ov.dtype)
 
 
-def spread_kernel(keys, values, order, copies):
-    del order
+def spread_kernel(keys, values, copies):
     width = keys.shape[2]
     for k in range(copies.shape[0]):
         copies[k, :, :width] = keys[0]
@@ -308,7 +307,7 @@
         out[:, :, wide:] = right[...]
 
 
-def far_kernel(left, right, out, done, sems):
+def far_kernel(left, right, out, sems):
     wide = left.shape[2]
     copies = [
         pltpu.make_async_copy(left, out.at[:, :, :wide], sems.at[0]),
@@ -316,7 +315,6 @@
     ]
     for copy in copies:
         copy.start()
-    done[0, 0] = 0
     for copy in copies:
         copy.wait()
 
@@ -338,19 +336,19 @@
     block = jax.ShapeDtypeStruct((1, tok, 2 * wide), keys.dtype)
     far = pl.pallas_call(
         far_kernel,
-        out_shape=[block, jax.ShapeDtypeStruct((1, 1), jnp.int32)],
+        out_shape=[block],
         in_specs=[FAR] * 2,
-        out_specs=[VMEM, SMEM],
+        out_specs=[VMEM],
         scratch_shapes=[pltpu.SemaphoreType.DMA((2,))],
         compiler_params=ALONE,
     )(queries, grad_out)
     copies = pl.pallas_call(
         spread_kernel,
         out_shape=jax.ShapeDtypeStruct((NZ, tok, 2 * width), keys.dtype),
-        in_specs=[VMEM] * 2 + [SMEM],
+        in_specs=[VMEM] * 2,
         out_specs=VMEM,
         compiler_params=PARAMS,
-    )(keys, values, far[1])
+    )(keys, values)
     asked, *near = pl.pallas_call(
         join_kernel,
         out_shape=[block] * (NY - 1),

time: 132 us -> 133 us (level)
  starting transfers between devices: 60.4 us -> 67.8 us
  waiting for transfers between devices: 30 us -> 25.3 us
  Pallas kernels: 13.3 us -> 11.1 us
    all_to_all x1, starting transfers between devices: 5.16 us -> 14 us  [per_device(): squares = lax.all_to_all(squares, ('y', 'dp'), 0, 0, tiled=True)]
    ppermute x10, waiting for transfers between devices: 13.1 us -> 8.35 us  [turn(): return lax.ppermute(x, axis, [(i, (i + by) % size) for i in range(size)])]
    all_to_all x1, starting transfers between devices: 6.51 us -> 5.01 us  [per_device(): pieces = lax.all_to_all(pair, 'z', 0, 0, tiled=True)]
  transfers between devices with their start and end apart: 13 -> 13, of which waited for: 6 -> 6; matrix products, arithmetic and copies ran while one was open for 1% -> 1% of each run, Pallas kernels for 3% -> 2%
where the time goes in v12:
time: 133 us; the launch traced here: 132 us
  starting transfers between devices  67.8 us (51%)
  waiting for transfers between devices  25.3 us (19%)
  blocking collectives  23.8 us (18%)
  Pallas kernels  11.1 us (8%)
  other arithmetic  1.55 us (1%)
  local copies, waits for them, and re-layouts  1.51 us (1%)
    ppermute x10, starting transfers between devices, turn(): return lax.ppermute(x, axis, [(i, (i + by) % size) for i in range(size)])  38.6 us
    all_to_all x1, blocking collectives, per_device(): squares = lax.all_to_all(squares, ('z', 'core'), 0, 0, tiled=True)  14.4 us
    all_to_all x1, starting transfers between devices, per_device(): squares = lax.all_to_all(squares, ('y', 'dp'), 0, 0, tiled=True)  14 us
    all_to_all x1, starting transfers between devices, per_device(): mine = lax.all_to_all(copies, 'z', 0, 0, tiled=True)  10.2 us
    all_to_all x1, blocking collectives, per_device(): stats = lax.all_to_all(stats, 'y', 0, 0, tiled=True)  9.43 us
    all_to_all x1, waiting for transfers between devices, per_device(): mine = lax.all_to_all(copies, 'z', 0, 0, tiled=True)  9.15 us
    ppermute x10, waiting for transfers between devices, turn(): return lax.ppermute(x, axis, [(i, (i + by) % size) for i in range(size)])  8.35 us
    all_to_all x1, waiting for transfers between devices, per_device(): squares = lax.all_to_all(squares, ('y', 'dp'), 0, 0, tiled=True)  7.76 us
  transfers between devices with their start and end apart: 13, of which 6 were waited for; matrix products, arithmetic and copies ran while one was open for 1% of the time, Pallas kernels for 2%

profile of v12, /device:TPU:1, one launch (start us, length us, event | category | flops | bytes accessed | tf_op | source)
XLA Modules:
  0.0 131.9 jit_solution(10674764428535905454)
XLA Ops:
  0.6 0.0 copy-start.3
  0.6 0.0 copy-start.2
  0.7 1.7 %shard_map.85 = bf16[1,128,1024]{2,1,0:T(8,128)(2,1)} custom-call(bf16[1,128,512]{2,1,0:T(8,128)(2,1)} %left.3, bf16[1,128,512]{2,1,0:T(8,128)(2,1)} %right.3), custom_call_target="tpu_custom_call" | custom-call | tf_op jit(solution)/shard_map/pallas_call | solution.py:337
  2.4 8.3 %collective-permute-start.1 = (bf16[1,128,1024]{2,1,0:T(8,128)(2,1)}, bf16[1,128,1024]{2,1,0:T(8,128)(2,1)S(1)}, u32[]{:S(2)}, u32[]{:S(2)}) collective-permute-start(bf16[1,128,1024]{2,1,0:T(8,128)(2,1)} %shard_map.85), channel_id=1, source_target_pairs={{0,32},{16,48},{32,0},{48,16},{1,33},{17,49},{33,1},{49,17},{2,34}... | collective-permute-start | bytes 786440 | tf_op jit(solution)/shard_map/ppermute | solution.py:323
  10.6 0.0 copy-done.3
  10.7 0.0 copy-done.2
  10.7 0.9 shard_map.86
  11.5 0.0 copy-start
  11.5 0.0 copy-start.1
  11.5 10.2 %all-to-all-start = ((bf16[8,128,256]{2,1,0:T(8,128)(2,1)}), bf16[8,128,256]{2,1,0:T(8,128)(2,1)S(1)}, u32[]{:S(2)}, u32[]{:S(2)}) async-start(bf16[8,128,256]{2,1,0:T(8,128)(2,1)} %shard_map.86), calls=%async_computation | async-start | bytes 1048576 | tf_op jit(solution)/shard_map/all_to_all | solution.py:359
  21.7 0.0 copy-done
  21.7 0.0 copy-done.1
  21.7 0.1 shard_map.84
  21.8 2.0 %collective-permute-start = (bf16[1,128,1024]{2,1,0:T(8,128)(2,1)S(1)}, bf16[1,128,1024]{2,1,0:T(8,128)(2,1)S(1)}, u32[]{:S(2)}, u32[]{:S(2)}) collective-permute-start(bf16[1,128,1024]{2,1,0:T(8,128)(2,1)S(1)} %get-tuple-element.27), channel_id=1, source_target_pairs={{0,48},{16,0},{32,16},{48,32},{1,49},{17,1},{33,17},{49,33},{2,50}... | collective-permute-start | bytes 786440 | tf_op jit(solution)/shard_map/ppermute | solution.py:323
  23.8 4.2 %collective-permute-start.2 = (bf16[1,128,1024]{2,1,0:T(8,128)(2,1)S(1)}, bf16[1,128,1024]{2,1,0:T(8,128)(2,1)S(1)}, u32[]{:S(2)}, u32[]{:S(2)}) collective-permute-start(bf16[1,128,1024]{2,1,0:T(8,128)(2,1)S(1)} %get-tuple-element.28), channel_id=1, source_target_pairs={{0,16},{16,32},{32,48},{48,0},{1,17},{17,33},{33,49},{49,1},{2,18}... | collective-permute-start | bytes 786440 | tf_op jit(solution)/shard_map/ppermute | solution.py:323
  28.0 0.0 copy-start.4
  28.0 0.6 copy-done.4
  28.7 0.1 eq.26
  28.8 0.1 eq.25
  28.9 0.1 add.218
  28.9 0.1 add.215
  29.0 0.2 select_reduce_fusion
  29.2 0.1 reshape.443
  29.3 0.1 reduce_min.11
  29.4 0.1 select_reduce_fusion.1
  29.6 9.1 %all-to-all-done.mine = bf16[8,128,256]{2,1,0:T(8,128)(2,1)S(1)} async-done(((bf16[8,128,256]{2,1,0:T(8,128)(2,1)}), bf16[8,128,256]{2,1,0:T(8,128)(2,1)S(1)}, u32[]{:S(2)}, u32[]{:S(2)}) %all-to-all-start) | async-done | bytes 524320 | tf_op jit(solution)/shard_map/all_to_all | solution.py:359
  38.7 3.3 %collective-permute-start.3 = (bf16[8,128,256]{2,1,0:T(8,128)(2,1)S(1)}, bf16[8,128,256]{2,1,0:T(8,128)(2,1)S(1)}, u32[]{:S(2)}, u32[]{:S(2)}) collective-permute-start(bf16[8,128,256]{2,1,0:T(8,128)(2,1)S(1)} %all-to-all-done.mine), channel_id=1, source_target_pairs={{0,8},{8,0},{1,9},{9,1},{2,10},{10,2},{3,11},{11,3},{4,12},{12,4},... | collective-permute-start | bytes 1572872 | tf_op jit(solution)/shard_map/ppermute | solution.py:323
  42.1 0.1 copy.13
  42.2 0.1 reshape.444
  42.3 0.1 add.220
  42.4 0.1 copy.14
  42.4 0.1 reshape.445
  42.5 0.1 pad_add_fusion.2.info
  42.6 1.0 collective-permute-done.3.other
  43.6 0.3 shard_map.87
  43.9 0.0 collective-permute-done.1.a2
  43.9 0.0 collective-permute-done.a1
  43.9 0.0 collective-permute-done.2.a3
  44.0 2.4 %shard_map.88 = (f32[2,128,1024]{2,1,0:T(8,128)S(1)}, f32[4,3,8,256]{3,2,1,0:T(8,128)S(1)}) custom-call(s32[34]{0:T(128)S(1)} %pad_add_fusion.2.info, bf16[1,128,1024]{2,1,0:T(8,128)(2,1)S(1)} %get-tuple-element.26.a0, bf16[1,128,1024]{2,1,0:T(8,128)(2,1)S(1)} %collective-permute-done.a1, bf16[1,128,1024]{2,1,0:T(8,128)(2,1)S(1)} %collective-permute-done.1.a2, ...), custom_call_target="tpu_custom_call" | custom-call | tf_op jit(solution)/shard_map/pallas_call | solution.py:375
  46.4 9.4 %all_to_all.25.stats = f32[4,3,8,256]{3,2,1,0:T(8,128)S(1)} all-to-all(f32[4,3,8,256]{3,2,1,0:T(8,128)S(1)} %get-tuple-element.32), channel_id=1, replica_groups=mesh['z'=8,'y'=4,'core'=2,'dp'=8] {'y'}, dimensions={0} | all-to-all | bytes 196608 | tf_op jit(solution)/shard_map/all_to_all | solution.py:383
  55.8 3.3 %shard_map.89 = (bf16[1,128,512]{2,1,0:T(8,128)(2,1)S(1)}, bf16[1,128,512]{2,1,0:T(8,128)(2,1)S(1)}, bf16[1,128,512]{2,1,0:T(8,128)(2,1)S(1)}, bf16[1,128,512]{2...) custom-call(s32[34]{0:T(128)S(1)} %pad_add_fusion.2.info, ...), custom_call_target="tpu_custom_call" | custom-call | tf_op jit(solution)/shard_map/pallas_call | solution.py:384
  59.1 4.2 %collective-permute-start.9 = (bf16[8,128,256]{2,1,0:T(8,128)(2,1)S(1)}, bf16[8,128,256]{2,1,0:T(8,128)(2,1)S(1)}, u32[]{:S(2)}, u32[]{:S(2)}) collective-permute-start(bf16[8,128,256]{2,1,0:T(8,128)(2,1)S(1)} %get-tuple-element.41), channel_id=1, source_target_pairs={{0,8},{8,0},{1,9},{9,1},{2,10},{10,2},{3,11},{11,3},{4,12},{12,4},... | collective-permute-start | bytes 1572872 | tf_op jit(solution)/shard_map/ppermute | solution.py:323
  63.3 1.5 %collective-permute-done.9 = bf16[8,128,256]{2,1,0:T(8,128)(2,1)S(1)} collective-permute-done((bf16[8,128,256]{2,1,0:T(8,128)(2,1)S(1)}, bf16[8,128,256]{2,1,0:T(8,128)(2,1)S(1)}, u32[]{:S(2)}, u32[]{:S(2)}) %collective-permute-start.9) | collective-permute-done | bytes 524320 | tf_op jit(solution)/shard_map/ppermute | solution.py:323
  64.8 0.9 add_convert_fusion
  65.8 5.0 %all-to-all-start.2 = ((bf16[8,128,256]{2,1,0:T(8,128)(2,1)}), bf16[8,128,256]{2,1,0:T(8,128)(2,1)S(1)}, u32[]{:S(2)}, u32[]{:S(2)}) async-start(bf16[8,128,256]{2,1,0:T(8,128)(2,1)} %add_convert_fusion), calls=%async_computation.2 | async-start | bytes 1048576 | tf_op jit(solution)/shard_map/all_to_all | solution.py:402
  70.8 1.9 %collective-permute-start.6 = (bf16[1,128,1024]{2,1,0:T(8,128)(2,1)S(1)}, bf16[1,128,1024]{2,1,0:T(8,128)(2,1)S(1)}, u32[]{:S(2)}, u32[]{:S(2)}) collective-permute-start(bf16[1,128,1024]{2,1,0:T(8,128)(2,1)S(1)} %get-tuple-element.36), channel_id=1, source_target_pairs={{0,32},{16,48},{32,0},{48,16},{1,33},{17,49},{33,1},{49,17},{2,34}... | collective-permute-start | bytes 786440 | tf_op jit(solution)/shard_map/ppermute | solution.py:323
  72.7 3.6 %collective-permute-start.7 = (bf16[1,128,512]{2,1,0:T(8,128)(2,1)S(1)}, bf16[1,128,512]{2,1,0:T(8,128)(2,1)S(1)}, u32[]{:S(2)}, u32[]{:S(2)}) collective-permute-start(bf16[1,128,512]{2,1,0:T(8,128)(2,1)S(1)} %get-tuple-element.38), channel_id=1, source_target_pairs={{0,16},{16,32},{32,48},{48,0},{1,17},{17,33},{33,49},{49,1},{2,18}... | collective-permute-start | bytes 393224 | tf_op jit(solution)/shard_map/ppermute | solution.py:323
  76.4 3.7 %collective-permute-start.8 = (bf16[1,128,512]{2,1,0:T(8,128)(2,1)S(1)}, bf16[1,128,512]{2,1,0:T(8,128)(2,1)S(1)}, u32[]{:S(2)}, u32[]{:S(2)}) collective-permute-start(bf16[1,128,512]{2,1,0:T(8,128)(2,1)S(1)} %get-tuple-element.39), channel_id=1, source_target_pairs={{0,48},{16,0},{32,16},{48,32},{1,49},{17,1},{33,17},{49,33},{2,50}... | collective-permute-start | bytes 393224 | tf_op jit(solution)/shard_map/ppermute | solution.py:323
  80.1 4.0 %collective-permute-start.4 = (bf16[1,128,512]{2,1,0:T(8,128)(2,1)S(1)}, bf16[1,128,512]{2,1,0:T(8,128)(2,1)S(1)}, u32[]{:S(2)}, u32[]{:S(2)}) collective-permute-start(bf16[1,128,512]{2,1,0:T(8,128)(2,1)S(1)} %get-tuple-element.34), channel_id=1, source_target_pairs={{0,16},{16,32},{32,48},{48,0},{1,17},{17,33},{33,49},{49,1},{2,18}... | collective-permute-start | bytes 393224 | tf_op jit(solution)/shard_map/ppermute | solution.py:323
  84.1 3.4 %collective-permute-start.5 = (bf16[1,128,512]{2,1,0:T(8,128)(2,1)S(1)}, bf16[1,128,512]{2,1,0:T(8,128)(2,1)S(1)}, u32[]{:S(2)}, u32[]{:S(2)}) collective-permute-start(bf16[1,128,512]{2,1,0:T(8,128)(2,1)S(1)} %get-tuple-element.35), channel_id=1, source_target_pairs={{0,48},{16,0},{32,16},{48,32},{1,49},{17,1},{33,17},{49,33},{2,50}... | collective-permute-start | bytes 393224 | tf_op jit(solution)/shard_map/ppermute | solution.py:323
  87.5 1.7 %collective-permute-done.7.o1 = bf16[1,128,512]{2,1,0:T(8,128)(2,1)S(1)} collective-permute-done((bf16[1,128,512]{2,1,0:T(8,128)(2,1)S(1)}, bf16[1,128,512]{2,1,0:T(8,128)(2,1)S(1)}, u32[]{:S(2)}, u32[]{:S(2)}) %collective-permute-start.7) | collective-permute-done | bytes 131104 | tf_op jit(solution)/shard_map/ppermute | solution.py:323
  89.2 4.2 %collective-permute-done.8.o3 = bf16[1,128,512]{2,1,0:T(8,128)(2,1)S(1)} collective-permute-done((bf16[1,128,512]{2,1,0:T(8,128)(2,1)S(1)}, bf16[1,128,512]{2,1,0:T(8,128)(2,1)S(1)}, u32[]{:S(2)}, u32[]{:S(2)}) %collective-permute-start.8) | collective-permute-done | bytes 131104 | tf_op jit(solution)/shard_map/ppermute | solution.py:323
  93.4 0.0 collective-permute-done.6.a3.o2
  93.4 0.0 all-to-all-done.2.dkv
  93.4 0.3 shard_map.91
  93.7 14.4 %all_to_all.26.parts = f32[16,1,128]{2,1,0:T(1,128)S(1)} all-to-all(f32[16,1,128]{2,1,0:T(1,128)S(1)} %get-tuple-element.42), channel_id=1, replica_groups=mesh['z'=8,'y'=4,'core'=2,'dp'=8] {'z','core'}, dimensions={0} | all-to-all | bytes 16384 | tf_op jit(solution)/shard_map/all_to_all | solution.py:414
  108.1 0.6 shard_map.92
  108.7 14.0 %all-to-all-start.4 = ((f32[32,1,128]{2,1,0:T(1,128)}), f32[32,1,128]{2,1,0:T(1,128)S(1)}, u32[]{:S(2)}, u32[]{:S(2)}) async-start(f32[32,1,128]{2,1,0:T(1,128)} %shard_map.92), calls=%async_computation.4 | async-start | bytes 32768 | tf_op jit(solution)/shard_map/all_to_all | solution.py:424
  122.7 0.0 collective-permute-done.4.a1
  122.7 0.0 collective-permute-done.5.a2
  122.7 0.7 shard_map.90
  123.4 7.8 %all-to-all-done.4.sums = f32[32,1,128]{2,1,0:T(1,128)S(1)} async-done(((f32[32,1,128]{2,1,0:T(1,128)}), f32[32,1,128]{2,1,0:T(1,128)S(1)}, u32[]{:S(2)}, u32[]{:S(2)}) %all-to-all-start.4) | async-done | bytes 16416 | tf_op jit(solution)/shard_map/all_to_all | solution.py:424
  131.2 0.7 shard_map.93
  (10 shorter events, 0.1 us)
Async XLA Ops:
  0.6 10.0 %copy-start.3 = (bf16[1,128,128]{2,1,0:T(8,128)(2,1)S(1)}, bf16[1,128,128]{2,1,0:T(8,128)(2,1)}, u32[]{:S(2)}) copy-start(bf16[1,128,128]{2,1,0:T(8,128)(2,1)} %values.1) | copy-start | bytes 98308
  0.6 10.0 %copy-start.2 = (bf16[1,128,128]{2,1,0:T(8,128)(2,1)S(1)}, bf16[1,128,128]{2,1,0:T(8,128)(2,1)}, u32[]{:S(2)}) copy-start(bf16[1,128,128]{2,1,0:T(8,128)(2,1)} %keys.1) | copy-start | bytes 98308
  2.4 41.6 %collective-permute-start.1 = (bf16[1,128,1024]{2,1,0:T(8,128)(2,1)}, bf16[1,128,1024]{2,1,0:T(8,128)(2,1)S(1)}, u32[]{:S(2)}, u32[]{:S(2)}) collective-permute-start(bf16[1,128,1024]{2,1,0:T(8,128)(2,1)} %shard_map.85), channel_id=1, source_target_pairs={{0,32},{16,48},{32,0},{48,16},{1,33},{17,49},{33,1},{49,17},{2,34}... | collective-permute-start | bytes 786440 | tf_op jit(solution)/shard_map/ppermute | solution.py:323
  11.5 10.2 %copy-start = (bf16[1,128,512]{2,1,0:T(8,128)(2,1)S(1)}, bf16[1,128,512]{2,1,0:T(8,128)(2,1)}, u32[]{:S(2)}) copy-start(bf16[1,128,512]{2,1,0:T(8,128)(2,1)} %left.3) | copy-start | bytes 393220
  11.5 10.2 %copy-start.1 = (bf16[1,128,512]{2,1,0:T(8,128)(2,1)S(1)}, bf16[1,128,512]{2,1,0:T(8,128)(2,1)}, u32[]{:S(2)}) copy-start(bf16[1,128,512]{2,1,0:T(8,128)(2,1)} %right.3) | copy-start | bytes 393220
  11.5 27.2 %all-to-all-start = ((bf16[8,128,256]{2,1,0:T(8,128)(2,1)}), bf16[8,128,256]{2,1,0:T(8,128)(2,1)S(1)}, u32[]{:S(2)}, u32[]{:S(2)}) async-start(bf16[8,128,256]{2,1,0:T(8,128)(2,1)} %shard_map.86), calls=%async_computation | async-start | bytes 1048576 | tf_op jit(solution)/shard_map/all_to_all | solution.py:359
  21.8 22.2 %collective-permute-start = (bf16[1,128,1024]{2,1,0:T(8,128)(2,1)S(1)}, bf16[1,128,1024]{2,1,0:T(8,128)(2,1)S(1)}, u32[]{:S(2)}, u32[]{:S(2)}) collective-permute-start(bf16[1,128,1024]{2,1,0:T(8,128)(2,1)S(1)} %get-tuple-element.27), channel_id=1, source_target_pairs={{0,48},{16,0},{32,16},{48,32},{1,49},{17,1},{33,17},{49,33},{2,50}... | collective-permute-start | bytes 786440 | tf_op jit(solution)/shard_map/ppermute | solution.py:323
  23.8 20.2 %collective-permute-start.2 = (bf16[1,128,1024]{2,1,0:T(8,128)(2,1)S(1)}, bf16[1,128,1024]{2,1,0:T(8,128)(2,1)S(1)}, u32[]{:S(2)}, u32[]{:S(2)}) collective-permute-start(bf16[1,128,1024]{2,1,0:T(8,128)(2,1)S(1)} %get-tuple-element.28), channel_id=1, source_target_pairs={{0,16},{16,32},{32,48},{48,0},{1,17},{17,33},{33,49},{49,1},{2,18}... | collective-permute-start | bytes 786440 | tf_op jit(solution)/shard_map/ppermute | solution.py:323
  28.0 0.7 copy-start.4
  38.7 4.8 %collective-permute-start.3 = (bf16[8,128,256]{2,1,0:T(8,128)(2,1)S(1)}, bf16[8,128,256]{2,1,0:T(8,128)(2,1)S(1)}, u32[]{:S(2)}, u32[]{:S(2)}) collective-permute-start(bf16[8,128,256]{2,1,0:T(8,128)(2,1)S(1)} %all-to-all-done.mine), channel_id=1, source_target_pairs={{0,8},{8,0},{1,9},{9,1},{2,10},{10,2},{3,11},{11,3},{4,12},{12,4},... | collective-permute-start | bytes 1572872 | tf_op jit(solution)/shard_map/ppermute | solution.py:323
  59.1 5.7 %collective-permute-start.9 = (bf16[8,128,256]{2,1,0:T(8,128)(2,1)S(1)}, bf16[8,128,256]{2,1,0:T(8,128)(2,1)S(1)}, u32[]{:S(2)}, u32[]{:S(2)}) collective-permute-start(bf16[8,128,256]{2,1,0:T(8,128)(2,1)S(1)} %get-tuple-element.41), channel_id=1, source_target_pairs={{0,8},{8,0},{1,9},{9,1},{2,10},{10,2},{3,11},{11,3},{4,12},{12,4},... | collective-permute-start | bytes 1572872 | tf_op jit(solution)/shard_map/ppermute | solution.py:323
  65.8 27.6 %all-to-all-start.2 = ((bf16[8,128,256]{2,1,0:T(8,128)(2,1)}), bf16[8,128,256]{2,1,0:T(8,128)(2,1)S(1)}, u32[]{:S(2)}, u32[]{:S(2)}) async-start(bf16[8,128,256]{2,1,0:T(8,128)(2,1)} %add_convert_fusion), calls=%async_computation.2 | async-start | bytes 1048576 | tf_op jit(solution)/shard_map/all_to_all | solution.py:402
  70.8 22.6 %collective-permute-start.6 = (bf16[1,128,1024]{2,1,0:T(8,128)(2,1)S(1)}, bf16[1,128,1024]{2,1,0:T(8,128)(2,1)S(1)}, u32[]{:S(2)}, u32[]{:S(2)}) collective-permute-start(bf16[1,128,1024]{2,1,0:T(8,128)(2,1)S(1)} %get-tuple-element.36), channel_id=1, source_target_pairs={{0,32},{16,48},{32,0},{48,16},{1,33},{17,49},{33,1},{49,17},{2,34}... | collective-permute-start | bytes 786440 | tf_op jit(solution)/shard_map/ppermute | solution.py:323
  72.7 16.5 %collective-permute-start.7 = (bf16[1,128,512]{2,1,0:T(8,128)(2,1)S(1)}, bf16[1,128,512]{2,1,0:T(8,128)(2,1)S(1)}, u32[]{:S(2)}, u32[]{:S(2)}) collective-permute-start(bf16[1,128,512]{2,1,0:T(8,128)(2,1)S(1)} %get-tuple-element.38), channel_id=1, source_target_pairs={{0,16},{16,32},{32,48},{48,0},{1,17},{17,33},{33,49},{49,1},{2,18}... | collective-permute-start | bytes 393224 | tf_op jit(solution)/shard_map/ppermute | solution.py:323
  76.4 17.0 %collective-permute-start.8 = (bf16[1,128,512]{2,1,0:T(8,128)(2,1)S(1)}, bf16[1,128,512]{2,1,0:T(8,128)(2,1)S(1)}, u32[]{:S(2)}, u32[]{:S(2)}) collective-permute-start(bf16[1,128,512]{2,1,0:T(8,128)(2,1)S(1)} %get-tuple-element.39), channel_id=1, source_target_pairs={{0,48},{16,0},{32,16},{48,32},{1,49},{17,1},{33,17},{49,33},{2,50}... | collective-permute-start | bytes 393224 | tf_op jit(solution)/shard_map/ppermute | solution.py:323
  80.1 42.6 %collective-permute-start.4 = (bf16[1,128,512]{2,1,0:T(8,128)(2,1)S(1)}, bf16[1,128,512]{2,1,0:T(8,128)(2,1)S(1)}, u32[]{:S(2)}, u32[]{:S(2)}) collective-permute-start(bf16[1,128,512]{2,1,0:T(8,128)(2,1)S(1)} %get-tuple-element.34), channel_id=1, source_target_pairs={{0,16},{16,32},{32,48},{48,0},{1,17},{17,33},{33,49},{49,1},{2,18}... | collective-permute-start | bytes 393224 | tf_op jit(solution)/shard_map/ppermute | solution.py:323
  84.1 38.6 %collective-permute-start.5 = (bf16[1,128,512]{2,1,0:T(8,128)(2,1)S(1)}, bf16[1,128,512]{2,1,0:T(8,128)(2,1)S(1)}, u32[]{:S(2)}, u32[]{:S(2)}) collective-permute-start(bf16[1,128,512]{2,1,0:T(8,128)(2,1)S(1)} %get-tuple-element.35), channel_id=1, source_target_pairs={{0,48},{16,0},{32,16},{48,32},{1,49},{17,1},{33,17},{49,33},{2,50}... | collective-permute-start | bytes 393224 | tf_op jit(solution)/shard_map/ppermute | solution.py:323
  108.7 22.5 %all-to-all-start.4 = ((f32[32,1,128]{2,1,0:T(1,128)}), f32[32,1,128]{2,1,0:T(1,128)S(1)}, u32[]{:S(2)}, u32[]{:S(2)}) async-start(f32[32,1,128]{2,1,0:T(1,128)} %shard_map.92), calls=%async_computation.4 | async-start | bytes 32768 | tf_op jit(solution)/shard_map/all_to_all | solution.py:424

commit v13 on v12

--- a/solution.py
+++ b/solution.py
@@ -385,7 +385,7 @@
         functools.partial(backward_kernel, heads),
         out_shape=[shape(queries.shape, bf16)] * (NY + 1)
         + [shape(asked.shape, bf16), shape(queries.shape, bf16)]
-        + [shape(mine.shape, f32), shape(mine.shape, bf16)],
+        + [shape(mine.shape, bf16)] * 2,
         in_specs=[SMEM] + [VMEM] * (NY + 4),
         out_specs=[VMEM] * (2 * NY + 1),
         scratch_shapes=[
@@ -398,7 +398,7 @@
     seen, sent = {0: sent[0], 1: sent[1], 3: sent[2]}, sent[3:]
     back = [sent[0]] + [turn(sent[k], "y", NY, k) for k in range(1, NY)]
     from_core = turn(dother, "core", NC, 1)
-    pair = (dmine + from_core.astype(f32)).astype(bf16)
+    pair = (dmine.astype(f32) + from_core.astype(f32)).astype(bf16)
     pieces = lax.all_to_all(pair, "z", 0, 0, tiled=True)
     dq, dkv, squares = pl.pallas_call(
         combine_kernel,

time: 133 us -> 135 us (1.015); the launches traced: 132 us -> 135 us
  waiting for transfers between devices: 25.3 us -> 29.4 us
  starting transfers between devices: 67.8 us -> 64 us
  Pallas kernels: 11.1 us -> 14.3 us
    ppermute x10, waiting for transfers between devices: 8.35 us -> 12.5 us  [turn(): return lax.ppermute(x, axis, [(i, (i + by) % size) for i in range(size)])]
    all_to_all x1, starting transfers between devices: 14 us -> 12 us  [per_device(): squares = lax.all_to_all(squares, ('y', 'dp'), 0, 0, tiled=True)]
    pallas_call x1, Pallas kernels: 3.33 us -> 5.19 us  [per_device(): pl.pallas_call(functools.partial(backward_kernel, heads), out_shape=[shap...]
    all_to_all x1, starting transfers between devices: 5.01 us -> 3.49 us  [per_device(): pieces = lax.all_to_all(pair, 'z', 0, 0, tiled=True)]
where the time goes in v13:
time: 135 us
  starting transfers between devices  64 us (47%)
  waiting for transfers between devices  29.4 us (22%)
  blocking collectives  23.8 us (18%)
  Pallas kernels  14.3 us (11%)
  other arithmetic  1.54 us (1%)
  local copies, waits for them, and re-layouts  1.51 us (1%)
    ppermute x10, starting transfers between devices, turn(): return lax.ppermute(x, axis, [(i, (i + by) % size) for i in range(size)])  38.4 us
    all_to_all x1, blocking collectives, per_device(): squares = lax.all_to_all(squares, ('z', 'core'), 0, 0, tiled=True)  14.3 us
    ppermute x10, waiting for transfers between devices, turn(): return lax.ppermute(x, axis, [(i, (i + by) % size) for i in range(size)])  12.5 us
    all_to_all x1, starting transfers between devices, per_device(): squares = lax.all_to_all(squares, ('y', 'dp'), 0, 0, tiled=True)  12 us
    all_to_all x1, starting transfers between devices, per_device(): mine = lax.all_to_all(copies, 'z', 0, 0, tiled=True)  10.2 us
    all_to_all x1, blocking collectives, per_device(): stats = lax.all_to_all(stats, 'y', 0, 0, tiled=True)  9.43 us
    all_to_all x1, waiting for transfers between devices, per_device(): mine = lax.all_to_all(copies, 'z', 0, 0, tiled=True)  9.15 us
    all_to_all x1, waiting for transfers between devices, per_device(): squares = lax.all_to_all(squares, ('y', 'dp'), 0, 0, tiled=True)  7.76 us
  transfers between devices with their start and end apart: 13, of which 6 were waited for; matrix products, arithmetic and copies ran while one was open for 1% of the time, Pallas kernels for 2%

profile of v13, /device:TPU:1, one launch (start us, length us, event | category | flops | bytes accessed | tf_op | source)
XLA Modules:
  0.0 135.5 jit_solution(13222611276135705138)
XLA Ops:
  0.6 0.0 copy-start.3
  0.6 0.0 copy-start.2
  0.7 1.7 %shard_map.85 = bf16[1,128,1024]{2,1,0:T(8,128)(2,1)} custom-call(bf16[1,128,512]{2,1,0:T(8,128)(2,1)} %left.3, bf16[1,128,512]{2,1,0:T(8,128)(2,1)} %right.3), custom_call_target="tpu_custom_call" | custom-call | tf_op jit(solution)/shard_map/pallas_call | solution.py:337
  2.4 8.3 %collective-permute-start.1 = (bf16[1,128,1024]{2,1,0:T(8,128)(2,1)}, bf16[1,128,1024]{2,1,0:T(8,128)(2,1)S(1)}, u32[]{:S(2)}, u32[]{:S(2)}) collective-permute-start(bf16[1,128,1024]{2,1,0:T(8,128)(2,1)} %shard_map.85), channel_id=1, source_target_pairs={{0,32},{16,48},{32,0},{48,16},{1,33},{17,49},{33,1},{49,17},{2,34}... | collective-permute-start | bytes 786440 | tf_op jit(solution)/shard_map/ppermute | solution.py:323
  10.6 0.0 copy-done.3
  10.7 0.0 copy-done.2
  10.7 0.9 shard_map.86
  11.5 0.0 copy-start
  11.5 0.0 copy-start.1
  11.5 10.2 %all-to-all-start = ((bf16[8,128,256]{2,1,0:T(8,128)(2,1)}), bf16[8,128,256]{2,1,0:T(8,128)(2,1)S(1)}, u32[]{:S(2)}, u32[]{:S(2)}) async-start(bf16[8,128,256]{2,1,0:T(8,128)(2,1)} %shard_map.86), calls=%async_computation | async-start | bytes 1048576 | tf_op jit(solution)/shard_map/all_to_all | solution.py:359
  21.7 0.0 copy-done
  21.7 0.0 copy-done.1
  21.7 0.1 shard_map.84
  21.8 2.0 %collective-permute-start = (bf16[1,128,1024]{2,1,0:T(8,128)(2,1)S(1)}, bf16[1,128,1024]{2,1,0:T(8,128)(2,1)S(1)}, u32[]{:S(2)}, u32[]{:S(2)}) collective-permute-start(bf16[1,128,1024]{2,1,0:T(8,128)(2,1)S(1)} %get-tuple-element.27), channel_id=1, source_target_pairs={{0,48},{16,0},{32,16},{48,32},{1,49},{17,1},{33,17},{49,33},{2,50}... | collective-permute-start | bytes 786440 | tf_op jit(solution)/shard_map/ppermute | solution.py:323
  23.8 4.2 %collective-permute-start.2 = (bf16[1,128,1024]{2,1,0:T(8,128)(2,1)S(1)}, bf16[1,128,1024]{2,1,0:T(8,128)(2,1)S(1)}, u32[]{:S(2)}, u32[]{:S(2)}) collective-permute-start(bf16[1,128,1024]{2,1,0:T(8,128)(2,1)S(1)} %get-tuple-element.28), channel_id=1, source_target_pairs={{0,16},{16,32},{32,48},{48,0},{1,17},{17,33},{33,49},{49,1},{2,18}... | collective-permute-start | bytes 786440 | tf_op jit(solution)/shard_map/ppermute | solution.py:323
  28.0 0.0 copy-start.4
  28.0 0.6 copy-done.4
  28.7 0.1 eq.26
  28.8 0.1 eq.25
  28.9 0.1 add.218
  28.9 0.1 add.215
  29.0 0.2 select_reduce_fusion
  29.2 0.1 reshape.443
  29.3 0.1 reduce_min.11
  29.4 0.1 select_reduce_fusion.1
  29.6 9.1 %all-to-all-done.mine = bf16[8,128,256]{2,1,0:T(8,128)(2,1)S(1)} async-done(((bf16[8,128,256]{2,1,0:T(8,128)(2,1)}), bf16[8,128,256]{2,1,0:T(8,128)(2,1)S(1)}, u32[]{:S(2)}, u32[]{:S(2)}) %all-to-all-start) | async-done | bytes 524320 | tf_op jit(solution)/shard_map/all_to_all | solution.py:359
  38.7 3.3 %collective-permute-start.3 = (bf16[8,128,256]{2,1,0:T(8,128)(2,1)S(1)}, bf16[8,128,256]{2,1,0:T(8,128)(2,1)S(1)}, u32[]{:S(2)}, u32[]{:S(2)}) collective-permute-start(bf16[8,128,256]{2,1,0:T(8,128)(2,1)S(1)} %all-to-all-done.mine), channel_id=1, source_target_pairs={{0,8},{8,0},{1,9},{9,1},{2,10},{10,2},{3,11},{11,3},{4,12},{12,4},... | collective-permute-start | bytes 1572872 | tf_op jit(solution)/shard_map/ppermute | solution.py:323
  42.1 0.1 copy.13
  42.2 0.1 reshape.444
  42.3 0.1 add.220
  42.4 0.1 copy.14
  42.4 0.1 reshape.445
  42.5 0.1 pad_add_fusion.2.info
  42.6 1.0 collective-permute-done.3.other
  43.6 0.3 shard_map.87
  43.9 0.0 collective-permute-done.1.a2
  43.9 0.0 collective-permute-done.a1
  43.9 0.0 collective-permute-done.2.a3
  44.0 3.7 %shard_map.88 = (f32[2,128,1024]{2,1,0:T(8,128)S(1)}, f32[4,3,8,256]{3,2,1,0:T(8,128)S(1)}) custom-call(s32[34]{0:T(128)S(1)} %pad_add_fusion.2.info, bf16[1,128,1024]{2,1,0:T(8,128)(2,1)S(1)} %get-tuple-element.26.a0, bf16[1,128,1024]{2,1,0:T(8,128)(2,1)S(1)} %collective-permute-done.a1, bf16[1,128,1024]{2,1,0:T(8,128)(2,1)S(1)} %collective-permute-done.1.a2, ...), custom_call_target="tpu_custom_call" | custom-call | tf_op jit(solution)/shard_map/pallas_call | solution.py:375
  47.7 9.4 %all_to_all.25.stats = f32[4,3,8,256]{3,2,1,0:T(8,128)S(1)} all-to-all(f32[4,3,8,256]{3,2,1,0:T(8,128)S(1)} %get-tuple-element.32), channel_id=1, replica_groups=mesh['z'=8,'y'=4,'core'=2,'dp'=8] {'y'}, dimensions={0} | all-to-all | bytes 196608 | tf_op jit(solution)/shard_map/all_to_all | solution.py:383
  57.1 5.2 %shard_map.89 = (bf16[1,128,512]{2,1,0:T(8,128)(2,1)S(1)}, bf16[1,128,512]{2,1,0:T(8,128)(2,1)S(1)}, bf16[1,128,512]{2,1,0:T(8,128)(2,1)S(1)}, bf16[1,128,512]{2...) custom-call(s32[34]{0:T(128)S(1)} %pad_add_fusion.2.info, ...), custom_call_target="tpu_custom_call" | custom-call | tf_op jit(solution)/shard_map/pallas_call | solution.py:384
  62.3 3.9 %collective-permute-start.9 = (bf16[8,128,256]{2,1,0:T(8,128)(2,1)S(1)}, bf16[8,128,256]{2,1,0:T(8,128)(2,1)S(1)}, u32[]{:S(2)}, u32[]{:S(2)}) collective-permute-start(bf16[8,128,256]{2,1,0:T(8,128)(2,1)S(1)} %get-tuple-element.41), channel_id=1, source_target_pairs={{0,8},{8,0},{1,9},{9,1},{2,10},{10,2},{3,11},{11,3},{4,12},{12,4},... | collective-permute-start | bytes 1572872 | tf_op jit(solution)/shard_map/ppermute | solution.py:323
  66.2 1.5 %collective-permute-done.9 = bf16[8,128,256]{2,1,0:T(8,128)(2,1)S(1)} collective-permute-done((bf16[8,128,256]{2,1,0:T(8,128)(2,1)S(1)}, bf16[8,128,256]{2,1,0:T(8,128)(2,1)S(1)}, u32[]{:S(2)}, u32[]{:S(2)}) %collective-permute-start.9) | collective-permute-done | bytes 524320 | tf_op jit(solution)/shard_map/ppermute | solution.py:323
  67.7 0.9 add_convert_fusion
  68.7 3.5 %all-to-all-start.2 = ((bf16[8,128,256]{2,1,0:T(8,128)(2,1)}), bf16[8,128,256]{2,1,0:T(8,128)(2,1)S(1)}, u32[]{:S(2)}, u32[]{:S(2)}) async-start(bf16[8,128,256]{2,1,0:T(8,128)(2,1)} %add_convert_fusion), calls=%async_computation.2 | async-start | bytes 1048576 | tf_op jit(solution)/shard_map/all_to_all | solution.py:402
  72.2 1.9 %collective-permute-start.6 = (bf16[1,128,1024]{2,1,0:T(8,128)(2,1)S(1)}, bf16[1,128,1024]{2,1,0:T(8,128)(2,1)S(1)}, u32[]{:S(2)}, u32[]{:S(2)}) collective-permute-start(bf16[1,128,1024]{2,1,0:T(8,128)(2,1)S(1)} %get-tuple-element.36), channel_id=1, source_target_pairs={{0,32},{16,48},{32,0},{48,16},{1,33},{17,49},{33,1},{49,17},{2,34}... | collective-permute-start | bytes 786440 | tf_op jit(solution)/shard_map/ppermute | solution.py:323
  74.1 4.1 %collective-permute-start.7 = (bf16[1,128,512]{2,1,0:T(8,128)(2,1)S(1)}, bf16[1,128,512]{2,1,0:T(8,128)(2,1)S(1)}, u32[]{:S(2)}, u32[]{:S(2)}) collective-permute-start(bf16[1,128,512]{2,1,0:T(8,128)(2,1)S(1)} %get-tuple-element.38), channel_id=1, source_target_pairs={{0,16},{16,32},{32,48},{48,0},{1,17},{17,33},{33,49},{49,1},{2,18}... | collective-permute-start | bytes 393224 | tf_op jit(solution)/shard_map/ppermute | solution.py:323
  78.2 3.3 %collective-permute-start.8 = (bf16[1,128,512]{2,1,0:T(8,128)(2,1)S(1)}, bf16[1,128,512]{2,1,0:T(8,128)(2,1)S(1)}, u32[]{:S(2)}, u32[]{:S(2)}) collective-permute-start(bf16[1,128,512]{2,1,0:T(8,128)(2,1)S(1)} %get-tuple-element.39), channel_id=1, source_target_pairs={{0,48},{16,0},{32,16},{48,32},{1,49},{17,1},{33,17},{49,33},{2,50}... | collective-permute-start | bytes 393224 | tf_op jit(solution)/shard_map/ppermute | solution.py:323
  81.5 4.0 %collective-permute-start.4 = (bf16[1,128,512]{2,1,0:T(8,128)(2,1)S(1)}, bf16[1,128,512]{2,1,0:T(8,128)(2,1)S(1)}, u32[]{:S(2)}, u32[]{:S(2)}) collective-permute-start(bf16[1,128,512]{2,1,0:T(8,128)(2,1)S(1)} %get-tuple-element.34), channel_id=1, source_target_pairs={{0,16},{16,32},{32,48},{48,0},{1,17},{17,33},{33,49},{49,1},{2,18}... | collective-permute-start | bytes 393224 | tf_op jit(solution)/shard_map/ppermute | solution.py:323
  85.5 3.4 %collective-permute-start.5 = (bf16[1,128,512]{2,1,0:T(8,128)(2,1)S(1)}, bf16[1,128,512]{2,1,0:T(8,128)(2,1)S(1)}, u32[]{:S(2)}, u32[]{:S(2)}) collective-permute-start(bf16[1,128,512]{2,1,0:T(8,128)(2,1)S(1)} %get-tuple-element.35), channel_id=1, source_target_pairs={{0,48},{16,0},{32,16},{48,32},{1,49},{17,1},{33,17},{49,33},{2,50}... | collective-permute-start | bytes 393224 | tf_op jit(solution)/shard_map/ppermute | solution.py:323
  88.9 2.7 %collective-permute-done.7.o1 = bf16[1,128,512]{2,1,0:T(8,128)(2,1)S(1)} collective-permute-done((bf16[1,128,512]{2,1,0:T(8,128)(2,1)S(1)}, bf16[1,128,512]{2,1,0:T(8,128)(2,1)S(1)}, u32[]{:S(2)}, u32[]{:S(2)}) %collective-permute-start.7) | collective-permute-done | bytes 131104 | tf_op jit(solution)/shard_map/ppermute | solution.py:323
  91.6 7.3 %collective-permute-done.8.o3 = bf16[1,128,512]{2,1,0:T(8,128)(2,1)S(1)} collective-permute-done((bf16[1,128,512]{2,1,0:T(8,128)(2,1)S(1)}, bf16[1,128,512]{2,1,0:T(8,128)(2,1)S(1)}, u32[]{:S(2)}, u32[]{:S(2)}) %collective-permute-start.8) | collective-permute-done | bytes 131104 | tf_op jit(solution)/shard_map/ppermute | solution.py:323
  98.9 0.0 collective-permute-done.6.a3.o2
  98.9 0.0 all-to-all-done.2.dkv
  98.9 0.3 shard_map.91
  99.3 14.3 %all_to_all.26.parts = f32[16,1,128]{2,1,0:T(1,128)S(1)} all-to-all(f32[16,1,128]{2,1,0:T(1,128)S(1)} %get-tuple-element.42), channel_id=1, replica_groups=mesh['z'=8,'y'=4,'core'=2,'dp'=8] {'z','core'}, dimensions={0} | all-to-all | bytes 16384 | tf_op jit(solution)/shard_map/all_to_all | solution.py:414
  113.6 0.6 shard_map.92
  114.2 12.0 %all-to-all-start.4 = ((f32[32,1,128]{2,1,0:T(1,128)}), f32[32,1,128]{2,1,0:T(1,128)S(1)}, u32[]{:S(2)}, u32[]{:S(2)}) async-start(f32[32,1,128]{2,1,0:T(1,128)} %shard_map.92), calls=%async_computation.4 | async-start | bytes 32768 | tf_op jit(solution)/shard_map/all_to_all | solution.py:424
  126.2 0.0 collective-permute-done.4.a1
  126.2 0.0 collective-permute-done.5.a2
  126.2 0.7 shard_map.90
  127.0 7.8 %all-to-all-done.4.sums = f32[32,1,128]{2,1,0:T(1,128)S(1)} async-done(((f32[32,1,128]{2,1,0:T(1,128)}), f32[32,1,128]{2,1,0:T(1,128)S(1)}, u32[]{:S(2)}, u32[]{:S(2)}) %all-to-all-start.4) | async-done | bytes 16416 | tf_op jit(solution)/shard_map/all_to_all | solution.py:424
  134.7 0.7 shard_map.93
  (10 shorter events, 0.1 us)
Async XLA Ops:
  0.6 10.0 %copy-start.3 = (bf16[1,128,128]{2,1,0:T(8,128)(2,1)S(1)}, bf16[1,128,128]{2,1,0:T(8,128)(2,1)}, u32[]{:S(2)}) copy-start(bf16[1,128,128]{2,1,0:T(8,128)(2,1)} %values.1) | copy-start | bytes 98308
  0.6 10.0 %copy-start.2 = (bf16[1,128,128]{2,1,0:T(8,128)(2,1)S(1)}, bf16[1,128,128]{2,1,0:T(8,128)(2,1)}, u32[]{:S(2)}) copy-start(bf16[1,128,128]{2,1,0:T(8,128)(2,1)} %keys.1) | copy-start | bytes 98308
  2.4 41.6 %collective-permute-start.1 = (bf16[1,128,1024]{2,1,0:T(8,128)(2,1)}, bf16[1,128,1024]{2,1,0:T(8,128)(2,1)S(1)}, u32[]{:S(2)}, u32[]{:S(2)}) collective-permute-start(bf16[1,128,1024]{2,1,0:T(8,128)(2,1)} %shard_map.85), channel_id=1, source_target_pairs={{0,32},{16,48},{32,0},{48,16},{1,33},{17,49},{33,1},{49,17},{2,34}... | collective-permute-start | bytes 786440 | tf_op jit(solution)/shard_map/ppermute | solution.py:323
  11.5 10.2 %copy-start = (bf16[1,128,512]{2,1,0:T(8,128)(2,1)S(1)}, bf16[1,128,512]{2,1,0:T(8,128)(2,1)}, u32[]{:S(2)}) copy-start(bf16[1,128,512]{2,1,0:T(8,128)(2,1)} %left.3) | copy-start | bytes 393220
  11.5 10.2 %copy-start.1 = (bf16[1,128,512]{2,1,0:T(8,128)(2,1)S(1)}, bf16[1,128,512]{2,1,0:T(8,128)(2,1)}, u32[]{:S(2)}) copy-start(bf16[1,128,512]{2,1,0:T(8,128)(2,1)} %right.3) | copy-start | bytes 393220
  11.5 27.2 %all-to-all-start = ((bf16[8,128,256]{2,1,0:T(8,128)(2,1)}), bf16[8,128,256]{2,1,0:T(8,128)(2,1)S(1)}, u32[]{:S(2)}, u32[]{:S(2)}) async-start(bf16[8,128,256]{2,1,0:T(8,128)(2,1)} %shard_map.86), calls=%async_computation | async-start | bytes 1048576 | tf_op jit(solution)/shard_map/all_to_all | solution.py:359
  21.8 22.2 %collective-permute-start = (bf16[1,128,1024]{2,1,0:T(8,128)(2,1)S(1)}, bf16[1,128,1024]{2,1,0:T(8,128)(2,1)S(1)}, u32[]{:S(2)}, u32[]{:S(2)}) collective-permute-start(bf16[1,128,1024]{2,1,0:T(8,128)(2,1)S(1)} %get-tuple-element.27), channel_id=1, source_target_pairs={{0,48},{16,0},{32,16},{48,32},{1,49},{17,1},{33,17},{49,33},{2,50}... | collective-permute-start | bytes 786440 | tf_op jit(solution)/shard_map/ppermute | solution.py:323
  23.8 20.2 %collective-permute-start.2 = (bf16[1,128,1024]{2,1,0:T(8,128)(2,1)S(1)}, bf16[1,128,1024]{2,1,0:T(8,128)(2,1)S(1)}, u32[]{:S(2)}, u32[]{:S(2)}) collective-permute-start(bf16[1,128,1024]{2,1,0:T(8,128)(2,1)S(1)} %get-tuple-element.28), channel_id=1, source_target_pairs={{0,16},{16,32},{32,48},{48,0},{1,17},{17,33},{33,49},{49,1},{2,18}... | collective-permute-start | bytes 786440 | tf_op jit(solution)/shard_map/ppermute | solution.py:323
  28.0 0.7 copy-start.4
  38.7 4.8 %collective-permute-start.3 = (bf16[8,128,256]{2,1,0:T(8,128)(2,1)S(1)}, bf16[8,128,256]{2,1,0:T(8,128)(2,1)S(1)}, u32[]{:S(2)}, u32[]{:S(2)}) collective-permute-start(bf16[8,128,256]{2,1,0:T(8,128)(2,1)S(1)} %all-to-all-done.mine), channel_id=1, source_target_pairs={{0,8},{8,0},{1,9},{9,1},{2,10},{10,2},{3,11},{11,3},{4,12},{12,4},... | collective-permute-start | bytes 1572872 | tf_op jit(solution)/shard_map/ppermute | solution.py:323
  62.3 5.4 %collective-permute-start.9 = (bf16[8,128,256]{2,1,0:T(8,128)(2,1)S(1)}, bf16[8,128,256]{2,1,0:T(8,128)(2,1)S(1)}, u32[]{:S(2)}, u32[]{:S(2)}) collective-permute-start(bf16[8,128,256]{2,1,0:T(8,128)(2,1)S(1)} %get-tuple-element.41), channel_id=1, source_target_pairs={{0,8},{8,0},{1,9},{9,1},{2,10},{10,2},{3,11},{11,3},{4,12},{12,4},... | collective-permute-start | bytes 1572872 | tf_op jit(solution)/shard_map/ppermute | solution.py:323
  68.7 30.3 %all-to-all-start.2 = ((bf16[8,128,256]{2,1,0:T(8,128)(2,1)}), bf16[8,128,256]{2,1,0:T(8,128)(2,1)S(1)}, u32[]{:S(2)}, u32[]{:S(2)}) async-start(bf16[8,128,256]{2,1,0:T(8,128)(2,1)} %add_convert_fusion), calls=%async_computation.2 | async-start | bytes 1048576 | tf_op jit(solution)/shard_map/all_to_all | solution.py:402
  72.2 26.8 %collective-permute-start.6 = (bf16[1,128,1024]{2,1,0:T(8,128)(2,1)S(1)}, bf16[1,128,1024]{2,1,0:T(8,128)(2,1)S(1)}, u32[]{:S(2)}, u32[]{:S(2)}) collective-permute-start(bf16[1,128,1024]{2,1,0:T(8,128)(2,1)S(1)} %get-tuple-element.36), channel_id=1, source_target_pairs={{0,32},{16,48},{32,0},{48,16},{1,33},{17,49},{33,1},{49,17},{2,34}... | collective-permute-start | bytes 786440 | tf_op jit(solution)/shard_map/ppermute | solution.py:323
  74.1 17.5 %collective-permute-start.7 = (bf16[1,128,512]{2,1,0:T(8,128)(2,1)S(1)}, bf16[1,128,512]{2,1,0:T(8,128)(2,1)S(1)}, u32[]{:S(2)}, u32[]{:S(2)}) collective-permute-start(bf16[1,128,512]{2,1,0:T(8,128)(2,1)S(1)} %get-tuple-element.38), channel_id=1, source_target_pairs={{0,16},{16,32},{32,48},{48,0},{1,17},{17,33},{33,49},{49,1},{2,18}... | collective-permute-start | bytes 393224 | tf_op jit(solution)/shard_map/ppermute | solution.py:323
  78.2 20.7 %collective-permute-start.8 = (bf16[1,128,512]{2,1,0:T(8,128)(2,1)S(1)}, bf16[1,128,512]{2,1,0:T(8,128)(2,1)S(1)}, u32[]{:S(2)}, u32[]{:S(2)}) collective-permute-start(bf16[1,128,512]{2,1,0:T(8,128)(2,1)S(1)} %get-tuple-element.39), channel_id=1, source_target_pairs={{0,48},{16,0},{32,16},{48,32},{1,49},{17,1},{33,17},{49,33},{2,50}... | collective-permute-start | bytes 393224 | tf_op jit(solution)/shard_map/ppermute | solution.py:323
  81.5 44.7 %collective-permute-start.4 = (bf16[1,128,512]{2,1,0:T(8,128)(2,1)S(1)}, bf16[1,128,512]{2,1,0:T(8,128)(2,1)S(1)}, u32[]{:S(2)}, u32[]{:S(2)}) collective-permute-start(bf16[1,128,512]{2,1,0:T(8,128)(2,1)S(1)} %get-tuple-element.34), channel_id=1, source_target_pairs={{0,16},{16,32},{32,48},{48,0},{1,17},{17,33},{33,49},{49,1},{2,18}... | collective-permute-start | bytes 393224 | tf_op jit(solution)/shard_map/ppermute | solution.py:323
  85.5 40.7 %collective-permute-start.5 = (bf16[1,128,512]{2,1,0:T(8,128)(2,1)S(1)}, bf16[1,128,512]{2,1,0:T(8,128)(2,1)S(1)}, u32[]{:S(2)}, u32[]{:S(2)}) collective-permute-start(bf16[1,128,512]{2,1,0:T(8,128)(2,1)S(1)} %get-tuple-element.35), channel_id=1, source_target_pairs={{0,48},{16,0},{32,16},{48,32},{1,49},{17,1},{33,17},{49,33},{2,50}... | collective-permute-start | bytes 393224 | tf_op jit(solution)/shard_map/ppermute | solution.py:323
  114.2 20.5 %all-to-all-start.4 = ((f32[32,1,128]{2,1,0:T(1,128)}), f32[32,1,128]{2,1,0:T(1,128)S(1)}, u32[]{:S(2)}, u32[]{:S(2)}) async-start(f32[32,1,128]{2,1,0:T(1,128)} %shard_map.92), calls=%async_computation.4 | async-start | bytes 32768 | tf_op jit(solution)/shard_map/all_to_all | solution.py:424
